TPU v7x, 256 devices: a whole 4x4x8 slice. The times are simulated.
256 devices in a mesh: cell: 32 (over x, y, core), gene: 8 (over z).
Axes of the slice: x: 4, y: 4, z: 8, core: 2. Of those that a mesh axis runs over, the one named last changes fastest.
Arguments:
- counts: int32 [3072, 32768], P('gene', 'cell'), may hold values from 0 to 11
- batch_id: int32 [32768], P('cell'), may hold values from 0 to 63
- live_cells: int32 [32], P('cell'), may hold values from 256 to 1024, as said below
- knot_bin: int32 [32768], P('cell'), may hold values from 0 to 14
- depth_frac: float32 [32768], P('cell'), may hold values from 0 to 1
- cell_covariates: float32 [16, 32768], P(None, 'cell'), may hold values from -3 to 3
- coefficients: float32 [3072, 32], P('gene'), may hold values from -1.2 to 1.2
- batch_effect: float32 [3072, 64], P('gene'), may hold values from -1.8 to 1.8
- factors: bfloat16 [32768, 64], P('cell'), may hold values from -4 to 4
- loadings: bfloat16 [3072, 64], P('gene'), may hold values from -0.19921875 to 0.19921875
Outputs:
- beta_step: float32 [3072, 32], P('gene')
- factor_step: float32 [32768, 64], P('cell')
- loading_score: float32 [3072, 64], P('gene')
Inputs may be any that keep to these rules, and one draw needn't show every extreme that they name: `live_cells`: each index of the cell axis has its live cells in its first slots, at least 256 of them; some index is full in every draw.
All inputs are finite; a program needn't handle non-finite values.
Results may differ from a plain program's by a relative error of at most 0.0003.
Values sent between devices are 32-bit elements; how exact they have to be, the bound alone decides.
No kernel may reach another device: no remote copies, remote signals or barrier semaphores. Data moves between devices by JAX's collectives and lax.ppermute only.
A program may use at most 64 MiB of HBM per device.

v0:
```python
import jax
import jax.numpy as jnp
from jax import lax
from jax.sharding import PartitionSpec as P

GENES = 3072
SPL = 16
BATCHES = 64


ridge_weight = 1.0


def sent_to_all(value, axis):
    copies = jnp.broadcast_to(value, (lax.axis_size(axis), *value.shape))
    return lax.all_to_all(copies, axis, split_axis=0, concat_axis=0, tiled=True)


def of_everyone(value, axis):
    everything = sent_to_all(value, axis)
    return jnp.sum(everything, axis=0)


def in_blocks(value, dim, count):
    shape = value.shape
    pieces = value.reshape(*shape[:dim], count, shape[dim] // count, *shape[dim + 1 :])
    return jnp.moveaxis(pieces, dim, 0)


def summed_on_arrival(value, axis, dim):
    pieces = in_blocks(value, dim, lax.axis_size(axis))
    arrived = lax.all_to_all(pieces, axis, split_axis=0, concat_axis=0, tiled=True)
    return arrived.sum(axis=0)


def in_one_piece(arrays, axis, dim, along):
    widths = [a.shape[along] for a in arrays]
    both = jnp.concatenate(arrays, axis=along)
    result = summed_on_arrival(both, axis, dim)
    return tuple(jnp.split(result, [sum(widths[:k]) for k in range(1, len(widths))], axis=along))


def joined_along(pieces, dim):
    pieces = jnp.moveaxis(pieces, 0, dim)
    shape = pieces.shape
    return pieces.reshape(*shape[:dim], shape[dim] * shape[dim + 1], *shape[dim + 2 :])


def gathered_copies(value, axis, dim):
    pieces = sent_to_all(value, axis)
    return joined_along(pieces, dim)


def packed_total(arrays, axis):
    ravelled, at, gathered = (jnp.concatenate([a.reshape(-1) for a in arrays]), 0, [])
    running = lax.psum(ravelled, axis)
    for a in arrays:
        gathered.append(running[at : at + a.size].reshape(a.shape))
        at += a.size
    return tuple(gathered)


def together(arrays, axis):
    ravelled, at, gathered = (jnp.concatenate([a.reshape(-1) for a in arrays]), 0, [])
    running = of_everyone(ravelled, axis)
    for a in arrays:
        gathered.append(running[at : at + a.size].reshape(a.shape))
        at += a.size
    return tuple(gathered)


def design_rows(knot_bin, depth_frac, cell_covariates):
    levels = jnp.arange(SPL, dtype=jnp.int32)[:, None]
    fraction = depth_frac[None, :]
    hat_basis = jnp.where(levels == knot_bin[None, :], 1.0 - fraction, 0.0)
    hat_basis = hat_basis + jnp.where(levels == knot_bin[None, :] + 1, fraction, 0.0)
    return jnp.concatenate([hat_basis, cell_covariates], axis=0)


def newton_solve(gram_flat, score):
    columns = score.shape[-1]
    identity = jnp.eye(columns, dtype=gram_flat.dtype)
    system = gram_flat.reshape(-1, columns, columns) + ridge_weight * identity
    factor_lower = jnp.linalg.cholesky(system)
    middle = jax.scipy.linalg.solve_triangular(factor_lower, score[..., None], lower=True)
    return jax.scipy.linalg.solve_triangular(factor_lower, middle, lower=True, trans=1)[..., 0]


def local(
    counts,
    batch_id,
    live_cells,
    knot_bin,
    depth_frac,
    cell_covariates,
    coefficients,
    batch_effect,
    factors,
    loadings,
):
    highest = lax.Precision.HIGHEST
    contract = (((1,), (1,)), ((), ()))
    observed = counts.astype(jnp.float32)
    totals = of_everyone(jnp.sum(observed, axis=0), "gene")
    offset = jnp.log((1.0 + totals) / GENES)
    slot_count = observed.shape[1]
    live_mask = (jnp.arange(slot_count, dtype=jnp.int32) < live_cells[0]).astype(jnp.float32)
    design = design_rows(knot_bin, depth_frac, cell_covariates)
    columns = design.shape[0]
    onehot = (jnp.arange(BATCHES, dtype=jnp.int32)[:, None] == batch_id[None, :]).astype(
        jnp.float32
    )
    stacked = jnp.concatenate([design, onehot], axis=0)
    linear = jnp.dot(
        jnp.concatenate([coefficients, batch_effect], axis=1), stacked, precision=highest
    )
    latent = lax.dot_general(loadings, factors, contract, preferred_element_type=jnp.float32)
    linear_pred = offset[None, :] + linear + latent
    expected = jnp.exp(linear_pred)
    weight = expected * live_mask
    residual = (observed - expected) * live_mask
    pairs = (design[:, None, :] * design[None, :, :]).reshape(columns * columns, slot_count)
    gram_part = lax.dot_general(weight, pairs, contract, precision=highest)
    score_part = lax.dot_general(residual, design, contract, precision=highest)
    gram_share, score_share = in_one_piece((gram_part, score_part), "cell", 0, 1)
    step_share = newton_solve(gram_share, score_share)
    beta_step = gathered_copies(step_share, "cell", 0)
    expected_next = jnp.exp(linear_pred + jnp.dot(beta_step, design, precision=highest))
    weight_next = expected_next * live_mask
    residual_next = (observed - expected_next) * live_mask
    factors_wide = factors.astype(jnp.float32)
    loads_wide = loadings.astype(jnp.float32)
    grad_load = jnp.dot(residual_next, factors_wide, precision=highest)
    curv_load = jnp.dot(weight_next, factors_wide * factors_wide, precision=highest)
    back = (((0,), (0,)), ((), ()))
    grad_fact = lax.dot_general(residual_next, loads_wide, back, precision=highest)
    curv_fact = lax.dot_general(weight_next, loads_wide * loads_wide, back, precision=highest)
    grad_load, curv_load = packed_total((grad_load, curv_load), "cell")
    grad_fact, curv_fact = together((grad_fact, curv_fact), "gene")
    factor_step = grad_fact / (curv_fact + 1.0)
    loading_score = grad_load / jnp.sqrt(curv_load + 1.0)
    return (beta_step, factor_step, loading_score)


def solution(mesh):
    placed = (
        P("gene", "cell"),
        P("cell"),
        P("cell"),
        P("cell"),
        P("cell"),
        P(None, "cell"),
        P("gene", None),
        P("gene", None),
        P("cell", None),
        P("gene", None),
    )
    return jax.shard_map(
        local,
        mesh=mesh,
        in_specs=placed,
        out_specs=(P("gene", None), P("cell", None), P("gene", None)),
        check_vma=False,
    )
```

profile of v0, /device:TPU:1, one launch (start us, length us, event | category | flops | bytes accessed | tf_op | source)
XLA Modules:
  0.0 307.1 jit_solution(11326244150568570992)
XLA Ops:
  7.2 1.6 convert_reduce_fusion
  8.8 0.6 broadcast_in_dim.28
  9.4 9.0 %all-to-all-start = ((f32[8,1,1024]{2,1,0:T(1,128)}), f32[8,1,1024]{2,1,0:T(1,128)S(1)}, u32[]{:S(2)}, u32[]{:S(2)}) async-start(f32[8,1,1024]{2,1,0:T(1,128)} %broadcast_in_dim.28), calls=%async_computation | async-start | bytes 65536 | tf_op jit(solution)/shard_map/all_to_all | solution.py:16
  19.2 2.5 broadcast_multiply_fusion
  21.7 1.4 fusion.18
  23.2 2.1 all-to-all-done
  25.4 0.4 add_add_fusion
  25.8 1.0 copy-done
  26.8 1.5 fusion
  28.3 0.3 copy-done.2
  28.6 5.4 %fusion.3 = f32[384,1024]{1,0:T(8,128)S(1)} fusion(f32[1024,1024]{1,0:T(8,128)S(1)} %bitcast.29, f32[384,1024]{1,0:T(8,128)S(1)} %add_add_fusion, f32[1024]{0:T(1024)S(1)} %fusion.43), kind=kOutput, calls=%fused_computation.7 | convolution fusion | flops 4832231424 | bytes 7344128 | tf_op jit(solution)/shard_map/dot_general | solution.py:123
  34.0 0.1 pad_maximum_fusion
  34.1 1.6 reshape.130
  35.7 9.2 %all-to-all-start.1 = ((f32[32,12,1056]{2,1,0:T(8,128)}), f32[32,12,1056]{2,1,0:T(8,128)}, u32[]{:S(2)}, u32[]{:S(2)}) async-start(f32[32,12,1056]{2,1,0:T(8,128)} %reshape.130), calls=%async_computation.1 | async-start | bytes 4718592 | tf_op jit(solution)/shard_map/all_to_all | solution.py:32
  45.1 31.1 %all-to-all-done.1 = f32[32,12,1056]{2,1,0:T(8,128)} async-done(((f32[32,12,1056]{2,1,0:T(8,128)}), f32[32,12,1056]{2,1,0:T(8,128)}, u32[]{:S(2)}, u32[]{:S(2)}) %all-to-all-start.1) | async-done | bytes 1622048 | tf_op jit(solution)/shard_map/all_to_all | solution.py:32
  76.2 1.8 reduce_sum.38
  78.1 0.1 copy.41
  78.2 0.1 copy.42
  78.4 35.2 %custom-call.11 = f32[12,32,32]{2,1,0:T(8,128)S(1)} custom-call(f32[12,32,32]{2,1,0:T(8,128)S(1)} %fusion.32), custom_call_target="Cholesky" | custom-call | tf_op jit(solution)/shard_map/jit(cholesky)/cholesky | solution.py:84
  113.6 0.1 compare_reduce_fusion
  113.8 29.6 %custom-call.12 = f32[12,1,32,32]{2,3,1,0:T(8,128)S(1)} custom-call(f32[12,1,32,32]{3,2,1,0:T(8,128)S(1)} %select_bitcast_fusion), custom_call_target="InvertDiagBlocksLowerTriangular" | custom-call | tf_op jit(solution)/shard_map/jit(_solve_triangular)/vmap()/triangular_solve | solution.py:86
  143.4 0.3 fusion.30
  143.7 0.4 fusion.28
  144.2 0.1 reshape.141
  144.3 11.1 %all_to_all.22 = f32[32,1,384]{2,1,0:T(1,128)S(1)} all-to-all(f32[32,1,384]{2,1,0:T(1,128)S(1)} %reshape.141), channel_id=1, replica_groups=mesh['cell'=32,'gene'=8] {'cell'}, dimensions={0} | all-to-all | bytes 98304 | tf_op jit(solution)/shard_map/all_to_all | solution.py:16
  155.5 0.5 broadcast.106
  156.0 0.8 reduce.8
  156.7 0.1 reshape.142
  156.9 2.9 add_exponential_fusion
  159.8 3.5 %fusion.8 = f32[1024,64]{1,0:T(8,128)} fusion(f32[384,1024]{1,0:T(8,128)S(1)} %add_exponential_fusion, f32[1024]{0:T(1024)S(1)} %fusion.43, bf16[384,64]{0,1:T(8,128)(2,1)S(1)} %copy-done.6), kind=kOutput, calls=%fused_computation.14 | convolution fusion | flops 302432256 | bytes 1888256 | tf_op jit(solution)/shard_map/dot_general | solution.py:137
  163.3 2.3 fusion.17
  165.6 1.9 reshape.133
  167.5 1.9 reshape.134
  169.3 1.1 pad_maximum_fusion.1
  170.4 4.1 %broadcast_in_dim.51 = f32[8,1,131072]{2,1,0:T(1,128)} broadcast(f32[131072]{0:T(1024)S(1)} %pad_maximum_fusion.1), dimensions={2} | broadcast | bytes 4718592 | tf_op jit(solution)/shard_map/broadcast_in_dim | solution.py:15
  174.5 4.5 %all-to-all-start.3 = ((f32[8,1,131072]{2,1,0:T(1,128)}), f32[8,1,131072]{2,1,0:T(1,128)}, u32[]{:S(2)}, u32[]{:S(2)}) async-start(f32[8,1,131072]{2,1,0:T(1,128)} %broadcast_in_dim.51), calls=%async_computation.3 | async-start | bytes 8388608 | tf_op jit(solution)/shard_map/all_to_all | solution.py:16
  179.1 0.3 all-reduce.2.cloned.1.call-start
  179.4 1.6 fusion.16
  181.0 1.0 reshape.135
  182.0 1.4 fusion.6
  183.5 0.7 pad_maximum_fusion.2
  184.2 0.7 copy.48
  184.9 107.2 %all-reduce.2.cloned.1.call-done = f32[49152]{0:T(1024)} async-done(((f32[49152]{0:T(1024)}), f32[49152]{0:T(1024)}) %all-reduce.2.cloned.1.call-update) | async-done | bytes 196624 | tf_op jit(solution)/shard_map/psum | solution.py:56
  292.1 1.0 fusion.37
  293.2 0.8 copy.50
  293.9 5.2 %reduce_sum.39 = f32[131072]{0:T(1024)S(1)} reduce(f32[8,1,131072]{2,1,0:T(1,128)} %all-to-all-done.3, f32[]{:T(128)} %constant.55.clone.1), dimensions={0,1}, to_apply=%region_5.6 | reduce | flops 917504 | bytes 4718596 | tf_op jit(solution)/shard_map/reduce_sum | solution.py:21
  299.2 0.1 div.30
  299.4 0.9 copy.49
  (50 shorter events, 0.8 us)
Async XLA Ops:
  7.2 11.9 %copy-start.10 = (s32[1024]{0:T(1024)S(1)}, s32[1024]{0:T(1024)}, u32[]{:S(2)}) copy-start(s32[1024]{0:T(1024)} %param.13) | copy-start | bytes 12292
  7.2 11.9 %copy-start.9 = (f32[1024]{0:T(1024)S(1)}, f32[1024]{0:T(1024)}, u32[]{:S(2)}) copy-start(f32[1024]{0:T(1024)} %param.14) | copy-start | bytes 12292
  7.2 11.9 %copy-start.11 = (s32[1024]{0:T(1024)S(1)}, s32[1024]{0:T(1024)}, u32[]{:S(2)}) copy-start(s32[1024]{0:T(1024)} %param.11) | copy-start | bytes 12292
  7.2 12.0 %copy-start.4 = (f32[16,1024]{1,0:T(8,128)S(1)}, f32[16,1024]{1,0:T(8,128)}, u32[]{:S(2)}) copy-start(f32[16,1024]{1,0:T(8,128)} %param.15) | copy-start | bytes 196612
  9.4 15.9 %all-to-all-start = ((f32[8,1,1024]{2,1,0:T(1,128)}), f32[8,1,1024]{2,1,0:T(1,128)S(1)}, u32[]{:S(2)}, u32[]{:S(2)}) async-start(f32[8,1,1024]{2,1,0:T(1,128)} %broadcast_in_dim.28), calls=%async_computation | async-start | bytes 65536 | tf_op jit(solution)/shard_map/all_to_all | solution.py:16
  19.2 2.5 copy-start.7
  19.2 2.5 copy-start.8
  21.7 3.7 %copy-start.3 = (bf16[1024,64]{0,1:T(8,128)(2,1)S(1)}, bf16[1024,64]{0,1:T(8,128)(2,1)}, u32[]{:S(2)}) copy-start(bf16[1024,64]{0,1:T(8,128)(2,1)} %param.18) | copy-start | bytes 393220
  21.7 3.7 %copy-start.5 = (bf16[384,64]{0,1:T(8,128)(2,1)S(1)}, bf16[384,64]{0,1:T(8,128)(2,1)}, u32[]{:S(2)}) copy-start(bf16[384,64]{0,1:T(8,128)(2,1)} %param.19) | copy-start | bytes 147460
  25.4 1.4 copy-start
  25.4 3.2 %copy-start.2 = (f32[32,32,1024]{2,1,0:T(8,128)S(1)}, f32[32,32,1024]{2,1,0:T(8,128)}, u32[]{:S(2)}) copy-start(f32[32,32,1024]{2,1,0:T(8,128)} %broadcast_multiply_fusion) | copy-start | bytes 12582916
  26.8 1.5 copy-start.1
  35.7 40.4 %all-to-all-start.1 = ((f32[32,12,1056]{2,1,0:T(8,128)}), f32[32,12,1056]{2,1,0:T(8,128)}, u32[]{:S(2)}, u32[]{:S(2)}) async-start(f32[32,12,1056]{2,1,0:T(8,128)} %reshape.130), calls=%async_computation.1 | async-start | bytes 4718592 | tf_op jit(solution)/shard_map/all_to_all | solution.py:32
  156.9 2.9 copy-start.6
  174.5 119.4 %all-to-all-start.3 = ((f32[8,1,131072]{2,1,0:T(1,128)}), f32[8,1,131072]{2,1,0:T(1,128)}, u32[]{:S(2)}, u32[]{:S(2)}) async-start(f32[8,1,131072]{2,1,0:T(1,128)} %broadcast_in_dim.51), calls=%async_computation.3 | async-start | bytes 8388608 | tf_op jit(solution)/shard_map/all_to_all | solution.py:16
  179.1 113.0 %all-reduce.2.cloned.1.call-start = ((), (), s32[]{:S(2)}) async-start(), calls=%async_computation.4 | async-start | bytes 393216 | tf_op jit(solution)/shard_map/psum | solution.py:56
Sparse Core Ops, SparseCore 0:
  184.3 107.7 all-reduce.1
where the time goes:
time: 308 us; the launch traced here: 307 us
  waiting for transfers between devices  140 us (45%)
  other arithmetic  79.9 us (26%)
  starting transfers between devices  23.1 us (8%)
  matrix products  21.1 us (7%)
  local copies, waits for them, and re-layouts  16.4 us (5%)
  between operations  15.1 us (5%)
  blocking collectives  11.1 us (4%)
    psum x1, waiting for transfers between devices, packed_total(): running = lax.psum(ravelled, axis)  107 us
    another operation x4, other arithmetic, newton_solve(): factor_lower = jnp.linalg.cholesky(system)  35.3 us
    all_to_all x1, waiting for transfers between devices, summed_on_arrival(): lax.all_to_all(pieces, axis, split_axis=0, concat_axis=0, tiled=True)  31.1 us
    another operation x3, other arithmetic, newton_solve(): jax.scipy.linalg.solve_triangular(factor_lower, middle, lower=True, trans=1)  29.7 us
    all_to_all x2, starting transfers between devices, sent_to_all(): return lax.all_to_all(copies, axis, split_axis=0, concat_axis=0, tiled=True)  13.6 us
    all_to_all x1, blocking collectives, sent_to_all(): return lax.all_to_all(copies, axis, split_axis=0, concat_axis=0, tiled=True)  11.1 us
    all_to_all x1, starting transfers between devices, summed_on_arrival(): lax.all_to_all(pieces, axis, split_axis=0, concat_axis=0, tiled=True)  9.24 us
  transfers between devices with their start and end apart: 4, of which 3 were waited for; matrix products, arithmetic and copies ran while one was open for 4% of the time, Pallas kernels for 0%

commit v1 on v0

v1 whole, which is shorter than its diff:
```python
import functools

import jax
import jax.numpy as jnp
from jax import lax
from jax.experimental import pallas as pl
from jax.experimental.pallas import tpu as pltpu
from jax.sharding import PartitionSpec as P

GENES = 3072
SPL = 16
COLS = 32
FACT = 64
CHUNK = 256
F32 = jnp.float32
BF16 = jnp.bfloat16
NN = (((1,), (0,)), ((), ()))
NT = (((1,), (1,)), ((), ()))
TN = (((0,), (0,)), ((), ()))
VMEM_LIMIT = 40 * 1024 * 1024


def dot(a, b, dims):
    return lax.dot_general(a, b, dims, preferred_element_type=F32)


def split2(x):
    hi = x.astype(BF16)
    return hi, (x - hi.astype(F32)).astype(BF16)


def split3(x):
    hi = x.astype(BF16)
    rest = x - hi.astype(F32)
    mid = rest.astype(BF16)
    return hi, mid, (rest - mid.astype(F32)).astype(BF16)


def full(shape):
    return pl.BlockSpec(shape, lambda c: (0,) * len(shape))


def lanes(rows, chunk=CHUNK):
    return pl.BlockSpec((rows, chunk), lambda c: (0, c))


def smem():
    return pl.BlockSpec(memory_space=pltpu.SMEM)


def params():
    return pltpu.CompilerParams(vmem_limit_bytes=VMEM_LIMIT)


def totals_kernel(counts_ref, out_ref, acc):
    step = pl.program_id(0)
    part = jnp.sum(counts_ref[...].astype(F32), axis=0, keepdims=True)

    @pl.when(step == 0)
    def _():
        acc[...] = part

    @pl.when(step > 0)
    def _():
        acc[...] += part

    @pl.when(step == pl.num_programs(0) - 1)
    def _():
        for i in range(8):
            row = acc[:, 128 * i : 128 * (i + 1)]
            out_ref[:, i : i + 1, :] = jnp.broadcast_to(row[None], (out_ref.shape[0], 1, 128))


def cell_totals(counts, peers):
    genes, cells = counts.shape
    return pl.pallas_call(
        totals_kernel,
        grid=(3,),
        in_specs=[pl.BlockSpec((genes // 3, cells), lambda c: (c, 0))],
        out_specs=full((peers, 8, 128)),
        out_shape=jax.ShapeDtypeStruct((peers, 8, 128), F32),
        scratch_shapes=[pltpu.VMEM((1, cells), F32)],
        compiler_params=params(),
        name="cell_totals",
    )(counts)


def prepare_kernel(
    knot_ref, frac_ref, batch_ref, cov_ref, coef_ref, shift_ref, load_ref, fact_ref,
    rest_ref, hi_ref, lo_ref, design_ref, left,
):
    @pl.when(pl.program_id(0) == 0)
    def _():
        c1, c2, c3 = split3(coef_ref[...])
        b1, b2, b3 = split3(shift_ref[...])
        left[...] = jnp.concatenate([c1, c1, c2, c2, c1, c3, b1, b2, b3, load_ref[...]], axis=0)

    knot, frac = knot_ref[...], frac_ref[...]
    width = knot.shape[1]
    cov = cov_ref[...]
    levels = lax.broadcasted_iota(jnp.int32, (SPL, width), 0)
    here, above = levels == knot, levels == knot + 1
    rest = 1.0 - frac
    hat = jnp.where(here, rest, 0.0) + jnp.where(above, frac, 0.0)
    d1, d2, d3 = split3(jnp.concatenate([hat, cov], axis=0))
    design_ref[...] = jnp.concatenate([d1, d2, d3], axis=0)
    batches = lax.broadcasted_iota(jnp.int32, (64, width), 0)
    onehot = (batches == batch_ref[...]).astype(F32).astype(BF16)
    right = jnp.concatenate(
        [d1, d2, d1, d2, d3, d1, onehot, onehot, onehot, fact_ref[...]], axis=0
    )
    rest_ref[...] = dot(left[...], right, TN)

    def put(at, value):
        hi, lo = split2(value)
        hi_ref[at : at + value.shape[0], :] = hi
        lo_ref[at : at + value.shape[0], :] = lo

    put(0, jnp.where(here, rest * rest, 0.0) + jnp.where(above, frac * frac, 0.0))
    put(16, jnp.where(here, rest * frac, 0.0))
    for p in range(SPL):
        put(32 + 16 * p, hat[p : p + 1, :] * cov)
    low, high = cov[:8], cov[8:]
    for i in range(0, 8, 2):
        put(288 + 8 * i, jnp.concatenate([low[i : i + 1] * low, low[i + 1 : i + 2] * low], axis=0))
        put(352 + 8 * i, jnp.concatenate([low[i : i + 1] * high, low[i + 1 : i + 2] * high], axis=0))
        put(416 + 8 * i, jnp.concatenate([high[i : i + 1] * high, high[i + 1 : i + 2] * high], axis=0))
    put(480, jnp.zeros((32, width), F32))


def prepare(knot, frac, batch, cov, coef, shift, load, fact):
    cells = knot.shape[1]
    genes = coef.shape[1]
    return pl.pallas_call(
        prepare_kernel,
        grid=(cells // CHUNK,),
        in_specs=[
            lanes(1), lanes(1), lanes(1), lanes(16),
            full((COLS, genes)), full((64, genes)), full((FACT, genes)), lanes(FACT),
        ],
        out_specs=[lanes(genes), lanes(512), lanes(512), lanes(96)],
        out_shape=[
            jax.ShapeDtypeStruct((genes, cells), F32),
            jax.ShapeDtypeStruct((512, cells), BF16),
            jax.ShapeDtypeStruct((512, cells), BF16),
            jax.ShapeDtypeStruct((96, cells), BF16),
        ],
        scratch_shapes=[pltpu.VMEM((448, genes), BF16)],
        compiler_params=params(),
        name="prepare",
    )(knot, frac, batch, cov, coef, shift, load, fact)


def gram_kernel(
    live_ref, tot_ref, rest_ref, counts_ref, hi_ref, lo_ref, design_ref,
    pred_ref, out_ref, offset, acc,
):
    step = pl.program_id(0)

    @pl.when(step == 0)
    def _():
        total = jnp.sum(tot_ref[...], axis=0)
        value = jnp.log((1.0 + total) / GENES)
        for i in range(8):
            offset[:, 128 * i : 128 * (i + 1)] = value[i : i + 1, :]

    at = pl.multiple_of(step * CHUNK, CHUNK)
    pred = rest_ref[...] + offset[:, pl.ds(at, CHUNK)]
    pred_ref[...] = pred
    expected = jnp.exp(pred)
    slot = lax.broadcasted_iota(jnp.int32, (1, CHUNK), 1) + at
    mask = (slot < live_ref[0]).astype(F32)
    weight = expected * mask
    residual = (counts_ref[...].astype(F32) - expected) * mask
    w1, w2 = split2(weight)
    r1, r2 = split2(residual)
    hi, lo = hi_ref[...], lo_ref[...]
    gram = dot(w1, hi, NT) + dot(w1, lo, NT) + dot(w2, hi, NT)
    blank = jnp.zeros((96, CHUNK), BF16)
    s1 = jnp.concatenate([blank, design_ref[:COLS, :]], axis=0)
    s2 = jnp.concatenate([blank, design_ref[COLS : 2 * COLS, :]], axis=0)
    score = dot(r1, s1, NT) + dot(r1, s2, NT) + dot(r2, s1, NT)

    @pl.when(step == 0)
    def _():
        acc[...] = jnp.zeros_like(acc)

    for t in range(4):
        part = gram[:, 128 * t : 128 * (t + 1)]
        acc[t] += part + score if t == 3 else part

    @pl.when(step == pl.num_programs(0) - 1)
    def _():
        for j in range(32):
            for t in range(4):
                out_ref[j, 12 * t : 12 * (t + 1), :] = acc[t, pl.ds(j, 12, stride=32), :]


def gram_sums(live, tot, rest, counts, hi, lo, design):
    genes, cells = counts.shape
    return pl.pallas_call(
        gram_kernel,
        grid=(cells // CHUNK,),
        in_specs=[
            smem(), full(tot.shape), lanes(genes), lanes(genes), lanes(512), lanes(512), lanes(96),
        ],
        out_specs=[lanes(genes), full((32, 48, 128))],
        out_shape=[
            jax.ShapeDtypeStruct((genes, cells), F32),
            jax.ShapeDtypeStruct((32, 48, 128), F32),
        ],
        scratch_shapes=[pltpu.VMEM((1, cells), F32), pltpu.VMEM((4, genes, 128), F32)],
        compiler_params=params(),
        name="gram_sums",
    )(live, tot, rest, counts, hi, lo, design)


def solve_kernel(parts_ref, out_ref, table):
    total = parts_ref[0]
    for j in range(1, 32):
        total = total + parts_ref[j]
    turned = jnp.concatenate([total, jnp.zeros((80, 128), F32)], axis=0).T
    for t in range(4):
        moved = turned if t == 0 else pltpu.roll(turned, 128 - 12 * t, axis=1)
        table[128 * t : 128 * (t + 1), :] = moved
    row16 = lax.broadcasted_iota(jnp.int32, (SPL, 128), 0)
    row32 = lax.broadcasted_iota(jnp.int32, (COLS, 128), 0)
    diag, near = table[0:16, :] + 1.0, table[16:32, :]
    below = pltpu.roll(near, 1, axis=0)
    system = []
    for j in range(SPL):
        top = jnp.where(row16 == j, diag, 0.0)
        top = jnp.where(row16 == j - 1, near, top)
        top = jnp.where(row16 == j + 1, below, top)
        system.append(jnp.concatenate([top, table[32 + 16 * j : 48 + 16 * j, :]], axis=0))
    for q in range(SPL):
        top = table[pl.ds(32 + q, 16, stride=16), :]
        if q < 8:
            first = table[288 + 8 * q : 296 + 8 * q, :]
            second = table[352 + 8 * q : 360 + 8 * q, :]
        else:
            first = table[pl.ds(344 + q, 8, stride=8), :]
            second = table[352 + 8 * q : 360 + 8 * q, :]
        column = jnp.concatenate([top, first, second], axis=0)
        system.append(jnp.where(row32 == 16 + q, column + 1.0, column))
    rhs = table[480:512, :]
    scale = jnp.zeros((COLS, 128), F32)
    for k in range(COLS):
        column = system[k]
        inverse = 1.0 / column[k : k + 1, :]
        scale = jnp.where(row32 == k, inverse, scale)
        ratio = jnp.where(row32 == k, 0.0, column * inverse)
        touched = [j for j in range(k + 1, COLS) if j >= SPL or j == k + 1]
        for j in touched:
            system[j] = system[j] - ratio * column[j : j + 1, :]
        rhs = rhs - ratio * rhs[k : k + 1, :]
    answer = rhs * scale
    flat = jnp.concatenate([answer, jnp.zeros((96, 128), F32)], axis=0).T
    line = jnp.concatenate([flat[g : g + 1, :COLS] for g in range(12)], axis=1)
    out_ref[...] = jnp.broadcast_to(line[None], out_ref.shape)


def solve(parts):
    return pl.pallas_call(
        solve_kernel,
        grid=(1,),
        in_specs=[full((32, 48, 128))],
        out_specs=full((32, 1, 384)),
        out_shape=jax.ShapeDtypeStruct((32, 1, 384), F32),
        scratch_shapes=[pltpu.VMEM((512, 128), F32)],
        compiler_params=params(),
        name="solve",
    )(parts)


def update_kernel(
    live_ref, steps_ref, pred_ref, counts_ref, design_ref, load_ref,
    expected_ref, out_ref, beta_ref, left,
):
    step = pl.program_id(0)

    @pl.when(step == 0)
    def _():
        steps = steps_ref[...]
        beta = jnp.concatenate([steps[:, COLS * g : COLS * (g + 1)] for g in range(12)], axis=0)
        b1, b2, b3 = split3(beta)
        left[...] = jnp.concatenate([b1, b1, b2, b2, b1, b3], axis=1)
        beta_ref[...] = beta.T

    at = step * CHUNK
    d1, d2, d3 = design_ref[0:32, :], design_ref[32:64, :], design_ref[64:96, :]
    change = dot(left[...], jnp.concatenate([d1, d2, d1, d2, d3, d1], axis=0), NN)
    expected = jnp.exp(pred_ref[...] + change)
    expected_ref[...] = expected
    slot = lax.broadcasted_iota(jnp.int32, (1, CHUNK), 1) + at
    mask = (slot < live_ref[0]).astype(F32)
    w1, w2 = split2(expected * mask)
    r1, r2 = split2((counts_ref[...].astype(F32) - expected) * mask)
    load = load_ref[...]
    wide = load.astype(F32)
    l1, l2 = split2(wide * wide)
    grad = dot(load, r1, NN) + dot(load, r2, NN)
    curv = dot(l1, w1, NN) + dot(l2, w1, NN) + dot(l1, w2, NN)
    for i in range(CHUNK // 128):
        out_ref[i, :FACT, :] = grad[:, 128 * i : 128 * (i + 1)]
        out_ref[i, FACT:, :] = curv[:, 128 * i : 128 * (i + 1)]


def update(live, steps, pred, counts, design, load):
    genes, cells = counts.shape
    return pl.pallas_call(
        update_kernel,
        grid=(cells // CHUNK,),
        in_specs=[
            smem(), full((32, 384)), lanes(genes), lanes(genes), lanes(96), full((FACT, genes)),
        ],
        out_specs=[
            lanes(genes),
            pl.BlockSpec((CHUNK // 128, 2 * FACT, 128), lambda c: (c, 0, 0)),
            full((COLS, genes)),
        ],
        out_shape=[
            jax.ShapeDtypeStruct((genes, cells), F32),
            jax.ShapeDtypeStruct((cells // 128, 2 * FACT, 128), F32),
            jax.ShapeDtypeStruct((COLS, genes), F32),
        ],
        scratch_shapes=[pltpu.VMEM((genes, 6 * COLS), BF16)],
        compiler_params=params(),
        name="update",
    )(live, steps, pred, counts, design, load)


def loading_kernel(live_ref, expected_ref, counts_ref, fact_ref, out_ref):
    step = pl.program_id(0)
    expected = expected_ref[...]
    slot = lax.broadcasted_iota(jnp.int32, (1, CHUNK), 1) + step * CHUNK
    mask = (slot < live_ref[0]).astype(F32)
    w1, w2 = split2(expected * mask)
    r1, r2 = split2((counts_ref[...].astype(F32) - expected) * mask)
    fact = fact_ref[...]
    wide = fact.astype(F32)
    f1, f2 = split2(wide * wide)
    grad = dot(fact, r1, NT) + dot(fact, r2, NT)
    curv = dot(f1, w1, NT) + dot(f2, w1, NT) + dot(f1, w2, NT)

    @pl.when(step == 0)
    def _():
        out_ref[...] = jnp.zeros_like(out_ref)

    for h in range(2):
        out_ref[h, :32, :] += grad[32 * h : 32 * (h + 1), :]
        out_ref[h, 32:, :] += curv[32 * h : 32 * (h + 1), :]


def loading_sums(live, expected, counts, fact):
    genes, cells = counts.shape
    return pl.pallas_call(
        loading_kernel,
        grid=(cells // CHUNK,),
        in_specs=[smem(), lanes(genes), lanes(genes), lanes(FACT)],
        out_specs=full((2, FACT, genes)),
        out_shape=jax.ShapeDtypeStruct((2, FACT, genes), F32),
        compiler_params=params(),
        name="loading_sums",
    )(live, expected, counts, fact)


def factor_kernel(parts_ref, out_ref):
    total = parts_ref[0]
    for j in range(1, parts_ref.shape[0]):
        total = total + parts_ref[j]
    value = total[:FACT, :] / (total[FACT:, :] + 1.0)
    out_ref[...] = jnp.broadcast_to(value[None], out_ref.shape)


def factor_share(parts):
    peers = parts.shape[0]
    return pl.pallas_call(
        factor_kernel,
        grid=(1,),
        in_specs=[full(parts.shape)],
        out_specs=full((peers, FACT, 128)),
        out_shape=jax.ShapeDtypeStruct((peers, FACT, 128), F32),
        compiler_params=params(),
        name="factor_share",
    )(parts)


def exchange(value, axis):
    return lax.all_to_all(value, axis, split_axis=0, concat_axis=0, tiled=True)


def partners(move):
    def index(x, y, core):
        return (x * 4 + y) * 2 + core

    return [
        (index(x, y, core), index(*move(x, y, core)))
        for x in range(4)
        for y in range(4)
        for core in range(2)
    ]


OTHER_CORE = partners(lambda x, y, c: (x, y, 1 - c))
NEIGHBOURS = (
    partners(lambda x, y, c: (x ^ 1, y, c)),
    partners(lambda x, y, c: (3 - x, y, c)),
    partners(lambda x, y, c: (x, y ^ 1, c)),
    partners(lambda x, y, c: (x, 3 - y, c)),
)


def local(
    counts, batch_id, live_cells, knot_bin, depth_frac, cell_covariates,
    coefficients, batch_effect, factors, loadings,
):
    fact, load = factors.T, loadings.T
    tot = exchange(cell_totals(counts, 8), "gene")
    rest, hi, lo, design = prepare(
        knot_bin[None], depth_frac[None], batch_id[None], cell_covariates,
        coefficients.T, batch_effect.T, load, fact,
    )
    pred, packed = gram_sums(live_cells, tot, rest, counts, hi, lo, design)
    steps = exchange(solve(exchange(packed, "cell")), "cell")
    expected, pieces, beta = update(
        live_cells, steps.reshape(32, 384), pred, counts, design, load
    )
    arrived = exchange(pieces, "gene")

    sums = loading_sums(live_cells, expected, counts, fact)
    first = lax.axis_index("cell") % 2 == 0
    kept = jnp.where(first, sums[0], sums[1])
    given = jnp.where(first, sums[1], sums[0])
    value = kept + lax.ppermute(given, "cell", OTHER_CORE)
    for pairs in NEIGHBOURS:
        value = value + lax.ppermute(value, "cell", pairs)
    mine = value[:32] / jnp.sqrt(value[32:] + 1.0)
    other = lax.ppermute(mine, "cell", OTHER_CORE)
    score = jnp.where(
        first, jnp.concatenate([mine, other]), jnp.concatenate([other, mine])
    )

    gathered = exchange(factor_share(arrived), "gene")
    factor_step = jnp.moveaxis(gathered, 0, 1).reshape(FACT, -1)
    return beta.T, factor_step.T, score.T


def solution(mesh):
    placed = (
        P("gene", "cell"),
        P("cell"),
        P("cell"),
        P("cell"),
        P("cell"),
        P(None, "cell"),
        P("gene", None),
        P("gene", None),
        P("cell", None),
        P("gene", None),
    )
    return jax.shard_map(
        local,
        mesh=mesh,
        in_specs=placed,
        out_specs=(P("gene", None), P("cell", None), P("gene", None)),
        check_vma=False,
    )
```

time: 308 us -> 112 us (0.36)
  the two profiles are of different devices: /device:TPU:1 before, /device:TPU:24 now
where the time goes in v1:
time: 112 us; the launch traced here: 111 us
  blocking collectives  30.6 us (27%)
  starting transfers between devices  27 us (24%)
  waiting for transfers between devices  24.7 us (22%)
  Pallas kernels  14.7 us (13%)
  local copies, waits for them, and re-layouts  11.8 us (11%)
  between operations  1.49 us (1%)
    all_to_all x2, blocking collectives, exchange(): return lax.all_to_all(value, axis, split_axis=0, concat_axis=0, tiled=True)  30.6 us
    all_to_all x3, starting transfers between devices, exchange(): return lax.all_to_all(value, axis, split_axis=0, concat_axis=0, tiled=True)  22.2 us
    ppermute x4, waiting for transfers between devices, local(): value = value + lax.ppermute(value, 'cell', pairs)  13 us
    unnamed x35, local copies, waits for them, and re-layouts  11 us
    all_to_all x3, waiting for transfers between devices, exchange(): return lax.all_to_all(value, axis, split_axis=0, concat_axis=0, tiled=True)  9.17 us
    ppermute x4, starting transfers between devices, local(): value = value + lax.ppermute(value, 'cell', pairs)  4.68 us
    pallas_call x1, Pallas kernels, gram_sums(): pl.pallas_call(gram_kernel, grid=(cells // CHUNK,), in_specs=[smem(), ful...  4.26 us
    pallas_call x1, Pallas kernels, update(): pl.pallas_call(update_kernel, grid=(cells // CHUNK,), in_specs=[smem(), f...  3.51 us
  transfers between devices with their start and end apart: 9, of which 7 were waited for; matrix products, arithmetic and copies ran while one was open for 1% of the time, Pallas kernels for 5%

profile of v1, /device:TPU:24, one launch (start us, length us, event | category | flops | bytes accessed | tf_op | source)
XLA Modules:
  0.0 111.0 jit_solution(4583835803801476123)
XLA Ops:
  0.6 0.0 copy-start
  0.6 1.4 %copy-done = s32[384,1024]{1,0:T(8,128)S(1)} copy-done((s32[384,1024]{1,0:T(8,128)S(1)}, s32[384,1024]{1,0:T(8,128)}, u32[]{:S(2)}) %copy-start) | copy-done | bytes 1572888
  2.1 0.9 cell_totals.1
  3.0 8.5 %all-to-all-start = ((f32[8,8,128]{2,1,0:T(8,128)}), f32[8,8,128]{2,1,0:T(8,128)S(1)}, u32[]{:S(2)}, u32[]{:S(2)}) async-start(f32[8,8,128]{2,1,0:T(8,128)} %cell_totals.1), calls=%async_computation | async-start | bytes 65536 | tf_op jit(solution)/shard_map/all_to_all | solution.py:390
  12.1 0.0 copy-done.10
  12.1 0.0 copy-done.13
  12.1 0.0 copy-done.14
  12.1 0.0 copy-done.15
  12.1 0.0 copy-done.16
  12.1 0.0 copy-start.8
  12.1 0.9 copy-done.8
  13.0 0.9 copy-done.11
  13.9 0.8 copy-done.12
  14.8 2.0 %prepare.1 = (f32[384,1024]{1,0:T(8,128)S(1)}, bf16[512,1024]{1,0:T(8,128)(2,1)S(1)}, bf16[512,1024]{1,0:T(8,128)(2,1)S(1)}, bf16[96,1024]{1,0:T(8,128)(2,1)S(1)}) custom-call(s32[1,1024]{1,0:T(1,128)S(1)} %bitcast.32, f32[1,1024]{1,0:T(1,128)S(1)} %bitcast.33, s32[1,1024]{1,0:T(1,128)S(1)} %bitcast.34, f32[16,1024]{1,0:T(8,128)S(1)} %copy-done.12, ...), custom_call_target="tpu_custom_call" | custom-call | tf_op jit(solution)/shard_map/prepare/pallas_call | solution.py:134
  16.8 0.0 copy-start.4
  16.8 1.0 copy-done.4
  17.8 1.0 copy-done.6
  18.7 0.7 all-to-all-done.tot_ref
  19.4 0.0 copy-done.1
  19.5 1.2 %copy-done.5 = bf16[512,1024]{1,0:T(8,128)(2,1)S(1)} copy-done((bf16[512,1024]{1,0:T(8,128)(2,1)S(1)}, bf16[512,1024]{1,0:T(8,128)(2,1)}, u32[]{:S(2)}) %copy-start.5) | copy-done | bytes 1048600
  20.7 1.2 %copy-done.7 = bf16[512,1024]{1,0:T(8,128)(2,1)S(1)} copy-done((bf16[512,1024]{1,0:T(8,128)(2,1)S(1)}, bf16[512,1024]{1,0:T(8,128)(2,1)}, u32[]{:S(2)}) %copy-start.7) | copy-done | bytes 1048600
  21.9 4.3 %gram_sums.1 = (f32[384,1024]{1,0:T(8,128)S(1)}, f32[32,48,128]{2,1,0:T(8,128)S(1)}) custom-call(s32[1]{0:T(128)S(6)} %copy.22.live_ref, f32[8,8,128]{2,1,0:T(8,128)S(1)} %all-to-all-done.tot_ref, f32[384,1024]{1,0:T(8,128)S(1)} %get-tuple-element.12.rest_ref, s32[384,1024]{1,0:T(8,128)S(1)} %copy-done.1, bf16[512,1024]{1,0:T(8,128)(2,1)S(1)} %copy-done.5, ...), custom_call_target="tpu_custom_call" | custom-call | tf_op jit(solution)/shard_map/gram_sums/pallas_call | solution.py:201
  26.2 19.6 %all_to_all.25.parts_ref = f32[32,48,128]{2,1,0:T(8,128)S(1)} all-to-all(f32[32,48,128]{2,1,0:T(8,128)S(1)} %get-tuple-element.16), channel_id=1, replica_groups=mesh['cell'=32,'gene'=8] {'cell'}, dimensions={0} | all-to-all | bytes 1572864 | tf_op jit(solution)/shard_map/all_to_all | solution.py:390
  45.8 1.0 solve.1
  46.8 11.0 %all_to_all.26 = f32[32,1,384]{2,1,0:T(1,128)S(1)} all-to-all(f32[32,1,384]{2,1,0:T(1,128)S(1)} %solve.1), channel_id=1, replica_groups=mesh['cell'=32,'gene'=8] {'cell'}, dimensions={0} | all-to-all | bytes 98304 | tf_op jit(solution)/shard_map/all_to_all | solution.py:390
  57.8 3.5 %update.1 = (f32[384,1024]{1,0:T(8,128)S(1)}, f32[8,128,128]{2,1,0:T(8,128)}, f32[32,384]{1,0:T(8,128)}) custom-call(s32[1]{0:T(128)S(6)} %copy.22.live_ref, f32[32,384]{1,0:T(8,128)S(1)} %bitcast.29, f32[384,1024]{1,0:T(8,128)S(1)} %get-tuple-element.17.pred_ref, s32[384,1024]{1,0:T(8,128)S(1)} %copy-done.1, ...), custom_call_target="tpu_custom_call" | custom-call | tf_op jit(solution)/shard_map/update/pallas_call | solution.py:311
  61.3 1.2 %copy-done.2 = f32[384,1024]{1,0:T(8,128)} copy-done((f32[384,1024]{1,0:T(8,128)}, f32[384,1024]{1,0:T(8,128)S(1)}, u32[]{:S(2)}) %copy-start.2) | copy-done | bytes 1572888
  62.5 6.5 %all-to-all-start.3 = ((f32[8,128,128]{2,1,0:T(8,128)}), f32[8,128,128]{2,1,0:T(8,128)S(1)}, u32[]{:S(2)}, u32[]{:S(2)}) async-start(f32[8,128,128]{2,1,0:T(8,128)} %get-tuple-element.19), calls=%async_computation.3 | async-start | bytes 1048576 | tf_op jit(solution)/shard_map/all_to_all | solution.py:390
  69.0 1.4 %copy-done.3 = f32[384,1024]{1,0:T(8,128)S(1)} copy-done((f32[384,1024]{1,0:T(8,128)S(1)}, f32[384,1024]{1,0:T(8,128)}, u32[]{:S(2)}) %copy-start.3) | copy-done | bytes 1572888
  70.4 2.2 %loading_sums.1 = f32[2,64,384]{2,1,0:T(8,128)S(1)} custom-call(s32[1]{0:T(128)S(6)} %copy.22.live_ref, f32[384,1024]{1,0:T(8,128)S(1)} %copy-done.3, s32[384,1024]{1,0:T(8,128)S(1)} %copy-done.1, bf16[64,1024]{1,0:T(8,128)(2,1)S(1)} %bitcast.26), custom_call_target="tpu_custom_call" | custom-call | tf_op jit(solution)/shard_map/loading_sums/pallas_call | solution.py:357
  72.7 0.1 collective-permute-start
  72.8 1.3 %collective-permute-done = f32[64,384]{1,0:T(8,128)S(1)} collective-permute-done((f32[64,384]{1,0:T(8,128)S(1)}, f32[64,384]{1,0:T(8,128)S(1)}, u32[]{:S(2)}, u32[]{:S(2)}) %collective-permute-start) | collective-permute-done | bytes 98336 | tf_op jit(solution)/shard_map/ppermute | solution.py:435
  74.1 0.7 collective-permute-start.1
  74.8 4.2 %collective-permute-done.1 = f32[64,384]{1,0:T(8,128)S(1)} collective-permute-done((f32[64,384]{1,0:T(8,128)S(1)}, f32[64,384]{1,0:T(8,128)S(1)}, u32[]{:S(2)}, u32[]{:S(2)}) %collective-permute-start.1) | collective-permute-done | bytes 98336 | tf_op jit(solution)/shard_map/ppermute | solution.py:437
  79.1 1.3 %collective-permute-start.2 = (f32[64,384]{1,0:T(8,128)S(1)}, f32[64,384]{1,0:T(8,128)S(1)}, u32[]{:S(2)}, u32[]{:S(2)}) collective-permute-start(f32[64,384]{1,0:T(8,128)S(1)} %add.27), channel_id=1, source_target_pairs={{0,192},{8,200},{16,208},{24,216},{32,224},{40,232},{48,240},{56,2... | collective-permute-start | bytes 294920 | tf_op jit(solution)/shard_map/ppermute | solution.py:437
  80.3 4.7 %collective-permute-done.2 = f32[64,384]{1,0:T(8,128)S(1)} collective-permute-done((f32[64,384]{1,0:T(8,128)S(1)}, f32[64,384]{1,0:T(8,128)S(1)}, u32[]{:S(2)}, u32[]{:S(2)}) %collective-permute-start.2) | collective-permute-done | bytes 98336 | tf_op jit(solution)/shard_map/ppermute | solution.py:437
  85.0 0.6 collective-permute-start.3
  85.6 4.1 %collective-permute-done.3 = f32[64,384]{1,0:T(8,128)S(1)} collective-permute-done((f32[64,384]{1,0:T(8,128)S(1)}, f32[64,384]{1,0:T(8,128)S(1)}, u32[]{:S(2)}, u32[]{:S(2)}) %collective-permute-start.3) | collective-permute-done | bytes 98336 | tf_op jit(solution)/shard_map/ppermute | solution.py:437
  89.7 2.2 %collective-permute-start.4 = (f32[64,384]{1,0:T(8,128)S(1)}, f32[64,384]{1,0:T(8,128)S(1)}, u32[]{:S(2)}, u32[]{:S(2)}) collective-permute-start(f32[64,384]{1,0:T(8,128)S(1)} %add.29), channel_id=1, source_target_pairs={{0,48},{8,56},{16,32},{24,40},{32,16},{40,24},{48,0},{56,8},{64,11... | collective-permute-start | bytes 294920 | tf_op jit(solution)/shard_map/ppermute | solution.py:437
  91.9 0.0 all-to-all-done.3.parts_ref
  91.9 0.7 factor_share.1
  92.6 7.2 %all-to-all-start.4 = ((f32[8,64,128]{2,1,0:T(8,128)}), f32[8,64,128]{2,1,0:T(8,128)S(1)}, u32[]{:S(2)}, u32[]{:S(2)}) async-start(f32[8,64,128]{2,1,0:T(8,128)} %factor_share.1), calls=%async_computation.4 | async-start | bytes 524288 | tf_op jit(solution)/shard_map/all_to_all | solution.py:390
  99.8 0.0 collective-permute-done.4
  99.9 0.1 collective-permute-start.5
  100.0 1.2 %collective-permute-done.5 = f32[32,384]{1,0:T(8,128)S(1)} collective-permute-done((f32[32,384]{1,0:T(8,128)S(1)}, f32[32,384]{1,0:T(8,128)S(1)}, u32[]{:S(2)}, u32[]{:S(2)}) %collective-permute-start.5) | collective-permute-done | bytes 49184 | tf_op jit(solution)/shard_map/ppermute | solution.py:439
  101.2 0.6 fusion
  101.8 8.5 %all-to-all-done.4 = f32[8,64,128]{2,1,0:T(8,128)S(1)} async-done(((f32[8,64,128]{2,1,0:T(8,128)}), f32[8,64,128]{2,1,0:T(8,128)S(1)}, u32[]{:S(2)}, u32[]{:S(2)}) %all-to-all-start.4) | async-done | bytes 262176 | tf_op jit(solution)/shard_map/all_to_all | solution.py:390
  110.3 0.7 bitcast_bitcast_fusion
  (23 shorter events, 0.1 us)
Async XLA Ops:
  0.6 1.4 %copy-start = (s32[384,1024]{1,0:T(8,128)S(1)}, s32[384,1024]{1,0:T(8,128)}, u32[]{:S(2)}) copy-start(s32[384,1024]{1,0:T(8,128)} %counts_ref.7) | copy-start | bytes 4718596
  2.0 10.0 %copy-start.10 = (bf16[384,64]{0,1:T(8,128)(2,1)S(1)}, bf16[384,64]{0,1:T(8,128)(2,1)}, u32[]{:S(2)}) copy-start(bf16[384,64]{0,1:T(8,128)(2,1)} %param.19) | copy-start | bytes 147460
  2.0 10.0 %copy-start.13 = (f32[384,32]{0,1:T(8,128)S(1)}, f32[384,32]{0,1:T(8,128)}, u32[]{:S(2)}) copy-start(f32[384,32]{0,1:T(8,128)} %param.16) | copy-start | bytes 147460
  2.0 10.0 %copy-start.14 = (s32[1024]{0:T(1024)S(1)}, s32[1024]{0:T(1024)}, u32[]{:S(2)}) copy-start(s32[1024]{0:T(1024)} %param.13) | copy-start | bytes 12292
  2.0 10.1 %copy-start.15 = (f32[1024]{0:T(1024)S(1)}, f32[1024]{0:T(1024)}, u32[]{:S(2)}) copy-start(f32[1024]{0:T(1024)} %param.14) | copy-start | bytes 12292
  2.1 10.1 %copy-start.16 = (s32[1024]{0:T(1024)S(1)}, s32[1024]{0:T(1024)}, u32[]{:S(2)}) copy-start(s32[1024]{0:T(1024)} %param.11) | copy-start | bytes 12292
  2.1 17.4 %copy-start.1 = (s32[384,1024]{1,0:T(8,128)S(1)}, s32[384,1024]{1,0:T(8,128)}, u32[]{:S(2)}) copy-start(s32[384,1024]{1,0:T(8,128)} %counts_ref.7) | copy-start | bytes 4718596
  3.0 16.5 %all-to-all-start = ((f32[8,8,128]{2,1,0:T(8,128)}), f32[8,8,128]{2,1,0:T(8,128)S(1)}, u32[]{:S(2)}, u32[]{:S(2)}) async-start(f32[8,8,128]{2,1,0:T(8,128)} %cell_totals.1), calls=%async_computation | async-start | bytes 65536 | tf_op jit(solution)/shard_map/all_to_all | solution.py:390
  12.1 0.9 copy-start.8
  13.0 0.9 copy-start.11
  13.9 0.8 copy-start.12
  16.8 1.0 copy-start.4
  17.8 1.0 copy-start.6
  19.4 1.2 %copy-start.5 = (bf16[512,1024]{1,0:T(8,128)(2,1)S(1)}, bf16[512,1024]{1,0:T(8,128)(2,1)}, u32[]{:S(2)}) copy-start(bf16[512,1024]{1,0:T(8,128)(2,1)} %copy-done.4) | copy-start | bytes 3145732
  20.7 1.2 %copy-start.7 = (bf16[512,1024]{1,0:T(8,128)(2,1)S(1)}, bf16[512,1024]{1,0:T(8,128)(2,1)}, u32[]{:S(2)}) copy-start(bf16[512,1024]{1,0:T(8,128)(2,1)} %copy-done.6) | copy-start | bytes 3145732
  57.8 11.2 %copy-start.9 = (bf16[1024,64]{0,1:T(8,128)(2,1)S(1)}, bf16[1024,64]{0,1:T(8,128)(2,1)}, u32[]{:S(2)}) copy-start(bf16[1024,64]{0,1:T(8,128)(2,1)} %param.18) | copy-start | bytes 393220
  61.3 1.2 %copy-start.2 = (f32[384,1024]{1,0:T(8,128)}, f32[384,1024]{1,0:T(8,128)S(1)}, u32[]{:S(2)}) copy-start(f32[384,1024]{1,0:T(8,128)S(1)} %get-tuple-element.20.expected_ref) | copy-start | bytes 4718596
  62.5 29.4 %all-to-all-start.3 = ((f32[8,128,128]{2,1,0:T(8,128)}), f32[8,128,128]{2,1,0:T(8,128)S(1)}, u32[]{:S(2)}, u32[]{:S(2)}) async-start(f32[8,128,128]{2,1,0:T(8,128)} %get-tuple-element.19), calls=%async_computation.3 | async-start | bytes 1048576 | tf_op jit(solution)/shard_map/all_to_all | solution.py:390
  69.0 1.4 %copy-start.3 = (f32[384,1024]{1,0:T(8,128)S(1)}, f32[384,1024]{1,0:T(8,128)}, u32[]{:S(2)}) copy-start(f32[384,1024]{1,0:T(8,128)} %copy-done.2) | copy-start | bytes 4718596
  72.7 1.4 %collective-permute-start = (f32[64,384]{1,0:T(8,128)S(1)}, f32[64,384]{1,0:T(8,128)S(1)}, u32[]{:S(2)}, u32[]{:S(2)}) collective-permute-start(f32[64,384]{1,0:T(8,128)S(1)} %select_bitcast_fusion), channel_id=1, source_target_pairs={{0,8},{8,0},{16,24},{24,16},{32,40},{40,32},{48,56},{56,48},{64,72... | collective-permute-start | bytes 294920 | tf_op jit(solution)/shard_map/ppermute | solution.py:435
  74.1 4.9 %collective-permute-start.1 = (f32[64,384]{1,0:T(8,128)S(1)}, f32[64,384]{1,0:T(8,128)S(1)}, u32[]{:S(2)}, u32[]{:S(2)}) collective-permute-start(f32[64,384]{1,0:T(8,128)S(1)} %bitcast_add_fusion), channel_id=1, source_target_pairs={{0,64},{8,72},{16,80},{24,88},{32,96},{40,104},{48,112},{56,120},{... | collective-permute-start | bytes 294920 | tf_op jit(solution)/shard_map/ppermute | solution.py:437
  79.1 5.9 %collective-permute-start.2 = (f32[64,384]{1,0:T(8,128)S(1)}, f32[64,384]{1,0:T(8,128)S(1)}, u32[]{:S(2)}, u32[]{:S(2)}) collective-permute-start(f32[64,384]{1,0:T(8,128)S(1)} %add.27), channel_id=1, source_target_pairs={{0,192},{8,200},{16,208},{24,216},{32,224},{40,232},{48,240},{56,2... | collective-permute-start | bytes 294920 | tf_op jit(solution)/shard_map/ppermute | solution.py:437
  85.0 4.7 %collective-permute-start.3 = (f32[64,384]{1,0:T(8,128)S(1)}, f32[64,384]{1,0:T(8,128)S(1)}, u32[]{:S(2)}, u32[]{:S(2)}) collective-permute-start(f32[64,384]{1,0:T(8,128)S(1)} %add.28), channel_id=1, source_target_pairs={{0,16},{8,24},{16,0},{24,8},{32,48},{40,56},{48,32},{56,40},{64,80... | collective-permute-start | bytes 294920 | tf_op jit(solution)/shard_map/ppermute | solution.py:437
  89.7 10.1 %collective-permute-start.4 = (f32[64,384]{1,0:T(8,128)S(1)}, f32[64,384]{1,0:T(8,128)S(1)}, u32[]{:S(2)}, u32[]{:S(2)}) collective-permute-start(f32[64,384]{1,0:T(8,128)S(1)} %add.29), channel_id=1, source_target_pairs={{0,48},{8,56},{16,32},{24,40},{32,16},{40,24},{48,0},{56,8},{64,11... | collective-permute-start | bytes 294920 | tf_op jit(solution)/shard_map/ppermute | solution.py:437
  92.6 17.7 %all-to-all-start.4 = ((f32[8,64,128]{2,1,0:T(8,128)}), f32[8,64,128]{2,1,0:T(8,128)S(1)}, u32[]{:S(2)}, u32[]{:S(2)}) async-start(f32[8,64,128]{2,1,0:T(8,128)} %factor_share.1), calls=%async_computation.4 | async-start | bytes 524288 | tf_op jit(solution)/shard_map/all_to_all | solution.py:390
  99.9 1.3 %collective-permute-start.5 = (f32[32,384]{1,0:T(8,128)S(1)}, f32[32,384]{1,0:T(8,128)S(1)}, u32[]{:S(2)}, u32[]{:S(2)}) collective-permute-start(f32[32,384]{1,0:T(8,128)S(1)} %fusion.2), channel_id=1, source_target_pairs={{0,8},{8,0},{16,24},{24,16},{32,40},{40,32},{48,56},{56,48},{64,72... | collective-permute-start | bytes 147464 | tf_op jit(solution)/shard_map/ppermute | solution.py:439

commit v2 on v1

--- a/solution.py
+++ b/solution.py
@@ -17,7 +17,7 @@
 NN = (((1,), (0,)), ((), ()))
 NT = (((1,), (1,)), ((), ()))
 TN = (((0,), (0,)), ((), ()))
-VMEM_LIMIT = 40 * 1024 * 1024
+MIB = 1024 * 1024
 
 
 def dot(a, b, dims):
@@ -48,8 +48,8 @@
     return pl.BlockSpec(memory_space=pltpu.SMEM)
 
 
-def params():
-    return pltpu.CompilerParams(vmem_limit_bytes=VMEM_LIMIT)
+def params(mib=60):
+    return pltpu.CompilerParams(vmem_limit_bytes=mib * MIB)
 
 
 def totals_kernel(counts_ref, out_ref, acc):
@@ -152,8 +152,8 @@
 
 
 def gram_kernel(
-    live_ref, tot_ref, rest_ref, counts_ref, hi_ref, lo_ref, design_ref,
-    pred_ref, out_ref, offset, acc,
+    live_ref, core_ref, tot_ref, rest_ref, counts_ref, hi_ref, lo_ref, design_ref,
+    pred_ref, kept_ref, given_ref, offset, acc,
 ):
     step = pl.program_id(0)
 
@@ -191,33 +191,37 @@
 
     @pl.when(step == pl.num_programs(0) - 1)
     def _():
-        for j in range(32):
-            for t in range(4):
-                out_ref[j, 12 * t : 12 * (t + 1), :] = acc[t, pl.ds(j, 12, stride=32), :]
-
-
-def gram_sums(live, tot, rest, counts, hi, lo, design):
+        core = core_ref[0]
+        for chip in range(16):
+            for ref, j in ((kept_ref, 2 * chip + core), (given_ref, 2 * chip + 1 - core)):
+                for t in range(4):
+                    ref[chip, 12 * t : 12 * (t + 1), :] = acc[t, pl.ds(j, 12, stride=32), :]
+
+
+def gram_sums(live, core, tot, rest, counts, hi, lo, design):
     genes, cells = counts.shape
     return pl.pallas_call(
         gram_kernel,
         grid=(cells // CHUNK,),
         in_specs=[
-            smem(), full(tot.shape), lanes(genes), lanes(genes), lanes(512), lanes(512), lanes(96),
-        ],
-        out_specs=[lanes(genes), full((32, 48, 128))],
+            smem(), smem(), full(tot.shape), lanes(genes), lanes(genes),
+            lanes(512), lanes(512), lanes(96),
+        ],
+        out_specs=[lanes(genes), full((16, 48, 128)), full((16, 48, 128))],
         out_shape=[
             jax.ShapeDtypeStruct((genes, cells), F32),
-            jax.ShapeDtypeStruct((32, 48, 128), F32),
+            jax.ShapeDtypeStruct((16, 48, 128), F32),
+            jax.ShapeDtypeStruct((16, 48, 128), F32),
         ],
         scratch_shapes=[pltpu.VMEM((1, cells), F32), pltpu.VMEM((4, genes, 128), F32)],
-        compiler_params=params(),
+        compiler_params=params(50),
         name="gram_sums",
-    )(live, tot, rest, counts, hi, lo, design)
+    )(live, core, tot, rest, counts, hi, lo, design)
 
 
 def solve_kernel(parts_ref, out_ref, table):
     total = parts_ref[0]
-    for j in range(1, 32):
+    for j in range(1, parts_ref.shape[0]):
         total = total + parts_ref[j]
     turned = jnp.concatenate([total, jnp.zeros((80, 128), F32)], axis=0).T
     for t in range(4):
@@ -264,18 +268,18 @@
     return pl.pallas_call(
         solve_kernel,
         grid=(1,),
-        in_specs=[full((32, 48, 128))],
+        in_specs=[full(parts.shape)],
         out_specs=full((32, 1, 384)),
         out_shape=jax.ShapeDtypeStruct((32, 1, 384), F32),
         scratch_shapes=[pltpu.VMEM((512, 128), F32)],
-        compiler_params=params(),
+        compiler_params=params(16),
         name="solve",
     )(parts)
 
 
 def update_kernel(
-    live_ref, steps_ref, pred_ref, counts_ref, design_ref, load_ref,
-    expected_ref, out_ref, beta_ref, left,
+    live_ref, steps_ref, pred_ref, counts_ref, design_ref, load_ref, fact_ref,
+    out_ref, sums_ref, beta_ref, left,
 ):
     step = pl.program_id(0)
 
@@ -286,12 +290,12 @@
         b1, b2, b3 = split3(beta)
         left[...] = jnp.concatenate([b1, b1, b2, b2, b1, b3], axis=1)
         beta_ref[...] = beta.T
+        sums_ref[...] = jnp.zeros_like(sums_ref)
 
     at = step * CHUNK
     d1, d2, d3 = design_ref[0:32, :], design_ref[32:64, :], design_ref[64:96, :]
     change = dot(left[...], jnp.concatenate([d1, d2, d1, d2, d3, d1], axis=0), NN)
     expected = jnp.exp(pred_ref[...] + change)
-    expected_ref[...] = expected
     slot = lax.broadcasted_iota(jnp.int32, (1, CHUNK), 1) + at
     mask = (slot < live_ref[0]).astype(F32)
     w1, w2 = split2(expected * mask)
@@ -304,65 +308,39 @@
     for i in range(CHUNK // 128):
         out_ref[i, :FACT, :] = grad[:, 128 * i : 128 * (i + 1)]
         out_ref[i, FACT:, :] = curv[:, 128 * i : 128 * (i + 1)]
-
-
-def update(live, steps, pred, counts, design, load):
-    genes, cells = counts.shape
-    return pl.pallas_call(
-        update_kernel,
-        grid=(cells // CHUNK,),
-        in_specs=[
-            smem(), full((32, 384)), lanes(genes), lanes(genes), lanes(96), full((FACT, genes)),
-        ],
-        out_specs=[
-            lanes(genes),
-            pl.BlockSpec((CHUNK // 128, 2 * FACT, 128), lambda c: (c, 0, 0)),
-            full((COLS, genes)),
-        ],
-        out_shape=[
-            jax.ShapeDtypeStruct((genes, cells), F32),
-            jax.ShapeDtypeStruct((cells // 128, 2 * FACT, 128), F32),
-            jax.ShapeDtypeStruct((COLS, genes), F32),
-        ],
-        scratch_shapes=[pltpu.VMEM((genes, 6 * COLS), BF16)],
-        compiler_params=params(),
-        name="update",
-    )(live, steps, pred, counts, design, load)
-
-
-def loading_kernel(live_ref, expected_ref, counts_ref, fact_ref, out_ref):
-    step = pl.program_id(0)
-    expected = expected_ref[...]
-    slot = lax.broadcasted_iota(jnp.int32, (1, CHUNK), 1) + step * CHUNK
-    mask = (slot < live_ref[0]).astype(F32)
-    w1, w2 = split2(expected * mask)
-    r1, r2 = split2((counts_ref[...].astype(F32) - expected) * mask)
     fact = fact_ref[...]
     wide = fact.astype(F32)
     f1, f2 = split2(wide * wide)
     grad = dot(fact, r1, NT) + dot(fact, r2, NT)
     curv = dot(f1, w1, NT) + dot(f2, w1, NT) + dot(f1, w2, NT)
-
-    @pl.when(step == 0)
-    def _():
-        out_ref[...] = jnp.zeros_like(out_ref)
-
     for h in range(2):
-        out_ref[h, :32, :] += grad[32 * h : 32 * (h + 1), :]
-        out_ref[h, 32:, :] += curv[32 * h : 32 * (h + 1), :]
-
-
-def loading_sums(live, expected, counts, fact):
+        sums_ref[h, :32, :] += grad[32 * h : 32 * (h + 1), :]
+        sums_ref[h, 32:, :] += curv[32 * h : 32 * (h + 1), :]
+
+
+def update(live, steps, pred, counts, design, load, fact):
     genes, cells = counts.shape
     return pl.pallas_call(
-        loading_kernel,
+        update_kernel,
         grid=(cells // CHUNK,),
-        in_specs=[smem(), lanes(genes), lanes(genes), lanes(FACT)],
-        out_specs=full((2, FACT, genes)),
-        out_shape=jax.ShapeDtypeStruct((2, FACT, genes), F32),
+        in_specs=[
+            smem(), full((32, 384)), lanes(genes), lanes(genes), lanes(96),
+            full((FACT, genes)), lanes(FACT),
+        ],
+        out_specs=[
+            pl.BlockSpec((CHUNK // 128, 2 * FACT, 128), lambda c: (c, 0, 0)),
+            full((2, FACT, genes)),
+            full((COLS, genes)),
+        ],
+        out_shape=[
+            jax.ShapeDtypeStruct((cells // 128, 2 * FACT, 128), F32),
+            jax.ShapeDtypeStruct((2, FACT, genes), F32),
+            jax.ShapeDtypeStruct((COLS, genes), F32),
+        ],
+        scratch_shapes=[pltpu.VMEM((genes, 6 * COLS), BF16)],
         compiler_params=params(),
-        name="loading_sums",
-    )(live, expected, counts, fact)
+        name="update",
+    )(live, steps, pred, counts, design, load, fact)
 
 
 def factor_kernel(parts_ref, out_ref):
@@ -381,13 +359,15 @@
         in_specs=[full(parts.shape)],
         out_specs=full((peers, FACT, 128)),
         out_shape=jax.ShapeDtypeStruct((peers, FACT, 128), F32),
-        compiler_params=params(),
+        compiler_params=params(16),
         name="factor_share",
     )(parts)
 
 
-def exchange(value, axis):
-    return lax.all_to_all(value, axis, split_axis=0, concat_axis=0, tiled=True)
+def exchange(value, axis, groups=None):
+    return lax.all_to_all(
+        value, axis, split_axis=0, concat_axis=0, tiled=True, axis_index_groups=groups
+    )
 
 
 def partners(move):
@@ -402,13 +382,10 @@
     ]
 
 
+SAME_CORE = [list(range(core, 32, 2)) for core in range(2)]
 OTHER_CORE = partners(lambda x, y, c: (x, y, 1 - c))
-NEIGHBOURS = (
-    partners(lambda x, y, c: (x ^ 1, y, c)),
-    partners(lambda x, y, c: (3 - x, y, c)),
-    partners(lambda x, y, c: (x, y ^ 1, c)),
-    partners(lambda x, y, c: (x, 3 - y, c)),
-)
+ALONG_X = [partners(lambda x, y, c, k=k: (x ^ k, y, c)) for k in (1, 2, 3)]
+ALONG_Y = [partners(lambda x, y, c, k=k: (x, y ^ k, c)) for k in (1, 2, 3)]
 
 
 def local(
@@ -421,27 +398,31 @@
         knot_bin[None], depth_frac[None], batch_id[None], cell_covariates,
         coefficients.T, batch_effect.T, load, fact,
     )
-    pred, packed = gram_sums(live_cells, tot, rest, counts, hi, lo, design)
-    steps = exchange(solve(exchange(packed, "cell")), "cell")
-    expected, pieces, beta = update(
-        live_cells, steps.reshape(32, 384), pred, counts, design, load
+    core = lax.axis_index("cell") % 2
+    first = core == 0
+    pred, kept, given = gram_sums(
+        live_cells, core[None], tot, rest, counts, hi, lo, design
+    )
+    packed = kept + lax.ppermute(given, "cell", OTHER_CORE)
+    steps = exchange(solve(exchange(packed, "cell", SAME_CORE)), "cell")
+    pieces, sums, beta = update(
+        live_cells, steps.reshape(32, 384), pred, counts, design, load, fact
     )
     arrived = exchange(pieces, "gene")
 
-    sums = loading_sums(live_cells, expected, counts, fact)
-    first = lax.axis_index("cell") % 2 == 0
     kept = jnp.where(first, sums[0], sums[1])
     given = jnp.where(first, sums[1], sums[0])
     value = kept + lax.ppermute(given, "cell", OTHER_CORE)
-    for pairs in NEIGHBOURS:
-        value = value + lax.ppermute(value, "cell", pairs)
+    for near, across, beside in (ALONG_X, ALONG_Y):
+        value = (value + lax.ppermute(value, "cell", near)) + (
+            lax.ppermute(value, "cell", across) + lax.ppermute(value, "cell", beside)
+        )
+    gathered = exchange(factor_share(arrived), "gene")
     mine = value[:32] / jnp.sqrt(value[32:] + 1.0)
     other = lax.ppermute(mine, "cell", OTHER_CORE)
     score = jnp.where(
         first, jnp.concatenate([mine, other]), jnp.concatenate([other, mine])
     )
-
-    gathered = exchange(factor_share(arrived), "gene")
     factor_step = jnp.moveaxis(gathered, 0, 1).reshape(FACT, -1)
     return beta.T, factor_step.T, score.T
 

time: 112 us -> 110 us (0.982)
  the two profiles are of different devices: /device:TPU:24 before, /device:TPU:1 now
where the time goes in v2:
time: 110 us; the launch traced here: 108 us
  starting transfers between devices  36.8 us (33%)
  waiting for transfers between devices  25 us (23%)
  Pallas kernels  21.6 us (20%)
  blocking collectives  15.8 us (14%)
  local copies, waits for them, and re-layouts  4.72 us (4%)
  other arithmetic  2.67 us (2%)
  between operations  1.37 us (1%)
    all_to_all x4, starting transfers between devices, exchange(): lax.all_to_all(value, axis, split_axis=0, concat_axis=0, tiled=True, axis...  24.2 us
    all_to_all x4, waiting for transfers between devices, exchange(): lax.all_to_all(value, axis, split_axis=0, concat_axis=0, tiled=True, axis...  16.4 us
    all_to_all x1, blocking collectives, exchange(): lax.all_to_all(value, axis, split_axis=0, concat_axis=0, tiled=True, axis...  15.8 us
    pallas_call x1, Pallas kernels, gram_sums(): pl.pallas_call(gram_kernel, grid=(cells // CHUNK,), in_specs=[smem(), sme...  6.16 us
    pallas_call x1, Pallas kernels, update(): pl.pallas_call(update_kernel, grid=(cells // CHUNK,), in_specs=[smem(), f...  5.86 us
    pallas_call x1, Pallas kernels, prepare(): pl.pallas_call(prepare_kernel, grid=(cells // CHUNK,), in_specs=[lanes(1)...  4.4 us
    unnamed x7, local copies, waits for them, and re-layouts  4 us
    ppermute x2, starting transfers between devices, local(): lax.ppermute(value, 'cell', beside)  3.57 us
  transfers between devices with their start and end apart: 13, of which 10 were waited for; matrix products, arithmetic and copies ran while one was open for 2% of the time, Pallas kernels for 5%

profile of v2, /device:TPU:1, one launch (start us, length us, event | category | flops | bytes accessed | tf_op | source)
XLA Modules:
  0.0 108.0 jit_solution(2308781836336936671)
XLA Ops:
  0.6 2.9 %cell_totals.1 = f32[8,8,128]{2,1,0:T(8,128)} custom-call(s32[384,1024]{1,0:T(8,128)} %counts_ref.5), custom_call_target="tpu_custom_call" | custom-call | tf_op jit(solution)/shard_map/cell_totals/pallas_call | solution.py:76
  3.5 9.0 %all-to-all-start = ((f32[8,8,128]{2,1,0:T(8,128)}), f32[8,8,128]{2,1,0:T(8,128)S(1)}, u32[]{:S(2)}, u32[]{:S(2)}) async-start(f32[8,8,128]{2,1,0:T(8,128)} %cell_totals.1), calls=%async_computation | async-start | bytes 65536 | tf_op jit(solution)/shard_map/all_to_all | solution.py:368
  13.2 4.4 %prepare.1 = (f32[384,1024]{1,0:T(8,128)}, bf16[512,1024]{1,0:T(8,128)(2,1)}, bf16[512,1024]{1,0:T(8,128)(2,1)}, bf16[96,1024]{1,0:T(8,128)(2,1)}) custom-call(s32[1,1024]{1,0:T(1,128)} %bitcast.33, f32[1,1024]{1,0:T(1,128)} %bitcast.34, s32[1,1024]{1,0:T(1,128)} %bitcast.35, f32[16,1024]{1,0:T(8,128)} %cov_ref.1, f32[32,384]{1,0:T(8,128)} %bitcast.32, ...), custom_call_target="tpu_custom_call" | custom-call | tf_op jit(solution)/shard_map/prepare/pallas_call | solution.py:134
  17.6 1.8 %all-to-all-done.tot_ref = f32[8,8,128]{2,1,0:T(8,128)S(1)} async-done(((f32[8,8,128]{2,1,0:T(8,128)}), f32[8,8,128]{2,1,0:T(8,128)S(1)}, u32[]{:S(2)}, u32[]{:S(2)}) %all-to-all-start) | async-done | bytes 32800 | tf_op jit(solution)/shard_map/all_to_all | solution.py:368
  19.4 0.0 copy-start
  19.4 1.2 %copy-done = bf16[512,1024]{1,0:T(8,128)(2,1)S(1)} copy-done((bf16[512,1024]{1,0:T(8,128)(2,1)S(1)}, bf16[512,1024]{1,0:T(8,128)(2,1)}, u32[]{:S(2)}) %copy-start) | copy-done | bytes 1048600
  20.6 0.0 copy-start.1
  20.6 1.2 %copy-done.1 = bf16[512,1024]{1,0:T(8,128)(2,1)S(1)} copy-done((bf16[512,1024]{1,0:T(8,128)(2,1)S(1)}, bf16[512,1024]{1,0:T(8,128)(2,1)}, u32[]{:S(2)}) %copy-start.1) | copy-done | bytes 1048600
  21.9 0.0 copy-start.2
  21.9 0.9 copy-done.2
  22.8 6.2 %gram_sums.1 = (f32[384,1024]{1,0:T(8,128)}, f32[16,48,128]{2,1,0:T(8,128)S(1)}, f32[16,48,128]{2,1,0:T(8,128)S(1)}) custom-call(s32[1]{0:T(128)S(6)} %copy.22.live_ref, s32[1]{0:T(128)} %bitcast.core_ref, f32[8,8,128]{2,1,0:T(8,128)S(1)} %all-to-all-done.tot_ref, f32[384,1024]{1,0:T(8,128)} %get-tuple-element.13.rest_ref, s32[384,1024]{1,0:T(8,128)} %counts_ref.5, ...), custom_call_target="tpu_custom_call" | custom-call | tf_op jit(solution)/shard_map/gram_sums/pallas_call | solution.py:203
  29.0 2.1 %collective-permute-start = (f32[16,48,128]{2,1,0:T(8,128)S(1)}, f32[16,48,128]{2,1,0:T(8,128)S(1)}, u32[]{:S(2)}, u32[]{:S(2)}) collective-permute-start(f32[16,48,128]{2,1,0:T(8,128)S(1)} %get-tuple-element.18), channel_id=1, source_target_pairs={{0,8},{8,0},{16,24},{24,16},{32,40},{40,32},{48,56},{56,48},{64,72... | collective-permute-start | bytes 1179656 | tf_op jit(solution)/shard_map/ppermute | solution.py:406
  31.1 1.3 %collective-permute-done = f32[16,48,128]{2,1,0:T(8,128)S(1)} collective-permute-done((f32[16,48,128]{2,1,0:T(8,128)S(1)}, f32[16,48,128]{2,1,0:T(8,128)S(1)}, u32[]{:S(2)}, u32[]{:S(2)}) %collective-permute-start) | collective-permute-done | bytes 393248 | tf_op jit(solution)/shard_map/ppermute | solution.py:406
  32.4 0.1 add.35
  32.5 15.8 %all_to_all.25.parts_ref = f32[16,48,128]{2,1,0:T(8,128)S(1)} all-to-all(f32[16,48,128]{2,1,0:T(8,128)S(1)} %add.35), channel_id=1, replica_groups={{0,16,32,48,64,80,96,112,128,144,160,176,192,208,224,240},{8,24,40,56,7..., dimensions={0} | all-to-all | bytes 786432 | tf_op jit(solution)/shard_map/all_to_all | solution.py:368
  48.3 1.6 %solve.1 = f32[32,1,384]{2,1,0:T(1,128)} custom-call(f32[16,48,128]{2,1,0:T(8,128)S(1)} %all_to_all.25.parts_ref), custom_call_target="tpu_custom_call" | custom-call | tf_op jit(solution)/shard_map/solve/pallas_call | solution.py:268
  49.9 5.3 %all-to-all-start.2 = ((f32[32,1,384]{2,1,0:T(1,128)}), f32[32,1,384]{2,1,0:T(1,128)S(1)}, u32[]{:S(2)}, u32[]{:S(2)}) async-start(f32[32,1,384]{2,1,0:T(1,128)} %solve.1), calls=%async_computation.2 | async-start | bytes 98304 | tf_op jit(solution)/shard_map/all_to_all | solution.py:368
  55.2 7.3 %all-to-all-done.2 = f32[32,1,384]{2,1,0:T(1,128)S(1)} async-done(((f32[32,1,384]{2,1,0:T(1,128)}), f32[32,1,384]{2,1,0:T(1,128)S(1)}, u32[]{:S(2)}, u32[]{:S(2)}) %all-to-all-start.2) | async-done | bytes 49184 | tf_op jit(solution)/shard_map/all_to_all | solution.py:368
  62.5 0.6 copy.21
  63.1 5.9 %update.1 = (f32[8,128,128]{2,1,0:T(8,128)}, f32[2,64,384]{2,1,0:T(8,128)}, f32[32,384]{1,0:T(8,128)}) custom-call(s32[1]{0:T(128)S(6)} %copy.22.live_ref, f32[32,384]{1,0:T(8,128)} %bitcast.30, f32[384,1024]{1,0:T(8,128)} %get-tuple-element.19.pred_ref, s32[384,1024]{1,0:T(8,128)} %counts_ref.5, bf16[96,1024]{1,0:T(8,128)(2,1)} %get-tuple-element.16.design_ref, ...), custom_call_target="tpu_custom_call" | custom-call | tf_op jit(solution)/shard_map/update/pallas_call | solution.py:323
  69.0 4.0 %all-to-all-start.3 = ((f32[8,128,128]{2,1,0:T(8,128)}), f32[8,128,128]{2,1,0:T(8,128)S(1)}, u32[]{:S(2)}, u32[]{:S(2)}) async-start(f32[8,128,128]{2,1,0:T(8,128)} %get-tuple-element.21), calls=%async_computation.3 | async-start | bytes 1048576 | tf_op jit(solution)/shard_map/all_to_all | solution.py:368
  73.0 1.0 select_bitcast_fusion
  73.9 0.8 collective-permute-start.1
  74.7 0.9 collective-permute-done.1
  75.6 1.0 bitcast_add_fusion
  76.6 0.4 collective-permute-start.2
  77.0 1.7 %collective-permute-start.3 = (f32[64,384]{1,0:T(8,128)S(1)}, f32[64,384]{1,0:T(8,128)S(1)}, u32[]{:S(2)}, u32[]{:S(2)}) collective-permute-start(f32[64,384]{1,0:T(8,128)S(1)} %bitcast_add_fusion), channel_id=1, source_target_pairs={{0,128},{8,136},{16,144},{24,152},{32,160},{40,168},{48,176},{56,1... | collective-permute-start | bytes 294920 | tf_op jit(solution)/shard_map/ppermute | solution.py:418
  78.7 1.8 %collective-permute-start.4 = (f32[64,384]{1,0:T(8,128)S(1)}, f32[64,384]{1,0:T(8,128)S(1)}, u32[]{:S(2)}, u32[]{:S(2)}) collective-permute-start(f32[64,384]{1,0:T(8,128)S(1)} %bitcast_add_fusion), channel_id=1, source_target_pairs={{0,192},{8,200},{16,208},{24,216},{32,224},{40,232},{48,240},{56,2... | collective-permute-start | bytes 294920 | tf_op jit(solution)/shard_map/ppermute | solution.py:418
  80.5 0.2 collective-permute-done.2
  80.7 2.7 %collective-permute-done.3 = f32[64,384]{1,0:T(8,128)S(1)} collective-permute-done((f32[64,384]{1,0:T(8,128)S(1)}, f32[64,384]{1,0:T(8,128)S(1)}, u32[]{:S(2)}, u32[]{:S(2)}) %collective-permute-start.3) | collective-permute-done | bytes 98336 | tf_op jit(solution)/shard_map/ppermute | solution.py:418
  83.4 2.6 %collective-permute-done.4 = f32[64,384]{1,0:T(8,128)S(1)} collective-permute-done((f32[64,384]{1,0:T(8,128)S(1)}, f32[64,384]{1,0:T(8,128)S(1)}, u32[]{:S(2)}, u32[]{:S(2)}) %collective-permute-start.4) | collective-permute-done | bytes 98336 | tf_op jit(solution)/shard_map/ppermute | solution.py:418
  86.0 0.4 collective-permute-start.5
  86.4 1.8 %collective-permute-start.6 = (f32[64,384]{1,0:T(8,128)S(1)}, f32[64,384]{1,0:T(8,128)S(1)}, u32[]{:S(2)}, u32[]{:S(2)}) collective-permute-start(f32[64,384]{1,0:T(8,128)S(1)} %add_add_fusion.1), channel_id=1, source_target_pairs={{0,32},{8,40},{16,48},{24,56},{32,0},{40,8},{48,16},{56,24},{64,96... | collective-permute-start | bytes 294920 | tf_op jit(solution)/shard_map/ppermute | solution.py:418
  88.2 1.8 %collective-permute-start.7 = (f32[64,384]{1,0:T(8,128)S(1)}, f32[64,384]{1,0:T(8,128)S(1)}, u32[]{:S(2)}, u32[]{:S(2)}) collective-permute-start(f32[64,384]{1,0:T(8,128)S(1)} %add_add_fusion.1), channel_id=1, source_target_pairs={{0,48},{8,56},{16,32},{24,40},{32,16},{40,24},{48,0},{56,8},{64,11... | collective-permute-start | bytes 294920 | tf_op jit(solution)/shard_map/ppermute | solution.py:418
  89.9 1.0 all-to-all-done.3.parts_ref
  90.9 0.7 factor_share.1
  91.7 5.9 %all-to-all-start.4 = ((f32[8,64,128]{2,1,0:T(8,128)}), f32[8,64,128]{2,1,0:T(8,128)S(1)}, u32[]{:S(2)}, u32[]{:S(2)}) async-start(f32[8,64,128]{2,1,0:T(8,128)} %factor_share.1), calls=%async_computation.4 | async-start | bytes 524288 | tf_op jit(solution)/shard_map/all_to_all | solution.py:368
  97.6 0.0 collective-permute-done.5
  97.6 0.0 collective-permute-done.6
  97.6 0.0 collective-permute-done.7
  97.7 1.8 %collective-permute-start.8 = (f32[32,384]{1,0:T(8,128)S(1)}, f32[32,384]{1,0:T(8,128)S(1)}, u32[]{:S(2)}, u32[]{:S(2)}) collective-permute-start(f32[32,384]{1,0:T(8,128)S(1)} %fusion.2), channel_id=1, source_target_pairs={{0,8},{8,0},{16,24},{24,16},{32,40},{40,32},{48,56},{56,48},{64,72... | collective-permute-start | bytes 147464 | tf_op jit(solution)/shard_map/ppermute | solution.py:422
  99.5 0.9 collective-permute-done.8
  100.4 0.6 fusion
  101.0 6.2 %all-to-all-done.4 = f32[8,64,128]{2,1,0:T(8,128)S(1)} async-done(((f32[8,64,128]{2,1,0:T(8,128)}), f32[8,64,128]{2,1,0:T(8,128)S(1)}, u32[]{:S(2)}, u32[]{:S(2)}) %all-to-all-start.4) | async-done | bytes 262176 | tf_op jit(solution)/shard_map/all_to_all | solution.py:368
  107.3 0.7 bitcast_bitcast_fusion
  (3 shorter events, 0.1 us)
Async XLA Ops:
  3.5 15.9 %all-to-all-start = ((f32[8,8,128]{2,1,0:T(8,128)}), f32[8,8,128]{2,1,0:T(8,128)S(1)}, u32[]{:S(2)}, u32[]{:S(2)}) async-start(f32[8,8,128]{2,1,0:T(8,128)} %cell_totals.1), calls=%async_computation | async-start | bytes 65536 | tf_op jit(solution)/shard_map/all_to_all | solution.py:368
  19.4 1.2 %copy-start = (bf16[512,1024]{1,0:T(8,128)(2,1)S(1)}, bf16[512,1024]{1,0:T(8,128)(2,1)}, u32[]{:S(2)}) copy-start(bf16[512,1024]{1,0:T(8,128)(2,1)} %get-tuple-element.14.hi_ref) | copy-start | bytes 3145732
  20.6 1.2 %copy-start.1 = (bf16[512,1024]{1,0:T(8,128)(2,1)S(1)}, bf16[512,1024]{1,0:T(8,128)(2,1)}, u32[]{:S(2)}) copy-start(bf16[512,1024]{1,0:T(8,128)(2,1)} %get-tuple-element.15.lo_ref) | copy-start | bytes 3145732
  21.9 0.9 copy-start.2
  29.0 3.5 %collective-permute-start = (f32[16,48,128]{2,1,0:T(8,128)S(1)}, f32[16,48,128]{2,1,0:T(8,128)S(1)}, u32[]{:S(2)}, u32[]{:S(2)}) collective-permute-start(f32[16,48,128]{2,1,0:T(8,128)S(1)} %get-tuple-element.18), channel_id=1, source_target_pairs={{0,8},{8,0},{16,24},{24,16},{32,40},{40,32},{48,56},{56,48},{64,72... | collective-permute-start | bytes 1179656 | tf_op jit(solution)/shard_map/ppermute | solution.py:406
  49.9 12.6 %all-to-all-start.2 = ((f32[32,1,384]{2,1,0:T(1,128)}), f32[32,1,384]{2,1,0:T(1,128)S(1)}, u32[]{:S(2)}, u32[]{:S(2)}) async-start(f32[32,1,384]{2,1,0:T(1,128)} %solve.1), calls=%async_computation.2 | async-start | bytes 98304 | tf_op jit(solution)/shard_map/all_to_all | solution.py:368
  69.0 21.9 %all-to-all-start.3 = ((f32[8,128,128]{2,1,0:T(8,128)}), f32[8,128,128]{2,1,0:T(8,128)S(1)}, u32[]{:S(2)}, u32[]{:S(2)}) async-start(f32[8,128,128]{2,1,0:T(8,128)} %get-tuple-element.21), calls=%async_computation.3 | async-start | bytes 1048576 | tf_op jit(solution)/shard_map/all_to_all | solution.py:368
  73.9 1.7 %collective-permute-start.1 = (f32[64,384]{1,0:T(8,128)S(1)}, f32[64,384]{1,0:T(8,128)S(1)}, u32[]{:S(2)}, u32[]{:S(2)}) collective-permute-start(f32[64,384]{1,0:T(8,128)S(1)} %select_bitcast_fusion), channel_id=1, source_target_pairs={{0,8},{8,0},{16,24},{24,16},{32,40},{40,32},{48,56},{56,48},{64,72... | collective-permute-start | bytes 294920 | tf_op jit(solution)/shard_map/ppermute | solution.py:415
  76.6 4.1 %collective-permute-start.2 = (f32[64,384]{1,0:T(8,128)S(1)}, f32[64,384]{1,0:T(8,128)S(1)}, u32[]{:S(2)}, u32[]{:S(2)}) collective-permute-start(f32[64,384]{1,0:T(8,128)S(1)} %bitcast_add_fusion), channel_id=1, source_target_pairs={{0,64},{8,72},{16,80},{24,88},{32,96},{40,104},{48,112},{56,120},{... | collective-permute-start | bytes 294920 | tf_op jit(solution)/shard_map/ppermute | solution.py:417
  77.0 6.4 %collective-permute-start.3 = (f32[64,384]{1,0:T(8,128)S(1)}, f32[64,384]{1,0:T(8,128)S(1)}, u32[]{:S(2)}, u32[]{:S(2)}) collective-permute-start(f32[64,384]{1,0:T(8,128)S(1)} %bitcast_add_fusion), channel_id=1, source_target_pairs={{0,128},{8,136},{16,144},{24,152},{32,160},{40,168},{48,176},{56,1... | collective-permute-start | bytes 294920 | tf_op jit(solution)/shard_map/ppermute | solution.py:418
  78.7 7.2 %collective-permute-start.4 = (f32[64,384]{1,0:T(8,128)S(1)}, f32[64,384]{1,0:T(8,128)S(1)}, u32[]{:S(2)}, u32[]{:S(2)}) collective-permute-start(f32[64,384]{1,0:T(8,128)S(1)} %bitcast_add_fusion), channel_id=1, source_target_pairs={{0,192},{8,200},{16,208},{24,216},{32,224},{40,232},{48,240},{56,2... | collective-permute-start | bytes 294920 | tf_op jit(solution)/shard_map/ppermute | solution.py:418
  86.0 11.6 %collective-permute-start.5 = (f32[64,384]{1,0:T(8,128)S(1)}, f32[64,384]{1,0:T(8,128)S(1)}, u32[]{:S(2)}, u32[]{:S(2)}) collective-permute-start(f32[64,384]{1,0:T(8,128)S(1)} %add_add_fusion.1), channel_id=1, source_target_pairs={{0,16},{8,24},{16,0},{24,8},{32,48},{40,56},{48,32},{56,40},{64,80... | collective-permute-start | bytes 294920 | tf_op jit(solution)/shard_map/ppermute | solution.py:417
  86.4 11.3 %collective-permute-start.6 = (f32[64,384]{1,0:T(8,128)S(1)}, f32[64,384]{1,0:T(8,128)S(1)}, u32[]{:S(2)}, u32[]{:S(2)}) collective-permute-start(f32[64,384]{1,0:T(8,128)S(1)} %add_add_fusion.1), channel_id=1, source_target_pairs={{0,32},{8,40},{16,48},{24,56},{32,0},{40,8},{48,16},{56,24},{64,96... | collective-permute-start | bytes 294920 | tf_op jit(solution)/shard_map/ppermute | solution.py:418
  88.2 9.5 %collective-permute-start.7 = (f32[64,384]{1,0:T(8,128)S(1)}, f32[64,384]{1,0:T(8,128)S(1)}, u32[]{:S(2)}, u32[]{:S(2)}) collective-permute-start(f32[64,384]{1,0:T(8,128)S(1)} %add_add_fusion.1), channel_id=1, source_target_pairs={{0,48},{8,56},{16,32},{24,40},{32,16},{40,24},{48,0},{56,8},{64,11... | collective-permute-start | bytes 294920 | tf_op jit(solution)/shard_map/ppermute | solution.py:418
  91.7 15.6 %all-to-all-start.4 = ((f32[8,64,128]{2,1,0:T(8,128)}), f32[8,64,128]{2,1,0:T(8,128)S(1)}, u32[]{:S(2)}, u32[]{:S(2)}) async-start(f32[8,64,128]{2,1,0:T(8,128)} %factor_share.1), calls=%async_computation.4 | async-start | bytes 524288 | tf_op jit(solution)/shard_map/all_to_all | solution.py:368
  97.7 2.7 %collective-permute-start.8 = (f32[32,384]{1,0:T(8,128)S(1)}, f32[32,384]{1,0:T(8,128)S(1)}, u32[]{:S(2)}, u32[]{:S(2)}) collective-permute-start(f32[32,384]{1,0:T(8,128)S(1)} %fusion.2), channel_id=1, source_target_pairs={{0,8},{8,0},{16,24},{24,16},{32,40},{40,32},{48,56},{56,48},{64,72... | collective-permute-start | bytes 147464 | tf_op jit(solution)/shard_map/ppermute | solution.py:422

commit v3 on v2

--- a/solution.py
+++ b/solution.py
@@ -48,46 +48,53 @@
     return pl.BlockSpec(memory_space=pltpu.SMEM)
 
 
-def params(mib=60):
+def params(mib=16):
     return pltpu.CompilerParams(vmem_limit_bytes=mib * MIB)
 
 
-def totals_kernel(counts_ref, out_ref, acc):
-    step = pl.program_id(0)
-    part = jnp.sum(counts_ref[...].astype(F32), axis=0, keepdims=True)
-
-    @pl.when(step == 0)
-    def _():
-        acc[...] = part
-
-    @pl.when(step > 0)
-    def _():
-        acc[...] += part
-
-    @pl.when(step == pl.num_programs(0) - 1)
-    def _():
-        for i in range(8):
-            row = acc[:, 128 * i : 128 * (i + 1)]
-            out_ref[:, i : i + 1, :] = jnp.broadcast_to(row[None], (out_ref.shape[0], 1, 128))
+def totals_kernel(counts_ref, out_ref, rows, arrived):
+    blocks = rows.shape[0]
+    size = rows.shape[1]
+
+    def copy(b):
+        return pltpu.make_async_copy(
+            counts_ref.at[pl.ds(b * size, size), :], rows.at[b], arrived.at[b]
+        )
+
+    for b in range(blocks):
+        copy(b).start()
+    total = jnp.zeros((8, rows.shape[2]), F32)
+    for b in range(blocks):
+        copy(b).wait()
+        for i in range(0, size, 8):
+            total = total + rows[b, i : i + 8, :].astype(F32)
+    total = jnp.sum(total, axis=0, keepdims=True)
+    for i in range(8):
+        row = total[:, 128 * i : 128 * (i + 1)]
+        out_ref[:, i : i + 1, :] = jnp.broadcast_to(row[None], (out_ref.shape[0], 1, 128))
 
 
 def cell_totals(counts, peers):
     genes, cells = counts.shape
+    blocks = 8
     return pl.pallas_call(
         totals_kernel,
-        grid=(3,),
-        in_specs=[pl.BlockSpec((genes // 3, cells), lambda c: (c, 0))],
+        grid=(1,),
+        in_specs=[pl.BlockSpec(memory_space=pl.ANY)],
         out_specs=full((peers, 8, 128)),
         out_shape=jax.ShapeDtypeStruct((peers, 8, 128), F32),
-        scratch_shapes=[pltpu.VMEM((1, cells), F32)],
-        compiler_params=params(),
+        scratch_shapes=[
+            pltpu.VMEM((blocks, genes // blocks, cells), jnp.int32),
+            pltpu.SemaphoreType.DMA((blocks,)),
+        ],
+        compiler_params=params(60),
         name="cell_totals",
     )(counts)
 
 
 def prepare_kernel(
     knot_ref, frac_ref, batch_ref, cov_ref, coef_ref, shift_ref, load_ref, fact_ref,
-    rest_ref, hi_ref, lo_ref, design_ref, left,
+    rest_ref, design_ref, left,
 ):
     @pl.when(pl.program_id(0) == 0)
     def _():
@@ -111,22 +118,6 @@
     )
     rest_ref[...] = dot(left[...], right, TN)
 
-    def put(at, value):
-        hi, lo = split2(value)
-        hi_ref[at : at + value.shape[0], :] = hi
-        lo_ref[at : at + value.shape[0], :] = lo
-
-    put(0, jnp.where(here, rest * rest, 0.0) + jnp.where(above, frac * frac, 0.0))
-    put(16, jnp.where(here, rest * frac, 0.0))
-    for p in range(SPL):
-        put(32 + 16 * p, hat[p : p + 1, :] * cov)
-    low, high = cov[:8], cov[8:]
-    for i in range(0, 8, 2):
-        put(288 + 8 * i, jnp.concatenate([low[i : i + 1] * low, low[i + 1 : i + 2] * low], axis=0))
-        put(352 + 8 * i, jnp.concatenate([low[i : i + 1] * high, low[i + 1 : i + 2] * high], axis=0))
-        put(416 + 8 * i, jnp.concatenate([high[i : i + 1] * high, high[i + 1 : i + 2] * high], axis=0))
-    put(480, jnp.zeros((32, width), F32))
-
 
 def prepare(knot, frac, batch, cov, coef, shift, load, fact):
     cells = knot.shape[1]
@@ -138,11 +129,9 @@
             lanes(1), lanes(1), lanes(1), lanes(16),
             full((COLS, genes)), full((64, genes)), full((FACT, genes)), lanes(FACT),
         ],
-        out_specs=[lanes(genes), lanes(512), lanes(512), lanes(96)],
+        out_specs=[lanes(genes), lanes(96)],
         out_shape=[
             jax.ShapeDtypeStruct((genes, cells), F32),
-            jax.ShapeDtypeStruct((512, cells), BF16),
-            jax.ShapeDtypeStruct((512, cells), BF16),
             jax.ShapeDtypeStruct((96, cells), BF16),
         ],
         scratch_shapes=[pltpu.VMEM((448, genes), BF16)],
@@ -152,8 +141,8 @@
 
 
 def gram_kernel(
-    live_ref, core_ref, tot_ref, rest_ref, counts_ref, hi_ref, lo_ref, design_ref,
-    pred_ref, kept_ref, given_ref, offset, acc,
+    live_ref, core_ref, tot_ref, rest_ref, counts_ref, design_ref,
+    pred_ref, kept_ref, given_ref, offset, acc, hi_ref, lo_ref,
 ):
     step = pl.program_id(0)
 
@@ -174,11 +163,30 @@
     residual = (counts_ref[...].astype(F32) - expected) * mask
     w1, w2 = split2(weight)
     r1, r2 = split2(residual)
+
+    def put(at, value):
+        hi, lo = split2(value)
+        hi_ref[at : at + value.shape[0], :] = hi
+        lo_ref[at : at + value.shape[0], :] = lo
+
+    d1, d2, d3 = design_ref[0:32, :], design_ref[32:64, :], design_ref[64:96, :]
+    design = (d1.astype(F32) + d2.astype(F32)) + d3.astype(F32)
+    hat, cov = design[:SPL], design[SPL:]
+    put(0, hat * hat)
+    put(16, hat * pltpu.roll(hat, SPL - 1, axis=0))
+    for p in range(SPL):
+        put(32 + 16 * p, hat[p : p + 1, :] * cov)
+    low, high = cov[:8], cov[8:]
+    for i in range(0, 8, 2):
+        put(288 + 8 * i, jnp.concatenate([low[i : i + 1] * low, low[i + 1 : i + 2] * low], axis=0))
+        put(352 + 8 * i, jnp.concatenate([low[i : i + 1] * high, low[i + 1 : i + 2] * high], axis=0))
+        put(416 + 8 * i, jnp.concatenate([high[i : i + 1] * high, high[i + 1 : i + 2] * high], axis=0))
+    put(480, jnp.zeros((32, CHUNK), F32))
     hi, lo = hi_ref[...], lo_ref[...]
     gram = dot(w1, hi, NT) + dot(w1, lo, NT) + dot(w2, hi, NT)
     blank = jnp.zeros((96, CHUNK), BF16)
-    s1 = jnp.concatenate([blank, design_ref[:COLS, :]], axis=0)
-    s2 = jnp.concatenate([blank, design_ref[COLS : 2 * COLS, :]], axis=0)
+    s1 = jnp.concatenate([blank, d1], axis=0)
+    s2 = jnp.concatenate([blank, d2], axis=0)
     score = dot(r1, s1, NT) + dot(r1, s2, NT) + dot(r2, s1, NT)
 
     @pl.when(step == 0)
@@ -198,14 +206,13 @@
                     ref[chip, 12 * t : 12 * (t + 1), :] = acc[t, pl.ds(j, 12, stride=32), :]
 
 
-def gram_sums(live, core, tot, rest, counts, hi, lo, design):
+def gram_sums(live, core, tot, rest, counts, design):
     genes, cells = counts.shape
     return pl.pallas_call(
         gram_kernel,
         grid=(cells // CHUNK,),
         in_specs=[
-            smem(), smem(), full(tot.shape), lanes(genes), lanes(genes),
-            lanes(512), lanes(512), lanes(96),
+            smem(), smem(), full(tot.shape), lanes(genes), lanes(genes), lanes(96),
         ],
         out_specs=[lanes(genes), full((16, 48, 128)), full((16, 48, 128))],
         out_shape=[
@@ -213,10 +220,13 @@
             jax.ShapeDtypeStruct((16, 48, 128), F32),
             jax.ShapeDtypeStruct((16, 48, 128), F32),
         ],
-        scratch_shapes=[pltpu.VMEM((1, cells), F32), pltpu.VMEM((4, genes, 128), F32)],
-        compiler_params=params(50),
+        scratch_shapes=[
+            pltpu.VMEM((1, cells), F32), pltpu.VMEM((4, genes, 128), F32),
+            pltpu.VMEM((512, CHUNK), BF16), pltpu.VMEM((512, CHUNK), BF16),
+        ],
+        compiler_params=params(),
         name="gram_sums",
-    )(live, core, tot, rest, counts, hi, lo, design)
+    )(live, core, tot, rest, counts, design)
 
 
 def solve_kernel(parts_ref, out_ref, table):
@@ -272,14 +282,14 @@
         out_specs=full((32, 1, 384)),
         out_shape=jax.ShapeDtypeStruct((32, 1, 384), F32),
         scratch_shapes=[pltpu.VMEM((512, 128), F32)],
-        compiler_params=params(16),
+        compiler_params=params(),
         name="solve",
     )(parts)
 
 
 def update_kernel(
-    live_ref, steps_ref, pred_ref, counts_ref, design_ref, load_ref, fact_ref,
-    out_ref, sums_ref, beta_ref, left,
+    live_ref, core_ref, steps_ref, pred_ref, counts_ref, design_ref, load_ref, fact_ref,
+    out_ref, kept_ref, given_ref, beta_ref, left, sums,
 ):
     step = pl.program_id(0)
 
@@ -290,7 +300,7 @@
         b1, b2, b3 = split3(beta)
         left[...] = jnp.concatenate([b1, b1, b2, b2, b1, b3], axis=1)
         beta_ref[...] = beta.T
-        sums_ref[...] = jnp.zeros_like(sums_ref)
+        sums[...] = jnp.zeros_like(sums)
 
     at = step * CHUNK
     d1, d2, d3 = design_ref[0:32, :], design_ref[32:64, :], design_ref[64:96, :]
@@ -314,33 +324,58 @@
     grad = dot(fact, r1, NT) + dot(fact, r2, NT)
     curv = dot(f1, w1, NT) + dot(f2, w1, NT) + dot(f1, w2, NT)
     for h in range(2):
-        sums_ref[h, :32, :] += grad[32 * h : 32 * (h + 1), :]
-        sums_ref[h, 32:, :] += curv[32 * h : 32 * (h + 1), :]
-
-
-def update(live, steps, pred, counts, design, load, fact):
+        sums[h, :32, :] += grad[32 * h : 32 * (h + 1), :]
+        sums[h, 32:, :] += curv[32 * h : 32 * (h + 1), :]
+
+    @pl.when(step == pl.num_programs(0) - 1)
+    def _():
+        kept_ref[...] = sums[core_ref[0]]
+        given_ref[...] = sums[1 - core_ref[0]]
+
+
+def update(live, core, steps, pred, counts, design, load, fact):
     genes, cells = counts.shape
     return pl.pallas_call(
         update_kernel,
         grid=(cells // CHUNK,),
         in_specs=[
-            smem(), full((32, 384)), lanes(genes), lanes(genes), lanes(96),
+            smem(), smem(), full((32, 384)), lanes(genes), lanes(genes), lanes(96),
             full((FACT, genes)), lanes(FACT),
         ],
         out_specs=[
             pl.BlockSpec((CHUNK // 128, 2 * FACT, 128), lambda c: (c, 0, 0)),
-            full((2, FACT, genes)),
+            full((FACT, genes)),
+            full((FACT, genes)),
             full((COLS, genes)),
         ],
         out_shape=[
-            jax.ShapeDtypeStruct((cells // 128, 2 * FACT, 128), F32),
-            jax.ShapeDtypeStruct((2, FACT, genes), F32),
+            pltpu.HBM((cells // 128, 2 * FACT, 128), F32),
+            jax.ShapeDtypeStruct((FACT, genes), F32),
+            jax.ShapeDtypeStruct((FACT, genes), F32),
             jax.ShapeDtypeStruct((COLS, genes), F32),
         ],
-        scratch_shapes=[pltpu.VMEM((genes, 6 * COLS), BF16)],
+        scratch_shapes=[pltpu.VMEM((genes, 6 * COLS), BF16), pltpu.VMEM((2, FACT, genes), F32)],
         compiler_params=params(),
         name="update",
-    )(live, steps, pred, counts, design, load, fact)
+    )(live, core, steps, pred, counts, design, load, fact)
+
+
+def score_kernel(core_ref, mine_ref, other_ref, out_ref):
+    core = core_ref[0]
+    for half, ref in ((core, mine_ref), (1 - core, other_ref)):
+        out_ref[pl.ds(pl.multiple_of(32 * half, 32), 32), :] = ref[...]
+
+
+def joined_score(core, mine, other):
+    return pl.pallas_call(
+        score_kernel,
+        grid=(1,),
+        in_specs=[smem(), full(mine.shape), full(mine.shape)],
+        out_specs=full((FACT, mine.shape[1])),
+        out_shape=jax.ShapeDtypeStruct((FACT, mine.shape[1]), F32),
+        compiler_params=params(),
+        name="joined_score",
+    )(core, mine, other)
 
 
 def factor_kernel(parts_ref, out_ref):
@@ -359,7 +394,7 @@
         in_specs=[full(parts.shape)],
         out_specs=full((peers, FACT, 128)),
         out_shape=jax.ShapeDtypeStruct((peers, FACT, 128), F32),
-        compiler_params=params(16),
+        compiler_params=params(),
         name="factor_share",
     )(parts)
 
@@ -385,7 +420,7 @@
 SAME_CORE = [list(range(core, 32, 2)) for core in range(2)]
 OTHER_CORE = partners(lambda x, y, c: (x, y, 1 - c))
 ALONG_X = [partners(lambda x, y, c, k=k: (x ^ k, y, c)) for k in (1, 2, 3)]
-ALONG_Y = [partners(lambda x, y, c, k=k: (x, y ^ k, c)) for k in (1, 2, 3)]
+ALONG_Y = [partners(lambda x, y, c, k=k: (x, y ^ k, c)) for k in (1, 3)]
 
 
 def local(
@@ -394,35 +429,33 @@
 ):
     fact, load = factors.T, loadings.T
     tot = exchange(cell_totals(counts, 8), "gene")
-    rest, hi, lo, design = prepare(
+    rest, design = prepare(
         knot_bin[None], depth_frac[None], batch_id[None], cell_covariates,
         coefficients.T, batch_effect.T, load, fact,
     )
-    core = lax.axis_index("cell") % 2
-    first = core == 0
+    core = (lax.axis_index("cell") % 2)[None]
     pred, kept, given = gram_sums(
-        live_cells, core[None], tot, rest, counts, hi, lo, design
+        live_cells, core, tot, rest, counts, design
     )
     packed = kept + lax.ppermute(given, "cell", OTHER_CORE)
     steps = exchange(solve(exchange(packed, "cell", SAME_CORE)), "cell")
-    pieces, sums, beta = update(
-        live_cells, steps.reshape(32, 384), pred, counts, design, load, fact
+    pieces, kept, given, beta = update(
+        live_cells, core, steps.reshape(32, 384), pred, counts, design, load, fact
     )
     arrived = exchange(pieces, "gene")
 
-    kept = jnp.where(first, sums[0], sums[1])
-    given = jnp.where(first, sums[1], sums[0])
     value = kept + lax.ppermute(given, "cell", OTHER_CORE)
-    for near, across, beside in (ALONG_X, ALONG_Y):
-        value = (value + lax.ppermute(value, "cell", near)) + (
-            lax.ppermute(value, "cell", across) + lax.ppermute(value, "cell", beside)
-        )
-    gathered = exchange(factor_share(arrived), "gene")
+    near, across, beside = (lax.ppermute(value, "cell", pairs) for pairs in ALONG_X)
+    value = (value + near) + (across + beside)
+    near = lax.ppermute(value, "cell", ALONG_Y[0])
+    shared = factor_share(arrived)
+    gathered = exchange(shared, "gene")
+    near, _ = lax.optimization_barrier((near, shared))
+    value = value + near
+    value = value + lax.ppermute(value, "cell", ALONG_Y[1])
     mine = value[:32] / jnp.sqrt(value[32:] + 1.0)
     other = lax.ppermute(mine, "cell", OTHER_CORE)
-    score = jnp.where(
-        first, jnp.concatenate([mine, other]), jnp.concatenate([other, mine])
-    )
+    score = joined_score(core, mine, other)
     factor_step = jnp.moveaxis(gathered, 0, 1).reshape(FACT, -1)
     return beta.T, factor_step.T, score.T
 

time: 110 us -> 101 us (0.918); the launches traced: 108 us -> 100 us
  blocking collectives: 15.8 us -> 28.2 us
  starting transfers between devices: 36.8 us -> 26.6 us
  Pallas kernels: 21.6 us -> 14.8 us
  other arithmetic: 2.67 us -> 0.13 us
    all_to_all x1 -> x2, blocking collectives: 15.8 us -> 28.2 us  [exchange(): lax.all_to_all(value, axis, split_axis=0, concat_axis=0, tiled=True, axis...]
    all_to_all x4 -> x3, starting transfers between devices: 24.2 us -> 17.6 us  [exchange(): lax.all_to_all(value, axis, split_axis=0, concat_axis=0, tiled=True, axis...]
    all_to_all x4 -> x3, waiting for transfers between devices: 16.4 us -> 12.6 us  [exchange(): lax.all_to_all(value, axis, split_axis=0, concat_axis=0, tiled=True, axis...]
    ppermute x6 -> x5, starting transfers between devices: 7.89 us -> 4.69 us  [the longest x3 3.34 us: local(): lax.ppermute(value, 'cell', pairs)]
    ppermute x6 -> x5, waiting for transfers between devices: 5.44 us -> 8.52 us  [the longest x3 4.34 us: local(): lax.ppermute(value, 'cell', pairs)]
    pallas_call x1, Pallas kernels: 4.4 us -> 1.54 us  [prepare(): pl.pallas_call(prepare_kernel, grid=(cells // CHUNK,), in_specs=[lanes(1)...]
    pallas_call x1, Pallas kernels: 6.16 us -> 4.02 us  [gram_sums(): pl.pallas_call(gram_kernel, grid=(cells // CHUNK,), in_specs=[smem(), sme...]
    pallas_call x2 -> x3, Pallas kernels: 8.74 us -> 7.54 us  [the longest x1 4.62 us: update(): pl.pallas_call(update_kernel, grid=(cells // CHUNK,), in_specs=[smem(), s...]
  transfers between devices with their start and end apart: 13 -> 11, of which waited for: 10 -> 9; matrix products, arithmetic and copies ran while one was open for 2% -> 0% of each run, Pallas kernels for 5% -> 3%
where the time goes in v3:
time: 101 us; the launch traced here: 100 us
  blocking collectives  28.2 us (28%)
  starting transfers between devices  26.6 us (26%)
  waiting for transfers between devices  24.3 us (24%)
  Pallas kernels  14.8 us (15%)
  local copies, waits for them, and re-layouts  4.76 us (5%)
  between operations  1.45 us (1%)
    all_to_all x2, blocking collectives, exchange(): lax.all_to_all(value, axis, split_axis=0, concat_axis=0, tiled=True, axis...  28.2 us
    all_to_all x3, starting transfers between devices, exchange(): lax.all_to_all(value, axis, split_axis=0, concat_axis=0, tiled=True, axis...  17.6 us
    all_to_all x3, waiting for transfers between devices, exchange(): lax.all_to_all(value, axis, split_axis=0, concat_axis=0, tiled=True, axis...  12.6 us
    pallas_call x1, Pallas kernels, update(): pl.pallas_call(update_kernel, grid=(cells // CHUNK,), in_specs=[smem(), s...  4.62 us
    ppermute x3, waiting for transfers between devices, local(): lax.ppermute(value, 'cell', pairs)  4.34 us
    ppermute x1, waiting for transfers between devices, local(): value = value + lax.ppermute(value, 'cell', ALONG_Y[1])  4.18 us
    unnamed x21, local copies, waits for them, and re-layouts  4.04 us
    pallas_call x1, Pallas kernels, gram_sums(): pl.pallas_call(gram_kernel, grid=(cells // CHUNK,), in_specs=[smem(), sme...  4.02 us
  transfers between devices with their start and end apart: 11, of which 9 were waited for; matrix products, arithmetic and copies ran while one was open for 0% of the time, Pallas kernels for 3%

profile of v3, /device:TPU:1, one launch (start us, length us, event | category | flops | bytes accessed | tf_op | source)
XLA Modules:
  0.0 100.3 jit_solution(2147811315042150819)
XLA Ops:
  0.6 0.0 copy-start
  0.6 0.0 copy-start.1
  0.7 0.0 copy-start.8
  0.7 0.0 copy-start.7
  0.7 2.3 %cell_totals.1 = f32[8,8,128]{2,1,0:T(8,128)} custom-call(s32[384,1024]{1,0:T(8,128)} %counts_ref.5), custom_call_target="tpu_custom_call" | custom-call | tf_op jit(solution)/shard_map/cell_totals/pallas_call | solution.py:80
  3.0 9.0 %all-to-all-start = ((f32[8,8,128]{2,1,0:T(8,128)}), f32[8,8,128]{2,1,0:T(8,128)S(1)}, u32[]{:S(2)}, u32[]{:S(2)}) async-start(f32[8,8,128]{2,1,0:T(8,128)} %cell_totals.1), calls=%async_computation | async-start | bytes 65536 | tf_op jit(solution)/shard_map/all_to_all | solution.py:403
  12.6 0.0 copy-done.1
  12.7 0.0 copy-done.8
  12.7 0.0 copy-done.7
  12.7 0.0 copy-start.2
  12.7 0.8 copy-done.2
  13.5 0.9 copy-done.4
  14.4 0.8 copy-done.5
  15.2 0.8 copy-done.6
  16.0 0.7 copy-done.9
  16.7 1.5 %prepare.1 = (f32[384,1024]{1,0:T(8,128)S(1)}, bf16[96,1024]{1,0:T(8,128)(2,1)S(1)}) custom-call(s32[1,1024]{1,0:T(1,128)S(1)} %bitcast.28, f32[1,1024]{1,0:T(1,128)S(1)} %bitcast.29, s32[1,1024]{1,0:T(1,128)S(1)} %bitcast.30, f32[16,1024]{1,0:T(8,128)S(1)} %copy-done.5, f32[32,384]{1,0:T(8,128)S(1)} %bitcast.27, f32[64,384]{1,0:T(8,128)S(1)} %bitcast.26, ...), custom_call_target="tpu_custom_call" | custom-call | tf_op jit(solution)/shard_map/prepare/pallas_call | solution.py:125
  18.2 0.6 all-to-all-done.tot_ref
  18.9 0.0 copy-done
  18.9 4.0 %gram_sums.1 = (f32[384,1024]{1,0:T(8,128)S(1)}, f32[16,48,128]{2,1,0:T(8,128)S(1)}, f32[16,48,128]{2,1,0:T(8,128)S(1)}) custom-call(s32[1]{0:T(128)S(6)} %copy.22.live_ref, s32[1]{0:T(128)} %bitcast.core_ref, f32[8,8,128]{2,1,0:T(8,128)S(1)} %all-to-all-done.tot_ref, f32[384,1024]{1,0:T(8,128)S(1)} %get-tuple-element.13.rest_ref, s32[384,1024]{1,0:T(8,128)S(1)} %copy-done, ...), custom_call_target="tpu_custom_call" | custom-call | tf_op jit(solution)/shard_map/gram_sums/pallas_call | solution.py:211
  22.9 0.0 copy-start.3
  22.9 2.2 %collective-permute-start = (f32[16,48,128]{2,1,0:T(8,128)S(1)}, f32[16,48,128]{2,1,0:T(8,128)S(1)}, u32[]{:S(2)}, u32[]{:S(2)}) collective-permute-start(f32[16,48,128]{2,1,0:T(8,128)S(1)} %get-tuple-element.16), channel_id=1, source_target_pairs={{0,8},{8,0},{16,24},{24,16},{32,40},{40,32},{48,56},{56,48},{64,72... | collective-permute-start | bytes 1179656 | tf_op jit(solution)/shard_map/ppermute | solution.py:440
  25.1 1.3 %collective-permute-done = f32[16,48,128]{2,1,0:T(8,128)S(1)} collective-permute-done((f32[16,48,128]{2,1,0:T(8,128)S(1)}, f32[16,48,128]{2,1,0:T(8,128)S(1)}, u32[]{:S(2)}, u32[]{:S(2)}) %collective-permute-start) | collective-permute-done | bytes 393248 | tf_op jit(solution)/shard_map/ppermute | solution.py:440
  26.4 0.1 add.32
  26.5 15.8 %all_to_all.25.parts_ref = f32[16,48,128]{2,1,0:T(8,128)S(1)} all-to-all(f32[16,48,128]{2,1,0:T(8,128)S(1)} %add.32), channel_id=1, replica_groups={{0,16,32,48,64,80,96,112,128,144,160,176,192,208,224,240},{8,24,40,56,7..., dimensions={0} | all-to-all | bytes 786432 | tf_op jit(solution)/shard_map/all_to_all | solution.py:403
  42.3 1.0 solve.1
  43.3 12.4 %all_to_all.26 = f32[32,1,384]{2,1,0:T(1,128)S(1)} all-to-all(f32[32,1,384]{2,1,0:T(1,128)S(1)} %solve.1), channel_id=1, replica_groups=mesh['cell'=32,'gene'=8] {'cell'}, dimensions={0} | all-to-all | bytes 98304 | tf_op jit(solution)/shard_map/all_to_all | solution.py:403
  55.7 4.6 %update.1 = (f32[8,128,128]{2,1,0:T(8,128)}, f32[64,384]{1,0:T(8,128)S(1)}, f32[64,384]{1,0:T(8,128)S(1)}, f32[32,384]{1,0:T(8,128)}) custom-call(s32[1]{0:T(128)S(6)} %copy.22.live_ref, s32[1]{0:T(128)} %bitcast.core_ref, f32[32,384]{1,0:T(8,128)S(1)} %bitcast.25, f32[384,1024]{1,0:T(8,128)S(1)} %get-tuple-element.17.pred_ref, s32[384,1024]{1,0:T(8,128)S(1)} %copy-done, ...), custom_call_target="tpu_custom_call" | custom-call | tf_op jit(solution)/shard_map/update/pallas_call | solution.py:338
  60.3 5.2 %all-to-all-start.3 = ((f32[8,128,128]{2,1,0:T(8,128)}), f32[8,128,128]{2,1,0:T(8,128)S(1)}, u32[]{:S(2)}, u32[]{:S(2)}) async-start(f32[8,128,128]{2,1,0:T(8,128)} %get-tuple-element.19), calls=%async_computation.3 | async-start | bytes 1048576 | tf_op jit(solution)/shard_map/all_to_all | solution.py:403
  65.5 0.7 collective-permute-start.1
  66.2 0.9 collective-permute-done.1
  67.1 0.9 collective-permute-start.4
  68.1 1.2 %collective-permute-start.3 = (f32[64,384]{1,0:T(8,128)S(1)}, f32[64,384]{1,0:T(8,128)S(1)}, u32[]{:S(2)}, u32[]{:S(2)}) collective-permute-start(f32[64,384]{1,0:T(8,128)S(1)} %add.33), channel_id=1, source_target_pairs={{0,128},{8,136},{16,144},{24,152},{32,160},{40,168},{48,176},{56,1... | collective-permute-start | bytes 294920 | tf_op jit(solution)/shard_map/ppermute | solution.py:448
  69.3 1.1 %collective-permute-start.2 = (f32[64,384]{1,0:T(8,128)S(1)}, f32[64,384]{1,0:T(8,128)S(1)}, u32[]{:S(2)}, u32[]{:S(2)}) collective-permute-start(f32[64,384]{1,0:T(8,128)S(1)} %add.33), channel_id=1, source_target_pairs={{0,64},{8,72},{16,80},{24,88},{32,96},{40,104},{48,112},{56,120},{... | collective-permute-start | bytes 294920 | tf_op jit(solution)/shard_map/ppermute | solution.py:448
  70.5 3.1 %collective-permute-done.4 = f32[64,384]{1,0:T(8,128)S(1)} collective-permute-done((f32[64,384]{1,0:T(8,128)S(1)}, f32[64,384]{1,0:T(8,128)S(1)}, u32[]{:S(2)}, u32[]{:S(2)}) %collective-permute-start.4) | collective-permute-done | bytes 98336 | tf_op jit(solution)/shard_map/ppermute | solution.py:448
  73.6 0.0 collective-permute-done.3
  73.6 1.2 %collective-permute-done.2 = f32[64,384]{1,0:T(8,128)S(1)} collective-permute-done((f32[64,384]{1,0:T(8,128)S(1)}, f32[64,384]{1,0:T(8,128)S(1)}, u32[]{:S(2)}, u32[]{:S(2)}) %collective-permute-start.2) | collective-permute-done | bytes 98336 | tf_op jit(solution)/shard_map/ppermute | solution.py:448
  74.9 0.4 collective-permute-start.5
  75.2 8.2 %all-to-all-done.3.parts_ref = f32[8,128,128]{2,1,0:T(8,128)S(1)} async-done(((f32[8,128,128]{2,1,0:T(8,128)}), f32[8,128,128]{2,1,0:T(8,128)S(1)}, u32[]{:S(2)}, u32[]{:S(2)}) %all-to-all-start.3) | async-done | bytes 524320 | tf_op jit(solution)/shard_map/all_to_all | solution.py:403
  83.5 0.7 factor_share.1
  84.2 3.4 %all-to-all-start.4 = ((f32[8,64,128]{2,1,0:T(8,128)}), f32[8,64,128]{2,1,0:T(8,128)S(1)}, u32[]{:S(2)}, u32[]{:S(2)}) async-start(f32[8,64,128]{2,1,0:T(8,128)} %factor_share.1), calls=%async_computation.4 | async-start | bytes 524288 | tf_op jit(solution)/shard_map/all_to_all | solution.py:403
  87.6 0.0 collective-permute-done.5
  87.7 1.0 collective-permute-start.6
  88.6 4.2 %collective-permute-done.6 = f32[64,384]{1,0:T(8,128)S(1)} collective-permute-done((f32[64,384]{1,0:T(8,128)S(1)}, f32[64,384]{1,0:T(8,128)S(1)}, u32[]{:S(2)}, u32[]{:S(2)}) %collective-permute-start.6) | collective-permute-done | bytes 98336 | tf_op jit(solution)/shard_map/ppermute | solution.py:455
  92.9 1.4 %collective-permute-start.7 = (f32[32,384]{1,0:T(8,128)S(1)}, f32[32,384]{1,0:T(8,128)S(1)}, u32[]{:S(2)}, u32[]{:S(2)}) collective-permute-start(f32[32,384]{1,0:T(8,128)S(1)} %fusion.1.mine_ref), channel_id=1, source_target_pairs={{0,8},{8,0},{16,24},{24,16},{32,40},{40,32},{48,56},{56,48},{64,72... | collective-permute-start | bytes 147464 | tf_op jit(solution)/shard_map/ppermute | solution.py:457
  94.3 0.9 collective-permute-done.7.other_ref
  95.2 0.6 joined_score.1
  95.8 3.8 %all-to-all-done.4 = f32[8,64,128]{2,1,0:T(8,128)S(1)} async-done(((f32[8,64,128]{2,1,0:T(8,128)}), f32[8,64,128]{2,1,0:T(8,128)S(1)}, u32[]{:S(2)}, u32[]{:S(2)}) %all-to-all-start.4) | async-done | bytes 262176 | tf_op jit(solution)/shard_map/all_to_all | solution.py:403
  99.6 0.7 bitcast_bitcast_fusion
  (11 shorter events, 0.1 us)
Async XLA Ops:
  0.6 18.2 %copy-start = (s32[384,1024]{1,0:T(8,128)S(1)}, s32[384,1024]{1,0:T(8,128)}, u32[]{:S(2)}) copy-start(s32[384,1024]{1,0:T(8,128)} %counts_ref.5) | copy-start | bytes 4718596
  0.6 12.0 %copy-start.1 = (bf16[1024,64]{0,1:T(8,128)(2,1)S(1)}, bf16[1024,64]{0,1:T(8,128)(2,1)}, u32[]{:S(2)}) copy-start(bf16[1024,64]{0,1:T(8,128)(2,1)} %param.18) | copy-start | bytes 393220
  0.7 12.0 %copy-start.8 = (f32[1024]{0:T(1024)S(1)}, f32[1024]{0:T(1024)}, u32[]{:S(2)}) copy-start(f32[1024]{0:T(1024)} %param.14) | copy-start | bytes 12292
  0.7 12.0 %copy-start.7 = (s32[1024]{0:T(1024)S(1)}, s32[1024]{0:T(1024)}, u32[]{:S(2)}) copy-start(s32[1024]{0:T(1024)} %param.13) | copy-start | bytes 12292
  3.0 15.9 %all-to-all-start = ((f32[8,8,128]{2,1,0:T(8,128)}), f32[8,8,128]{2,1,0:T(8,128)S(1)}, u32[]{:S(2)}, u32[]{:S(2)}) async-start(f32[8,8,128]{2,1,0:T(8,128)} %cell_totals.1), calls=%async_computation | async-start | bytes 65536 | tf_op jit(solution)/shard_map/all_to_all | solution.py:403
  12.7 0.8 copy-start.2
  13.5 0.9 copy-start.4
  14.4 0.8 copy-start.5
  15.2 0.8 copy-start.6
  16.0 0.7 copy-start.9
  22.9 32.8 %copy-start.3 = (bf16[384,64]{0,1:T(8,128)(2,1)S(1)}, bf16[384,64]{0,1:T(8,128)(2,1)}, u32[]{:S(2)}) copy-start(bf16[384,64]{0,1:T(8,128)(2,1)} %param.19) | copy-start | bytes 147460
  22.9 3.5 %collective-permute-start = (f32[16,48,128]{2,1,0:T(8,128)S(1)}, f32[16,48,128]{2,1,0:T(8,128)S(1)}, u32[]{:S(2)}, u32[]{:S(2)}) collective-permute-start(f32[16,48,128]{2,1,0:T(8,128)S(1)} %get-tuple-element.16), channel_id=1, source_target_pairs={{0,8},{8,0},{16,24},{24,16},{32,40},{40,32},{48,56},{56,48},{64,72... | collective-permute-start | bytes 1179656 | tf_op jit(solution)/shard_map/ppermute | solution.py:440
  60.3 23.1 %all-to-all-start.3 = ((f32[8,128,128]{2,1,0:T(8,128)}), f32[8,128,128]{2,1,0:T(8,128)S(1)}, u32[]{:S(2)}, u32[]{:S(2)}) async-start(f32[8,128,128]{2,1,0:T(8,128)} %get-tuple-element.19), calls=%async_computation.3 | async-start | bytes 1048576 | tf_op jit(solution)/shard_map/all_to_all | solution.py:403
  65.5 1.6 %collective-permute-start.1 = (f32[64,384]{1,0:T(8,128)S(1)}, f32[64,384]{1,0:T(8,128)S(1)}, u32[]{:S(2)}, u32[]{:S(2)}) collective-permute-start(f32[64,384]{1,0:T(8,128)S(1)} %get-tuple-element.21), channel_id=1, source_target_pairs={{0,8},{8,0},{16,24},{24,16},{32,40},{40,32},{48,56},{56,48},{64,72... | collective-permute-start | bytes 294920 | tf_op jit(solution)/shard_map/ppermute | solution.py:447
  67.1 6.5 %collective-permute-start.4 = (f32[64,384]{1,0:T(8,128)S(1)}, f32[64,384]{1,0:T(8,128)S(1)}, u32[]{:S(2)}, u32[]{:S(2)}) collective-permute-start(f32[64,384]{1,0:T(8,128)S(1)} %add.33), channel_id=1, source_target_pairs={{0,192},{8,200},{16,208},{24,216},{32,224},{40,232},{48,240},{56,2... | collective-permute-start | bytes 294920 | tf_op jit(solution)/shard_map/ppermute | solution.py:448
  68.1 5.5 %collective-permute-start.3 = (f32[64,384]{1,0:T(8,128)S(1)}, f32[64,384]{1,0:T(8,128)S(1)}, u32[]{:S(2)}, u32[]{:S(2)}) collective-permute-start(f32[64,384]{1,0:T(8,128)S(1)} %add.33), channel_id=1, source_target_pairs={{0,128},{8,136},{16,144},{24,152},{32,160},{40,168},{48,176},{56,1... | collective-permute-start | bytes 294920 | tf_op jit(solution)/shard_map/ppermute | solution.py:448
  69.3 5.5 %collective-permute-start.2 = (f32[64,384]{1,0:T(8,128)S(1)}, f32[64,384]{1,0:T(8,128)S(1)}, u32[]{:S(2)}, u32[]{:S(2)}) collective-permute-start(f32[64,384]{1,0:T(8,128)S(1)} %add.33), channel_id=1, source_target_pairs={{0,64},{8,72},{16,80},{24,88},{32,96},{40,104},{48,112},{56,120},{... | collective-permute-start | bytes 294920 | tf_op jit(solution)/shard_map/ppermute | solution.py:448
  74.9 12.8 %collective-permute-start.5 = (f32[64,384]{1,0:T(8,128)S(1)}, f32[64,384]{1,0:T(8,128)S(1)}, u32[]{:S(2)}, u32[]{:S(2)}) collective-permute-start(f32[64,384]{1,0:T(8,128)S(1)} %add_add_fusion), channel_id=1, source_target_pairs={{0,16},{8,24},{16,0},{24,8},{32,48},{40,56},{48,32},{56,40},{64,80... | collective-permute-start | bytes 294920 | tf_op jit(solution)/shard_map/ppermute | solution.py:450
  84.2 15.4 %all-to-all-start.4 = ((f32[8,64,128]{2,1,0:T(8,128)}), f32[8,64,128]{2,1,0:T(8,128)S(1)}, u32[]{:S(2)}, u32[]{:S(2)}) async-start(f32[8,64,128]{2,1,0:T(8,128)} %factor_share.1), calls=%async_computation.4 | async-start | bytes 524288 | tf_op jit(solution)/shard_map/all_to_all | solution.py:403
  87.7 5.2 %collective-permute-start.6 = (f32[64,384]{1,0:T(8,128)S(1)}, f32[64,384]{1,0:T(8,128)S(1)}, u32[]{:S(2)}, u32[]{:S(2)}) collective-permute-start(f32[64,384]{1,0:T(8,128)S(1)} %add.37), channel_id=1, source_target_pairs={{0,48},{8,56},{16,32},{24,40},{32,16},{40,24},{48,0},{56,8},{64,11... | collective-permute-start | bytes 294920 | tf_op jit(solution)/shard_map/ppermute | solution.py:455
  92.9 2.3 %collective-permute-start.7 = (f32[32,384]{1,0:T(8,128)S(1)}, f32[32,384]{1,0:T(8,128)S(1)}, u32[]{:S(2)}, u32[]{:S(2)}) collective-permute-start(f32[32,384]{1,0:T(8,128)S(1)} %fusion.1.mine_ref), channel_id=1, source_target_pairs={{0,8},{8,0},{16,24},{24,16},{32,40},{40,32},{48,56},{56,48},{64,72... | collective-permute-start | bytes 147464 | tf_op jit(solution)/shard_map/ppermute | solution.py:457

commit v4 on v3

--- a/solution.py
+++ b/solution.py
@@ -93,55 +93,91 @@
 
 
 def prepare_kernel(
-    knot_ref, frac_ref, batch_ref, cov_ref, coef_ref, shift_ref, load_ref, fact_ref,
-    rest_ref, design_ref, left,
+    live_ref, counts_ref, knot_hbm, frac_hbm, batch_hbm, cov_hbm, coef_hbm, shift_hbm,
+    load_hbm, fact_hbm,
+    rest_ref, design_ref, score_ref, by_load_ref, by_fact_ref,
+    left, knot_all, frac_all, batch_all, cov_all, coef, shift, load, fact_all, score, arrived,
 ):
-    @pl.when(pl.program_id(0) == 0)
+    step = pl.program_id(0)
+
+    @pl.when(step == 0)
     def _():
-        c1, c2, c3 = split3(coef_ref[...])
-        b1, b2, b3 = split3(shift_ref[...])
-        left[...] = jnp.concatenate([c1, c1, c2, c2, c1, c3, b1, b2, b3, load_ref[...]], axis=0)
-
-    knot, frac = knot_ref[...], frac_ref[...]
-    width = knot.shape[1]
-    cov = cov_ref[...]
-    levels = lax.broadcasted_iota(jnp.int32, (SPL, width), 0)
-    here, above = levels == knot, levels == knot + 1
-    rest = 1.0 - frac
-    hat = jnp.where(here, rest, 0.0) + jnp.where(above, frac, 0.0)
+        pairs = (
+            (coef_hbm, coef), (shift_hbm, shift), (load_hbm, load), (fact_hbm, fact_all),
+            (knot_hbm, knot_all), (frac_hbm, frac_all), (batch_hbm, batch_all), (cov_hbm, cov_all),
+        )
+        copies = [
+            pltpu.make_async_copy(source, target, arrived.at[i])
+            for i, (source, target) in enumerate(pairs)
+        ]
+        for copy in copies:
+            copy.start()
+        for copy in copies:
+            copy.wait()
+        c1, c2, c3 = split3(coef[...])
+        b1, b2, b3 = split3(shift[...])
+        left[...] = jnp.concatenate([c1, c1, c2, c2, c1, c3, b1, b2, b3, load[...]], axis=0)
+        score[...] = jnp.zeros_like(score)
+        by_fact_ref[...] = jnp.zeros_like(by_fact_ref)
+
+    at = pl.multiple_of(step * CHUNK, CHUNK)
+    here = pl.ds(at, CHUNK)
+    knot, frac, cov, fact = knot_all[:, here], frac_all[:, here], cov_all[:, here], fact_all[:, here]
+    levels = lax.broadcasted_iota(jnp.int32, (SPL, CHUNK), 0)
+    hat = jnp.where(levels == knot, 1.0 - frac, 0.0) + jnp.where(levels == knot + 1, frac, 0.0)
     d1, d2, d3 = split3(jnp.concatenate([hat, cov], axis=0))
-    design_ref[...] = jnp.concatenate([d1, d2, d3], axis=0)
-    batches = lax.broadcasted_iota(jnp.int32, (64, width), 0)
-    onehot = (batches == batch_ref[...]).astype(F32).astype(BF16)
-    right = jnp.concatenate(
-        [d1, d2, d1, d2, d3, d1, onehot, onehot, onehot, fact_ref[...]], axis=0
-    )
+    terms = jnp.concatenate([d1, d2, d3], axis=0)
+    design_ref[...] = terms
+    batches = lax.broadcasted_iota(jnp.int32, (64, CHUNK), 0)
+    onehot = (batches == batch_all[:, here]).astype(F32).astype(BF16)
+    right = jnp.concatenate([d1, d2, d1, d2, d3, d1, onehot, onehot, onehot, fact], axis=0)
     rest_ref[...] = dot(left[...], right, TN)
 
-
-def prepare(knot, frac, batch, cov, coef, shift, load, fact):
-    cells = knot.shape[1]
-    genes = coef.shape[1]
+    slot = lax.broadcasted_iota(jnp.int32, (1, CHUNK), 1) + at
+    mask = (slot < live_ref[0]).astype(F32)
+    counts = (counts_ref[...].astype(F32) * mask).astype(BF16)
+    by_load_ref[...] = dot(load[...], counts, NN)
+    by_fact_ref[...] += dot(fact, counts, NT)
+    score[...] += dot(counts, terms, NT)
+
+    @pl.when(step == pl.num_programs(0) - 1)
+    def _():
+        value = score[:, :32] + score[:, 32:64] + score[:, 64:96]
+        blank = jnp.zeros((value.shape[0], 96), F32)
+        score_ref[...] = jnp.concatenate([blank, value], axis=1)
+
+
+def prepare(live, counts, knot, frac, batch, cov, coef, shift, load, fact):
+    genes, cells = counts.shape
+    small = [
+        pltpu.with_memory_space_constraint(a, pltpu.HBM)
+        for a in (knot, frac, batch, cov, coef, shift, load, fact)
+    ]
+    counts = pltpu.with_memory_space_constraint(counts, pltpu.HBM)
     return pl.pallas_call(
         prepare_kernel,
         grid=(cells // CHUNK,),
-        in_specs=[
-            lanes(1), lanes(1), lanes(1), lanes(16),
-            full((COLS, genes)), full((64, genes)), full((FACT, genes)), lanes(FACT),
-        ],
-        out_specs=[lanes(genes), lanes(96)],
+        in_specs=[smem(), lanes(genes)] + [pl.BlockSpec(memory_space=pltpu.HBM)] * 8,
+        out_specs=[
+            lanes(genes), lanes(96), full((genes, 128)), lanes(FACT), full((FACT, genes)),
+        ],
         out_shape=[
             jax.ShapeDtypeStruct((genes, cells), F32),
             jax.ShapeDtypeStruct((96, cells), BF16),
-        ],
-        scratch_shapes=[pltpu.VMEM((448, genes), BF16)],
+            jax.ShapeDtypeStruct((genes, 128), F32),
+            jax.ShapeDtypeStruct((FACT, cells), F32),
+            jax.ShapeDtypeStruct((FACT, genes), F32),
+        ],
+        scratch_shapes=[pltpu.VMEM((448, genes), BF16)]
+        + [pltpu.VMEM(a.shape, a.dtype) for a in small]
+        + [pltpu.VMEM((genes, 96), F32), pltpu.SemaphoreType.DMA((8,))],
         compiler_params=params(),
         name="prepare",
-    )(knot, frac, batch, cov, coef, shift, load, fact)
+    )(live, counts, *small)
 
 
 def gram_kernel(
-    live_ref, core_ref, tot_ref, rest_ref, counts_ref, design_ref,
+    live_ref, core_ref, tot_ref, rest_ref, design_ref, score_ref,
     pred_ref, kept_ref, given_ref, offset, acc, hi_ref, lo_ref,
 ):
     step = pl.program_id(0)
@@ -152,17 +188,15 @@
         value = jnp.log((1.0 + total) / GENES)
         for i in range(8):
             offset[:, 128 * i : 128 * (i + 1)] = value[i : i + 1, :]
+        acc[:3] = jnp.zeros_like(acc[:3])
+        acc[3] = score_ref[...]
 
     at = pl.multiple_of(step * CHUNK, CHUNK)
     pred = rest_ref[...] + offset[:, pl.ds(at, CHUNK)]
     pred_ref[...] = pred
-    expected = jnp.exp(pred)
     slot = lax.broadcasted_iota(jnp.int32, (1, CHUNK), 1) + at
     mask = (slot < live_ref[0]).astype(F32)
-    weight = expected * mask
-    residual = (counts_ref[...].astype(F32) - expected) * mask
-    w1, w2 = split2(weight)
-    r1, r2 = split2(residual)
+    w1, w2 = split2(jnp.exp(pred) * mask)
 
     def put(at, value):
         hi, lo = split2(value)
@@ -181,21 +215,11 @@
         put(288 + 8 * i, jnp.concatenate([low[i : i + 1] * low, low[i + 1 : i + 2] * low], axis=0))
         put(352 + 8 * i, jnp.concatenate([low[i : i + 1] * high, low[i + 1 : i + 2] * high], axis=0))
         put(416 + 8 * i, jnp.concatenate([high[i : i + 1] * high, high[i + 1 : i + 2] * high], axis=0))
-    put(480, jnp.zeros((32, CHUNK), F32))
+    put(480, -design)
     hi, lo = hi_ref[...], lo_ref[...]
     gram = dot(w1, hi, NT) + dot(w1, lo, NT) + dot(w2, hi, NT)
-    blank = jnp.zeros((96, CHUNK), BF16)
-    s1 = jnp.concatenate([blank, d1], axis=0)
-    s2 = jnp.concatenate([blank, d2], axis=0)
-    score = dot(r1, s1, NT) + dot(r1, s2, NT) + dot(r2, s1, NT)
-
-    @pl.when(step == 0)
-    def _():
-        acc[...] = jnp.zeros_like(acc)
-
     for t in range(4):
-        part = gram[:, 128 * t : 128 * (t + 1)]
-        acc[t] += part + score if t == 3 else part
+        acc[t] += gram[:, 128 * t : 128 * (t + 1)]
 
     @pl.when(step == pl.num_programs(0) - 1)
     def _():
@@ -206,13 +230,13 @@
                     ref[chip, 12 * t : 12 * (t + 1), :] = acc[t, pl.ds(j, 12, stride=32), :]
 
 
-def gram_sums(live, core, tot, rest, counts, design):
-    genes, cells = counts.shape
+def gram_sums(live, core, tot, rest, design, score):
+    genes, cells = rest.shape
     return pl.pallas_call(
         gram_kernel,
         grid=(cells // CHUNK,),
         in_specs=[
-            smem(), smem(), full(tot.shape), lanes(genes), lanes(genes), lanes(96),
+            smem(), smem(), full(tot.shape), lanes(genes), lanes(96), full(score.shape),
         ],
         out_specs=[lanes(genes), full((16, 48, 128)), full((16, 48, 128))],
         out_shape=[
@@ -226,7 +250,7 @@
         ],
         compiler_params=params(),
         name="gram_sums",
-    )(live, core, tot, rest, counts, design)
+    )(live, core, tot, rest, design, score)
 
 
 def solve_kernel(parts_ref, out_ref, table):
@@ -288,8 +312,9 @@
 
 
 def update_kernel(
-    live_ref, core_ref, steps_ref, pred_ref, counts_ref, design_ref, load_ref, fact_ref,
-    out_ref, kept_ref, given_ref, beta_ref, left, sums,
+    live_ref, core_ref, steps_ref, pred_ref, design_ref, load_ref, fact_ref,
+    by_load_ref, by_fact_ref,
+    out_ref, kept_ref, given_ref, beta_ref, left, loads, sums,
 ):
     step = pl.program_id(0)
 
@@ -300,31 +325,36 @@
         b1, b2, b3 = split3(beta)
         left[...] = jnp.concatenate([b1, b1, b2, b2, b1, b3], axis=1)
         beta_ref[...] = beta.T
-        sums[...] = jnp.zeros_like(sums)
+        load = load_ref[...]
+        wide = load.astype(F32)
+        l1, l2 = split2(wide * wide)
+        loads[...] = jnp.concatenate([load, l1, l2], axis=0)
+        for h in range(2):
+            sums[h, :32, :] = by_fact_ref[32 * h : 32 * (h + 1), :]
+            sums[h, 32:, :] = jnp.zeros_like(sums[h, 32:, :])
 
     at = step * CHUNK
     d1, d2, d3 = design_ref[0:32, :], design_ref[32:64, :], design_ref[64:96, :]
     change = dot(left[...], jnp.concatenate([d1, d2, d1, d2, d3, d1], axis=0), NN)
-    expected = jnp.exp(pred_ref[...] + change)
     slot = lax.broadcasted_iota(jnp.int32, (1, CHUNK), 1) + at
     mask = (slot < live_ref[0]).astype(F32)
-    w1, w2 = split2(expected * mask)
-    r1, r2 = split2((counts_ref[...].astype(F32) - expected) * mask)
-    load = load_ref[...]
-    wide = load.astype(F32)
-    l1, l2 = split2(wide * wide)
-    grad = dot(load, r1, NN) + dot(load, r2, NN)
-    curv = dot(l1, w1, NN) + dot(l2, w1, NN) + dot(l1, w2, NN)
+    w1, w2 = split2(jnp.exp(pred_ref[...] + change) * mask)
+    first = dot(loads[...], w1, NN)
+    second = dot(loads[: 2 * FACT], w2, NN)
+    grad = by_load_ref[...] - (first[:FACT] + second[:FACT])
+    curv = (first[FACT : 2 * FACT] + first[2 * FACT :]) + second[FACT:]
     for i in range(CHUNK // 128):
         out_ref[i, :FACT, :] = grad[:, 128 * i : 128 * (i + 1)]
         out_ref[i, FACT:, :] = curv[:, 128 * i : 128 * (i + 1)]
     fact = fact_ref[...]
     wide = fact.astype(F32)
     f1, f2 = split2(wide * wide)
-    grad = dot(fact, r1, NT) + dot(fact, r2, NT)
-    curv = dot(f1, w1, NT) + dot(f2, w1, NT) + dot(f1, w2, NT)
+    first = dot(jnp.concatenate([fact, f1, f2], axis=0), w1, NT)
+    second = dot(jnp.concatenate([fact, f1], axis=0), w2, NT)
+    grad = first[:FACT] + second[:FACT]
+    curv = (first[FACT : 2 * FACT] + first[2 * FACT :]) + second[FACT:]
     for h in range(2):
-        sums[h, :32, :] += grad[32 * h : 32 * (h + 1), :]
+        sums[h, :32, :] -= grad[32 * h : 32 * (h + 1), :]
         sums[h, 32:, :] += curv[32 * h : 32 * (h + 1), :]
 
     @pl.when(step == pl.num_programs(0) - 1)
@@ -333,14 +363,14 @@
         given_ref[...] = sums[1 - core_ref[0]]
 
 
-def update(live, core, steps, pred, counts, design, load, fact):
-    genes, cells = counts.shape
+def update(live, core, steps, pred, design, load, fact, by_load, by_fact):
+    genes, cells = pred.shape
     return pl.pallas_call(
         update_kernel,
         grid=(cells // CHUNK,),
         in_specs=[
-            smem(), smem(), full((32, 384)), lanes(genes), lanes(genes), lanes(96),
-            full((FACT, genes)), lanes(FACT),
+            smem(), smem(), full((32, 384)), lanes(genes), lanes(96),
+            full((FACT, genes)), lanes(FACT), lanes(FACT), full((FACT, genes)),
         ],
         out_specs=[
             pl.BlockSpec((CHUNK // 128, 2 * FACT, 128), lambda c: (c, 0, 0)),
@@ -354,10 +384,13 @@
             jax.ShapeDtypeStruct((FACT, genes), F32),
             jax.ShapeDtypeStruct((COLS, genes), F32),
         ],
-        scratch_shapes=[pltpu.VMEM((genes, 6 * COLS), BF16), pltpu.VMEM((2, FACT, genes), F32)],
+        scratch_shapes=[
+            pltpu.VMEM((genes, 6 * COLS), BF16), pltpu.VMEM((3 * FACT, genes), BF16),
+            pltpu.VMEM((2, FACT, genes), F32),
+        ],
         compiler_params=params(),
         name="update",
-    )(live, core, steps, pred, counts, design, load, fact)
+    )(live, core, steps, pred, design, load, fact, by_load, by_fact)
 
 
 def score_kernel(core_ref, mine_ref, other_ref, out_ref):
@@ -429,18 +462,18 @@
 ):
     fact, load = factors.T, loadings.T
     tot = exchange(cell_totals(counts, 8), "gene")
-    rest, design = prepare(
-        knot_bin[None], depth_frac[None], batch_id[None], cell_covariates,
-        coefficients.T, batch_effect.T, load, fact,
+    rest, design, score, by_load, by_fact = prepare(
+        live_cells, counts, knot_bin[None], depth_frac[None], batch_id[None],
+        cell_covariates, coefficients.T, batch_effect.T, load, fact,
     )
     core = (lax.axis_index("cell") % 2)[None]
     pred, kept, given = gram_sums(
-        live_cells, core, tot, rest, counts, design
+        live_cells, core, tot, rest, design, score
     )
     packed = kept + lax.ppermute(given, "cell", OTHER_CORE)
     steps = exchange(solve(exchange(packed, "cell", SAME_CORE)), "cell")
     pieces, kept, given, beta = update(
-        live_cells, core, steps.reshape(32, 384), pred, counts, design, load, fact
+        live_cells, core, steps.reshape(32, 384), pred, design, load, fact, by_load, by_fact
     )
     arrived = exchange(pieces, "gene")
 

time: 101 us -> 98.1 us (0.971)
  local copies, waits for them, and re-layouts: 4.76 us -> 0.74 us
  Pallas kernels: 14.8 us -> 16.1 us
    unnamed x21 -> x5, local copies, waits for them, and re-layouts: 4.04 us -> 0.02 us
    pallas_call x1, Pallas kernels: 1.54 us -> 4.87 us  [prepare(): pl.pallas_call(prepare_kernel, grid=(cells // CHUNK,), in_specs=[smem(),...]
  transfers between devices with their start and end apart: 11 -> 11, of which waited for: 9 -> 9; matrix products, arithmetic and copies ran while one was open for 0% -> 0% of each run, Pallas kernels for 3% -> 6%
where the time goes in v4:
time: 98.1 us; the launch traced here: 97.5 us
  blocking collectives  28.2 us (29%)
  starting transfers between devices  25.9 us (26%)
  waiting for transfers between devices  25.1 us (26%)
  Pallas kernels  16.1 us (16%)
  between operations  1.39 us (1%)
    all_to_all x2, blocking collectives, exchange(): lax.all_to_all(value, axis, split_axis=0, concat_axis=0, tiled=True, axis...  28.2 us
    all_to_all x3, starting transfers between devices, exchange(): lax.all_to_all(value, axis, split_axis=0, concat_axis=0, tiled=True, axis...  16.9 us
    all_to_all x3, waiting for transfers between devices, exchange(): lax.all_to_all(value, axis, split_axis=0, concat_axis=0, tiled=True, axis...  13.4 us
    pallas_call x1, Pallas kernels, prepare(): pl.pallas_call(prepare_kernel, grid=(cells // CHUNK,), in_specs=[smem(),...  4.87 us
    ppermute x3, waiting for transfers between devices, local(): lax.ppermute(value, 'cell', pairs)  4.34 us
    ppermute x1, waiting for transfers between devices, local(): value = value + lax.ppermute(value, 'cell', ALONG_Y[1])  4.19 us
    pallas_call x1, Pallas kernels, update(): pl.pallas_call(update_kernel, grid=(cells // CHUNK,), in_specs=[smem(), s...  3.66 us
    ppermute x3, starting transfers between devices, local(): lax.ppermute(value, 'cell', pairs)  3.34 us
  transfers between devices with their start and end apart: 11, of which 9 were waited for; matrix products, arithmetic and copies ran while one was open for 0% of the time, Pallas kernels for 6%

profile of v4, /device:TPU:1, one launch (start us, length us, event | category | flops | bytes accessed | tf_op | source)
XLA Modules:
  0.0 97.5 jit_solution(8326163084936587298)
XLA Ops:
  0.6 2.2 %cell_totals.1 = f32[8,8,128]{2,1,0:T(8,128)} custom-call(s32[384,1024]{1,0:T(8,128)} %counts_ref.3), custom_call_target="tpu_custom_call" | custom-call | tf_op jit(solution)/shard_map/cell_totals/pallas_call | solution.py:80
  2.8 9.0 %all-to-all-start = ((f32[8,8,128]{2,1,0:T(8,128)}), f32[8,8,128]{2,1,0:T(8,128)S(1)}, u32[]{:S(2)}, u32[]{:S(2)}) async-start(f32[8,8,128]{2,1,0:T(8,128)} %cell_totals.1), calls=%async_computation | async-start | bytes 65536 | tf_op jit(solution)/shard_map/all_to_all | solution.py:436
  12.5 4.9 %prepare.1 = (f32[384,1024]{1,0:T(8,128)S(1)}, bf16[96,1024]{1,0:T(8,128)(2,1)S(1)}, f32[384,128]{1,0:T(8,128)S(1)}, f32[64,1024]{1,0:T(8,128)S(1)}, f32[64,384]{1,0:T(8,128)S(1)}) custom-call(s32[1]{0:T(128)S(6)} %copy.22.live_ref, s32[384,1024]{1,0:T(8,128)} %counts_ref.3, s32[1,1024]{1,0:T(1,128)} %bitcast.29, f32[1,1024]{1,0:T(1,128)} %bitcast.30, ...), custom_call_target="tpu_custom_call" | custom-call | tf_op jit(solution)/shard_map/prepare/pallas_call | solution.py:157
  17.4 1.3 %all-to-all-done.tot_ref = f32[8,8,128]{2,1,0:T(8,128)S(1)} async-done(((f32[8,8,128]{2,1,0:T(8,128)}), f32[8,8,128]{2,1,0:T(8,128)S(1)}, u32[]{:S(2)}, u32[]{:S(2)}) %all-to-all-start) | async-done | bytes 32800 | tf_op jit(solution)/shard_map/all_to_all | solution.py:436
  18.7 3.1 %gram_sums.1 = (f32[384,1024]{1,0:T(8,128)S(1)}, f32[16,48,128]{2,1,0:T(8,128)S(1)}, f32[16,48,128]{2,1,0:T(8,128)S(1)}) custom-call(s32[1]{0:T(128)S(6)} %copy.22.live_ref, s32[1]{0:T(128)} %bitcast.core_ref, f32[8,8,128]{2,1,0:T(8,128)S(1)} %all-to-all-done.tot_ref, f32[384,1024]{1,0:T(8,128)S(1)} %get-tuple-element.16.rest_ref, ...), custom_call_target="tpu_custom_call" | custom-call | tf_op jit(solution)/shard_map/gram_sums/pallas_call | solution.py:235
  21.8 0.0 copy-start
  21.8 0.0 copy-start.1
  21.8 2.2 %collective-permute-start = (f32[16,48,128]{2,1,0:T(8,128)S(1)}, f32[16,48,128]{2,1,0:T(8,128)S(1)}, u32[]{:S(2)}, u32[]{:S(2)}) collective-permute-start(f32[16,48,128]{2,1,0:T(8,128)S(1)} %get-tuple-element.20), channel_id=1, source_target_pairs={{0,8},{8,0},{16,24},{24,16},{32,40},{40,32},{48,56},{56,48},{64,72... | collective-permute-start | bytes 1179656 | tf_op jit(solution)/shard_map/ppermute | solution.py:473
  24.0 1.3 %collective-permute-done = f32[16,48,128]{2,1,0:T(8,128)S(1)} collective-permute-done((f32[16,48,128]{2,1,0:T(8,128)S(1)}, f32[16,48,128]{2,1,0:T(8,128)S(1)}, u32[]{:S(2)}, u32[]{:S(2)}) %collective-permute-start) | collective-permute-done | bytes 393248 | tf_op jit(solution)/shard_map/ppermute | solution.py:473
  25.3 0.1 add.32
  25.4 15.8 %all_to_all.25.parts_ref = f32[16,48,128]{2,1,0:T(8,128)S(1)} all-to-all(f32[16,48,128]{2,1,0:T(8,128)S(1)} %add.32), channel_id=1, replica_groups={{0,16,32,48,64,80,96,112,128,144,160,176,192,208,224,240},{8,24,40,56,7..., dimensions={0} | all-to-all | bytes 786432 | tf_op jit(solution)/shard_map/all_to_all | solution.py:436
  41.2 1.0 solve.1
  42.2 12.4 %all_to_all.26 = f32[32,1,384]{2,1,0:T(1,128)S(1)} all-to-all(f32[32,1,384]{2,1,0:T(1,128)S(1)} %solve.1), channel_id=1, replica_groups=mesh['cell'=32,'gene'=8] {'cell'}, dimensions={0} | all-to-all | bytes 98304 | tf_op jit(solution)/shard_map/all_to_all | solution.py:436
  54.6 0.0 copy-done
  54.6 0.0 copy-done.1
  54.6 3.7 %update.1 = (f32[8,128,128]{2,1,0:T(8,128)}, f32[64,384]{1,0:T(8,128)S(1)}, f32[64,384]{1,0:T(8,128)S(1)}, f32[32,384]{1,0:T(8,128)}) custom-call(s32[1]{0:T(128)S(6)} %copy.22.live_ref, s32[1]{0:T(128)} %bitcast.core_ref, f32[32,384]{1,0:T(8,128)S(1)} %bitcast.23, f32[384,1024]{1,0:T(8,128)S(1)} %get-tuple-element.21.pred_ref, ...), custom_call_target="tpu_custom_call" | custom-call | tf_op jit(solution)/shard_map/update/pallas_call | solution.py:368
  58.3 4.5 %all-to-all-start.3 = ((f32[8,128,128]{2,1,0:T(8,128)}), f32[8,128,128]{2,1,0:T(8,128)S(1)}, u32[]{:S(2)}, u32[]{:S(2)}) async-start(f32[8,128,128]{2,1,0:T(8,128)} %get-tuple-element.25), calls=%async_computation.3 | async-start | bytes 1048576 | tf_op jit(solution)/shard_map/all_to_all | solution.py:436
  62.7 0.7 collective-permute-start.1
  63.4 0.9 collective-permute-done.1
  64.4 0.9 collective-permute-start.4
  65.3 1.2 %collective-permute-start.3 = (f32[64,384]{1,0:T(8,128)S(1)}, f32[64,384]{1,0:T(8,128)S(1)}, u32[]{:S(2)}, u32[]{:S(2)}) collective-permute-start(f32[64,384]{1,0:T(8,128)S(1)} %add.33), channel_id=1, source_target_pairs={{0,128},{8,136},{16,144},{24,152},{32,160},{40,168},{48,176},{56,1... | collective-permute-start | bytes 294920 | tf_op jit(solution)/shard_map/ppermute | solution.py:481
  66.6 1.1 %collective-permute-start.2 = (f32[64,384]{1,0:T(8,128)S(1)}, f32[64,384]{1,0:T(8,128)S(1)}, u32[]{:S(2)}, u32[]{:S(2)}) collective-permute-start(f32[64,384]{1,0:T(8,128)S(1)} %add.33), channel_id=1, source_target_pairs={{0,64},{8,72},{16,80},{24,88},{32,96},{40,104},{48,112},{56,120},{... | collective-permute-start | bytes 294920 | tf_op jit(solution)/shard_map/ppermute | solution.py:481
  67.7 3.1 %collective-permute-done.4 = f32[64,384]{1,0:T(8,128)S(1)} collective-permute-done((f32[64,384]{1,0:T(8,128)S(1)}, f32[64,384]{1,0:T(8,128)S(1)}, u32[]{:S(2)}, u32[]{:S(2)}) %collective-permute-start.4) | collective-permute-done | bytes 98336 | tf_op jit(solution)/shard_map/ppermute | solution.py:481
  70.8 0.0 collective-permute-done.3
  70.8 1.2 %collective-permute-done.2 = f32[64,384]{1,0:T(8,128)S(1)} collective-permute-done((f32[64,384]{1,0:T(8,128)S(1)}, f32[64,384]{1,0:T(8,128)S(1)}, u32[]{:S(2)}, u32[]{:S(2)}) %collective-permute-start.2) | collective-permute-done | bytes 98336 | tf_op jit(solution)/shard_map/ppermute | solution.py:481
  72.1 0.4 collective-permute-start.5
  72.4 8.2 %all-to-all-done.3.parts_ref = f32[8,128,128]{2,1,0:T(8,128)S(1)} async-done(((f32[8,128,128]{2,1,0:T(8,128)}), f32[8,128,128]{2,1,0:T(8,128)S(1)}, u32[]{:S(2)}, u32[]{:S(2)}) %all-to-all-start.3) | async-done | bytes 524320 | tf_op jit(solution)/shard_map/all_to_all | solution.py:436
  80.7 0.7 factor_share.1
  81.4 3.4 %all-to-all-start.4 = ((f32[8,64,128]{2,1,0:T(8,128)}), f32[8,64,128]{2,1,0:T(8,128)S(1)}, u32[]{:S(2)}, u32[]{:S(2)}) async-start(f32[8,64,128]{2,1,0:T(8,128)} %factor_share.1), calls=%async_computation.4 | async-start | bytes 524288 | tf_op jit(solution)/shard_map/all_to_all | solution.py:436
  84.9 0.0 collective-permute-done.5
  84.9 1.0 %collective-permute-start.6 = (f32[64,384]{1,0:T(8,128)S(1)}, f32[64,384]{1,0:T(8,128)S(1)}, u32[]{:S(2)}, u32[]{:S(2)}) collective-permute-start(f32[64,384]{1,0:T(8,128)S(1)} %add.37), channel_id=1, source_target_pairs={{0,48},{8,56},{16,32},{24,40},{32,16},{40,24},{48,0},{56,8},{64,11... | collective-permute-start | bytes 294920 | tf_op jit(solution)/shard_map/ppermute | solution.py:488
  85.9 4.2 %collective-permute-done.6 = f32[64,384]{1,0:T(8,128)S(1)} collective-permute-done((f32[64,384]{1,0:T(8,128)S(1)}, f32[64,384]{1,0:T(8,128)S(1)}, u32[]{:S(2)}, u32[]{:S(2)}) %collective-permute-start.6) | collective-permute-done | bytes 98336 | tf_op jit(solution)/shard_map/ppermute | solution.py:488
  90.1 1.4 %collective-permute-start.7 = (f32[32,384]{1,0:T(8,128)S(1)}, f32[32,384]{1,0:T(8,128)S(1)}, u32[]{:S(2)}, u32[]{:S(2)}) collective-permute-start(f32[32,384]{1,0:T(8,128)S(1)} %fusion.1.mine_ref), channel_id=1, source_target_pairs={{0,8},{8,0},{16,24},{24,16},{32,40},{40,32},{48,56},{56,48},{64,72... | collective-permute-start | bytes 147464 | tf_op jit(solution)/shard_map/ppermute | solution.py:490
  91.5 0.9 collective-permute-done.7.other_ref
  92.4 0.6 joined_score.1
  93.1 3.8 %all-to-all-done.4 = f32[8,64,128]{2,1,0:T(8,128)S(1)} async-done(((f32[8,64,128]{2,1,0:T(8,128)}), f32[8,64,128]{2,1,0:T(8,128)S(1)}, u32[]{:S(2)}, u32[]{:S(2)}) %all-to-all-start.4) | async-done | bytes 262176 | tf_op jit(solution)/shard_map/all_to_all | solution.py:436
  96.8 0.7 bitcast_bitcast_fusion
  (6 shorter events, 0.1 us)
Async XLA Ops:
  2.8 15.9 %all-to-all-start = ((f32[8,8,128]{2,1,0:T(8,128)}), f32[8,8,128]{2,1,0:T(8,128)S(1)}, u32[]{:S(2)}, u32[]{:S(2)}) async-start(f32[8,8,128]{2,1,0:T(8,128)} %cell_totals.1), calls=%async_computation | async-start | bytes 65536 | tf_op jit(solution)/shard_map/all_to_all | solution.py:436
  21.8 32.8 %copy-start = (bf16[1024,64]{0,1:T(8,128)(2,1)S(1)}, bf16[1024,64]{0,1:T(8,128)(2,1)}, u32[]{:S(2)}) copy-start(bf16[1024,64]{0,1:T(8,128)(2,1)} %param.18) | copy-start | bytes 393220
  21.8 32.8 %copy-start.1 = (bf16[384,64]{0,1:T(8,128)(2,1)S(1)}, bf16[384,64]{0,1:T(8,128)(2,1)}, u32[]{:S(2)}) copy-start(bf16[384,64]{0,1:T(8,128)(2,1)} %param.19) | copy-start | bytes 147460
  21.8 3.5 %collective-permute-start = (f32[16,48,128]{2,1,0:T(8,128)S(1)}, f32[16,48,128]{2,1,0:T(8,128)S(1)}, u32[]{:S(2)}, u32[]{:S(2)}) collective-permute-start(f32[16,48,128]{2,1,0:T(8,128)S(1)} %get-tuple-element.20), channel_id=1, source_target_pairs={{0,8},{8,0},{16,24},{24,16},{32,40},{40,32},{48,56},{56,48},{64,72... | collective-permute-start | bytes 1179656 | tf_op jit(solution)/shard_map/ppermute | solution.py:473
  58.3 22.4 %all-to-all-start.3 = ((f32[8,128,128]{2,1,0:T(8,128)}), f32[8,128,128]{2,1,0:T(8,128)S(1)}, u32[]{:S(2)}, u32[]{:S(2)}) async-start(f32[8,128,128]{2,1,0:T(8,128)} %get-tuple-element.25), calls=%async_computation.3 | async-start | bytes 1048576 | tf_op jit(solution)/shard_map/all_to_all | solution.py:436
  62.7 1.6 %collective-permute-start.1 = (f32[64,384]{1,0:T(8,128)S(1)}, f32[64,384]{1,0:T(8,128)S(1)}, u32[]{:S(2)}, u32[]{:S(2)}) collective-permute-start(f32[64,384]{1,0:T(8,128)S(1)} %get-tuple-element.27), channel_id=1, source_target_pairs={{0,8},{8,0},{16,24},{24,16},{32,40},{40,32},{48,56},{56,48},{64,72... | collective-permute-start | bytes 294920 | tf_op jit(solution)/shard_map/ppermute | solution.py:480
  64.4 6.5 %collective-permute-start.4 = (f32[64,384]{1,0:T(8,128)S(1)}, f32[64,384]{1,0:T(8,128)S(1)}, u32[]{:S(2)}, u32[]{:S(2)}) collective-permute-start(f32[64,384]{1,0:T(8,128)S(1)} %add.33), channel_id=1, source_target_pairs={{0,192},{8,200},{16,208},{24,216},{32,224},{40,232},{48,240},{56,2... | collective-permute-start | bytes 294920 | tf_op jit(solution)/shard_map/ppermute | solution.py:481
  65.3 5.5 %collective-permute-start.3 = (f32[64,384]{1,0:T(8,128)S(1)}, f32[64,384]{1,0:T(8,128)S(1)}, u32[]{:S(2)}, u32[]{:S(2)}) collective-permute-start(f32[64,384]{1,0:T(8,128)S(1)} %add.33), channel_id=1, source_target_pairs={{0,128},{8,136},{16,144},{24,152},{32,160},{40,168},{48,176},{56,1... | collective-permute-start | bytes 294920 | tf_op jit(solution)/shard_map/ppermute | solution.py:481
  66.6 5.5 %collective-permute-start.2 = (f32[64,384]{1,0:T(8,128)S(1)}, f32[64,384]{1,0:T(8,128)S(1)}, u32[]{:S(2)}, u32[]{:S(2)}) collective-permute-start(f32[64,384]{1,0:T(8,128)S(1)} %add.33), channel_id=1, source_target_pairs={{0,64},{8,72},{16,80},{24,88},{32,96},{40,104},{48,112},{56,120},{... | collective-permute-start | bytes 294920 | tf_op jit(solution)/shard_map/ppermute | solution.py:481
  72.1 12.8 %collective-permute-start.5 = (f32[64,384]{1,0:T(8,128)S(1)}, f32[64,384]{1,0:T(8,128)S(1)}, u32[]{:S(2)}, u32[]{:S(2)}) collective-permute-start(f32[64,384]{1,0:T(8,128)S(1)} %add_add_fusion), channel_id=1, source_target_pairs={{0,16},{8,24},{16,0},{24,8},{32,48},{40,56},{48,32},{56,40},{64,80... | collective-permute-start | bytes 294920 | tf_op jit(solution)/shard_map/ppermute | solution.py:483
  81.4 15.4 %all-to-all-start.4 = ((f32[8,64,128]{2,1,0:T(8,128)}), f32[8,64,128]{2,1,0:T(8,128)S(1)}, u32[]{:S(2)}, u32[]{:S(2)}) async-start(f32[8,64,128]{2,1,0:T(8,128)} %factor_share.1), calls=%async_computation.4 | async-start | bytes 524288 | tf_op jit(solution)/shard_map/all_to_all | solution.py:436
  84.9 5.2 %collective-permute-start.6 = (f32[64,384]{1,0:T(8,128)S(1)}, f32[64,384]{1,0:T(8,128)S(1)}, u32[]{:S(2)}, u32[]{:S(2)}) collective-permute-start(f32[64,384]{1,0:T(8,128)S(1)} %add.37), channel_id=1, source_target_pairs={{0,48},{8,56},{16,32},{24,40},{32,16},{40,24},{48,0},{56,8},{64,11... | collective-permute-start | bytes 294920 | tf_op jit(solution)/shard_map/ppermute | solution.py:488
  90.1 2.3 %collective-permute-start.7 = (f32[32,384]{1,0:T(8,128)S(1)}, f32[32,384]{1,0:T(8,128)S(1)}, u32[]{:S(2)}, u32[]{:S(2)}) collective-permute-start(f32[32,384]{1,0:T(8,128)S(1)} %fusion.1.mine_ref), channel_id=1, source_target_pairs={{0,8},{8,0},{16,24},{24,16},{32,40},{40,32},{48,56},{56,48},{64,72... | collective-permute-start | bytes 147464 | tf_op jit(solution)/shard_map/ppermute | solution.py:490

commit v5 on v4

--- a/solution.py
+++ b/solution.py
@@ -48,13 +48,20 @@
     return pl.BlockSpec(memory_space=pltpu.SMEM)
 
 
+def vmem():
+    return pl.BlockSpec(memory_space=pltpu.VMEM)
+
+
+def hbm():
+    return pl.BlockSpec(memory_space=pltpu.HBM)
+
+
 def params(mib=16):
     return pltpu.CompilerParams(vmem_limit_bytes=mib * MIB)
 
 
-def totals_kernel(counts_ref, out_ref, rows, arrived):
-    blocks = rows.shape[0]
-    size = rows.shape[1]
+def totals_kernel(counts_ref, out_ref, rows, stage, arrived, sent):
+    blocks, size = rows.shape[0], rows.shape[1]
 
     def copy(b):
         return pltpu.make_async_copy(
@@ -66,30 +73,39 @@
     total = jnp.zeros((8, rows.shape[2]), F32)
     for b in range(blocks):
         copy(b).wait()
-        for i in range(0, size, 8):
-            total = total + rows[b, i : i + 8, :].astype(F32)
+        part = rows[b, :8, :]
+        for i in range(8, size, 8):
+            part = part + rows[b, i : i + 8, :]
+        total = total + part.astype(F32)
     total = jnp.sum(total, axis=0, keepdims=True)
     for i in range(8):
-        row = total[:, 128 * i : 128 * (i + 1)]
-        out_ref[:, i : i + 1, :] = jnp.broadcast_to(row[None], (out_ref.shape[0], 1, 128))
+        stage[i : i + 1, :] = total[:, 128 * i : 128 * (i + 1)]
+    sends = [
+        pltpu.make_async_copy(stage, out_ref.at[z], sent.at[z]) for z in range(out_ref.shape[0])
+    ]
+    for send in sends:
+        send.start()
+    for send in sends:
+        send.wait()
 
 
 def cell_totals(counts, peers):
     genes, cells = counts.shape
-    blocks = 8
+    blocks = 12
     return pl.pallas_call(
         totals_kernel,
-        grid=(1,),
-        in_specs=[pl.BlockSpec(memory_space=pl.ANY)],
-        out_specs=full((peers, 8, 128)),
-        out_shape=jax.ShapeDtypeStruct((peers, 8, 128), F32),
+        in_specs=[hbm()],
+        out_specs=hbm(),
+        out_shape=pltpu.HBM((peers, 8, 128), F32),
         scratch_shapes=[
             pltpu.VMEM((blocks, genes // blocks, cells), jnp.int32),
+            pltpu.VMEM((8, 128), F32),
             pltpu.SemaphoreType.DMA((blocks,)),
-        ],
-        compiler_params=params(60),
+            pltpu.SemaphoreType.DMA((peers,)),
+        ],
+        compiler_params=params(),
         name="cell_totals",
-    )(counts)
+    )(pltpu.with_memory_space_constraint(counts, pltpu.HBM))
 
 
 def prepare_kernel(
@@ -178,67 +194,63 @@
 
 def gram_kernel(
     live_ref, core_ref, tot_ref, rest_ref, design_ref, score_ref,
-    pred_ref, kept_ref, given_ref, offset, acc, hi_ref, lo_ref,
+    pred_ref, kept_ref, given_ref, offset, acc, terms_hi, terms_lo,
 ):
-    step = pl.program_id(0)
-
-    @pl.when(step == 0)
-    def _():
-        total = jnp.sum(tot_ref[...], axis=0)
-        value = jnp.log((1.0 + total) / GENES)
-        for i in range(8):
-            offset[:, 128 * i : 128 * (i + 1)] = value[i : i + 1, :]
-        acc[:3] = jnp.zeros_like(acc[:3])
-        acc[3] = score_ref[...]
-
-    at = pl.multiple_of(step * CHUNK, CHUNK)
-    pred = rest_ref[...] + offset[:, pl.ds(at, CHUNK)]
-    pred_ref[...] = pred
-    slot = lax.broadcasted_iota(jnp.int32, (1, CHUNK), 1) + at
-    mask = (slot < live_ref[0]).astype(F32)
-    w1, w2 = split2(jnp.exp(pred) * mask)
-
-    def put(at, value):
-        hi, lo = split2(value)
-        hi_ref[at : at + value.shape[0], :] = hi
-        lo_ref[at : at + value.shape[0], :] = lo
-
-    d1, d2, d3 = design_ref[0:32, :], design_ref[32:64, :], design_ref[64:96, :]
-    design = (d1.astype(F32) + d2.astype(F32)) + d3.astype(F32)
-    hat, cov = design[:SPL], design[SPL:]
-    put(0, hat * hat)
-    put(16, hat * pltpu.roll(hat, SPL - 1, axis=0))
-    for p in range(SPL):
-        put(32 + 16 * p, hat[p : p + 1, :] * cov)
-    low, high = cov[:8], cov[8:]
-    for i in range(0, 8, 2):
-        put(288 + 8 * i, jnp.concatenate([low[i : i + 1] * low, low[i + 1 : i + 2] * low], axis=0))
-        put(352 + 8 * i, jnp.concatenate([low[i : i + 1] * high, low[i + 1 : i + 2] * high], axis=0))
-        put(416 + 8 * i, jnp.concatenate([high[i : i + 1] * high, high[i + 1 : i + 2] * high], axis=0))
-    put(480, -design)
-    hi, lo = hi_ref[...], lo_ref[...]
-    gram = dot(w1, hi, NT) + dot(w1, lo, NT) + dot(w2, hi, NT)
-    for t in range(4):
-        acc[t] += gram[:, 128 * t : 128 * (t + 1)]
-
-    @pl.when(step == pl.num_programs(0) - 1)
-    def _():
-        core = core_ref[0]
-        for chip in range(16):
-            for ref, j in ((kept_ref, 2 * chip + core), (given_ref, 2 * chip + 1 - core)):
-                for t in range(4):
-                    ref[chip, 12 * t : 12 * (t + 1), :] = acc[t, pl.ds(j, 12, stride=32), :]
+    total = jnp.sum(tot_ref[...], axis=0)
+    value = jnp.log((1.0 + total) / GENES)
+    for i in range(8):
+        offset[:, 128 * i : 128 * (i + 1)] = value[i : i + 1, :]
+
+    for at in range(0, rest_ref.shape[1], CHUNK):
+        here = pl.ds(at, CHUNK)
+        hi_ref, lo_ref = terms_hi.at[:, here], terms_lo.at[:, here]
+
+        def put(row, value):
+            hi, lo = split2(value)
+            hi_ref[row : row + value.shape[0], :] = hi
+            lo_ref[row : row + value.shape[0], :] = lo
+
+        d1, d2, d3 = (design_ref[32 * i : 32 * (i + 1), here] for i in range(3))
+        design = (d1.astype(F32) + d2.astype(F32)) + d3.astype(F32)
+        hat, cov = design[:SPL], design[SPL:]
+        put(0, hat * hat)
+        put(16, hat * pltpu.roll(hat, SPL - 1, axis=0))
+        for p in range(SPL):
+            put(32 + 16 * p, hat[p : p + 1, :] * cov)
+        low, high = cov[:8], cov[8:]
+        for i in range(0, 8, 2):
+            for row, left, right in ((288, low, low), (352, low, high), (416, high, high)):
+                both = [left[i : i + 1] * right, left[i + 1 : i + 2] * right]
+                put(row + 8 * i, jnp.concatenate(both, axis=0))
+        put(480, -design)
+
+        pred = rest_ref[:, here] + offset[:, here]
+        pred_ref[:, here] = pred
+        slot = lax.broadcasted_iota(jnp.int32, (1, CHUNK), 1) + at
+        mask = (slot < live_ref[0]).astype(F32)
+        w1, w2 = split2(jnp.exp(pred) * mask)
+        hi, lo = hi_ref[...], lo_ref[...]
+        gram = dot(w1, hi, NT) + dot(w1, lo, NT) + dot(w2, hi, NT)
+        for t in range(4):
+            part = gram[:, 128 * t : 128 * (t + 1)]
+            if at > 0:
+                acc[t] += part
+            else:
+                acc[t] = part + score_ref[...] if t == 3 else part
+
+    core = core_ref[0]
+    for chip in range(16):
+        for ref, j in ((kept_ref, 2 * chip + core), (given_ref, 2 * chip + 1 - core)):
+            for t in range(4):
+                ref[chip, 12 * t : 12 * (t + 1), :] = acc[t, pl.ds(j, 12, stride=32), :]
 
 
 def gram_sums(live, core, tot, rest, design, score):
     genes, cells = rest.shape
     return pl.pallas_call(
         gram_kernel,
-        grid=(cells // CHUNK,),
-        in_specs=[
-            smem(), smem(), full(tot.shape), lanes(genes), lanes(96), full(score.shape),
-        ],
-        out_specs=[lanes(genes), full((16, 48, 128)), full((16, 48, 128))],
+        in_specs=[smem(), smem(), vmem(), vmem(), vmem(), vmem()],
+        out_specs=[vmem(), vmem(), vmem()],
         out_shape=[
             jax.ShapeDtypeStruct((genes, cells), F32),
             jax.ShapeDtypeStruct((16, 48, 128), F32),
@@ -246,7 +258,7 @@
         ],
         scratch_shapes=[
             pltpu.VMEM((1, cells), F32), pltpu.VMEM((4, genes, 128), F32),
-            pltpu.VMEM((512, CHUNK), BF16), pltpu.VMEM((512, CHUNK), BF16),
+            pltpu.VMEM((512, cells), BF16), pltpu.VMEM((512, cells), BF16),
         ],
         compiler_params=params(),
         name="gram_sums",
@@ -301,9 +313,8 @@
 def solve(parts):
     return pl.pallas_call(
         solve_kernel,
-        grid=(1,),
-        in_specs=[full(parts.shape)],
-        out_specs=full((32, 1, 384)),
+        in_specs=[vmem()],
+        out_specs=vmem(),
         out_shape=jax.ShapeDtypeStruct((32, 1, 384), F32),
         scratch_shapes=[pltpu.VMEM((512, 128), F32)],
         compiler_params=params(),
@@ -314,79 +325,81 @@
 def update_kernel(
     live_ref, core_ref, steps_ref, pred_ref, design_ref, load_ref, fact_ref,
     by_load_ref, by_fact_ref,
-    out_ref, kept_ref, given_ref, beta_ref, left, loads, sums,
+    out_hbm, kept_ref, given_ref, beta_hbm, left, loads, sums, out, beta_out, sent,
 ):
-    step = pl.program_id(0)
-
-    @pl.when(step == 0)
-    def _():
-        steps = steps_ref[...]
-        beta = jnp.concatenate([steps[:, COLS * g : COLS * (g + 1)] for g in range(12)], axis=0)
-        b1, b2, b3 = split3(beta)
-        left[...] = jnp.concatenate([b1, b1, b2, b2, b1, b3], axis=1)
-        beta_ref[...] = beta.T
-        load = load_ref[...]
-        wide = load.astype(F32)
-        l1, l2 = split2(wide * wide)
-        loads[...] = jnp.concatenate([load, l1, l2], axis=0)
+    steps = steps_ref[...]
+    beta = jnp.concatenate([steps[:, COLS * g : COLS * (g + 1)] for g in range(12)], axis=0)
+    b1, b2, b3 = split3(beta)
+    left[...] = jnp.concatenate([b1, b1, b2, b2, b1, b3], axis=1)
+    load = load_ref[...]
+    wide = load.astype(F32)
+    l1, l2 = split2(wide * wide)
+    loads[...] = jnp.concatenate([load, l1, l2], axis=0)
+
+    cells = pred_ref.shape[1]
+    sends = []
+    for at in range(0, cells, CHUNK):
+        here = pl.ds(at, CHUNK)
+        d1, d2, d3 = (design_ref[32 * i : 32 * (i + 1), here] for i in range(3))
+        change = dot(left[...], jnp.concatenate([d1, d2, d1, d2, d3, d1], axis=0), NN)
+        slot = lax.broadcasted_iota(jnp.int32, (1, CHUNK), 1) + at
+        mask = (slot < live_ref[0]).astype(F32)
+        w1, w2 = split2(jnp.exp(pred_ref[:, here] + change) * mask)
+        first = dot(loads[...], w1, NN)
+        second = dot(loads[: 2 * FACT], w2, NN)
+        grad = by_load_ref[:, here] - (first[:FACT] + second[:FACT])
+        curv = (first[FACT : 2 * FACT] + first[2 * FACT :]) + second[FACT:]
+        for z in range(8):
+            out[z, :8, here] = grad[8 * z : 8 * (z + 1), :]
+            out[z, 8:, here] = curv[8 * z : 8 * (z + 1), :]
+        send = pltpu.make_async_copy(
+            out.at[:, :, here], out_hbm.at[:, :, here], sent.at[at // CHUNK]
+        )
+        send.start()
+        sends.append(send)
+        fact = fact_ref[:, here]
+        wide = fact.astype(F32)
+        f1, f2 = split2(wide * wide)
+        first = dot(jnp.concatenate([fact, f1, f2], axis=0), w1, NT)
+        second = dot(jnp.concatenate([fact, f1], axis=0), w2, NT)
+        grad = first[:FACT] + second[:FACT]
+        curv = (first[FACT : 2 * FACT] + first[2 * FACT :]) + second[FACT:]
         for h in range(2):
-            sums[h, :32, :] = by_fact_ref[32 * h : 32 * (h + 1), :]
-            sums[h, 32:, :] = jnp.zeros_like(sums[h, 32:, :])
-
-    at = step * CHUNK
-    d1, d2, d3 = design_ref[0:32, :], design_ref[32:64, :], design_ref[64:96, :]
-    change = dot(left[...], jnp.concatenate([d1, d2, d1, d2, d3, d1], axis=0), NN)
-    slot = lax.broadcasted_iota(jnp.int32, (1, CHUNK), 1) + at
-    mask = (slot < live_ref[0]).astype(F32)
-    w1, w2 = split2(jnp.exp(pred_ref[...] + change) * mask)
-    first = dot(loads[...], w1, NN)
-    second = dot(loads[: 2 * FACT], w2, NN)
-    grad = by_load_ref[...] - (first[:FACT] + second[:FACT])
-    curv = (first[FACT : 2 * FACT] + first[2 * FACT :]) + second[FACT:]
-    for i in range(CHUNK // 128):
-        out_ref[i, :FACT, :] = grad[:, 128 * i : 128 * (i + 1)]
-        out_ref[i, FACT:, :] = curv[:, 128 * i : 128 * (i + 1)]
-    fact = fact_ref[...]
-    wide = fact.astype(F32)
-    f1, f2 = split2(wide * wide)
-    first = dot(jnp.concatenate([fact, f1, f2], axis=0), w1, NT)
-    second = dot(jnp.concatenate([fact, f1], axis=0), w2, NT)
-    grad = first[:FACT] + second[:FACT]
-    curv = (first[FACT : 2 * FACT] + first[2 * FACT :]) + second[FACT:]
-    for h in range(2):
-        sums[h, :32, :] -= grad[32 * h : 32 * (h + 1), :]
-        sums[h, 32:, :] += curv[32 * h : 32 * (h + 1), :]
-
-    @pl.when(step == pl.num_programs(0) - 1)
-    def _():
-        kept_ref[...] = sums[core_ref[0]]
-        given_ref[...] = sums[1 - core_ref[0]]
+            rows = slice(32 * h, 32 * (h + 1))
+            if at > 0:
+                sums[h, :32, :] -= grad[rows]
+                sums[h, 32:, :] += curv[rows]
+            else:
+                sums[h, :32, :] = by_fact_ref[rows, :] - grad[rows]
+                sums[h, 32:, :] = curv[rows]
+
+    beta_out[...] = beta.T
+    send = pltpu.make_async_copy(beta_out, beta_hbm, sent.at[cells // CHUNK])
+    send.start()
+    sends.append(send)
+    kept_ref[...] = sums[core_ref[0]]
+    given_ref[...] = sums[1 - core_ref[0]]
+    for send in sends:
+        send.wait()
 
 
 def update(live, core, steps, pred, design, load, fact, by_load, by_fact):
     genes, cells = pred.shape
     return pl.pallas_call(
         update_kernel,
-        grid=(cells // CHUNK,),
-        in_specs=[
-            smem(), smem(), full((32, 384)), lanes(genes), lanes(96),
-            full((FACT, genes)), lanes(FACT), lanes(FACT), full((FACT, genes)),
-        ],
-        out_specs=[
-            pl.BlockSpec((CHUNK // 128, 2 * FACT, 128), lambda c: (c, 0, 0)),
-            full((FACT, genes)),
-            full((FACT, genes)),
-            full((COLS, genes)),
-        ],
+        in_specs=[smem(), smem()] + [vmem()] * 7,
+        out_specs=[hbm(), vmem(), vmem(), hbm()],
         out_shape=[
-            pltpu.HBM((cells // 128, 2 * FACT, 128), F32),
+            pltpu.HBM((8, 16, cells), F32),
             jax.ShapeDtypeStruct((FACT, genes), F32),
             jax.ShapeDtypeStruct((FACT, genes), F32),
-            jax.ShapeDtypeStruct((COLS, genes), F32),
+            pltpu.HBM((COLS, genes), F32),
         ],
         scratch_shapes=[
             pltpu.VMEM((genes, 6 * COLS), BF16), pltpu.VMEM((3 * FACT, genes), BF16),
-            pltpu.VMEM((2, FACT, genes), F32),
+            pltpu.VMEM((2, FACT, genes), F32), pltpu.VMEM((8, 16, cells), F32),
+            pltpu.VMEM((COLS, genes), F32),
+            pltpu.SemaphoreType.DMA((cells // CHUNK + 1,)),
         ],
         compiler_params=params(),
         name="update",
@@ -411,22 +424,28 @@
     )(core, mine, other)
 
 
-def factor_kernel(parts_ref, out_ref):
+def factor_kernel(parts_ref, out_hbm, stage, sent):
     total = parts_ref[0]
     for j in range(1, parts_ref.shape[0]):
         total = total + parts_ref[j]
-    value = total[:FACT, :] / (total[FACT:, :] + 1.0)
-    out_ref[...] = jnp.broadcast_to(value[None], out_ref.shape)
+    stage[...] = total[:8, :] / (total[8:, :] + 1.0)
+    sends = [
+        pltpu.make_async_copy(stage, out_hbm.at[z], sent.at[z]) for z in range(out_hbm.shape[0])
+    ]
+    for send in sends:
+        send.start()
+    for send in sends:
+        send.wait()
 
 
 def factor_share(parts):
-    peers = parts.shape[0]
+    peers, _, cells = parts.shape
     return pl.pallas_call(
         factor_kernel,
-        grid=(1,),
-        in_specs=[full(parts.shape)],
-        out_specs=full((peers, FACT, 128)),
-        out_shape=jax.ShapeDtypeStruct((peers, FACT, 128), F32),
+        in_specs=[vmem()],
+        out_specs=hbm(),
+        out_shape=pltpu.HBM((peers, 8, cells), F32),
+        scratch_shapes=[pltpu.VMEM((8, cells), F32), pltpu.SemaphoreType.DMA((peers,))],
         compiler_params=params(),
         name="factor_share",
     )(parts)
@@ -489,7 +508,7 @@
     mine = value[:32] / jnp.sqrt(value[32:] + 1.0)
     other = lax.ppermute(mine, "cell", OTHER_CORE)
     score = joined_score(core, mine, other)
-    factor_step = jnp.moveaxis(gathered, 0, 1).reshape(FACT, -1)
+    factor_step = gathered.reshape(FACT, -1)
     return beta.T, factor_step.T, score.T
 
 

time: 98.1 us -> 96 us (0.979)
  Pallas kernels: 16.1 us -> 14.1 us
    pallas_call x5, Pallas kernels: 10.6 us -> 8.57 us  [the longest x1 2.59 us: update(): pl.pallas_call(update_kernel, in_specs=[smem(), smem()] + [vmem()] * 7, o...]
  transfers between devices with their start and end apart: 11 -> 11, of which waited for: 9 -> 9; matrix products, arithmetic and copies ran while one was open for 0% -> 0% of each run, Pallas kernels for 6% -> 7%
where the time goes in v5:
time: 96 us; the launch traced here: 95.5 us
  blocking collectives  28.2 us (29%)
  starting transfers between devices  25.9 us (27%)
  waiting for transfers between devices  25.1 us (26%)
  Pallas kernels  14.1 us (15%)
  between operations  1.41 us (1%)
    all_to_all x2, blocking collectives, exchange(): lax.all_to_all(value, axis, split_axis=0, concat_axis=0, tiled=True, axis...  28.2 us
    all_to_all x3, starting transfers between devices, exchange(): lax.all_to_all(value, axis, split_axis=0, concat_axis=0, tiled=True, axis...  16.9 us
    all_to_all x3, waiting for transfers between devices, exchange(): lax.all_to_all(value, axis, split_axis=0, concat_axis=0, tiled=True, axis...  13.4 us
    pallas_call x1, Pallas kernels, prepare(): pl.pallas_call(prepare_kernel, grid=(cells // CHUNK,), in_specs=[smem(),...  4.87 us
    ppermute x3, waiting for transfers between devices, local(): lax.ppermute(value, 'cell', pairs)  4.34 us
    ppermute x1, waiting for transfers between devices, local(): value = value + lax.ppermute(value, 'cell', ALONG_Y[1])  4.18 us
    ppermute x3, starting transfers between devices, local(): lax.ppermute(value, 'cell', pairs)  3.34 us
    pallas_call x1, Pallas kernels, update(): pl.pallas_call(update_kernel, in_specs=[smem(), smem()] + [vmem()] * 7, o...  2.59 us
  transfers between devices with their start and end apart: 11, of which 9 were waited for; matrix products, arithmetic and copies ran while one was open for 0% of the time, Pallas kernels for 7%

profile of v5, /device:TPU:1, one launch (start us, length us, event | category | flops | bytes accessed | tf_op | source)
XLA Modules:
  0.0 95.5 jit_solution(13050790790163256743)
XLA Ops:
  0.6 2.3 %cell_totals.1 = f32[8,8,128]{2,1,0:T(8,128)} custom-call(s32[384,1024]{1,0:T(8,128)} %counts_ref.3), custom_call_target="tpu_custom_call" | custom-call | tf_op jit(solution)/shard_map/cell_totals/pallas_call | solution.py:95
  2.9 9.0 %all-to-all-start = ((f32[8,8,128]{2,1,0:T(8,128)}), f32[8,8,128]{2,1,0:T(8,128)S(1)}, u32[]{:S(2)}, u32[]{:S(2)}) async-start(f32[8,8,128]{2,1,0:T(8,128)} %cell_totals.1), calls=%async_computation | async-start | bytes 65536 | tf_op jit(solution)/shard_map/all_to_all | solution.py:455
  12.6 4.9 %prepare.1 = (f32[384,1024]{1,0:T(8,128)S(1)}, bf16[96,1024]{1,0:T(8,128)(2,1)S(1)}, f32[384,128]{1,0:T(8,128)S(1)}, f32[64,1024]{1,0:T(8,128)S(1)}, f32[64,384]{1,0:T(8,128)S(1)}) custom-call(s32[1]{0:T(128)S(6)} %copy.18.live_ref, s32[384,1024]{1,0:T(8,128)} %counts_ref.3, s32[1,1024]{1,0:T(1,128)} %bitcast.25, f32[1,1024]{1,0:T(1,128)} %bitcast.26, ...), custom_call_target="tpu_custom_call" | custom-call | tf_op jit(solution)/shard_map/prepare/pallas_call | solution.py:173
  17.5 1.3 %all-to-all-done.tot_ref = f32[8,8,128]{2,1,0:T(8,128)S(1)} async-done(((f32[8,8,128]{2,1,0:T(8,128)}), f32[8,8,128]{2,1,0:T(8,128)S(1)}, u32[]{:S(2)}, u32[]{:S(2)}) %all-to-all-start) | async-done | bytes 32800 | tf_op jit(solution)/shard_map/all_to_all | solution.py:455
  18.8 2.0 %gram_sums.1 = (f32[384,1024]{1,0:T(8,128)S(1)}, f32[16,48,128]{2,1,0:T(8,128)S(1)}, f32[16,48,128]{2,1,0:T(8,128)S(1)}) custom-call(s32[1]{0:T(128)S(6)} %copy.18.live_ref, s32[1]{0:T(128)} %bitcast.core_ref, f32[8,8,128]{2,1,0:T(8,128)S(1)} %all-to-all-done.tot_ref, f32[384,1024]{1,0:T(8,128)S(1)} %get-tuple-element.16.rest_ref, ...), custom_call_target="tpu_custom_call" | custom-call | tf_op jit(solution)/shard_map/gram_sums/pallas_call | solution.py:250
  20.8 0.0 copy-start
  20.8 0.0 copy-start.1
  20.8 2.2 %collective-permute-start = (f32[16,48,128]{2,1,0:T(8,128)S(1)}, f32[16,48,128]{2,1,0:T(8,128)S(1)}, u32[]{:S(2)}, u32[]{:S(2)}) collective-permute-start(f32[16,48,128]{2,1,0:T(8,128)S(1)} %get-tuple-element.20), channel_id=1, source_target_pairs={{0,8},{8,0},{16,24},{24,16},{32,40},{40,32},{48,56},{56,48},{64,72... | collective-permute-start | bytes 1179656 | tf_op jit(solution)/shard_map/ppermute | solution.py:492
  23.0 1.3 %collective-permute-done = f32[16,48,128]{2,1,0:T(8,128)S(1)} collective-permute-done((f32[16,48,128]{2,1,0:T(8,128)S(1)}, f32[16,48,128]{2,1,0:T(8,128)S(1)}, u32[]{:S(2)}, u32[]{:S(2)}) %collective-permute-start) | collective-permute-done | bytes 393248 | tf_op jit(solution)/shard_map/ppermute | solution.py:492
  24.3 0.1 add.32
  24.4 15.8 %all_to_all.25.parts_ref = f32[16,48,128]{2,1,0:T(8,128)S(1)} all-to-all(f32[16,48,128]{2,1,0:T(8,128)S(1)} %add.32), channel_id=1, replica_groups={{0,16,32,48,64,80,96,112,128,144,160,176,192,208,224,240},{8,24,40,56,7..., dimensions={0} | all-to-all | bytes 786432 | tf_op jit(solution)/shard_map/all_to_all | solution.py:455
  40.2 1.0 %solve.1 = f32[32,1,384]{2,1,0:T(1,128)S(1)} custom-call(f32[16,48,128]{2,1,0:T(8,128)S(1)} %all_to_all.25.parts_ref), custom_call_target="tpu_custom_call" | custom-call | tf_op jit(solution)/shard_map/solve/pallas_call | solution.py:314
  41.2 12.4 %all_to_all.26 = f32[32,1,384]{2,1,0:T(1,128)S(1)} all-to-all(f32[32,1,384]{2,1,0:T(1,128)S(1)} %solve.1), channel_id=1, replica_groups=mesh['cell'=32,'gene'=8] {'cell'}, dimensions={0} | all-to-all | bytes 98304 | tf_op jit(solution)/shard_map/all_to_all | solution.py:455
  53.6 0.0 copy-done
  53.6 0.0 copy-done.1
  53.6 2.6 %update.1 = (f32[8,16,1024]{2,1,0:T(8,128)}, f32[64,384]{1,0:T(8,128)S(1)}, f32[64,384]{1,0:T(8,128)S(1)}, f32[32,384]{1,0:T(8,128)}) custom-call(s32[1]{0:T(128)S(6)} %copy.18.live_ref, s32[1]{0:T(128)} %bitcast.core_ref, f32[32,384]{1,0:T(8,128)S(1)} %bitcast.18, f32[384,1024]{1,0:T(8,128)S(1)} %get-tuple-element.21.pred_ref, ...), custom_call_target="tpu_custom_call" | custom-call | tf_op jit(solution)/shard_map/update/pallas_call | solution.py:388
  56.2 4.5 %all-to-all-start.3 = ((f32[8,16,1024]{2,1,0:T(8,128)}), f32[8,16,1024]{2,1,0:T(8,128)S(1)}, u32[]{:S(2)}, u32[]{:S(2)}) async-start(f32[8,16,1024]{2,1,0:T(8,128)} %get-tuple-element.25), calls=%async_computation.3 | async-start | bytes 1048576 | tf_op jit(solution)/shard_map/all_to_all | solution.py:455
  60.7 0.7 collective-permute-start.1
  61.3 0.9 collective-permute-done.1
  62.3 0.9 collective-permute-start.4
  63.2 1.2 %collective-permute-start.3 = (f32[64,384]{1,0:T(8,128)S(1)}, f32[64,384]{1,0:T(8,128)S(1)}, u32[]{:S(2)}, u32[]{:S(2)}) collective-permute-start(f32[64,384]{1,0:T(8,128)S(1)} %add.33), channel_id=1, source_target_pairs={{0,128},{8,136},{16,144},{24,152},{32,160},{40,168},{48,176},{56,1... | collective-permute-start | bytes 294920 | tf_op jit(solution)/shard_map/ppermute | solution.py:500
  64.5 1.1 %collective-permute-start.2 = (f32[64,384]{1,0:T(8,128)S(1)}, f32[64,384]{1,0:T(8,128)S(1)}, u32[]{:S(2)}, u32[]{:S(2)}) collective-permute-start(f32[64,384]{1,0:T(8,128)S(1)} %add.33), channel_id=1, source_target_pairs={{0,64},{8,72},{16,80},{24,88},{32,96},{40,104},{48,112},{56,120},{... | collective-permute-start | bytes 294920 | tf_op jit(solution)/shard_map/ppermute | solution.py:500
  65.6 3.1 %collective-permute-done.4 = f32[64,384]{1,0:T(8,128)S(1)} collective-permute-done((f32[64,384]{1,0:T(8,128)S(1)}, f32[64,384]{1,0:T(8,128)S(1)}, u32[]{:S(2)}, u32[]{:S(2)}) %collective-permute-start.4) | collective-permute-done | bytes 98336 | tf_op jit(solution)/shard_map/ppermute | solution.py:500
  68.8 0.0 collective-permute-done.3
  68.8 1.2 %collective-permute-done.2 = f32[64,384]{1,0:T(8,128)S(1)} collective-permute-done((f32[64,384]{1,0:T(8,128)S(1)}, f32[64,384]{1,0:T(8,128)S(1)}, u32[]{:S(2)}, u32[]{:S(2)}) %collective-permute-start.2) | collective-permute-done | bytes 98336 | tf_op jit(solution)/shard_map/ppermute | solution.py:500
  70.0 0.4 collective-permute-start.5
  70.4 8.2 %all-to-all-done.3.parts_ref = f32[8,16,1024]{2,1,0:T(8,128)S(1)} async-done(((f32[8,16,1024]{2,1,0:T(8,128)}), f32[8,16,1024]{2,1,0:T(8,128)S(1)}, u32[]{:S(2)}, u32[]{:S(2)}) %all-to-all-start.3) | async-done | bytes 524320 | tf_op jit(solution)/shard_map/all_to_all | solution.py:455
  78.6 0.8 factor_share.1
  79.4 3.4 %all-to-all-start.4 = ((f32[8,8,1024]{2,1,0:T(8,128)}), f32[8,8,1024]{2,1,0:T(8,128)S(1)}, u32[]{:S(2)}, u32[]{:S(2)}) async-start(f32[8,8,1024]{2,1,0:T(8,128)} %factor_share.1), calls=%async_computation.4 | async-start | bytes 524288 | tf_op jit(solution)/shard_map/all_to_all | solution.py:455
  82.9 0.0 collective-permute-done.5
  82.9 1.0 %collective-permute-start.6 = (f32[64,384]{1,0:T(8,128)S(1)}, f32[64,384]{1,0:T(8,128)S(1)}, u32[]{:S(2)}, u32[]{:S(2)}) collective-permute-start(f32[64,384]{1,0:T(8,128)S(1)} %add.37), channel_id=1, source_target_pairs={{0,48},{8,56},{16,32},{24,40},{32,16},{40,24},{48,0},{56,8},{64,11... | collective-permute-start | bytes 294920 | tf_op jit(solution)/shard_map/ppermute | solution.py:507
  83.9 4.2 %collective-permute-done.6 = f32[64,384]{1,0:T(8,128)S(1)} collective-permute-done((f32[64,384]{1,0:T(8,128)S(1)}, f32[64,384]{1,0:T(8,128)S(1)}, u32[]{:S(2)}, u32[]{:S(2)}) %collective-permute-start.6) | collective-permute-done | bytes 98336 | tf_op jit(solution)/shard_map/ppermute | solution.py:507
  88.1 1.4 %collective-permute-start.7 = (f32[32,384]{1,0:T(8,128)S(1)}, f32[32,384]{1,0:T(8,128)S(1)}, u32[]{:S(2)}, u32[]{:S(2)}) collective-permute-start(f32[32,384]{1,0:T(8,128)S(1)} %fusion.1.mine_ref), channel_id=1, source_target_pairs={{0,8},{8,0},{16,24},{24,16},{32,40},{40,32},{48,56},{56,48},{64,72... | collective-permute-start | bytes 147464 | tf_op jit(solution)/shard_map/ppermute | solution.py:509
  89.5 0.9 collective-permute-done.7.other_ref
  90.4 0.6 joined_score.1
  91.0 3.8 %all-to-all-done.4 = f32[8,8,1024]{2,1,0:T(8,128)S(1)} async-done(((f32[8,8,1024]{2,1,0:T(8,128)}), f32[8,8,1024]{2,1,0:T(8,128)S(1)}, u32[]{:S(2)}, u32[]{:S(2)}) %all-to-all-start.4) | async-done | bytes 262176 | tf_op jit(solution)/shard_map/all_to_all | solution.py:455
  94.8 0.7 copy.19
  (6 shorter events, 0.1 us)
Async XLA Ops:
  2.9 15.9 %all-to-all-start = ((f32[8,8,128]{2,1,0:T(8,128)}), f32[8,8,128]{2,1,0:T(8,128)S(1)}, u32[]{:S(2)}, u32[]{:S(2)}) async-start(f32[8,8,128]{2,1,0:T(8,128)} %cell_totals.1), calls=%async_computation | async-start | bytes 65536 | tf_op jit(solution)/shard_map/all_to_all | solution.py:455
  20.8 32.8 %copy-start = (bf16[1024,64]{0,1:T(8,128)(2,1)S(1)}, bf16[1024,64]{0,1:T(8,128)(2,1)}, u32[]{:S(2)}) copy-start(bf16[1024,64]{0,1:T(8,128)(2,1)} %param.18) | copy-start | bytes 393220
  20.8 32.8 %copy-start.1 = (bf16[384,64]{0,1:T(8,128)(2,1)S(1)}, bf16[384,64]{0,1:T(8,128)(2,1)}, u32[]{:S(2)}) copy-start(bf16[384,64]{0,1:T(8,128)(2,1)} %param.19) | copy-start | bytes 147460
  20.8 3.5 %collective-permute-start = (f32[16,48,128]{2,1,0:T(8,128)S(1)}, f32[16,48,128]{2,1,0:T(8,128)S(1)}, u32[]{:S(2)}, u32[]{:S(2)}) collective-permute-start(f32[16,48,128]{2,1,0:T(8,128)S(1)} %get-tuple-element.20), channel_id=1, source_target_pairs={{0,8},{8,0},{16,24},{24,16},{32,40},{40,32},{48,56},{56,48},{64,72... | collective-permute-start | bytes 1179656 | tf_op jit(solution)/shard_map/ppermute | solution.py:492
  56.2 22.4 %all-to-all-start.3 = ((f32[8,16,1024]{2,1,0:T(8,128)}), f32[8,16,1024]{2,1,0:T(8,128)S(1)}, u32[]{:S(2)}, u32[]{:S(2)}) async-start(f32[8,16,1024]{2,1,0:T(8,128)} %get-tuple-element.25), calls=%async_computation.3 | async-start | bytes 1048576 | tf_op jit(solution)/shard_map/all_to_all | solution.py:455
  60.7 1.6 %collective-permute-start.1 = (f32[64,384]{1,0:T(8,128)S(1)}, f32[64,384]{1,0:T(8,128)S(1)}, u32[]{:S(2)}, u32[]{:S(2)}) collective-permute-start(f32[64,384]{1,0:T(8,128)S(1)} %get-tuple-element.27), channel_id=1, source_target_pairs={{0,8},{8,0},{16,24},{24,16},{32,40},{40,32},{48,56},{56,48},{64,72... | collective-permute-start | bytes 294920 | tf_op jit(solution)/shard_map/ppermute | solution.py:499
  62.3 6.5 %collective-permute-start.4 = (f32[64,384]{1,0:T(8,128)S(1)}, f32[64,384]{1,0:T(8,128)S(1)}, u32[]{:S(2)}, u32[]{:S(2)}) collective-permute-start(f32[64,384]{1,0:T(8,128)S(1)} %add.33), channel_id=1, source_target_pairs={{0,192},{8,200},{16,208},{24,216},{32,224},{40,232},{48,240},{56,2... | collective-permute-start | bytes 294920 | tf_op jit(solution)/shard_map/ppermute | solution.py:500
  63.2 5.5 %collective-permute-start.3 = (f32[64,384]{1,0:T(8,128)S(1)}, f32[64,384]{1,0:T(8,128)S(1)}, u32[]{:S(2)}, u32[]{:S(2)}) collective-permute-start(f32[64,384]{1,0:T(8,128)S(1)} %add.33), channel_id=1, source_target_pairs={{0,128},{8,136},{16,144},{24,152},{32,160},{40,168},{48,176},{56,1... | collective-permute-start | bytes 294920 | tf_op jit(solution)/shard_map/ppermute | solution.py:500
  64.5 5.5 %collective-permute-start.2 = (f32[64,384]{1,0:T(8,128)S(1)}, f32[64,384]{1,0:T(8,128)S(1)}, u32[]{:S(2)}, u32[]{:S(2)}) collective-permute-start(f32[64,384]{1,0:T(8,128)S(1)} %add.33), channel_id=1, source_target_pairs={{0,64},{8,72},{16,80},{24,88},{32,96},{40,104},{48,112},{56,120},{... | collective-permute-start | bytes 294920 | tf_op jit(solution)/shard_map/ppermute | solution.py:500
  70.0 12.8 %collective-permute-start.5 = (f32[64,384]{1,0:T(8,128)S(1)}, f32[64,384]{1,0:T(8,128)S(1)}, u32[]{:S(2)}, u32[]{:S(2)}) collective-permute-start(f32[64,384]{1,0:T(8,128)S(1)} %add_add_fusion), channel_id=1, source_target_pairs={{0,16},{8,24},{16,0},{24,8},{32,48},{40,56},{48,32},{56,40},{64,80... | collective-permute-start | bytes 294920 | tf_op jit(solution)/shard_map/ppermute | solution.py:502
  79.4 15.4 %all-to-all-start.4 = ((f32[8,8,1024]{2,1,0:T(8,128)}), f32[8,8,1024]{2,1,0:T(8,128)S(1)}, u32[]{:S(2)}, u32[]{:S(2)}) async-start(f32[8,8,1024]{2,1,0:T(8,128)} %factor_share.1), calls=%async_computation.4 | async-start | bytes 524288 | tf_op jit(solution)/shard_map/all_to_all | solution.py:455
  82.9 5.2 %collective-permute-start.6 = (f32[64,384]{1,0:T(8,128)S(1)}, f32[64,384]{1,0:T(8,128)S(1)}, u32[]{:S(2)}, u32[]{:S(2)}) collective-permute-start(f32[64,384]{1,0:T(8,128)S(1)} %add.37), channel_id=1, source_target_pairs={{0,48},{8,56},{16,32},{24,40},{32,16},{40,24},{48,0},{56,8},{64,11... | collective-permute-start | bytes 294920 | tf_op jit(solution)/shard_map/ppermute | solution.py:507
  88.1 2.3 %collective-permute-start.7 = (f32[32,384]{1,0:T(8,128)S(1)}, f32[32,384]{1,0:T(8,128)S(1)}, u32[]{:S(2)}, u32[]{:S(2)}) collective-permute-start(f32[32,384]{1,0:T(8,128)S(1)} %fusion.1.mine_ref), channel_id=1, source_target_pairs={{0,8},{8,0},{16,24},{24,16},{32,40},{40,32},{48,56},{56,48},{64,72... | collective-permute-start | bytes 147464 | tf_op jit(solution)/shard_map/ppermute | solution.py:509

commit v6 on v5

--- a/solution.py
+++ b/solution.py
@@ -240,7 +240,7 @@
 
     core = core_ref[0]
     for chip in range(16):
-        for ref, j in ((kept_ref, 2 * chip + core), (given_ref, 2 * chip + 1 - core)):
+        for ref, j in ((kept_ref, 16 * core + chip), (given_ref, 16 * (1 - core) + chip)):
             for t in range(4):
                 ref[chip, 12 * t : 12 * (t + 1), :] = acc[t, pl.ds(j, 12, stride=32), :]
 
@@ -451,6 +451,29 @@
     )(parts)
 
 
+def settle_kernel(value_ref, out_hbm, sent):
+    sends = [
+        pltpu.make_async_copy(value_ref.at[z], out_hbm.at[z], sent.at[z])
+        for z in range(value_ref.shape[0])
+    ]
+    for send in sends:
+        send.start()
+    for send in sends:
+        send.wait()
+
+
+def settled(value):
+    return pl.pallas_call(
+        settle_kernel,
+        in_specs=[vmem()],
+        out_specs=hbm(),
+        out_shape=pltpu.HBM(value.shape, value.dtype),
+        scratch_shapes=[pltpu.SemaphoreType.DMA((value.shape[0],))],
+        compiler_params=params(),
+        name="settled",
+    )(value)
+
+
 def exchange(value, axis, groups=None):
     return lax.all_to_all(
         value, axis, split_axis=0, concat_axis=0, tiled=True, axis_index_groups=groups
@@ -469,7 +492,9 @@
     ]
 
 
-SAME_CORE = [list(range(core, 32, 2)) for core in range(2)]
+SAME_CORE = [[(4 * x + y) * 2 + core for y in range(4) for x in range(4)] for core in range(2)]
+CORE_FIRST = [SAME_CORE[0] + SAME_CORE[1]]
+RING = [[3, 4, 2, 5, 1, 6, 0, 7]]
 OTHER_CORE = partners(lambda x, y, c: (x, y, 1 - c))
 ALONG_X = [partners(lambda x, y, c, k=k: (x ^ k, y, c)) for k in (1, 2, 3)]
 ALONG_Y = [partners(lambda x, y, c, k=k: (x, y ^ k, c)) for k in (1, 3)]
@@ -490,18 +515,18 @@
         live_cells, core, tot, rest, design, score
     )
     packed = kept + lax.ppermute(given, "cell", OTHER_CORE)
-    steps = exchange(solve(exchange(packed, "cell", SAME_CORE)), "cell")
+    steps = exchange(solve(exchange(packed, "cell", SAME_CORE)), "cell", CORE_FIRST)
     pieces, kept, given, beta = update(
         live_cells, core, steps.reshape(32, 384), pred, design, load, fact, by_load, by_fact
     )
-    arrived = exchange(pieces, "gene")
+    arrived = exchange(pieces, "gene", RING)
 
     value = kept + lax.ppermute(given, "cell", OTHER_CORE)
     near, across, beside = (lax.ppermute(value, "cell", pairs) for pairs in ALONG_X)
     value = (value + near) + (across + beside)
     near = lax.ppermute(value, "cell", ALONG_Y[0])
     shared = factor_share(arrived)
-    gathered = exchange(shared, "gene")
+    gathered = settled(exchange(shared, "gene", RING))
     near, _ = lax.optimization_barrier((near, shared))
     value = value + near
     value = value + lax.ppermute(value, "cell", ALONG_Y[1])

time: 96 us -> 90.7 us (0.945)
  waiting for transfers between devices: 25.1 us -> 15.5 us
  starting transfers between devices: 25.9 us -> 30.6 us
    all_to_all x3, waiting for transfers between devices: 13.4 us -> 4.51 us  [exchange(): lax.all_to_all(value, axis, split_axis=0, concat_axis=0, tiled=True, axis...]
    all_to_all x3, starting transfers between devices: 16.9 us -> 19.5 us  [exchange(): lax.all_to_all(value, axis, split_axis=0, concat_axis=0, tiled=True, axis...]
    ppermute x1, starting transfers between devices: 1.43 us -> 2.57 us  [local(): other = lax.ppermute(mine, 'cell', OTHER_CORE)]
where the time goes in v6:
time: 90.7 us; the launch traced here: 90.2 us
  starting transfers between devices  30.6 us (34%)
  blocking collectives  27.6 us (30%)
  waiting for transfers between devices  15.5 us (17%)
  Pallas kernels  14.9 us (16%)
  between operations  1.39 us (2%)
    all_to_all x2, blocking collectives, exchange(): lax.all_to_all(value, axis, split_axis=0, concat_axis=0, tiled=True, axis...  27.6 us
    all_to_all x3, starting transfers between devices, exchange(): lax.all_to_all(value, axis, split_axis=0, concat_axis=0, tiled=True, axis...  19.5 us
    pallas_call x1, Pallas kernels, prepare(): pl.pallas_call(prepare_kernel, grid=(cells // CHUNK,), in_specs=[smem(),...  4.87 us
    all_to_all x3, waiting for transfers between devices, exchange(): lax.all_to_all(value, axis, split_axis=0, concat_axis=0, tiled=True, axis...  4.51 us
    ppermute x3, waiting for transfers between devices, local(): lax.ppermute(value, 'cell', pairs)  4.44 us
    ppermute x1, waiting for transfers between devices, local(): value = value + lax.ppermute(value, 'cell', ALONG_Y[1])  3.39 us
    ppermute x3, starting transfers between devices, local(): lax.ppermute(value, 'cell', pairs)  3.34 us
    pallas_call x1, Pallas kernels, update(): pl.pallas_call(update_kernel, in_specs=[smem(), smem()] + [vmem()] * 7, o...  2.59 us
  transfers between devices with their start and end apart: 11, of which 9 were waited for; matrix products, arithmetic and copies ran while one was open for 0% of the time, Pallas kernels for 7%

profile of v6, /device:TPU:1, one launch (start us, length us, event | category | flops | bytes accessed | tf_op | source)
XLA Modules:
  0.0 90.2 jit_solution(17966757661275879581)
XLA Ops:
  0.6 2.3 %cell_totals.1 = f32[8,8,128]{2,1,0:T(8,128)} custom-call(s32[384,1024]{1,0:T(8,128)} %counts_ref.3), custom_call_target="tpu_custom_call" | custom-call | tf_op jit(solution)/shard_map/cell_totals/pallas_call | solution.py:95
  2.9 9.0 %all-to-all-start = ((f32[8,8,128]{2,1,0:T(8,128)}), f32[8,8,128]{2,1,0:T(8,128)S(1)}, u32[]{:S(2)}, u32[]{:S(2)}) async-start(f32[8,8,128]{2,1,0:T(8,128)} %cell_totals.1), calls=%async_computation | async-start | bytes 65536 | tf_op jit(solution)/shard_map/all_to_all | solution.py:478
  12.6 4.9 %prepare.1 = (f32[384,1024]{1,0:T(8,128)S(1)}, bf16[96,1024]{1,0:T(8,128)(2,1)S(1)}, f32[384,128]{1,0:T(8,128)S(1)}, f32[64,1024]{1,0:T(8,128)S(1)}, f32[64,384]{1,0:T(8,128)S(1)}) custom-call(s32[1]{0:T(128)S(6)} %copy.17.live_ref, s32[384,1024]{1,0:T(8,128)} %counts_ref.3, s32[1,1024]{1,0:T(1,128)} %bitcast.25, f32[1,1024]{1,0:T(1,128)} %bitcast.26, ...), custom_call_target="tpu_custom_call" | custom-call | tf_op jit(solution)/shard_map/prepare/pallas_call | solution.py:173
  17.5 1.3 %all-to-all-done.tot_ref = f32[8,8,128]{2,1,0:T(8,128)S(1)} async-done(((f32[8,8,128]{2,1,0:T(8,128)}), f32[8,8,128]{2,1,0:T(8,128)S(1)}, u32[]{:S(2)}, u32[]{:S(2)}) %all-to-all-start) | async-done | bytes 32800 | tf_op jit(solution)/shard_map/all_to_all | solution.py:478
  18.8 2.0 %gram_sums.1 = (f32[384,1024]{1,0:T(8,128)S(1)}, f32[16,48,128]{2,1,0:T(8,128)S(1)}, f32[16,48,128]{2,1,0:T(8,128)S(1)}) custom-call(s32[1]{0:T(128)S(6)} %copy.17.live_ref, s32[1]{0:T(128)} %bitcast.core_ref, f32[8,8,128]{2,1,0:T(8,128)S(1)} %all-to-all-done.tot_ref, f32[384,1024]{1,0:T(8,128)S(1)} %get-tuple-element.16.rest_ref, ...), custom_call_target="tpu_custom_call" | custom-call | tf_op jit(solution)/shard_map/gram_sums/pallas_call | solution.py:250
  20.9 0.0 copy-start
  20.9 0.0 copy-start.1
  20.9 2.2 %collective-permute-start = (f32[16,48,128]{2,1,0:T(8,128)S(1)}, f32[16,48,128]{2,1,0:T(8,128)S(1)}, u32[]{:S(2)}, u32[]{:S(2)}) collective-permute-start(f32[16,48,128]{2,1,0:T(8,128)S(1)} %get-tuple-element.20), channel_id=1, source_target_pairs={{0,8},{8,0},{16,24},{24,16},{32,40},{40,32},{48,56},{56,48},{64,72... | collective-permute-start | bytes 1179656 | tf_op jit(solution)/shard_map/ppermute | solution.py:517
  23.1 1.3 %collective-permute-done = f32[16,48,128]{2,1,0:T(8,128)S(1)} collective-permute-done((f32[16,48,128]{2,1,0:T(8,128)S(1)}, f32[16,48,128]{2,1,0:T(8,128)S(1)}, u32[]{:S(2)}, u32[]{:S(2)}) %collective-permute-start) | collective-permute-done | bytes 393248 | tf_op jit(solution)/shard_map/ppermute | solution.py:517
  24.4 0.1 add.32
  24.5 16.1 %all_to_all.25.parts_ref = f32[16,48,128]{2,1,0:T(8,128)S(1)} all-to-all(f32[16,48,128]{2,1,0:T(8,128)S(1)} %add.32), channel_id=1, replica_groups={{0,64,128,192,16,80,144,208,32,96,160,224,48,112,176,240},{8,72,136,200..., dimensions={0} | all-to-all | bytes 786432 | tf_op jit(solution)/shard_map/all_to_all | solution.py:478
  40.5 1.0 %solve.1 = f32[32,1,384]{2,1,0:T(1,128)S(1)} custom-call(f32[16,48,128]{2,1,0:T(8,128)S(1)} %all_to_all.25.parts_ref), custom_call_target="tpu_custom_call" | custom-call | tf_op jit(solution)/shard_map/solve/pallas_call | solution.py:314
  41.5 11.5 %all_to_all.26 = f32[32,1,384]{2,1,0:T(1,128)S(1)} all-to-all(f32[32,1,384]{2,1,0:T(1,128)S(1)} %solve.1), channel_id=1, replica_groups={{0,64,128,192,16,80,144,208,32,96,160,224,48,112,176,240,8,72,136,200,2..., dimensions={0} | all-to-all | bytes 98304 | tf_op jit(solution)/shard_map/all_to_all | solution.py:478
  53.1 0.0 copy-done
  53.1 0.0 copy-done.1
  53.1 2.6 %update.1 = (f32[8,16,1024]{2,1,0:T(8,128)}, f32[64,384]{1,0:T(8,128)S(1)}, f32[64,384]{1,0:T(8,128)S(1)}, f32[32,384]{1,0:T(8,128)}) custom-call(s32[1]{0:T(128)S(6)} %copy.17.live_ref, s32[1]{0:T(128)} %bitcast.core_ref, f32[32,384]{1,0:T(8,128)S(1)} %bitcast.18, f32[384,1024]{1,0:T(8,128)S(1)} %get-tuple-element.21.pred_ref, ...), custom_call_target="tpu_custom_call" | custom-call | tf_op jit(solution)/shard_map/update/pallas_call | solution.py:388
  55.7 4.7 %all-to-all-start.3 = ((f32[8,16,1024]{2,1,0:T(8,128)}), f32[8,16,1024]{2,1,0:T(8,128)S(1)}, u32[]{:S(2)}, u32[]{:S(2)}) async-start(f32[8,16,1024]{2,1,0:T(8,128)} %get-tuple-element.25), calls=%async_computation.3 | async-start | bytes 1048576 | tf_op jit(solution)/shard_map/all_to_all | solution.py:478
  60.4 1.2 %collective-permute-start.1 = (f32[64,384]{1,0:T(8,128)S(1)}, f32[64,384]{1,0:T(8,128)S(1)}, u32[]{:S(2)}, u32[]{:S(2)}) collective-permute-start(f32[64,384]{1,0:T(8,128)S(1)} %get-tuple-element.27), channel_id=1, source_target_pairs={{0,8},{8,0},{16,24},{24,16},{32,40},{40,32},{48,56},{56,48},{64,72... | collective-permute-start | bytes 294920 | tf_op jit(solution)/shard_map/ppermute | solution.py:524
  61.6 0.9 %collective-permute-done.1 = f32[64,384]{1,0:T(8,128)S(1)} collective-permute-done((f32[64,384]{1,0:T(8,128)S(1)}, f32[64,384]{1,0:T(8,128)S(1)}, u32[]{:S(2)}, u32[]{:S(2)}) %collective-permute-start.1) | collective-permute-done | bytes 98336 | tf_op jit(solution)/shard_map/ppermute | solution.py:524
  62.6 1.1 %collective-permute-start.4 = (f32[64,384]{1,0:T(8,128)S(1)}, f32[64,384]{1,0:T(8,128)S(1)}, u32[]{:S(2)}, u32[]{:S(2)}) collective-permute-start(f32[64,384]{1,0:T(8,128)S(1)} %add.33), channel_id=1, source_target_pairs={{0,192},{8,200},{16,208},{24,216},{32,224},{40,232},{48,240},{56,2... | collective-permute-start | bytes 294920 | tf_op jit(solution)/shard_map/ppermute | solution.py:525
  63.7 1.0 %collective-permute-start.3 = (f32[64,384]{1,0:T(8,128)S(1)}, f32[64,384]{1,0:T(8,128)S(1)}, u32[]{:S(2)}, u32[]{:S(2)}) collective-permute-start(f32[64,384]{1,0:T(8,128)S(1)} %add.33), channel_id=1, source_target_pairs={{0,128},{8,136},{16,144},{24,152},{32,160},{40,168},{48,176},{56,1... | collective-permute-start | bytes 294920 | tf_op jit(solution)/shard_map/ppermute | solution.py:525
  64.7 1.2 %collective-permute-start.2 = (f32[64,384]{1,0:T(8,128)S(1)}, f32[64,384]{1,0:T(8,128)S(1)}, u32[]{:S(2)}, u32[]{:S(2)}) collective-permute-start(f32[64,384]{1,0:T(8,128)S(1)} %add.33), channel_id=1, source_target_pairs={{0,64},{8,72},{16,80},{24,88},{32,96},{40,104},{48,112},{56,120},{... | collective-permute-start | bytes 294920 | tf_op jit(solution)/shard_map/ppermute | solution.py:525
  65.9 2.0 %collective-permute-done.4 = f32[64,384]{1,0:T(8,128)S(1)} collective-permute-done((f32[64,384]{1,0:T(8,128)S(1)}, f32[64,384]{1,0:T(8,128)S(1)}, u32[]{:S(2)}, u32[]{:S(2)}) %collective-permute-start.4) | collective-permute-done | bytes 98336 | tf_op jit(solution)/shard_map/ppermute | solution.py:525
  67.9 1.1 %collective-permute-done.3 = f32[64,384]{1,0:T(8,128)S(1)} collective-permute-done((f32[64,384]{1,0:T(8,128)S(1)}, f32[64,384]{1,0:T(8,128)S(1)}, u32[]{:S(2)}, u32[]{:S(2)}) %collective-permute-start.3) | collective-permute-done | bytes 98336 | tf_op jit(solution)/shard_map/ppermute | solution.py:525
  69.0 1.3 %collective-permute-done.2 = f32[64,384]{1,0:T(8,128)S(1)} collective-permute-done((f32[64,384]{1,0:T(8,128)S(1)}, f32[64,384]{1,0:T(8,128)S(1)}, u32[]{:S(2)}, u32[]{:S(2)}) %collective-permute-start.2) | collective-permute-done | bytes 98336 | tf_op jit(solution)/shard_map/ppermute | solution.py:525
  70.4 0.4 collective-permute-start.5
  70.7 3.2 %all-to-all-done.3.parts_ref = f32[8,16,1024]{2,1,0:T(8,128)S(1)} async-done(((f32[8,16,1024]{2,1,0:T(8,128)}), f32[8,16,1024]{2,1,0:T(8,128)S(1)}, u32[]{:S(2)}, u32[]{:S(2)}) %all-to-all-start.3) | async-done | bytes 524320 | tf_op jit(solution)/shard_map/all_to_all | solution.py:478
  73.9 0.8 factor_share.1
  74.7 5.8 %all-to-all-start.4 = ((f32[8,8,1024]{2,1,0:T(8,128)}), f32[8,8,1024]{2,1,0:T(8,128)S(1)}, u32[]{:S(2)}, u32[]{:S(2)}) async-start(f32[8,8,1024]{2,1,0:T(8,128)} %factor_share.1), calls=%async_computation.4 | async-start | bytes 524288 | tf_op jit(solution)/shard_map/all_to_all | solution.py:478
  80.5 0.0 collective-permute-done.5
  80.5 1.4 %collective-permute-start.6 = (f32[64,384]{1,0:T(8,128)S(1)}, f32[64,384]{1,0:T(8,128)S(1)}, u32[]{:S(2)}, u32[]{:S(2)}) collective-permute-start(f32[64,384]{1,0:T(8,128)S(1)} %add.37), channel_id=1, source_target_pairs={{0,48},{8,56},{16,32},{24,40},{32,16},{40,24},{48,0},{56,8},{64,11... | collective-permute-start | bytes 294920 | tf_op jit(solution)/shard_map/ppermute | solution.py:532
  81.9 3.4 %collective-permute-done.6 = f32[64,384]{1,0:T(8,128)S(1)} collective-permute-done((f32[64,384]{1,0:T(8,128)S(1)}, f32[64,384]{1,0:T(8,128)S(1)}, u32[]{:S(2)}, u32[]{:S(2)}) %collective-permute-start.6) | collective-permute-done | bytes 98336 | tf_op jit(solution)/shard_map/ppermute | solution.py:532
  85.3 2.6 %collective-permute-start.7 = (f32[32,384]{1,0:T(8,128)S(1)}, f32[32,384]{1,0:T(8,128)S(1)}, u32[]{:S(2)}, u32[]{:S(2)}) collective-permute-start(f32[32,384]{1,0:T(8,128)S(1)} %fusion.1.mine_ref), channel_id=1, source_target_pairs={{0,8},{8,0},{16,24},{24,16},{32,40},{40,32},{48,56},{56,48},{64,72... | collective-permute-start | bytes 147464 | tf_op jit(solution)/shard_map/ppermute | solution.py:534
  87.9 0.9 collective-permute-done.7.other_ref
  88.7 0.6 joined_score.1
  89.4 0.0 all-to-all-done.4.value_ref
  89.4 0.8 settled.1
  (6 shorter events, 0.1 us)
Async XLA Ops:
  2.9 15.9 %all-to-all-start = ((f32[8,8,128]{2,1,0:T(8,128)}), f32[8,8,128]{2,1,0:T(8,128)S(1)}, u32[]{:S(2)}, u32[]{:S(2)}) async-start(f32[8,8,128]{2,1,0:T(8,128)} %cell_totals.1), calls=%async_computation | async-start | bytes 65536 | tf_op jit(solution)/shard_map/all_to_all | solution.py:478
  20.9 32.2 %copy-start = (bf16[1024,64]{0,1:T(8,128)(2,1)S(1)}, bf16[1024,64]{0,1:T(8,128)(2,1)}, u32[]{:S(2)}) copy-start(bf16[1024,64]{0,1:T(8,128)(2,1)} %param.18) | copy-start | bytes 393220
  20.9 32.2 %copy-start.1 = (bf16[384,64]{0,1:T(8,128)(2,1)S(1)}, bf16[384,64]{0,1:T(8,128)(2,1)}, u32[]{:S(2)}) copy-start(bf16[384,64]{0,1:T(8,128)(2,1)} %param.19) | copy-start | bytes 147460
  20.9 3.5 %collective-permute-start = (f32[16,48,128]{2,1,0:T(8,128)S(1)}, f32[16,48,128]{2,1,0:T(8,128)S(1)}, u32[]{:S(2)}, u32[]{:S(2)}) collective-permute-start(f32[16,48,128]{2,1,0:T(8,128)S(1)} %get-tuple-element.20), channel_id=1, source_target_pairs={{0,8},{8,0},{16,24},{24,16},{32,40},{40,32},{48,56},{56,48},{64,72... | collective-permute-start | bytes 1179656 | tf_op jit(solution)/shard_map/ppermute | solution.py:517
  55.7 18.2 %all-to-all-start.3 = ((f32[8,16,1024]{2,1,0:T(8,128)}), f32[8,16,1024]{2,1,0:T(8,128)S(1)}, u32[]{:S(2)}, u32[]{:S(2)}) async-start(f32[8,16,1024]{2,1,0:T(8,128)} %get-tuple-element.25), calls=%async_computation.3 | async-start | bytes 1048576 | tf_op jit(solution)/shard_map/all_to_all | solution.py:478
  60.4 2.1 %collective-permute-start.1 = (f32[64,384]{1,0:T(8,128)S(1)}, f32[64,384]{1,0:T(8,128)S(1)}, u32[]{:S(2)}, u32[]{:S(2)}) collective-permute-start(f32[64,384]{1,0:T(8,128)S(1)} %get-tuple-element.27), channel_id=1, source_target_pairs={{0,8},{8,0},{16,24},{24,16},{32,40},{40,32},{48,56},{56,48},{64,72... | collective-permute-start | bytes 294920 | tf_op jit(solution)/shard_map/ppermute | solution.py:524
  62.6 5.3 %collective-permute-start.4 = (f32[64,384]{1,0:T(8,128)S(1)}, f32[64,384]{1,0:T(8,128)S(1)}, u32[]{:S(2)}, u32[]{:S(2)}) collective-permute-start(f32[64,384]{1,0:T(8,128)S(1)} %add.33), channel_id=1, source_target_pairs={{0,192},{8,200},{16,208},{24,216},{32,224},{40,232},{48,240},{56,2... | collective-permute-start | bytes 294920 | tf_op jit(solution)/shard_map/ppermute | solution.py:525
  63.7 5.3 %collective-permute-start.3 = (f32[64,384]{1,0:T(8,128)S(1)}, f32[64,384]{1,0:T(8,128)S(1)}, u32[]{:S(2)}, u32[]{:S(2)}) collective-permute-start(f32[64,384]{1,0:T(8,128)S(1)} %add.33), channel_id=1, source_target_pairs={{0,128},{8,136},{16,144},{24,152},{32,160},{40,168},{48,176},{56,1... | collective-permute-start | bytes 294920 | tf_op jit(solution)/shard_map/ppermute | solution.py:525
  64.7 5.6 %collective-permute-start.2 = (f32[64,384]{1,0:T(8,128)S(1)}, f32[64,384]{1,0:T(8,128)S(1)}, u32[]{:S(2)}, u32[]{:S(2)}) collective-permute-start(f32[64,384]{1,0:T(8,128)S(1)} %add.33), channel_id=1, source_target_pairs={{0,64},{8,72},{16,80},{24,88},{32,96},{40,104},{48,112},{56,120},{... | collective-permute-start | bytes 294920 | tf_op jit(solution)/shard_map/ppermute | solution.py:525
  70.4 10.1 %collective-permute-start.5 = (f32[64,384]{1,0:T(8,128)S(1)}, f32[64,384]{1,0:T(8,128)S(1)}, u32[]{:S(2)}, u32[]{:S(2)}) collective-permute-start(f32[64,384]{1,0:T(8,128)S(1)} %add_add_fusion), channel_id=1, source_target_pairs={{0,16},{8,24},{16,0},{24,8},{32,48},{40,56},{48,32},{56,40},{64,80... | collective-permute-start | bytes 294920 | tf_op jit(solution)/shard_map/ppermute | solution.py:527
  74.7 14.7 %all-to-all-start.4 = ((f32[8,8,1024]{2,1,0:T(8,128)}), f32[8,8,1024]{2,1,0:T(8,128)S(1)}, u32[]{:S(2)}, u32[]{:S(2)}) async-start(f32[8,8,1024]{2,1,0:T(8,128)} %factor_share.1), calls=%async_computation.4 | async-start | bytes 524288 | tf_op jit(solution)/shard_map/all_to_all | solution.py:478
  80.5 4.8 %collective-permute-start.6 = (f32[64,384]{1,0:T(8,128)S(1)}, f32[64,384]{1,0:T(8,128)S(1)}, u32[]{:S(2)}, u32[]{:S(2)}) collective-permute-start(f32[64,384]{1,0:T(8,128)S(1)} %add.37), channel_id=1, source_target_pairs={{0,48},{8,56},{16,32},{24,40},{32,16},{40,24},{48,0},{56,8},{64,11... | collective-permute-start | bytes 294920 | tf_op jit(solution)/shard_map/ppermute | solution.py:532
  85.3 3.5 %collective-permute-start.7 = (f32[32,384]{1,0:T(8,128)S(1)}, f32[32,384]{1,0:T(8,128)S(1)}, u32[]{:S(2)}, u32[]{:S(2)}) collective-permute-start(f32[32,384]{1,0:T(8,128)S(1)} %fusion.1.mine_ref), channel_id=1, source_target_pairs={{0,8},{8,0},{16,24},{24,16},{32,40},{40,32},{48,56},{56,48},{64,72... | collective-permute-start | bytes 147464 | tf_op jit(solution)/shard_map/ppermute | solution.py:534

commit v7 on v6

--- a/solution.py
+++ b/solution.py
@@ -109,74 +109,73 @@
 
 
 def prepare_kernel(
-    live_ref, counts_ref, knot_hbm, frac_hbm, batch_hbm, cov_hbm, coef_hbm, shift_hbm,
+    live_ref, counts_hbm, knot_hbm, frac_hbm, batch_hbm, cov_hbm, coef_hbm, shift_hbm,
     load_hbm, fact_hbm,
     rest_ref, design_ref, score_ref, by_load_ref, by_fact_ref,
-    left, knot_all, frac_all, batch_all, cov_all, coef, shift, load, fact_all, score, arrived,
+    counts_all, knot_all, frac_all, batch_all, cov_all, coef, shift, load, fact_all, arrived,
 ):
-    step = pl.program_id(0)
-
-    @pl.when(step == 0)
-    def _():
-        pairs = (
-            (coef_hbm, coef), (shift_hbm, shift), (load_hbm, load), (fact_hbm, fact_all),
-            (knot_hbm, knot_all), (frac_hbm, frac_all), (batch_hbm, batch_all), (cov_hbm, cov_all),
+    pairs = (
+        (knot_hbm, knot_all), (frac_hbm, frac_all), (batch_hbm, batch_all), (cov_hbm, cov_all),
+        (coef_hbm, coef), (shift_hbm, shift), (load_hbm, load), (fact_hbm, fact_all),
+    )
+    copies = [
+        pltpu.make_async_copy(source, target, arrived.at[i])
+        for i, (source, target) in enumerate(pairs)
+    ]
+    cells = rest_ref.shape[1]
+    blocks = [
+        pltpu.make_async_copy(
+            counts_hbm.at[:, pl.ds(at, CHUNK)], counts_all.at[:, pl.ds(at, CHUNK)],
+            arrived.at[len(pairs) + at // CHUNK],
         )
-        copies = [
-            pltpu.make_async_copy(source, target, arrived.at[i])
-            for i, (source, target) in enumerate(pairs)
-        ]
-        for copy in copies:
-            copy.start()
-        for copy in copies:
-            copy.wait()
-        c1, c2, c3 = split3(coef[...])
-        b1, b2, b3 = split3(shift[...])
-        left[...] = jnp.concatenate([c1, c1, c2, c2, c1, c3, b1, b2, b3, load[...]], axis=0)
-        score[...] = jnp.zeros_like(score)
-        by_fact_ref[...] = jnp.zeros_like(by_fact_ref)
-
-    at = pl.multiple_of(step * CHUNK, CHUNK)
-    here = pl.ds(at, CHUNK)
-    knot, frac, cov, fact = knot_all[:, here], frac_all[:, here], cov_all[:, here], fact_all[:, here]
-    levels = lax.broadcasted_iota(jnp.int32, (SPL, CHUNK), 0)
-    hat = jnp.where(levels == knot, 1.0 - frac, 0.0) + jnp.where(levels == knot + 1, frac, 0.0)
-    d1, d2, d3 = split3(jnp.concatenate([hat, cov], axis=0))
-    terms = jnp.concatenate([d1, d2, d3], axis=0)
-    design_ref[...] = terms
-    batches = lax.broadcasted_iota(jnp.int32, (64, CHUNK), 0)
-    onehot = (batches == batch_all[:, here]).astype(F32).astype(BF16)
-    right = jnp.concatenate([d1, d2, d1, d2, d3, d1, onehot, onehot, onehot, fact], axis=0)
-    rest_ref[...] = dot(left[...], right, TN)
-
-    slot = lax.broadcasted_iota(jnp.int32, (1, CHUNK), 1) + at
-    mask = (slot < live_ref[0]).astype(F32)
-    counts = (counts_ref[...].astype(F32) * mask).astype(BF16)
-    by_load_ref[...] = dot(load[...], counts, NN)
-    by_fact_ref[...] += dot(fact, counts, NT)
-    score[...] += dot(counts, terms, NT)
-
-    @pl.when(step == pl.num_programs(0) - 1)
-    def _():
-        value = score[:, :32] + score[:, 32:64] + score[:, 64:96]
-        blank = jnp.zeros((value.shape[0], 96), F32)
-        score_ref[...] = jnp.concatenate([blank, value], axis=1)
+        for at in range(0, cells, CHUNK)
+    ]
+    for copy in copies + blocks:
+        copy.start()
+    for copy in copies:
+        copy.wait()
+    c1, c2, c3 = split3(coef[...])
+    b1, b2, b3 = split3(shift[...])
+    left = jnp.concatenate([c1, c1, c2, c2, c1, c3, b1, b2, b3, load[...]], axis=0)
+    score, by_fact = 0.0, 0.0
+    for at in range(0, cells, CHUNK):
+        here = pl.ds(at, CHUNK)
+        knot, frac = knot_all[:, here], frac_all[:, here]
+        cov, fact = cov_all[:, here], fact_all[:, here]
+        levels = lax.broadcasted_iota(jnp.int32, (SPL, CHUNK), 0)
+        hat = jnp.where(levels == knot, 1.0 - frac, 0.0)
+        hat = hat + jnp.where(levels == knot + 1, frac, 0.0)
+        d1, d2, d3 = split3(jnp.concatenate([hat, cov], axis=0))
+        terms = jnp.concatenate([d1, d2, d3], axis=0)
+        design_ref[:, here] = terms
+        batches = lax.broadcasted_iota(jnp.int32, (64, CHUNK), 0)
+        onehot = (batches == batch_all[:, here]).astype(F32).astype(BF16)
+        right = jnp.concatenate([d1, d2, d1, d2, d3, d1, onehot, onehot, onehot, fact], axis=0)
+        rest_ref[:, here] = dot(left, right, TN)
+
+        blocks[at // CHUNK].wait()
+        slot = lax.broadcasted_iota(jnp.int32, (1, CHUNK), 1) + at
+        mask = (slot < live_ref[0]).astype(F32)
+        counts = (counts_all[:, here].astype(F32) * mask).astype(BF16)
+        by_load_ref[:, here] = dot(load[...], counts, NN)
+        by_fact = by_fact + dot(fact, counts, NT)
+        score = score + dot(counts, terms, NT)
+    by_fact_ref[...] = by_fact
+    value = score[:, :32] + score[:, 32:64] + score[:, 64:96]
+    blank = jnp.zeros((value.shape[0], 96), F32)
+    score_ref[...] = jnp.concatenate([blank, value], axis=1)
 
 
 def prepare(live, counts, knot, frac, batch, cov, coef, shift, load, fact):
     genes, cells = counts.shape
-    small = [
+    arrays = [
         pltpu.with_memory_space_constraint(a, pltpu.HBM)
-        for a in (knot, frac, batch, cov, coef, shift, load, fact)
-    ]
-    counts = pltpu.with_memory_space_constraint(counts, pltpu.HBM)
+        for a in (counts, knot, frac, batch, cov, coef, shift, load, fact)
+    ]
     return pl.pallas_call(
         prepare_kernel,
-        grid=(cells // CHUNK,),
-        in_specs=[smem(), lanes(genes)] + [pl.BlockSpec(memory_space=pltpu.HBM)] * 8,
-        out_specs=[
-            lanes(genes), lanes(96), full((genes, 128)), lanes(FACT), full((FACT, genes)),
-        ],
+        in_specs=[smem()] + [hbm()] * len(arrays),
+        out_specs=[vmem()] * 5,
         out_shape=[
             jax.ShapeDtypeStruct((genes, cells), F32),
             jax.ShapeDtypeStruct((96, cells), BF16),
@@ -184,12 +183,11 @@
             jax.ShapeDtypeStruct((FACT, cells), F32),
             jax.ShapeDtypeStruct((FACT, genes), F32),
         ],
-        scratch_shapes=[pltpu.VMEM((448, genes), BF16)]
-        + [pltpu.VMEM(a.shape, a.dtype) for a in small]
-        + [pltpu.VMEM((genes, 96), F32), pltpu.SemaphoreType.DMA((8,))],
+        scratch_shapes=[pltpu.VMEM(a.shape, a.dtype) for a in arrays]
+        + [pltpu.SemaphoreType.DMA((len(arrays) - 1 + cells // CHUNK,))],
         compiler_params=params(),
         name="prepare",
-    )(live, counts, *small)
+    )(live, *arrays)
 
 
 def gram_kernel(
@@ -406,19 +404,27 @@
     )(live, core, steps, pred, design, load, fact, by_load, by_fact)
 
 
-def score_kernel(core_ref, mine_ref, other_ref, out_ref):
+def score_kernel(core_ref, mine_ref, other_ref, out_hbm, sent):
     core = core_ref[0]
-    for half, ref in ((core, mine_ref), (1 - core, other_ref)):
-        out_ref[pl.ds(pl.multiple_of(32 * half, 32), 32), :] = ref[...]
+    sends = [
+        pltpu.make_async_copy(
+            ref, out_hbm.at[pl.ds(pl.multiple_of(32 * half, 32), 32), :], sent.at[i]
+        )
+        for i, (half, ref) in enumerate(((core, mine_ref), (1 - core, other_ref)))
+    ]
+    for send in sends:
+        send.start()
+    for send in sends:
+        send.wait()
 
 
 def joined_score(core, mine, other):
     return pl.pallas_call(
         score_kernel,
-        grid=(1,),
-        in_specs=[smem(), full(mine.shape), full(mine.shape)],
-        out_specs=full((FACT, mine.shape[1])),
-        out_shape=jax.ShapeDtypeStruct((FACT, mine.shape[1]), F32),
+        in_specs=[smem(), vmem(), vmem()],
+        out_specs=hbm(),
+        out_shape=pltpu.HBM((FACT, mine.shape[1]), F32),
+        scratch_shapes=[pltpu.SemaphoreType.DMA((2,))],
         compiler_params=params(),
         name="joined_score",
     )(core, mine, other)
@@ -505,7 +511,7 @@
     coefficients, batch_effect, factors, loadings,
 ):
     fact, load = factors.T, loadings.T
-    tot = exchange(cell_totals(counts, 8), "gene")
+    tot = exchange(cell_totals(counts, 8), "gene", RING)
     rest, design, score, by_load, by_fact = prepare(
         live_cells, counts, knot_bin[None], depth_frac[None], batch_id[None],
         cell_covariates, coefficients.T, batch_effect.T, load, fact,

time: 90.7 us -> 90.9 us (level)
  starting transfers between devices: 30.6 us -> 32.9 us
  Pallas kernels: 14.9 us -> 13.5 us
    all_to_all x3, starting transfers between devices: 19.5 us -> 22.8 us  [exchange(): lax.all_to_all(value, axis, split_axis=0, concat_axis=0, tiled=True, axis...]
    pallas_call x2, Pallas kernels: 5.52 us -> 4.06 us  [the longest x1 3.4 us: prepare(): pl.pallas_call(prepare_kernel, in_specs=[smem()] + [hbm()] * len(arrays),...]
  transfers between devices with their start and end apart: 11 -> 11, of which waited for: 9 -> 8; matrix products, arithmetic and copies ran while one was open for 0% -> 0% of each run, Pallas kernels for 7% -> 5%
where the time goes in v7:
time: 90.9 us; the launch traced here: 90.5 us
  starting transfers between devices  32.9 us (36%)
  blocking collectives  27.6 us (30%)
  waiting for transfers between devices  14.9 us (16%)
  Pallas kernels  13.5 us (15%)
  between operations  1.41 us (2%)
    all_to_all x2, blocking collectives, exchange(): lax.all_to_all(value, axis, split_axis=0, concat_axis=0, tiled=True, axis...  27.6 us
    all_to_all x3, starting transfers between devices, exchange(): lax.all_to_all(value, axis, split_axis=0, concat_axis=0, tiled=True, axis...  22.8 us
    ppermute x3, waiting for transfers between devices, local(): lax.ppermute(value, 'cell', pairs)  4.44 us
    all_to_all x3, waiting for transfers between devices, exchange(): lax.all_to_all(value, axis, split_axis=0, concat_axis=0, tiled=True, axis...  3.72 us
    ppermute x1, waiting for transfers between devices, local(): value = value + lax.ppermute(value, 'cell', ALONG_Y[1])  3.6 us
    pallas_call x1, Pallas kernels, prepare(): pl.pallas_call(prepare_kernel, in_specs=[smem()] + [hbm()] * len(arrays),...  3.4 us
    ppermute x3, starting transfers between devices, local(): lax.ppermute(value, 'cell', pairs)  3.34 us
    pallas_call x1, Pallas kernels, update(): pl.pallas_call(update_kernel, in_specs=[smem(), smem()] + [vmem()] * 7, o...  2.59 us
  transfers between devices with their start and end apart: 11, of which 8 were waited for; matrix products, arithmetic and copies ran while one was open for 0% of the time, Pallas kernels for 5%

profile of v7, /device:TPU:1, one launch (start us, length us, event | category | flops | bytes accessed | tf_op | source)
XLA Modules:
  0.0 90.5 jit_solution(13959053543537851327)
XLA Ops:
  0.6 2.3 %cell_totals.1 = f32[8,8,128]{2,1,0:T(8,128)} custom-call(s32[384,1024]{1,0:T(8,128)} %counts_hbm.1), custom_call_target="tpu_custom_call" | custom-call | tf_op jit(solution)/shard_map/cell_totals/pallas_call | solution.py:95
  2.9 10.7 %all-to-all-start = ((f32[8,8,128]{2,1,0:T(8,128)}), f32[8,8,128]{2,1,0:T(8,128)S(1)}, u32[]{:S(2)}, u32[]{:S(2)}) async-start(f32[8,8,128]{2,1,0:T(8,128)} %cell_totals.1), calls=%async_computation | async-start | bytes 65536 | tf_op jit(solution)/shard_map/all_to_all | solution.py:484
  14.2 3.4 %prepare.1 = (f32[384,1024]{1,0:T(8,128)S(1)}, bf16[96,1024]{1,0:T(8,128)(2,1)S(1)}, f32[384,128]{1,0:T(8,128)S(1)}, f32[64,1024]{1,0:T(8,128)S(1)}, f32[64,384]{1,0:T(8,128)S(1)}) custom-call(s32[1]{0:T(128)S(6)} %copy.17.live_ref, s32[384,1024]{1,0:T(8,128)} %counts_hbm.1, s32[1,1024]{1,0:T(1,128)} %bitcast.25, f32[1,1024]{1,0:T(1,128)} %bitcast.26, ...), custom_call_target="tpu_custom_call" | custom-call | tf_op jit(solution)/shard_map/prepare/pallas_call | solution.py:175
  17.6 0.0 all-to-all-done.tot_ref
  17.6 2.1 %gram_sums.1 = (f32[384,1024]{1,0:T(8,128)S(1)}, f32[16,48,128]{2,1,0:T(8,128)S(1)}, f32[16,48,128]{2,1,0:T(8,128)S(1)}) custom-call(s32[1]{0:T(128)S(6)} %copy.17.live_ref, s32[1]{0:T(128)} %bitcast.core_ref, f32[8,8,128]{2,1,0:T(8,128)S(1)} %all-to-all-done.tot_ref, f32[384,1024]{1,0:T(8,128)S(1)} %get-tuple-element.16.rest_ref, ...), custom_call_target="tpu_custom_call" | custom-call | tf_op jit(solution)/shard_map/gram_sums/pallas_call | solution.py:248
  19.7 0.0 copy-start
  19.7 0.0 copy-start.1
  19.7 2.0 %collective-permute-start = (f32[16,48,128]{2,1,0:T(8,128)S(1)}, f32[16,48,128]{2,1,0:T(8,128)S(1)}, u32[]{:S(2)}, u32[]{:S(2)}) collective-permute-start(f32[16,48,128]{2,1,0:T(8,128)S(1)} %get-tuple-element.20), channel_id=1, source_target_pairs={{0,8},{8,0},{16,24},{24,16},{32,40},{40,32},{48,56},{56,48},{64,72... | collective-permute-start | bytes 1179656 | tf_op jit(solution)/shard_map/ppermute | solution.py:523
  21.7 1.3 %collective-permute-done = f32[16,48,128]{2,1,0:T(8,128)S(1)} collective-permute-done((f32[16,48,128]{2,1,0:T(8,128)S(1)}, f32[16,48,128]{2,1,0:T(8,128)S(1)}, u32[]{:S(2)}, u32[]{:S(2)}) %collective-permute-start) | collective-permute-done | bytes 393248 | tf_op jit(solution)/shard_map/ppermute | solution.py:523
  23.1 0.1 add.32
  23.1 16.1 %all_to_all.25.parts_ref = f32[16,48,128]{2,1,0:T(8,128)S(1)} all-to-all(f32[16,48,128]{2,1,0:T(8,128)S(1)} %add.32), channel_id=1, replica_groups={{0,64,128,192,16,80,144,208,32,96,160,224,48,112,176,240},{8,72,136,200..., dimensions={0} | all-to-all | bytes 786432 | tf_op jit(solution)/shard_map/all_to_all | solution.py:484
  39.2 1.0 %solve.1 = f32[32,1,384]{2,1,0:T(1,128)S(1)} custom-call(f32[16,48,128]{2,1,0:T(8,128)S(1)} %all_to_all.25.parts_ref), custom_call_target="tpu_custom_call" | custom-call | tf_op jit(solution)/shard_map/solve/pallas_call | solution.py:312
  40.2 11.5 %all_to_all.26 = f32[32,1,384]{2,1,0:T(1,128)S(1)} all-to-all(f32[32,1,384]{2,1,0:T(1,128)S(1)} %solve.1), channel_id=1, replica_groups={{0,64,128,192,16,80,144,208,32,96,160,224,48,112,176,240,8,72,136,200,2..., dimensions={0} | all-to-all | bytes 98304 | tf_op jit(solution)/shard_map/all_to_all | solution.py:484
  51.7 0.0 copy-done
  51.7 0.0 copy-done.1
  51.7 2.6 %update.1 = (f32[8,16,1024]{2,1,0:T(8,128)}, f32[64,384]{1,0:T(8,128)S(1)}, f32[64,384]{1,0:T(8,128)S(1)}, f32[32,384]{1,0:T(8,128)}) custom-call(s32[1]{0:T(128)S(6)} %copy.17.live_ref, s32[1]{0:T(128)} %bitcast.core_ref, f32[32,384]{1,0:T(8,128)S(1)} %bitcast.18, f32[384,1024]{1,0:T(8,128)S(1)} %get-tuple-element.21.pred_ref, ...), custom_call_target="tpu_custom_call" | custom-call | tf_op jit(solution)/shard_map/update/pallas_call | solution.py:386
  54.3 6.4 %all-to-all-start.3 = ((f32[8,16,1024]{2,1,0:T(8,128)}), f32[8,16,1024]{2,1,0:T(8,128)S(1)}, u32[]{:S(2)}, u32[]{:S(2)}) async-start(f32[8,16,1024]{2,1,0:T(8,128)} %get-tuple-element.25), calls=%async_computation.3 | async-start | bytes 1048576 | tf_op jit(solution)/shard_map/all_to_all | solution.py:484
  60.7 0.9 collective-permute-start.1
  61.6 0.9 %collective-permute-done.1 = f32[64,384]{1,0:T(8,128)S(1)} collective-permute-done((f32[64,384]{1,0:T(8,128)S(1)}, f32[64,384]{1,0:T(8,128)S(1)}, u32[]{:S(2)}, u32[]{:S(2)}) %collective-permute-start.1) | collective-permute-done | bytes 98336 | tf_op jit(solution)/shard_map/ppermute | solution.py:530
  62.6 1.1 %collective-permute-start.4 = (f32[64,384]{1,0:T(8,128)S(1)}, f32[64,384]{1,0:T(8,128)S(1)}, u32[]{:S(2)}, u32[]{:S(2)}) collective-permute-start(f32[64,384]{1,0:T(8,128)S(1)} %add.33), channel_id=1, source_target_pairs={{0,192},{8,200},{16,208},{24,216},{32,224},{40,232},{48,240},{56,2... | collective-permute-start | bytes 294920 | tf_op jit(solution)/shard_map/ppermute | solution.py:531
  63.7 1.0 %collective-permute-start.3 = (f32[64,384]{1,0:T(8,128)S(1)}, f32[64,384]{1,0:T(8,128)S(1)}, u32[]{:S(2)}, u32[]{:S(2)}) collective-permute-start(f32[64,384]{1,0:T(8,128)S(1)} %add.33), channel_id=1, source_target_pairs={{0,128},{8,136},{16,144},{24,152},{32,160},{40,168},{48,176},{56,1... | collective-permute-start | bytes 294920 | tf_op jit(solution)/shard_map/ppermute | solution.py:531
  64.7 1.2 %collective-permute-start.2 = (f32[64,384]{1,0:T(8,128)S(1)}, f32[64,384]{1,0:T(8,128)S(1)}, u32[]{:S(2)}, u32[]{:S(2)}) collective-permute-start(f32[64,384]{1,0:T(8,128)S(1)} %add.33), channel_id=1, source_target_pairs={{0,64},{8,72},{16,80},{24,88},{32,96},{40,104},{48,112},{56,120},{... | collective-permute-start | bytes 294920 | tf_op jit(solution)/shard_map/ppermute | solution.py:531
  65.9 2.0 %collective-permute-done.4 = f32[64,384]{1,0:T(8,128)S(1)} collective-permute-done((f32[64,384]{1,0:T(8,128)S(1)}, f32[64,384]{1,0:T(8,128)S(1)}, u32[]{:S(2)}, u32[]{:S(2)}) %collective-permute-start.4) | collective-permute-done | bytes 98336 | tf_op jit(solution)/shard_map/ppermute | solution.py:531
  67.9 1.1 %collective-permute-done.3 = f32[64,384]{1,0:T(8,128)S(1)} collective-permute-done((f32[64,384]{1,0:T(8,128)S(1)}, f32[64,384]{1,0:T(8,128)S(1)}, u32[]{:S(2)}, u32[]{:S(2)}) %collective-permute-start.3) | collective-permute-done | bytes 98336 | tf_op jit(solution)/shard_map/ppermute | solution.py:531
  69.0 1.3 %collective-permute-done.2 = f32[64,384]{1,0:T(8,128)S(1)} collective-permute-done((f32[64,384]{1,0:T(8,128)S(1)}, f32[64,384]{1,0:T(8,128)S(1)}, u32[]{:S(2)}, u32[]{:S(2)}) %collective-permute-start.2) | collective-permute-done | bytes 98336 | tf_op jit(solution)/shard_map/ppermute | solution.py:531
  70.4 0.4 collective-permute-start.5
  70.7 3.7 %all-to-all-done.3.parts_ref = f32[8,16,1024]{2,1,0:T(8,128)S(1)} async-done(((f32[8,16,1024]{2,1,0:T(8,128)}), f32[8,16,1024]{2,1,0:T(8,128)S(1)}, u32[]{:S(2)}, u32[]{:S(2)}) %all-to-all-start.3) | async-done | bytes 524320 | tf_op jit(solution)/shard_map/all_to_all | solution.py:484
  74.5 0.8 factor_share.1
  75.3 5.7 %all-to-all-start.4 = ((f32[8,8,1024]{2,1,0:T(8,128)}), f32[8,8,1024]{2,1,0:T(8,128)S(1)}, u32[]{:S(2)}, u32[]{:S(2)}) async-start(f32[8,8,1024]{2,1,0:T(8,128)} %factor_share.1), calls=%async_computation.4 | async-start | bytes 524288 | tf_op jit(solution)/shard_map/all_to_all | solution.py:484
  81.0 0.0 collective-permute-done.5
  81.0 1.2 %collective-permute-start.6 = (f32[64,384]{1,0:T(8,128)S(1)}, f32[64,384]{1,0:T(8,128)S(1)}, u32[]{:S(2)}, u32[]{:S(2)}) collective-permute-start(f32[64,384]{1,0:T(8,128)S(1)} %add.37), channel_id=1, source_target_pairs={{0,48},{8,56},{16,32},{24,40},{32,16},{40,24},{48,0},{56,8},{64,11... | collective-permute-start | bytes 294920 | tf_op jit(solution)/shard_map/ppermute | solution.py:538
  82.2 3.6 %collective-permute-done.6 = f32[64,384]{1,0:T(8,128)S(1)} collective-permute-done((f32[64,384]{1,0:T(8,128)S(1)}, f32[64,384]{1,0:T(8,128)S(1)}, u32[]{:S(2)}, u32[]{:S(2)}) %collective-permute-start.6) | collective-permute-done | bytes 98336 | tf_op jit(solution)/shard_map/ppermute | solution.py:538
  85.8 2.3 %collective-permute-start.7 = (f32[32,384]{1,0:T(8,128)S(1)}, f32[32,384]{1,0:T(8,128)S(1)}, u32[]{:S(2)}, u32[]{:S(2)}) collective-permute-start(f32[32,384]{1,0:T(8,128)S(1)} %fusion.1.mine_ref), channel_id=1, source_target_pairs={{0,8},{8,0},{16,24},{24,16},{32,40},{40,32},{48,56},{56,48},{64,72... | collective-permute-start | bytes 147464 | tf_op jit(solution)/shard_map/ppermute | solution.py:540
  88.2 0.9 collective-permute-done.7.other_ref
  89.0 0.7 joined_score.1
  89.7 0.0 all-to-all-done.4.value_ref
  89.7 0.8 settled.1
  (6 shorter events, 0.1 us)
Async XLA Ops:
  2.9 14.7 %all-to-all-start = ((f32[8,8,128]{2,1,0:T(8,128)}), f32[8,8,128]{2,1,0:T(8,128)S(1)}, u32[]{:S(2)}, u32[]{:S(2)}) async-start(f32[8,8,128]{2,1,0:T(8,128)} %cell_totals.1), calls=%async_computation | async-start | bytes 65536 | tf_op jit(solution)/shard_map/all_to_all | solution.py:484
  19.7 32.0 %copy-start = (bf16[1024,64]{0,1:T(8,128)(2,1)S(1)}, bf16[1024,64]{0,1:T(8,128)(2,1)}, u32[]{:S(2)}) copy-start(bf16[1024,64]{0,1:T(8,128)(2,1)} %param.18) | copy-start | bytes 393220
  19.7 32.0 %copy-start.1 = (bf16[384,64]{0,1:T(8,128)(2,1)S(1)}, bf16[384,64]{0,1:T(8,128)(2,1)}, u32[]{:S(2)}) copy-start(bf16[384,64]{0,1:T(8,128)(2,1)} %param.19) | copy-start | bytes 147460
  19.7 3.4 %collective-permute-start = (f32[16,48,128]{2,1,0:T(8,128)S(1)}, f32[16,48,128]{2,1,0:T(8,128)S(1)}, u32[]{:S(2)}, u32[]{:S(2)}) collective-permute-start(f32[16,48,128]{2,1,0:T(8,128)S(1)} %get-tuple-element.20), channel_id=1, source_target_pairs={{0,8},{8,0},{16,24},{24,16},{32,40},{40,32},{48,56},{56,48},{64,72... | collective-permute-start | bytes 1179656 | tf_op jit(solution)/shard_map/ppermute | solution.py:523
  54.3 20.1 %all-to-all-start.3 = ((f32[8,16,1024]{2,1,0:T(8,128)}), f32[8,16,1024]{2,1,0:T(8,128)S(1)}, u32[]{:S(2)}, u32[]{:S(2)}) async-start(f32[8,16,1024]{2,1,0:T(8,128)} %get-tuple-element.25), calls=%async_computation.3 | async-start | bytes 1048576 | tf_op jit(solution)/shard_map/all_to_all | solution.py:484
  60.7 1.8 %collective-permute-start.1 = (f32[64,384]{1,0:T(8,128)S(1)}, f32[64,384]{1,0:T(8,128)S(1)}, u32[]{:S(2)}, u32[]{:S(2)}) collective-permute-start(f32[64,384]{1,0:T(8,128)S(1)} %get-tuple-element.27), channel_id=1, source_target_pairs={{0,8},{8,0},{16,24},{24,16},{32,40},{40,32},{48,56},{56,48},{64,72... | collective-permute-start | bytes 294920 | tf_op jit(solution)/shard_map/ppermute | solution.py:530
  62.6 5.3 %collective-permute-start.4 = (f32[64,384]{1,0:T(8,128)S(1)}, f32[64,384]{1,0:T(8,128)S(1)}, u32[]{:S(2)}, u32[]{:S(2)}) collective-permute-start(f32[64,384]{1,0:T(8,128)S(1)} %add.33), channel_id=1, source_target_pairs={{0,192},{8,200},{16,208},{24,216},{32,224},{40,232},{48,240},{56,2... | collective-permute-start | bytes 294920 | tf_op jit(solution)/shard_map/ppermute | solution.py:531
  63.7 5.3 %collective-permute-start.3 = (f32[64,384]{1,0:T(8,128)S(1)}, f32[64,384]{1,0:T(8,128)S(1)}, u32[]{:S(2)}, u32[]{:S(2)}) collective-permute-start(f32[64,384]{1,0:T(8,128)S(1)} %add.33), channel_id=1, source_target_pairs={{0,128},{8,136},{16,144},{24,152},{32,160},{40,168},{48,176},{56,1... | collective-permute-start | bytes 294920 | tf_op jit(solution)/shard_map/ppermute | solution.py:531
  64.7 5.6 %collective-permute-start.2 = (f32[64,384]{1,0:T(8,128)S(1)}, f32[64,384]{1,0:T(8,128)S(1)}, u32[]{:S(2)}, u32[]{:S(2)}) collective-permute-start(f32[64,384]{1,0:T(8,128)S(1)} %add.33), channel_id=1, source_target_pairs={{0,64},{8,72},{16,80},{24,88},{32,96},{40,104},{48,112},{56,120},{... | collective-permute-start | bytes 294920 | tf_op jit(solution)/shard_map/ppermute | solution.py:531
  70.4 10.6 %collective-permute-start.5 = (f32[64,384]{1,0:T(8,128)S(1)}, f32[64,384]{1,0:T(8,128)S(1)}, u32[]{:S(2)}, u32[]{:S(2)}) collective-permute-start(f32[64,384]{1,0:T(8,128)S(1)} %add_add_fusion), channel_id=1, source_target_pairs={{0,16},{8,24},{16,0},{24,8},{32,48},{40,56},{48,32},{56,40},{64,80... | collective-permute-start | bytes 294920 | tf_op jit(solution)/shard_map/ppermute | solution.py:533
  75.3 14.4 %all-to-all-start.4 = ((f32[8,8,1024]{2,1,0:T(8,128)}), f32[8,8,1024]{2,1,0:T(8,128)S(1)}, u32[]{:S(2)}, u32[]{:S(2)}) async-start(f32[8,8,1024]{2,1,0:T(8,128)} %factor_share.1), calls=%async_computation.4 | async-start | bytes 524288 | tf_op jit(solution)/shard_map/all_to_all | solution.py:484
  81.0 4.8 %collective-permute-start.6 = (f32[64,384]{1,0:T(8,128)S(1)}, f32[64,384]{1,0:T(8,128)S(1)}, u32[]{:S(2)}, u32[]{:S(2)}) collective-permute-start(f32[64,384]{1,0:T(8,128)S(1)} %add.37), channel_id=1, source_target_pairs={{0,48},{8,56},{16,32},{24,40},{32,16},{40,24},{48,0},{56,8},{64,11... | collective-permute-start | bytes 294920 | tf_op jit(solution)/shard_map/ppermute | solution.py:538
  85.8 3.2 %collective-permute-start.7 = (f32[32,384]{1,0:T(8,128)S(1)}, f32[32,384]{1,0:T(8,128)S(1)}, u32[]{:S(2)}, u32[]{:S(2)}) collective-permute-start(f32[32,384]{1,0:T(8,128)S(1)} %fusion.1.mine_ref), channel_id=1, source_target_pairs={{0,8},{8,0},{16,24},{24,16},{32,40},{40,32},{48,56},{56,48},{64,72... | collective-permute-start | bytes 147464 | tf_op jit(solution)/shard_map/ppermute | solution.py:540

commit v8 on v7

--- a/solution.py
+++ b/solution.py
@@ -34,14 +34,6 @@
     rest = x - hi.astype(F32)
     mid = rest.astype(BF16)
     return hi, mid, (rest - mid.astype(F32)).astype(BF16)
-
-
-def full(shape):
-    return pl.BlockSpec(shape, lambda c: (0,) * len(shape))
-
-
-def lanes(rows, chunk=CHUNK):
-    return pl.BlockSpec((rows, chunk), lambda c: (0, c))
 
 
 def smem():
@@ -498,9 +490,20 @@
     ]
 
 
-SAME_CORE = [[(4 * x + y) * 2 + core for y in range(4) for x in range(4)] for core in range(2)]
+def around(at, size):
+    return [min((i - at) % size, (at - i) % size) for i in range(size)]
+
+
+def nearest_first(x, y):
+    far_x, far_y = around(x, 4), around(y, 4)
+    chips = [(i, j) for i in range(4) for j in range(4)]
+    return sorted(chips, key=lambda chip: far_x[chip[0]] + far_y[chip[1]])
+
+
+FIRST = (3, 2, 5)
+SAME_CORE = [[(4 * x + y) * 2 + core for x, y in nearest_first(*FIRST[:2])] for core in range(2)]
 CORE_FIRST = [SAME_CORE[0] + SAME_CORE[1]]
-RING = [[3, 4, 2, 5, 1, 6, 0, 7]]
+RING = [sorted(range(8), key=around(FIRST[2], 8).__getitem__)]
 OTHER_CORE = partners(lambda x, y, c: (x, y, 1 - c))
 ALONG_X = [partners(lambda x, y, c, k=k: (x ^ k, y, c)) for k in (1, 2, 3)]
 ALONG_Y = [partners(lambda x, y, c, k=k: (x, y ^ k, c)) for k in (1, 3)]

time: 90.9 us -> 90.1 us (level)
  starting transfers between devices: 32.9 us -> 38.2 us
  waiting for transfers between devices: 14.9 us -> 10.8 us
  blocking collectives: 27.6 us -> 25.6 us
    all_to_all x3, starting transfers between devices: 22.8 us -> 26.8 us  [exchange(): lax.all_to_all(value, axis, split_axis=0, concat_axis=0, tiled=True, axis...]
    all_to_all x3, waiting for transfers between devices: 3.72 us -> 0.5 us  [exchange(): lax.all_to_all(value, axis, split_axis=0, concat_axis=0, tiled=True, axis...]
    all_to_all x2, blocking collectives: 27.6 us -> 25.6 us  [exchange(): lax.all_to_all(value, axis, split_axis=0, concat_axis=0, tiled=True, axis...]
    ppermute x1, starting transfers between devices: 1.16 us -> 2.39 us  [local(): value = value + lax.ppermute(value, 'cell', ALONG_Y[1])]
    ppermute x1, starting transfers between devices: 2.01 us -> 1.04 us  [local(): packed = kept + lax.ppermute(given, 'cell', OTHER_CORE)]
    ppermute x1, waiting for transfers between devices: 3.6 us -> 2.67 us  [local(): value = value + lax.ppermute(value, 'cell', ALONG_Y[1])]
    ppermute x1, starting transfers between devices: 0.37 us -> 1.28 us  [local(): near = lax.ppermute(value, 'cell', ALONG_Y[0])]
where the time goes in v8:
time: 90.1 us; the launch traced here: 89.7 us
  starting transfers between devices  38.2 us (42%)
  blocking collectives  25.6 us (28%)
  Pallas kernels  13.5 us (15%)
  waiting for transfers between devices  10.8 us (12%)
  between operations  1.41 us (2%)
    all_to_all x3, starting transfers between devices, exchange(): lax.all_to_all(value, axis, split_axis=0, concat_axis=0, tiled=True, axis...  26.8 us
    all_to_all x2, blocking collectives, exchange(): lax.all_to_all(value, axis, split_axis=0, concat_axis=0, tiled=True, axis...  25.6 us
    ppermute x3, waiting for transfers between devices, local(): lax.ppermute(value, 'cell', pairs)  4.43 us
    pallas_call x1, Pallas kernels, prepare(): pl.pallas_call(prepare_kernel, in_specs=[smem()] + [hbm()] * len(arrays),...  3.41 us
    ppermute x3, starting transfers between devices, local(): lax.ppermute(value, 'cell', pairs)  3.34 us
    ppermute x1, starting transfers between devices, local(): other = lax.ppermute(mine, 'cell', OTHER_CORE)  2.67 us
    ppermute x1, waiting for transfers between devices, local(): value = value + lax.ppermute(value, 'cell', ALONG_Y[1])  2.67 us
    pallas_call x1, Pallas kernels, update(): pl.pallas_call(update_kernel, in_specs=[smem(), smem()] + [vmem()] * 7, o...  2.59 us
  transfers between devices with their start and end apart: 11, of which 8 were waited for; matrix products, arithmetic and copies ran while one was open for 0% of the time, Pallas kernels for 5%

profile of v8, /device:TPU:1, one launch (start us, length us, event | category | flops | bytes accessed | tf_op | source)
XLA Modules:
  0.0 89.7 jit_solution(6105928816219680370)
XLA Ops:
  0.6 2.3 %cell_totals.1 = f32[8,8,128]{2,1,0:T(8,128)} custom-call(s32[384,1024]{1,0:T(8,128)} %counts_hbm.1), custom_call_target="tpu_custom_call" | custom-call | tf_op jit(solution)/shard_map/cell_totals/pallas_call | solution.py:87
  2.9 10.6 %all-to-all-start = ((f32[8,8,128]{2,1,0:T(8,128)}), f32[8,8,128]{2,1,0:T(8,128)S(1)}, u32[]{:S(2)}, u32[]{:S(2)}) async-start(f32[8,8,128]{2,1,0:T(8,128)} %cell_totals.1), calls=%async_computation | async-start | bytes 65536 | tf_op jit(solution)/shard_map/all_to_all | solution.py:476
  14.1 3.4 %prepare.1 = (f32[384,1024]{1,0:T(8,128)S(1)}, bf16[96,1024]{1,0:T(8,128)(2,1)S(1)}, f32[384,128]{1,0:T(8,128)S(1)}, f32[64,1024]{1,0:T(8,128)S(1)}, f32[64,384]{1,0:T(8,128)S(1)}) custom-call(s32[1]{0:T(128)S(6)} %copy.17.live_ref, s32[384,1024]{1,0:T(8,128)} %counts_hbm.1, s32[1,1024]{1,0:T(1,128)} %bitcast.25, f32[1,1024]{1,0:T(1,128)} %bitcast.26, ...), custom_call_target="tpu_custom_call" | custom-call | tf_op jit(solution)/shard_map/prepare/pallas_call | solution.py:167
  17.5 0.0 all-to-all-done.tot_ref
  17.5 2.1 %gram_sums.1 = (f32[384,1024]{1,0:T(8,128)S(1)}, f32[16,48,128]{2,1,0:T(8,128)S(1)}, f32[16,48,128]{2,1,0:T(8,128)S(1)}) custom-call(s32[1]{0:T(128)S(6)} %copy.17.live_ref, s32[1]{0:T(128)} %bitcast.core_ref, f32[8,8,128]{2,1,0:T(8,128)S(1)} %all-to-all-done.tot_ref, f32[384,1024]{1,0:T(8,128)S(1)} %get-tuple-element.16.rest_ref, ...), custom_call_target="tpu_custom_call" | custom-call | tf_op jit(solution)/shard_map/gram_sums/pallas_call | solution.py:240
  19.6 0.0 copy-start
  19.6 0.0 copy-start.1
  19.6 1.0 %collective-permute-start = (f32[16,48,128]{2,1,0:T(8,128)S(1)}, f32[16,48,128]{2,1,0:T(8,128)S(1)}, u32[]{:S(2)}, u32[]{:S(2)}) collective-permute-start(f32[16,48,128]{2,1,0:T(8,128)S(1)} %get-tuple-element.20), channel_id=1, source_target_pairs={{0,8},{8,0},{16,24},{24,16},{32,40},{40,32},{48,56},{56,48},{64,72... | collective-permute-start | bytes 1179656 | tf_op jit(solution)/shard_map/ppermute | solution.py:526
  20.7 1.3 %collective-permute-done = f32[16,48,128]{2,1,0:T(8,128)S(1)} collective-permute-done((f32[16,48,128]{2,1,0:T(8,128)S(1)}, f32[16,48,128]{2,1,0:T(8,128)S(1)}, u32[]{:S(2)}, u32[]{:S(2)}) %collective-permute-start) | collective-permute-done | bytes 393248 | tf_op jit(solution)/shard_map/ppermute | solution.py:526
  22.0 0.1 add.32
  22.1 13.5 %all_to_all.25.parts_ref = f32[16,48,128]{2,1,0:T(8,128)S(1)} all-to-all(f32[16,48,128]{2,1,0:T(8,128)S(1)} %add.32), channel_id=1, replica_groups={{224,32,160,208,240,16,48,96,144,176,192,0,80,112,128,64},{232,40,168,2..., dimensions={0} | all-to-all | bytes 786432 | tf_op jit(solution)/shard_map/all_to_all | solution.py:476
  35.5 1.0 %solve.1 = f32[32,1,384]{2,1,0:T(1,128)S(1)} custom-call(f32[16,48,128]{2,1,0:T(8,128)S(1)} %all_to_all.25.parts_ref), custom_call_target="tpu_custom_call" | custom-call | tf_op jit(solution)/shard_map/solve/pallas_call | solution.py:304
  36.5 12.1 %all_to_all.26 = f32[32,1,384]{2,1,0:T(1,128)S(1)} all-to-all(f32[32,1,384]{2,1,0:T(1,128)S(1)} %solve.1), channel_id=1, replica_groups={{224,32,160,208,240,16,48,96,144,176,192,0,80,112,128,64,232,40,168,216..., dimensions={0} | all-to-all | bytes 98304 | tf_op jit(solution)/shard_map/all_to_all | solution.py:476
  48.7 0.0 copy-done
  48.7 0.0 copy-done.1
  48.7 2.6 %update.1 = (f32[8,16,1024]{2,1,0:T(8,128)}, f32[64,384]{1,0:T(8,128)S(1)}, f32[64,384]{1,0:T(8,128)S(1)}, f32[32,384]{1,0:T(8,128)}) custom-call(s32[1]{0:T(128)S(6)} %copy.17.live_ref, s32[1]{0:T(128)} %bitcast.core_ref, f32[32,384]{1,0:T(8,128)S(1)} %bitcast.18, f32[384,1024]{1,0:T(8,128)S(1)} %get-tuple-element.21.pred_ref, ...), custom_call_target="tpu_custom_call" | custom-call | tf_op jit(solution)/shard_map/update/pallas_call | solution.py:378
  51.3 7.1 %all-to-all-start.3 = ((f32[8,16,1024]{2,1,0:T(8,128)}), f32[8,16,1024]{2,1,0:T(8,128)S(1)}, u32[]{:S(2)}, u32[]{:S(2)}) async-start(f32[8,16,1024]{2,1,0:T(8,128)} %get-tuple-element.25), calls=%async_computation.3 | async-start | bytes 1048576 | tf_op jit(solution)/shard_map/all_to_all | solution.py:476
  58.4 0.7 collective-permute-start.1
  59.1 0.9 %collective-permute-done.1 = f32[64,384]{1,0:T(8,128)S(1)} collective-permute-done((f32[64,384]{1,0:T(8,128)S(1)}, f32[64,384]{1,0:T(8,128)S(1)}, u32[]{:S(2)}, u32[]{:S(2)}) %collective-permute-start.1) | collective-permute-done | bytes 98336 | tf_op jit(solution)/shard_map/ppermute | solution.py:533
  60.0 2.0 %collective-permute-start.4 = (f32[64,384]{1,0:T(8,128)S(1)}, f32[64,384]{1,0:T(8,128)S(1)}, u32[]{:S(2)}, u32[]{:S(2)}) collective-permute-start(f32[64,384]{1,0:T(8,128)S(1)} %add.33), channel_id=1, source_target_pairs={{0,192},{8,200},{16,208},{24,216},{32,224},{40,232},{48,240},{56,2... | collective-permute-start | bytes 294920 | tf_op jit(solution)/shard_map/ppermute | solution.py:534
  62.0 0.1 collective-permute-start.3
  62.1 1.2 %collective-permute-start.2 = (f32[64,384]{1,0:T(8,128)S(1)}, f32[64,384]{1,0:T(8,128)S(1)}, u32[]{:S(2)}, u32[]{:S(2)}) collective-permute-start(f32[64,384]{1,0:T(8,128)S(1)} %add.33), channel_id=1, source_target_pairs={{0,64},{8,72},{16,80},{24,88},{32,96},{40,104},{48,112},{56,120},{... | collective-permute-start | bytes 294920 | tf_op jit(solution)/shard_map/ppermute | solution.py:534
  63.4 2.0 %collective-permute-done.4 = f32[64,384]{1,0:T(8,128)S(1)} collective-permute-done((f32[64,384]{1,0:T(8,128)S(1)}, f32[64,384]{1,0:T(8,128)S(1)}, u32[]{:S(2)}, u32[]{:S(2)}) %collective-permute-start.4) | collective-permute-done | bytes 98336 | tf_op jit(solution)/shard_map/ppermute | solution.py:534
  65.4 1.9 %collective-permute-done.3 = f32[64,384]{1,0:T(8,128)S(1)} collective-permute-done((f32[64,384]{1,0:T(8,128)S(1)}, f32[64,384]{1,0:T(8,128)S(1)}, u32[]{:S(2)}, u32[]{:S(2)}) %collective-permute-start.3) | collective-permute-done | bytes 98336 | tf_op jit(solution)/shard_map/ppermute | solution.py:534
  67.3 0.5 collective-permute-done.2
  67.8 1.3 %collective-permute-start.5 = (f32[64,384]{1,0:T(8,128)S(1)}, f32[64,384]{1,0:T(8,128)S(1)}, u32[]{:S(2)}, u32[]{:S(2)}) collective-permute-start(f32[64,384]{1,0:T(8,128)S(1)} %add_add_fusion), channel_id=1, source_target_pairs={{0,16},{8,24},{16,0},{24,8},{32,48},{40,56},{48,32},{56,40},{64,80... | collective-permute-start | bytes 294920 | tf_op jit(solution)/shard_map/ppermute | solution.py:536
  69.1 0.5 all-to-all-done.3.parts_ref
  69.6 0.8 factor_share.1
  70.4 9.1 %all-to-all-start.4 = ((f32[8,8,1024]{2,1,0:T(8,128)}), f32[8,8,1024]{2,1,0:T(8,128)S(1)}, u32[]{:S(2)}, u32[]{:S(2)}) async-start(f32[8,8,1024]{2,1,0:T(8,128)} %factor_share.1), calls=%async_computation.4 | async-start | bytes 524288 | tf_op jit(solution)/shard_map/all_to_all | solution.py:476
  79.6 0.0 collective-permute-done.5
  79.6 2.4 %collective-permute-start.6 = (f32[64,384]{1,0:T(8,128)S(1)}, f32[64,384]{1,0:T(8,128)S(1)}, u32[]{:S(2)}, u32[]{:S(2)}) collective-permute-start(f32[64,384]{1,0:T(8,128)S(1)} %add.37), channel_id=1, source_target_pairs={{0,48},{8,56},{16,32},{24,40},{32,16},{40,24},{48,0},{56,8},{64,11... | collective-permute-start | bytes 294920 | tf_op jit(solution)/shard_map/ppermute | solution.py:541
  82.0 2.7 %collective-permute-done.6 = f32[64,384]{1,0:T(8,128)S(1)} collective-permute-done((f32[64,384]{1,0:T(8,128)S(1)}, f32[64,384]{1,0:T(8,128)S(1)}, u32[]{:S(2)}, u32[]{:S(2)}) %collective-permute-start.6) | collective-permute-done | bytes 98336 | tf_op jit(solution)/shard_map/ppermute | solution.py:541
  84.7 2.7 %collective-permute-start.7 = (f32[32,384]{1,0:T(8,128)S(1)}, f32[32,384]{1,0:T(8,128)S(1)}, u32[]{:S(2)}, u32[]{:S(2)}) collective-permute-start(f32[32,384]{1,0:T(8,128)S(1)} %fusion.1.mine_ref), channel_id=1, source_target_pairs={{0,8},{8,0},{16,24},{24,16},{32,40},{40,32},{48,56},{56,48},{64,72... | collective-permute-start | bytes 147464 | tf_op jit(solution)/shard_map/ppermute | solution.py:543
  87.4 0.9 collective-permute-done.7.other_ref
  88.2 0.7 joined_score.1
  88.9 0.0 all-to-all-done.4.value_ref
  88.9 0.8 settled.1
  (6 shorter events, 0.1 us)
Async XLA Ops:
  2.9 14.7 %all-to-all-start = ((f32[8,8,128]{2,1,0:T(8,128)}), f32[8,8,128]{2,1,0:T(8,128)S(1)}, u32[]{:S(2)}, u32[]{:S(2)}) async-start(f32[8,8,128]{2,1,0:T(8,128)} %cell_totals.1), calls=%async_computation | async-start | bytes 65536 | tf_op jit(solution)/shard_map/all_to_all | solution.py:476
  19.6 29.1 %copy-start = (bf16[1024,64]{0,1:T(8,128)(2,1)S(1)}, bf16[1024,64]{0,1:T(8,128)(2,1)}, u32[]{:S(2)}) copy-start(bf16[1024,64]{0,1:T(8,128)(2,1)} %param.18) | copy-start | bytes 393220
  19.6 29.1 %copy-start.1 = (bf16[384,64]{0,1:T(8,128)(2,1)S(1)}, bf16[384,64]{0,1:T(8,128)(2,1)}, u32[]{:S(2)}) copy-start(bf16[384,64]{0,1:T(8,128)(2,1)} %param.19) | copy-start | bytes 147460
  19.6 2.4 %collective-permute-start = (f32[16,48,128]{2,1,0:T(8,128)S(1)}, f32[16,48,128]{2,1,0:T(8,128)S(1)}, u32[]{:S(2)}, u32[]{:S(2)}) collective-permute-start(f32[16,48,128]{2,1,0:T(8,128)S(1)} %get-tuple-element.20), channel_id=1, source_target_pairs={{0,8},{8,0},{16,24},{24,16},{32,40},{40,32},{48,56},{56,48},{64,72... | collective-permute-start | bytes 1179656 | tf_op jit(solution)/shard_map/ppermute | solution.py:526
  51.3 18.3 %all-to-all-start.3 = ((f32[8,16,1024]{2,1,0:T(8,128)}), f32[8,16,1024]{2,1,0:T(8,128)S(1)}, u32[]{:S(2)}, u32[]{:S(2)}) async-start(f32[8,16,1024]{2,1,0:T(8,128)} %get-tuple-element.25), calls=%async_computation.3 | async-start | bytes 1048576 | tf_op jit(solution)/shard_map/all_to_all | solution.py:476
  58.4 1.6 %collective-permute-start.1 = (f32[64,384]{1,0:T(8,128)S(1)}, f32[64,384]{1,0:T(8,128)S(1)}, u32[]{:S(2)}, u32[]{:S(2)}) collective-permute-start(f32[64,384]{1,0:T(8,128)S(1)} %get-tuple-element.27), channel_id=1, source_target_pairs={{0,8},{8,0},{16,24},{24,16},{32,40},{40,32},{48,56},{56,48},{64,72... | collective-permute-start | bytes 294920 | tf_op jit(solution)/shard_map/ppermute | solution.py:533
  60.0 5.3 %collective-permute-start.4 = (f32[64,384]{1,0:T(8,128)S(1)}, f32[64,384]{1,0:T(8,128)S(1)}, u32[]{:S(2)}, u32[]{:S(2)}) collective-permute-start(f32[64,384]{1,0:T(8,128)S(1)} %add.33), channel_id=1, source_target_pairs={{0,192},{8,200},{16,208},{24,216},{32,224},{40,232},{48,240},{56,2... | collective-permute-start | bytes 294920 | tf_op jit(solution)/shard_map/ppermute | solution.py:534
  62.0 5.3 %collective-permute-start.3 = (f32[64,384]{1,0:T(8,128)S(1)}, f32[64,384]{1,0:T(8,128)S(1)}, u32[]{:S(2)}, u32[]{:S(2)}) collective-permute-start(f32[64,384]{1,0:T(8,128)S(1)} %add.33), channel_id=1, source_target_pairs={{0,128},{8,136},{16,144},{24,152},{32,160},{40,168},{48,176},{56,1... | collective-permute-start | bytes 294920 | tf_op jit(solution)/shard_map/ppermute | solution.py:534
  62.1 5.7 %collective-permute-start.2 = (f32[64,384]{1,0:T(8,128)S(1)}, f32[64,384]{1,0:T(8,128)S(1)}, u32[]{:S(2)}, u32[]{:S(2)}) collective-permute-start(f32[64,384]{1,0:T(8,128)S(1)} %add.33), channel_id=1, source_target_pairs={{0,64},{8,72},{16,80},{24,88},{32,96},{40,104},{48,112},{56,120},{... | collective-permute-start | bytes 294920 | tf_op jit(solution)/shard_map/ppermute | solution.py:534
  67.8 11.7 %collective-permute-start.5 = (f32[64,384]{1,0:T(8,128)S(1)}, f32[64,384]{1,0:T(8,128)S(1)}, u32[]{:S(2)}, u32[]{:S(2)}) collective-permute-start(f32[64,384]{1,0:T(8,128)S(1)} %add_add_fusion), channel_id=1, source_target_pairs={{0,16},{8,24},{16,0},{24,8},{32,48},{40,56},{48,32},{56,40},{64,80... | collective-permute-start | bytes 294920 | tf_op jit(solution)/shard_map/ppermute | solution.py:536
  70.4 18.5 %all-to-all-start.4 = ((f32[8,8,1024]{2,1,0:T(8,128)}), f32[8,8,1024]{2,1,0:T(8,128)S(1)}, u32[]{:S(2)}, u32[]{:S(2)}) async-start(f32[8,8,1024]{2,1,0:T(8,128)} %factor_share.1), calls=%async_computation.4 | async-start | bytes 524288 | tf_op jit(solution)/shard_map/all_to_all | solution.py:476
  79.6 5.1 %collective-permute-start.6 = (f32[64,384]{1,0:T(8,128)S(1)}, f32[64,384]{1,0:T(8,128)S(1)}, u32[]{:S(2)}, u32[]{:S(2)}) collective-permute-start(f32[64,384]{1,0:T(8,128)S(1)} %add.37), channel_id=1, source_target_pairs={{0,48},{8,56},{16,32},{24,40},{32,16},{40,24},{48,0},{56,8},{64,11... | collective-permute-start | bytes 294920 | tf_op jit(solution)/shard_map/ppermute | solution.py:541
  84.7 3.6 %collective-permute-start.7 = (f32[32,384]{1,0:T(8,128)S(1)}, f32[32,384]{1,0:T(8,128)S(1)}, u32[]{:S(2)}, u32[]{:S(2)}) collective-permute-start(f32[32,384]{1,0:T(8,128)S(1)} %fusion.1.mine_ref), channel_id=1, source_target_pairs={{0,8},{8,0},{16,24},{24,16},{32,40},{40,32},{48,56},{56,48},{64,72... | collective-permute-start | bytes 147464 | tf_op jit(solution)/shard_map/ppermute | solution.py:543

commit v9 on v8

--- a/solution.py
+++ b/solution.py
@@ -506,7 +506,7 @@
 RING = [sorted(range(8), key=around(FIRST[2], 8).__getitem__)]
 OTHER_CORE = partners(lambda x, y, c: (x, y, 1 - c))
 ALONG_X = [partners(lambda x, y, c, k=k: (x ^ k, y, c)) for k in (1, 2, 3)]
-ALONG_Y = [partners(lambda x, y, c, k=k: (x, y ^ k, c)) for k in (1, 3)]
+ALONG_Y = [partners(lambda x, y, c, k=k: (x, y ^ k, c)) for k in (1, 2, 3)]
 
 
 def local(
@@ -531,14 +531,10 @@
     arrived = exchange(pieces, "gene", RING)
 
     value = kept + lax.ppermute(given, "cell", OTHER_CORE)
-    near, across, beside = (lax.ppermute(value, "cell", pairs) for pairs in ALONG_X)
-    value = (value + near) + (across + beside)
-    near = lax.ppermute(value, "cell", ALONG_Y[0])
-    shared = factor_share(arrived)
-    gathered = settled(exchange(shared, "gene", RING))
-    near, _ = lax.optimization_barrier((near, shared))
-    value = value + near
-    value = value + lax.ppermute(value, "cell", ALONG_Y[1])
+    for moves in (ALONG_X, ALONG_Y):
+        near, across, beside = (lax.ppermute(value, "cell", pairs) for pairs in moves)
+        value = (value + near) + (across + beside)
+    gathered = settled(exchange(factor_share(arrived), "gene", RING))
     mine = value[:32] / jnp.sqrt(value[32:] + 1.0)
     other = lax.ppermute(mine, "cell", OTHER_CORE)
     score = joined_score(core, mine, other)

time: 90.1 us -> 87.4 us (0.970)
  the two profiles are of different devices: /device:TPU:1 before, /device:TPU:24 now
where the time goes in v9:
time: 87.4 us; the launch traced here: 87 us
  starting transfers between devices  33.2 us (38%)
  blocking collectives  25.2 us (29%)
  Pallas kernels  13.5 us (15%)
  waiting for transfers between devices  13.5 us (15%)
  between operations  1.43 us (2%)
    all_to_all x2, blocking collectives, exchange(): lax.all_to_all(value, axis, split_axis=0, concat_axis=0, tiled=True, axis...  25.2 us
    all_to_all x3, starting transfers between devices, exchange(): lax.all_to_all(value, axis, split_axis=0, concat_axis=0, tiled=True, axis...  24.7 us
    ppermute x6, starting transfers between devices, local(): lax.ppermute(value, 'cell', pairs)  8.36 us
    ppermute x6, waiting for transfers between devices, local(): lax.ppermute(value, 'cell', pairs)  5.35 us
    all_to_all x3, waiting for transfers between devices, exchange(): lax.all_to_all(value, axis, split_axis=0, concat_axis=0, tiled=True, axis...  3.97 us
    pallas_call x1, Pallas kernels, prepare(): pl.pallas_call(prepare_kernel, in_specs=[smem()] + [hbm()] * len(arrays),...  3.41 us
    pallas_call x1, Pallas kernels, update(): pl.pallas_call(update_kernel, in_specs=[smem(), smem()] + [vmem()] * 7, o...  2.58 us
    pallas_call x1, Pallas kernels, cell_totals(): pl.pallas_call(totals_kernel, in_specs=[hbm()], out_specs=hbm(), out_shap...  2.25 us
  transfers between devices with their start and end apart: 12, of which 6 were waited for; matrix products, arithmetic and copies ran while one was open for 0% of the time, Pallas kernels for 6%

profile of v9, /device:TPU:24, one launch (start us, length us, event | category | flops | bytes accessed | tf_op | source)
XLA Modules:
  0.0 87.0 jit_solution(2921203596728503052)
XLA Ops:
  0.6 2.3 %cell_totals.1 = f32[8,8,128]{2,1,0:T(8,128)} custom-call(s32[384,1024]{1,0:T(8,128)} %counts_hbm.1), custom_call_target="tpu_custom_call" | custom-call | tf_op jit(solution)/shard_map/cell_totals/pallas_call | solution.py:87
  2.9 10.0 %all-to-all-start = ((f32[8,8,128]{2,1,0:T(8,128)}), f32[8,8,128]{2,1,0:T(8,128)S(1)}, u32[]{:S(2)}, u32[]{:S(2)}) async-start(f32[8,8,128]{2,1,0:T(8,128)} %cell_totals.1), calls=%async_computation | async-start | bytes 65536 | tf_op jit(solution)/shard_map/all_to_all | solution.py:476
  13.6 3.4 %prepare.1 = (f32[384,1024]{1,0:T(8,128)S(1)}, bf16[96,1024]{1,0:T(8,128)(2,1)S(1)}, f32[384,128]{1,0:T(8,128)S(1)}, f32[64,1024]{1,0:T(8,128)S(1)}, f32[64,384]{1,0:T(8,128)S(1)}) custom-call(s32[1]{0:T(128)S(6)} %copy.17.live_ref, s32[384,1024]{1,0:T(8,128)} %counts_hbm.1, s32[1,1024]{1,0:T(1,128)} %bitcast.25, f32[1,1024]{1,0:T(1,128)} %bitcast.26, ...), custom_call_target="tpu_custom_call" | custom-call | tf_op jit(solution)/shard_map/prepare/pallas_call | solution.py:167
  17.0 0.0 all-to-all-done.tot_ref
  17.0 2.1 %gram_sums.1 = (f32[384,1024]{1,0:T(8,128)S(1)}, f32[16,48,128]{2,1,0:T(8,128)S(1)}, f32[16,48,128]{2,1,0:T(8,128)S(1)}) custom-call(s32[1]{0:T(128)S(6)} %copy.17.live_ref, s32[1]{0:T(128)} %bitcast.core_ref, f32[8,8,128]{2,1,0:T(8,128)S(1)} %all-to-all-done.tot_ref, f32[384,1024]{1,0:T(8,128)S(1)} %get-tuple-element.15.rest_ref, ...), custom_call_target="tpu_custom_call" | custom-call | tf_op jit(solution)/shard_map/gram_sums/pallas_call | solution.py:240
  19.1 0.0 copy-start
  19.1 0.0 copy-start.1
  19.1 0.1 collective-permute-start
  19.2 1.7 %collective-permute-done = f32[16,48,128]{2,1,0:T(8,128)S(1)} collective-permute-done((f32[16,48,128]{2,1,0:T(8,128)S(1)}, f32[16,48,128]{2,1,0:T(8,128)S(1)}, u32[]{:S(2)}, u32[]{:S(2)}) %collective-permute-start) | collective-permute-done | bytes 393248 | tf_op jit(solution)/shard_map/ppermute | solution.py:526
  20.9 0.1 add.35
  21.0 13.6 %all_to_all.25.parts_ref = f32[16,48,128]{2,1,0:T(8,128)S(1)} all-to-all(f32[16,48,128]{2,1,0:T(8,128)S(1)} %add.35), channel_id=1, replica_groups={{224,32,160,208,240,16,48,96,144,176,192,0,80,112,128,64},{232,40,168,2..., dimensions={0} | all-to-all | bytes 786432 | tf_op jit(solution)/shard_map/all_to_all | solution.py:476
  34.5 1.0 %solve.1 = f32[32,1,384]{2,1,0:T(1,128)S(1)} custom-call(f32[16,48,128]{2,1,0:T(8,128)S(1)} %all_to_all.25.parts_ref), custom_call_target="tpu_custom_call" | custom-call | tf_op jit(solution)/shard_map/solve/pallas_call | solution.py:304
  35.5 11.6 %all_to_all.26 = f32[32,1,384]{2,1,0:T(1,128)S(1)} all-to-all(f32[32,1,384]{2,1,0:T(1,128)S(1)} %solve.1), channel_id=1, replica_groups={{224,32,160,208,240,16,48,96,144,176,192,0,80,112,128,64,232,40,168,216..., dimensions={0} | all-to-all | bytes 98304 | tf_op jit(solution)/shard_map/all_to_all | solution.py:476
  47.1 0.0 copy-done
  47.1 0.0 copy-done.1
  47.1 2.6 %update.1 = (f32[8,16,1024]{2,1,0:T(8,128)}, f32[64,384]{1,0:T(8,128)S(1)}, f32[64,384]{1,0:T(8,128)S(1)}, f32[32,384]{1,0:T(8,128)}) custom-call(s32[1]{0:T(128)S(6)} %copy.17.live_ref, s32[1]{0:T(128)} %bitcast.core_ref, f32[32,384]{1,0:T(8,128)S(1)} %bitcast.18, f32[384,1024]{1,0:T(8,128)S(1)} %get-tuple-element.20.pred_ref, ...), custom_call_target="tpu_custom_call" | custom-call | tf_op jit(solution)/shard_map/update/pallas_call | solution.py:378
  49.7 7.4 %all-to-all-start.3 = ((f32[8,16,1024]{2,1,0:T(8,128)}), f32[8,16,1024]{2,1,0:T(8,128)S(1)}, u32[]{:S(2)}, u32[]{:S(2)}) async-start(f32[8,16,1024]{2,1,0:T(8,128)} %get-tuple-element.24), calls=%async_computation.3 | async-start | bytes 1048576 | tf_op jit(solution)/shard_map/all_to_all | solution.py:476
  57.1 0.0 collective-permute-start.1
  57.1 1.3 %collective-permute-done.1 = f32[64,384]{1,0:T(8,128)S(1)} collective-permute-done((f32[64,384]{1,0:T(8,128)S(1)}, f32[64,384]{1,0:T(8,128)S(1)}, u32[]{:S(2)}, u32[]{:S(2)}) %collective-permute-start.1) | collective-permute-done | bytes 98336 | tf_op jit(solution)/shard_map/ppermute | solution.py:533
  58.4 2.4 %collective-permute-start.4 = (f32[64,384]{1,0:T(8,128)S(1)}, f32[64,384]{1,0:T(8,128)S(1)}, u32[]{:S(2)}, u32[]{:S(2)}) collective-permute-start(f32[64,384]{1,0:T(8,128)S(1)} %add.36), channel_id=1, source_target_pairs={{0,192},{8,200},{16,208},{24,216},{32,224},{40,232},{48,240},{56,2... | collective-permute-start | bytes 294920 | tf_op jit(solution)/shard_map/ppermute | solution.py:535
  60.8 0.5 collective-permute-start.3
  61.3 1.3 %collective-permute-start.2 = (f32[64,384]{1,0:T(8,128)S(1)}, f32[64,384]{1,0:T(8,128)S(1)}, u32[]{:S(2)}, u32[]{:S(2)}) collective-permute-start(f32[64,384]{1,0:T(8,128)S(1)} %add.36), channel_id=1, source_target_pairs={{0,64},{8,72},{16,80},{24,88},{32,96},{40,104},{48,112},{56,120},{... | collective-permute-start | bytes 294920 | tf_op jit(solution)/shard_map/ppermute | solution.py:535
  62.6 2.6 %collective-permute-done.4 = f32[64,384]{1,0:T(8,128)S(1)} collective-permute-done((f32[64,384]{1,0:T(8,128)S(1)}, f32[64,384]{1,0:T(8,128)S(1)}, u32[]{:S(2)}, u32[]{:S(2)}) %collective-permute-start.4) | collective-permute-done | bytes 98336 | tf_op jit(solution)/shard_map/ppermute | solution.py:535
  65.2 2.8 %collective-permute-done.3 = f32[64,384]{1,0:T(8,128)S(1)} collective-permute-done((f32[64,384]{1,0:T(8,128)S(1)}, f32[64,384]{1,0:T(8,128)S(1)}, u32[]{:S(2)}, u32[]{:S(2)}) %collective-permute-start.3) | collective-permute-done | bytes 98336 | tf_op jit(solution)/shard_map/ppermute | solution.py:535
  67.9 0.0 collective-permute-done.2
  68.0 0.6 collective-permute-start.7
  68.6 2.2 %collective-permute-start.6 = (f32[64,384]{1,0:T(8,128)S(1)}, f32[64,384]{1,0:T(8,128)S(1)}, u32[]{:S(2)}, u32[]{:S(2)}) collective-permute-start(f32[64,384]{1,0:T(8,128)S(1)} %add_add_fusion.1), channel_id=1, source_target_pairs={{0,32},{8,40},{16,48},{24,56},{32,0},{40,8},{48,16},{56,24},{64,96... | collective-permute-start | bytes 294920 | tf_op jit(solution)/shard_map/ppermute | solution.py:535
  70.8 1.3 %collective-permute-start.5 = (f32[64,384]{1,0:T(8,128)S(1)}, f32[64,384]{1,0:T(8,128)S(1)}, u32[]{:S(2)}, u32[]{:S(2)}) collective-permute-start(f32[64,384]{1,0:T(8,128)S(1)} %add_add_fusion.1), channel_id=1, source_target_pairs={{0,16},{8,24},{16,0},{24,8},{32,48},{40,56},{48,32},{56,40},{64,80... | collective-permute-start | bytes 294920 | tf_op jit(solution)/shard_map/ppermute | solution.py:535
  72.1 0.0 all-to-all-done.3.parts_ref
  72.1 0.8 factor_share.1
  72.9 7.2 %all-to-all-start.4 = ((f32[8,8,1024]{2,1,0:T(8,128)}), f32[8,8,1024]{2,1,0:T(8,128)S(1)}, u32[]{:S(2)}, u32[]{:S(2)}) async-start(f32[8,8,1024]{2,1,0:T(8,128)} %factor_share.1), calls=%async_computation.4 | async-start | bytes 524288 | tf_op jit(solution)/shard_map/all_to_all | solution.py:476
  80.2 0.0 collective-permute-done.7
  80.2 0.0 collective-permute-done.6
  80.2 0.0 collective-permute-done.5
  80.3 0.1 collective-permute-start.8
  80.4 1.2 %collective-permute-done.8.other_ref = f32[32,384]{1,0:T(8,128)S(1)} collective-permute-done((f32[32,384]{1,0:T(8,128)S(1)}, f32[32,384]{1,0:T(8,128)S(1)}, u32[]{:S(2)}, u32[]{:S(2)}) %collective-permute-start.8) | collective-permute-done | bytes 49184 | tf_op jit(solution)/shard_map/ppermute | solution.py:539
  81.6 0.7 joined_score.1
  82.2 4.0 %all-to-all-done.4.value_ref = f32[8,8,1024]{2,1,0:T(8,128)S(1)} async-done(((f32[8,8,1024]{2,1,0:T(8,128)}), f32[8,8,1024]{2,1,0:T(8,128)S(1)}, u32[]{:S(2)}, u32[]{:S(2)}) %all-to-all-start.4) | async-done | bytes 262176 | tf_op jit(solution)/shard_map/all_to_all | solution.py:476
  86.2 0.8 settled.1
  (5 shorter events, 0.1 us)
Async XLA Ops:
  2.9 14.1 %all-to-all-start = ((f32[8,8,128]{2,1,0:T(8,128)}), f32[8,8,128]{2,1,0:T(8,128)S(1)}, u32[]{:S(2)}, u32[]{:S(2)}) async-start(f32[8,8,128]{2,1,0:T(8,128)} %cell_totals.1), calls=%async_computation | async-start | bytes 65536 | tf_op jit(solution)/shard_map/all_to_all | solution.py:476
  19.1 28.0 %copy-start = (bf16[1024,64]{0,1:T(8,128)(2,1)S(1)}, bf16[1024,64]{0,1:T(8,128)(2,1)}, u32[]{:S(2)}) copy-start(bf16[1024,64]{0,1:T(8,128)(2,1)} %param.18) | copy-start | bytes 393220
  19.1 28.0 %copy-start.1 = (bf16[384,64]{0,1:T(8,128)(2,1)S(1)}, bf16[384,64]{0,1:T(8,128)(2,1)}, u32[]{:S(2)}) copy-start(bf16[384,64]{0,1:T(8,128)(2,1)} %param.19) | copy-start | bytes 147460
  19.1 1.8 %collective-permute-start = (f32[16,48,128]{2,1,0:T(8,128)S(1)}, f32[16,48,128]{2,1,0:T(8,128)S(1)}, u32[]{:S(2)}, u32[]{:S(2)}) collective-permute-start(f32[16,48,128]{2,1,0:T(8,128)S(1)} %get-tuple-element.19), channel_id=1, source_target_pairs={{0,8},{8,0},{16,24},{24,16},{32,40},{40,32},{48,56},{56,48},{64,72... | collective-permute-start | bytes 1179656 | tf_op jit(solution)/shard_map/ppermute | solution.py:526
  49.7 22.4 %all-to-all-start.3 = ((f32[8,16,1024]{2,1,0:T(8,128)}), f32[8,16,1024]{2,1,0:T(8,128)S(1)}, u32[]{:S(2)}, u32[]{:S(2)}) async-start(f32[8,16,1024]{2,1,0:T(8,128)} %get-tuple-element.24), calls=%async_computation.3 | async-start | bytes 1048576 | tf_op jit(solution)/shard_map/all_to_all | solution.py:476
  57.1 1.3 %collective-permute-start.1 = (f32[64,384]{1,0:T(8,128)S(1)}, f32[64,384]{1,0:T(8,128)S(1)}, u32[]{:S(2)}, u32[]{:S(2)}) collective-permute-start(f32[64,384]{1,0:T(8,128)S(1)} %get-tuple-element.26), channel_id=1, source_target_pairs={{0,8},{8,0},{16,24},{24,16},{32,40},{40,32},{48,56},{56,48},{64,72... | collective-permute-start | bytes 294920 | tf_op jit(solution)/shard_map/ppermute | solution.py:533
  58.4 6.8 %collective-permute-start.4 = (f32[64,384]{1,0:T(8,128)S(1)}, f32[64,384]{1,0:T(8,128)S(1)}, u32[]{:S(2)}, u32[]{:S(2)}) collective-permute-start(f32[64,384]{1,0:T(8,128)S(1)} %add.36), channel_id=1, source_target_pairs={{0,192},{8,200},{16,208},{24,216},{32,224},{40,232},{48,240},{56,2... | collective-permute-start | bytes 294920 | tf_op jit(solution)/shard_map/ppermute | solution.py:535
  60.8 7.1 %collective-permute-start.3 = (f32[64,384]{1,0:T(8,128)S(1)}, f32[64,384]{1,0:T(8,128)S(1)}, u32[]{:S(2)}, u32[]{:S(2)}) collective-permute-start(f32[64,384]{1,0:T(8,128)S(1)} %add.36), channel_id=1, source_target_pairs={{0,128},{8,136},{16,144},{24,152},{32,160},{40,168},{48,176},{56,1... | collective-permute-start | bytes 294920 | tf_op jit(solution)/shard_map/ppermute | solution.py:535
  61.3 6.7 %collective-permute-start.2 = (f32[64,384]{1,0:T(8,128)S(1)}, f32[64,384]{1,0:T(8,128)S(1)}, u32[]{:S(2)}, u32[]{:S(2)}) collective-permute-start(f32[64,384]{1,0:T(8,128)S(1)} %add.36), channel_id=1, source_target_pairs={{0,64},{8,72},{16,80},{24,88},{32,96},{40,104},{48,112},{56,120},{... | collective-permute-start | bytes 294920 | tf_op jit(solution)/shard_map/ppermute | solution.py:535
  68.0 12.2 %collective-permute-start.7 = (f32[64,384]{1,0:T(8,128)S(1)}, f32[64,384]{1,0:T(8,128)S(1)}, u32[]{:S(2)}, u32[]{:S(2)}) collective-permute-start(f32[64,384]{1,0:T(8,128)S(1)} %add_add_fusion.1), channel_id=1, source_target_pairs={{0,48},{8,56},{16,32},{24,40},{32,16},{40,24},{48,0},{56,8},{64,11... | collective-permute-start | bytes 294920 | tf_op jit(solution)/shard_map/ppermute | solution.py:535
  68.6 11.6 %collective-permute-start.6 = (f32[64,384]{1,0:T(8,128)S(1)}, f32[64,384]{1,0:T(8,128)S(1)}, u32[]{:S(2)}, u32[]{:S(2)}) collective-permute-start(f32[64,384]{1,0:T(8,128)S(1)} %add_add_fusion.1), channel_id=1, source_target_pairs={{0,32},{8,40},{16,48},{24,56},{32,0},{40,8},{48,16},{56,24},{64,96... | collective-permute-start | bytes 294920 | tf_op jit(solution)/shard_map/ppermute | solution.py:535
  70.8 9.4 %collective-permute-start.5 = (f32[64,384]{1,0:T(8,128)S(1)}, f32[64,384]{1,0:T(8,128)S(1)}, u32[]{:S(2)}, u32[]{:S(2)}) collective-permute-start(f32[64,384]{1,0:T(8,128)S(1)} %add_add_fusion.1), channel_id=1, source_target_pairs={{0,16},{8,24},{16,0},{24,8},{32,48},{40,56},{48,32},{56,40},{64,80... | collective-permute-start | bytes 294920 | tf_op jit(solution)/shard_map/ppermute | solution.py:535
  72.9 13.2 %all-to-all-start.4 = ((f32[8,8,1024]{2,1,0:T(8,128)}), f32[8,8,1024]{2,1,0:T(8,128)S(1)}, u32[]{:S(2)}, u32[]{:S(2)}) async-start(f32[8,8,1024]{2,1,0:T(8,128)} %factor_share.1), calls=%async_computation.4 | async-start | bytes 524288 | tf_op jit(solution)/shard_map/all_to_all | solution.py:476
  80.3 1.3 %collective-permute-start.8 = (f32[32,384]{1,0:T(8,128)S(1)}, f32[32,384]{1,0:T(8,128)S(1)}, u32[]{:S(2)}, u32[]{:S(2)}) collective-permute-start(f32[32,384]{1,0:T(8,128)S(1)} %fusion.1.mine_ref), channel_id=1, source_target_pairs={{0,8},{8,0},{16,24},{24,16},{32,40},{40,32},{48,56},{56,48},{64,72... | collective-permute-start | bytes 147464 | tf_op jit(solution)/shard_map/ppermute | solution.py:539

commit v10 on v9

--- a/solution.py
+++ b/solution.py
@@ -503,7 +503,7 @@
 FIRST = (3, 2, 5)
 SAME_CORE = [[(4 * x + y) * 2 + core for x, y in nearest_first(*FIRST[:2])] for core in range(2)]
 CORE_FIRST = [SAME_CORE[0] + SAME_CORE[1]]
-RING = [sorted(range(8), key=around(FIRST[2], 8).__getitem__)]
+RING = [[(FIRST[2] + step) % 8 for step in (0, 1, -1, 2, -2, 3, -3, 4)]]
 OTHER_CORE = partners(lambda x, y, c: (x, y, 1 - c))
 ALONG_X = [partners(lambda x, y, c, k=k: (x ^ k, y, c)) for k in (1, 2, 3)]
 ALONG_Y = [partners(lambda x, y, c, k=k: (x, y ^ k, c)) for k in (1, 2, 3)]

time: 87.4 us -> 87.3 us (level)
  the two profiles are of different devices: /device:TPU:24 before, /device:TPU:8 now
where the time goes in v10:
time: 87.3 us; the launch traced here: 86.9 us
  starting transfers between devices  33.1 us (38%)
  blocking collectives  25.5 us (29%)
  Pallas kernels  13.5 us (15%)
  waiting for transfers between devices  13.2 us (15%)
  between operations  1.43 us (2%)
    all_to_all x2, blocking collectives, exchange(): lax.all_to_all(value, axis, split_axis=0, concat_axis=0, tiled=True, axis...  25.5 us
    all_to_all x3, starting transfers between devices, exchange(): lax.all_to_all(value, axis, split_axis=0, concat_axis=0, tiled=True, axis...  24.6 us
    ppermute x6, starting transfers between devices, local(): lax.ppermute(value, 'cell', pairs)  8.36 us
    ppermute x6, waiting for transfers between devices, local(): lax.ppermute(value, 'cell', pairs)  5.11 us
    all_to_all x3, waiting for transfers between devices, exchange(): lax.all_to_all(value, axis, split_axis=0, concat_axis=0, tiled=True, axis...  3.82 us
    pallas_call x1, Pallas kernels, prepare(): pl.pallas_call(prepare_kernel, in_specs=[smem()] + [hbm()] * len(arrays),...  3.4 us
    pallas_call x1, Pallas kernels, update(): pl.pallas_call(update_kernel, in_specs=[smem(), smem()] + [vmem()] * 7, o...  2.57 us
    pallas_call x1, Pallas kernels, cell_totals(): pl.pallas_call(totals_kernel, in_specs=[hbm()], out_specs=hbm(), out_shap...  2.25 us
  transfers between devices with their start and end apart: 12, of which 6 were waited for; matrix products, arithmetic and copies ran while one was open for 0% of the time, Pallas kernels for 6%

profile of v10, /device:TPU:8, one launch (start us, length us, event | category | flops | bytes accessed | tf_op | source)
XLA Modules:
  0.0 86.9 jit_solution(2330958263665588855)
XLA Ops:
  0.6 2.3 %cell_totals.1 = f32[8,8,128]{2,1,0:T(8,128)} custom-call(s32[384,1024]{1,0:T(8,128)} %counts_hbm.1), custom_call_target="tpu_custom_call" | custom-call | tf_op jit(solution)/shard_map/cell_totals/pallas_call | solution.py:87
  2.9 10.0 %all-to-all-start = ((f32[8,8,128]{2,1,0:T(8,128)}), f32[8,8,128]{2,1,0:T(8,128)S(1)}, u32[]{:S(2)}, u32[]{:S(2)}) async-start(f32[8,8,128]{2,1,0:T(8,128)} %cell_totals.1), calls=%async_computation | async-start | bytes 65536 | tf_op jit(solution)/shard_map/all_to_all | solution.py:476
  13.6 3.4 %prepare.1 = (f32[384,1024]{1,0:T(8,128)S(1)}, bf16[96,1024]{1,0:T(8,128)(2,1)S(1)}, f32[384,128]{1,0:T(8,128)S(1)}, f32[64,1024]{1,0:T(8,128)S(1)}, f32[64,384]{1,0:T(8,128)S(1)}) custom-call(s32[1]{0:T(128)S(6)} %copy.17.live_ref, s32[384,1024]{1,0:T(8,128)} %counts_hbm.1, s32[1,1024]{1,0:T(1,128)} %bitcast.25, f32[1,1024]{1,0:T(1,128)} %bitcast.26, ...), custom_call_target="tpu_custom_call" | custom-call | tf_op jit(solution)/shard_map/prepare/pallas_call | solution.py:167
  17.0 0.0 all-to-all-done.tot_ref
  17.0 2.1 %gram_sums.1 = (f32[384,1024]{1,0:T(8,128)S(1)}, f32[16,48,128]{2,1,0:T(8,128)S(1)}, f32[16,48,128]{2,1,0:T(8,128)S(1)}) custom-call(s32[1]{0:T(128)S(6)} %copy.17.live_ref, s32[1]{0:T(128)} %bitcast.core_ref, f32[8,8,128]{2,1,0:T(8,128)S(1)} %all-to-all-done.tot_ref, f32[384,1024]{1,0:T(8,128)S(1)} %get-tuple-element.15.rest_ref, ...), custom_call_target="tpu_custom_call" | custom-call | tf_op jit(solution)/shard_map/gram_sums/pallas_call | solution.py:240
  19.1 0.0 copy-start
  19.1 0.0 copy-start.1
  19.1 0.1 collective-permute-start
  19.2 1.7 %collective-permute-done = f32[16,48,128]{2,1,0:T(8,128)S(1)} collective-permute-done((f32[16,48,128]{2,1,0:T(8,128)S(1)}, f32[16,48,128]{2,1,0:T(8,128)S(1)}, u32[]{:S(2)}, u32[]{:S(2)}) %collective-permute-start) | collective-permute-done | bytes 393248 | tf_op jit(solution)/shard_map/ppermute | solution.py:526
  20.9 0.1 add.35
  21.0 14.4 %all_to_all.25.parts_ref = f32[16,48,128]{2,1,0:T(8,128)S(1)} all-to-all(f32[16,48,128]{2,1,0:T(8,128)S(1)} %add.35), channel_id=1, replica_groups={{224,32,160,208,240,16,48,96,144,176,192,0,80,112,128,64},{232,40,168,2..., dimensions={0} | all-to-all | bytes 786432 | tf_op jit(solution)/shard_map/all_to_all | solution.py:476
  35.4 1.0 %solve.1 = f32[32,1,384]{2,1,0:T(1,128)S(1)} custom-call(f32[16,48,128]{2,1,0:T(8,128)S(1)} %all_to_all.25.parts_ref), custom_call_target="tpu_custom_call" | custom-call | tf_op jit(solution)/shard_map/solve/pallas_call | solution.py:304
  36.4 11.1 %all_to_all.26 = f32[32,1,384]{2,1,0:T(1,128)S(1)} all-to-all(f32[32,1,384]{2,1,0:T(1,128)S(1)} %solve.1), channel_id=1, replica_groups={{224,32,160,208,240,16,48,96,144,176,192,0,80,112,128,64,232,40,168,216..., dimensions={0} | all-to-all | bytes 98304 | tf_op jit(solution)/shard_map/all_to_all | solution.py:476
  47.5 0.0 copy-done
  47.5 0.0 copy-done.1
  47.5 2.6 %update.1 = (f32[8,16,1024]{2,1,0:T(8,128)}, f32[64,384]{1,0:T(8,128)S(1)}, f32[64,384]{1,0:T(8,128)S(1)}, f32[32,384]{1,0:T(8,128)}) custom-call(s32[1]{0:T(128)S(6)} %copy.17.live_ref, s32[1]{0:T(128)} %bitcast.core_ref, f32[32,384]{1,0:T(8,128)S(1)} %bitcast.18, f32[384,1024]{1,0:T(8,128)S(1)} %get-tuple-element.20.pred_ref, ...), custom_call_target="tpu_custom_call" | custom-call | tf_op jit(solution)/shard_map/update/pallas_call | solution.py:378
  50.1 7.3 %all-to-all-start.3 = ((f32[8,16,1024]{2,1,0:T(8,128)}), f32[8,16,1024]{2,1,0:T(8,128)S(1)}, u32[]{:S(2)}, u32[]{:S(2)}) async-start(f32[8,16,1024]{2,1,0:T(8,128)} %get-tuple-element.24), calls=%async_computation.3 | async-start | bytes 1048576 | tf_op jit(solution)/shard_map/all_to_all | solution.py:476
  57.4 0.0 collective-permute-start.1
  57.4 1.3 %collective-permute-done.1 = f32[64,384]{1,0:T(8,128)S(1)} collective-permute-done((f32[64,384]{1,0:T(8,128)S(1)}, f32[64,384]{1,0:T(8,128)S(1)}, u32[]{:S(2)}, u32[]{:S(2)}) %collective-permute-start.1) | collective-permute-done | bytes 98336 | tf_op jit(solution)/shard_map/ppermute | solution.py:533
  58.7 2.2 %collective-permute-start.4 = (f32[64,384]{1,0:T(8,128)S(1)}, f32[64,384]{1,0:T(8,128)S(1)}, u32[]{:S(2)}, u32[]{:S(2)}) collective-permute-start(f32[64,384]{1,0:T(8,128)S(1)} %add.36), channel_id=1, source_target_pairs={{0,192},{8,200},{16,208},{24,216},{32,224},{40,232},{48,240},{56,2... | collective-permute-start | bytes 294920 | tf_op jit(solution)/shard_map/ppermute | solution.py:535
  60.9 0.4 collective-permute-start.3
  61.3 1.6 %collective-permute-start.2 = (f32[64,384]{1,0:T(8,128)S(1)}, f32[64,384]{1,0:T(8,128)S(1)}, u32[]{:S(2)}, u32[]{:S(2)}) collective-permute-start(f32[64,384]{1,0:T(8,128)S(1)} %add.36), channel_id=1, source_target_pairs={{0,64},{8,72},{16,80},{24,88},{32,96},{40,104},{48,112},{56,120},{... | collective-permute-start | bytes 294920 | tf_op jit(solution)/shard_map/ppermute | solution.py:535
  62.9 2.1 %collective-permute-done.4 = f32[64,384]{1,0:T(8,128)S(1)} collective-permute-done((f32[64,384]{1,0:T(8,128)S(1)}, f32[64,384]{1,0:T(8,128)S(1)}, u32[]{:S(2)}, u32[]{:S(2)}) %collective-permute-start.4) | collective-permute-done | bytes 98336 | tf_op jit(solution)/shard_map/ppermute | solution.py:535
  65.0 3.0 %collective-permute-done.3 = f32[64,384]{1,0:T(8,128)S(1)} collective-permute-done((f32[64,384]{1,0:T(8,128)S(1)}, f32[64,384]{1,0:T(8,128)S(1)}, u32[]{:S(2)}, u32[]{:S(2)}) %collective-permute-start.3) | collective-permute-done | bytes 98336 | tf_op jit(solution)/shard_map/ppermute | solution.py:535
  68.0 0.0 collective-permute-done.2
  68.0 1.5 %collective-permute-start.7 = (f32[64,384]{1,0:T(8,128)S(1)}, f32[64,384]{1,0:T(8,128)S(1)}, u32[]{:S(2)}, u32[]{:S(2)}) collective-permute-start(f32[64,384]{1,0:T(8,128)S(1)} %add_add_fusion.1), channel_id=1, source_target_pairs={{0,48},{8,56},{16,32},{24,40},{32,16},{40,24},{48,0},{56,8},{64,11... | collective-permute-start | bytes 294920 | tf_op jit(solution)/shard_map/ppermute | solution.py:535
  69.5 1.3 %collective-permute-start.6 = (f32[64,384]{1,0:T(8,128)S(1)}, f32[64,384]{1,0:T(8,128)S(1)}, u32[]{:S(2)}, u32[]{:S(2)}) collective-permute-start(f32[64,384]{1,0:T(8,128)S(1)} %add_add_fusion.1), channel_id=1, source_target_pairs={{0,32},{8,40},{16,48},{24,56},{32,0},{40,8},{48,16},{56,24},{64,96... | collective-permute-start | bytes 294920 | tf_op jit(solution)/shard_map/ppermute | solution.py:535
  70.8 1.4 %collective-permute-start.5 = (f32[64,384]{1,0:T(8,128)S(1)}, f32[64,384]{1,0:T(8,128)S(1)}, u32[]{:S(2)}, u32[]{:S(2)}) collective-permute-start(f32[64,384]{1,0:T(8,128)S(1)} %add_add_fusion.1), channel_id=1, source_target_pairs={{0,16},{8,24},{16,0},{24,8},{32,48},{40,56},{48,32},{56,40},{64,80... | collective-permute-start | bytes 294920 | tf_op jit(solution)/shard_map/ppermute | solution.py:535
  72.2 0.0 all-to-all-done.3.parts_ref
  72.2 0.8 factor_share.1
  73.0 7.2 %all-to-all-start.4 = ((f32[8,8,1024]{2,1,0:T(8,128)}), f32[8,8,1024]{2,1,0:T(8,128)S(1)}, u32[]{:S(2)}, u32[]{:S(2)}) async-start(f32[8,8,1024]{2,1,0:T(8,128)} %factor_share.1), calls=%async_computation.4 | async-start | bytes 524288 | tf_op jit(solution)/shard_map/all_to_all | solution.py:476
  80.2 0.0 collective-permute-done.7
  80.2 0.0 collective-permute-done.6
  80.2 0.0 collective-permute-done.5
  80.3 0.1 collective-permute-start.8
  80.4 1.2 %collective-permute-done.8.other_ref = f32[32,384]{1,0:T(8,128)S(1)} collective-permute-done((f32[32,384]{1,0:T(8,128)S(1)}, f32[32,384]{1,0:T(8,128)S(1)}, u32[]{:S(2)}, u32[]{:S(2)}) %collective-permute-start.8) | collective-permute-done | bytes 49184 | tf_op jit(solution)/shard_map/ppermute | solution.py:539
  81.6 0.7 joined_score.1
  82.3 3.8 %all-to-all-done.4.value_ref = f32[8,8,1024]{2,1,0:T(8,128)S(1)} async-done(((f32[8,8,1024]{2,1,0:T(8,128)}), f32[8,8,1024]{2,1,0:T(8,128)S(1)}, u32[]{:S(2)}, u32[]{:S(2)}) %all-to-all-start.4) | async-done | bytes 262176 | tf_op jit(solution)/shard_map/all_to_all | solution.py:476
  86.1 0.8 settled.1
  (5 shorter events, 0.1 us)
Async XLA Ops:
  2.9 14.1 %all-to-all-start = ((f32[8,8,128]{2,1,0:T(8,128)}), f32[8,8,128]{2,1,0:T(8,128)S(1)}, u32[]{:S(2)}, u32[]{:S(2)}) async-start(f32[8,8,128]{2,1,0:T(8,128)} %cell_totals.1), calls=%async_computation | async-start | bytes 65536 | tf_op jit(solution)/shard_map/all_to_all | solution.py:476
  19.1 28.4 %copy-start = (bf16[1024,64]{0,1:T(8,128)(2,1)S(1)}, bf16[1024,64]{0,1:T(8,128)(2,1)}, u32[]{:S(2)}) copy-start(bf16[1024,64]{0,1:T(8,128)(2,1)} %param.18) | copy-start | bytes 393220
  19.1 28.4 %copy-start.1 = (bf16[384,64]{0,1:T(8,128)(2,1)S(1)}, bf16[384,64]{0,1:T(8,128)(2,1)}, u32[]{:S(2)}) copy-start(bf16[384,64]{0,1:T(8,128)(2,1)} %param.19) | copy-start | bytes 147460
  19.1 1.8 %collective-permute-start = (f32[16,48,128]{2,1,0:T(8,128)S(1)}, f32[16,48,128]{2,1,0:T(8,128)S(1)}, u32[]{:S(2)}, u32[]{:S(2)}) collective-permute-start(f32[16,48,128]{2,1,0:T(8,128)S(1)} %get-tuple-element.19), channel_id=1, source_target_pairs={{0,8},{8,0},{16,24},{24,16},{32,40},{40,32},{48,56},{56,48},{64,72... | collective-permute-start | bytes 1179656 | tf_op jit(solution)/shard_map/ppermute | solution.py:526
  50.1 22.1 %all-to-all-start.3 = ((f32[8,16,1024]{2,1,0:T(8,128)}), f32[8,16,1024]{2,1,0:T(8,128)S(1)}, u32[]{:S(2)}, u32[]{:S(2)}) async-start(f32[8,16,1024]{2,1,0:T(8,128)} %get-tuple-element.24), calls=%async_computation.3 | async-start | bytes 1048576 | tf_op jit(solution)/shard_map/all_to_all | solution.py:476
  57.4 1.3 %collective-permute-start.1 = (f32[64,384]{1,0:T(8,128)S(1)}, f32[64,384]{1,0:T(8,128)S(1)}, u32[]{:S(2)}, u32[]{:S(2)}) collective-permute-start(f32[64,384]{1,0:T(8,128)S(1)} %get-tuple-element.26), channel_id=1, source_target_pairs={{0,8},{8,0},{16,24},{24,16},{32,40},{40,32},{48,56},{56,48},{64,72... | collective-permute-start | bytes 294920 | tf_op jit(solution)/shard_map/ppermute | solution.py:533
  58.7 6.3 %collective-permute-start.4 = (f32[64,384]{1,0:T(8,128)S(1)}, f32[64,384]{1,0:T(8,128)S(1)}, u32[]{:S(2)}, u32[]{:S(2)}) collective-permute-start(f32[64,384]{1,0:T(8,128)S(1)} %add.36), channel_id=1, source_target_pairs={{0,192},{8,200},{16,208},{24,216},{32,224},{40,232},{48,240},{56,2... | collective-permute-start | bytes 294920 | tf_op jit(solution)/shard_map/ppermute | solution.py:535
  60.9 7.1 %collective-permute-start.3 = (f32[64,384]{1,0:T(8,128)S(1)}, f32[64,384]{1,0:T(8,128)S(1)}, u32[]{:S(2)}, u32[]{:S(2)}) collective-permute-start(f32[64,384]{1,0:T(8,128)S(1)} %add.36), channel_id=1, source_target_pairs={{0,128},{8,136},{16,144},{24,152},{32,160},{40,168},{48,176},{56,1... | collective-permute-start | bytes 294920 | tf_op jit(solution)/shard_map/ppermute | solution.py:535
  61.3 6.7 %collective-permute-start.2 = (f32[64,384]{1,0:T(8,128)S(1)}, f32[64,384]{1,0:T(8,128)S(1)}, u32[]{:S(2)}, u32[]{:S(2)}) collective-permute-start(f32[64,384]{1,0:T(8,128)S(1)} %add.36), channel_id=1, source_target_pairs={{0,64},{8,72},{16,80},{24,88},{32,96},{40,104},{48,112},{56,120},{... | collective-permute-start | bytes 294920 | tf_op jit(solution)/shard_map/ppermute | solution.py:535
  68.0 12.2 %collective-permute-start.7 = (f32[64,384]{1,0:T(8,128)S(1)}, f32[64,384]{1,0:T(8,128)S(1)}, u32[]{:S(2)}, u32[]{:S(2)}) collective-permute-start(f32[64,384]{1,0:T(8,128)S(1)} %add_add_fusion.1), channel_id=1, source_target_pairs={{0,48},{8,56},{16,32},{24,40},{32,16},{40,24},{48,0},{56,8},{64,11... | collective-permute-start | bytes 294920 | tf_op jit(solution)/shard_map/ppermute | solution.py:535
  69.5 10.7 %collective-permute-start.6 = (f32[64,384]{1,0:T(8,128)S(1)}, f32[64,384]{1,0:T(8,128)S(1)}, u32[]{:S(2)}, u32[]{:S(2)}) collective-permute-start(f32[64,384]{1,0:T(8,128)S(1)} %add_add_fusion.1), channel_id=1, source_target_pairs={{0,32},{8,40},{16,48},{24,56},{32,0},{40,8},{48,16},{56,24},{64,96... | collective-permute-start | bytes 294920 | tf_op jit(solution)/shard_map/ppermute | solution.py:535
  70.8 9.4 %collective-permute-start.5 = (f32[64,384]{1,0:T(8,128)S(1)}, f32[64,384]{1,0:T(8,128)S(1)}, u32[]{:S(2)}, u32[]{:S(2)}) collective-permute-start(f32[64,384]{1,0:T(8,128)S(1)} %add_add_fusion.1), channel_id=1, source_target_pairs={{0,16},{8,24},{16,0},{24,8},{32,48},{40,56},{48,32},{56,40},{64,80... | collective-permute-start | bytes 294920 | tf_op jit(solution)/shard_map/ppermute | solution.py:535
  73.0 13.1 %all-to-all-start.4 = ((f32[8,8,1024]{2,1,0:T(8,128)}), f32[8,8,1024]{2,1,0:T(8,128)S(1)}, u32[]{:S(2)}, u32[]{:S(2)}) async-start(f32[8,8,1024]{2,1,0:T(8,128)} %factor_share.1), calls=%async_computation.4 | async-start | bytes 524288 | tf_op jit(solution)/shard_map/all_to_all | solution.py:476
  80.3 1.3 %collective-permute-start.8 = (f32[32,384]{1,0:T(8,128)S(1)}, f32[32,384]{1,0:T(8,128)S(1)}, u32[]{:S(2)}, u32[]{:S(2)}) collective-permute-start(f32[32,384]{1,0:T(8,128)S(1)} %fusion.1.mine_ref), channel_id=1, source_target_pairs={{0,8},{8,0},{16,24},{24,16},{32,40},{40,32},{48,56},{56,48},{64,72... | collective-permute-start | bytes 147464 | tf_op jit(solution)/shard_map/ppermute | solution.py:539

commit v11 on v10

--- a/solution.py
+++ b/solution.py
@@ -182,9 +182,35 @@
     )(live, *arrays)
 
 
-def gram_kernel(
-    live_ref, core_ref, tot_ref, rest_ref, design_ref, score_ref,
-    pred_ref, kept_ref, given_ref, offset, acc, terms_hi, terms_lo,
+def half_rows(ref, half, here):
+    rows = [
+        ref[pl.ds(pl.multiple_of(32 * g + 16 * half, 16), 16), here] for g in range(12)
+    ]
+    return jnp.concatenate(rows, axis=0)
+
+
+def half_sums(live_ref, half, pred_ref, score_ref, hi_ref, lo_ref, out_ref, acc, at):
+    here = pl.ds(at, CHUNK)
+    slot = lax.broadcasted_iota(jnp.int32, (1, CHUNK), 1) + at
+    mask = (slot < live_ref[0]).astype(F32)
+    w1, w2 = split2(jnp.exp(half_rows(pred_ref, half, here)) * mask)
+    hi, lo = hi_ref[:, here], lo_ref[:, here]
+    gram = dot(w1, hi, NT) + dot(w1, lo, NT) + dot(w2, hi, NT)
+    for t in range(4):
+        part = gram[:, 128 * t : 128 * (t + 1)]
+        if at > 0:
+            acc[t] += part
+        else:
+            acc[t] = part + half_rows(score_ref, half, slice(None)) if t == 3 else part
+    if at + CHUNK == pred_ref.shape[1]:
+        for chip in range(16):
+            for t in range(4):
+                out_ref[chip, 12 * t : 12 * (t + 1), :] = acc[t, pl.ds(chip, 12, stride=16), :]
+
+
+def given_kernel(
+    live_ref, half_ref, tot_ref, rest_ref, design_ref, score_ref,
+    pred_ref, hi_ref, lo_ref, out_ref, offset, acc,
 ):
     total = jnp.sum(tot_ref[...], axis=0)
     value = jnp.log((1.0 + total) / GENES)
@@ -193,12 +219,11 @@
 
     for at in range(0, rest_ref.shape[1], CHUNK):
         here = pl.ds(at, CHUNK)
-        hi_ref, lo_ref = terms_hi.at[:, here], terms_lo.at[:, here]
 
         def put(row, value):
             hi, lo = split2(value)
-            hi_ref[row : row + value.shape[0], :] = hi
-            lo_ref[row : row + value.shape[0], :] = lo
+            hi_ref[row : row + value.shape[0], here] = hi
+            lo_ref[row : row + value.shape[0], here] = lo
 
         d1, d2, d3 = (design_ref[32 * i : 32 * (i + 1), here] for i in range(3))
         design = (d1.astype(F32) + d2.astype(F32)) + d3.astype(F32)
@@ -213,46 +238,44 @@
                 both = [left[i : i + 1] * right, left[i + 1 : i + 2] * right]
                 put(row + 8 * i, jnp.concatenate(both, axis=0))
         put(480, -design)
-
-        pred = rest_ref[:, here] + offset[:, here]
-        pred_ref[:, here] = pred
-        slot = lax.broadcasted_iota(jnp.int32, (1, CHUNK), 1) + at
-        mask = (slot < live_ref[0]).astype(F32)
-        w1, w2 = split2(jnp.exp(pred) * mask)
-        hi, lo = hi_ref[...], lo_ref[...]
-        gram = dot(w1, hi, NT) + dot(w1, lo, NT) + dot(w2, hi, NT)
-        for t in range(4):
-            part = gram[:, 128 * t : 128 * (t + 1)]
-            if at > 0:
-                acc[t] += part
-            else:
-                acc[t] = part + score_ref[...] if t == 3 else part
-
-    core = core_ref[0]
-    for chip in range(16):
-        for ref, j in ((kept_ref, 16 * core + chip), (given_ref, 16 * (1 - core) + chip)):
-            for t in range(4):
-                ref[chip, 12 * t : 12 * (t + 1), :] = acc[t, pl.ds(j, 12, stride=32), :]
+        pred_ref[:, here] = rest_ref[:, here] + offset[:, here]
+        half_sums(live_ref, half_ref[0], pred_ref, score_ref, hi_ref, lo_ref, out_ref, acc, at)
+
+
+def kept_kernel(live_ref, half_ref, pred_ref, score_ref, hi_ref, lo_ref, out_ref, acc):
+    for at in range(0, pred_ref.shape[1], CHUNK):
+        half_sums(live_ref, half_ref[0], pred_ref, score_ref, hi_ref, lo_ref, out_ref, acc, at)
 
 
 def gram_sums(live, core, tot, rest, design, score):
     genes, cells = rest.shape
-    return pl.pallas_call(
-        gram_kernel,
+    packed = jax.ShapeDtypeStruct((16, 48, 128), F32)
+    acc = pltpu.VMEM((4, genes // 2, 128), F32)
+    pred, hi, lo, given = pl.pallas_call(
+        given_kernel,
         in_specs=[smem(), smem(), vmem(), vmem(), vmem(), vmem()],
-        out_specs=[vmem(), vmem(), vmem()],
+        out_specs=[vmem()] * 4,
         out_shape=[
             jax.ShapeDtypeStruct((genes, cells), F32),
-            jax.ShapeDtypeStruct((16, 48, 128), F32),
-            jax.ShapeDtypeStruct((16, 48, 128), F32),
+            jax.ShapeDtypeStruct((512, cells), BF16),
+            jax.ShapeDtypeStruct((512, cells), BF16),
+            packed,
         ],
-        scratch_shapes=[
-            pltpu.VMEM((1, cells), F32), pltpu.VMEM((4, genes, 128), F32),
-            pltpu.VMEM((512, cells), BF16), pltpu.VMEM((512, cells), BF16),
-        ],
-        compiler_params=params(),
-        name="gram_sums",
-    )(live, core, tot, rest, design, score)
+        scratch_shapes=[pltpu.VMEM((1, cells), F32), acc],
+        compiler_params=params(),
+        name="gram_given",
+    )(live, 1 - core, tot, rest, design, score)
+    arrived = lax.ppermute(given, "cell", OTHER_CORE)
+    kept = pl.pallas_call(
+        kept_kernel,
+        in_specs=[smem(), smem(), vmem(), vmem(), vmem(), vmem()],
+        out_specs=vmem(),
+        out_shape=packed,
+        scratch_shapes=[acc],
+        compiler_params=params(),
+        name="gram_kept",
+    )(live, core, pred, score, hi, lo)
+    return pred, kept + arrived
 
 
 def solve_kernel(parts_ref, out_ref, table):
@@ -520,10 +543,7 @@
         cell_covariates, coefficients.T, batch_effect.T, load, fact,
     )
     core = (lax.axis_index("cell") % 2)[None]
-    pred, kept, given = gram_sums(
-        live_cells, core, tot, rest, design, score
-    )
-    packed = kept + lax.ppermute(given, "cell", OTHER_CORE)
+    pred, packed = gram_sums(live_cells, core, tot, rest, design, score)
     steps = exchange(solve(exchange(packed, "cell", SAME_CORE)), "cell", CORE_FIRST)
     pieces, kept, given, beta = update(
         live_cells, core, steps.reshape(32, 384), pred, design, load, fact, by_load, by_fact

time: 87.3 us -> 86.8 us (level)
  waiting for transfers between devices: 13.2 us -> 11.8 us
    ppermute x1, waiting for transfers between devices: 1.71 us -> 0.38 us  [gram_sums(): arrived = lax.ppermute(given, 'cell', OTHER_CORE)]
    pallas_call x1 -> x2, Pallas kernels: 2.06 us -> 2.86 us  [the longest x1 1.56 us: gram_sums(): pl.pallas_call(given_kernel, in_specs=[smem(), smem(), vmem(), vmem(), vm...]
  transfers between devices with their start and end apart: 12 -> 12, of which waited for: 6 -> 6; matrix products, arithmetic and copies ran while one was open for 0% -> 0% of each run, Pallas kernels for 6% -> 7%
where the time goes in v11:
time: 86.8 us; the launch traced here: 86.3 us
  starting transfers between devices  33.1 us (38%)
  blocking collectives  25.5 us (29%)
  Pallas kernels  14.3 us (16%)
  waiting for transfers between devices  11.8 us (14%)
  between operations  1.44 us (2%)
    all_to_all x2, blocking collectives, exchange(): lax.all_to_all(value, axis, split_axis=0, concat_axis=0, tiled=True, axis...  25.5 us
    all_to_all x3, starting transfers between devices, exchange(): lax.all_to_all(value, axis, split_axis=0, concat_axis=0, tiled=True, axis...  24.6 us
    ppermute x6, starting transfers between devices, local(): lax.ppermute(value, 'cell', pairs)  8.36 us
    ppermute x6, waiting for transfers between devices, local(): lax.ppermute(value, 'cell', pairs)  5.11 us
    all_to_all x3, waiting for transfers between devices, exchange(): lax.all_to_all(value, axis, split_axis=0, concat_axis=0, tiled=True, axis...  3.82 us
    pallas_call x1, Pallas kernels, prepare(): pl.pallas_call(prepare_kernel, in_specs=[smem()] + [hbm()] * len(arrays),...  3.4 us
    pallas_call x1, Pallas kernels, update(): pl.pallas_call(update_kernel, in_specs=[smem(), smem()] + [vmem()] * 7, o...  2.58 us
    pallas_call x1, Pallas kernels, cell_totals(): pl.pallas_call(totals_kernel, in_specs=[hbm()], out_specs=hbm(), out_shap...  2.25 us
  transfers between devices with their start and end apart: 12, of which 6 were waited for; matrix products, arithmetic and copies ran while one was open for 0% of the time, Pallas kernels for 7%

profile of v11, /device:TPU:8, one launch (start us, length us, event | category | flops | bytes accessed | tf_op | source)
XLA Modules:
  0.0 86.3 jit_solution(14979099666742061478)
XLA Ops:
  0.6 2.3 %cell_totals.1 = f32[8,8,128]{2,1,0:T(8,128)} custom-call(s32[384,1024]{1,0:T(8,128)} %counts_hbm.1), custom_call_target="tpu_custom_call" | custom-call | tf_op jit(solution)/shard_map/cell_totals/pallas_call | solution.py:87
  2.9 10.0 %all-to-all-start = ((f32[8,8,128]{2,1,0:T(8,128)}), f32[8,8,128]{2,1,0:T(8,128)S(1)}, u32[]{:S(2)}, u32[]{:S(2)}) async-start(f32[8,8,128]{2,1,0:T(8,128)} %cell_totals.1), calls=%async_computation | async-start | bytes 65536 | tf_op jit(solution)/shard_map/all_to_all | solution.py:499
  13.6 3.4 %prepare.1 = (f32[384,1024]{1,0:T(8,128)S(1)}, bf16[96,1024]{1,0:T(8,128)(2,1)S(1)}, f32[384,128]{1,0:T(8,128)S(1)}, f32[64,1024]{1,0:T(8,128)S(1)}, f32[64,384]{1,0:T(8,128)S(1)}) custom-call(s32[1]{0:T(128)S(6)} %copy.17.live_ref, s32[384,1024]{1,0:T(8,128)} %counts_hbm.1, s32[1,1024]{1,0:T(1,128)} %bitcast.25, f32[1,1024]{1,0:T(1,128)} %bitcast.26, ...), custom_call_target="tpu_custom_call" | custom-call | tf_op jit(solution)/shard_map/prepare/pallas_call | solution.py:167
  17.0 0.0 all-to-all-done.tot_ref
  17.0 1.6 %gram_given.1 = (f32[384,1024]{1,0:T(8,128)S(1)}, bf16[512,1024]{1,0:T(8,128)(2,1)S(1)}, bf16[512,1024]{1,0:T(8,128)(2,1)S(1)}, f32[16,48,128]{2,1,0:T(8,128)S(1)}) custom-call(s32[1]{0:T(128)S(6)} %copy.17.live_ref, s32[1]{0:T(128)S(6)} %sub.3.half_ref, f32[8,8,128]{2,1,0:T(8,128)S(1)} %all-to-all-done.tot_ref, f32[384,1024]{1,0:T(8,128)S(1)} %get-tuple-element.16.rest_ref, ...), custom_call_target="tpu_custom_call" | custom-call | tf_op jit(solution)/shard_map/gram_given/pallas_call | solution.py:254
  18.6 0.1 collective-permute-start
  18.7 1.3 %gram_kept.1 = f32[16,48,128]{2,1,0:T(8,128)S(1)} custom-call(s32[1]{0:T(128)S(6)} %copy.17.live_ref, s32[1]{0:T(128)} %bitcast.half_ref.core_ref, f32[384,1024]{1,0:T(8,128)S(1)} %get-tuple-element.19.pred_ref, f32[384,128]{1,0:T(8,128)S(1)} %get-tuple-element.18.score_ref, bf16[512,1024]{1,0:T(8,128)(2,1)S(1)} %get-tuple-element.20.hi_ref, ...), custom_call_target="tpu_custom_call" | custom-call | tf_op jit(solution)/shard_map/gram_kept/pallas_call | solution.py:269
  20.0 0.0 copy-start
  20.0 0.0 copy-start.1
  20.0 0.4 collective-permute-done
  20.4 14.4 %all_to_all.25.parts_ref = f32[16,48,128]{2,1,0:T(8,128)S(1)} all-to-all(f32[16,48,128]{2,1,0:T(8,128)S(1)} %add.35), channel_id=1, replica_groups={{224,32,160,208,240,16,48,96,144,176,192,0,80,112,128,64},{232,40,168,2..., dimensions={0} | all-to-all | bytes 786432 | tf_op jit(solution)/shard_map/all_to_all | solution.py:499
  34.9 1.0 %solve.1 = f32[32,1,384]{2,1,0:T(1,128)S(1)} custom-call(f32[16,48,128]{2,1,0:T(8,128)S(1)} %all_to_all.25.parts_ref), custom_call_target="tpu_custom_call" | custom-call | tf_op jit(solution)/shard_map/solve/pallas_call | solution.py:327
  35.9 11.1 %all_to_all.26 = f32[32,1,384]{2,1,0:T(1,128)S(1)} all-to-all(f32[32,1,384]{2,1,0:T(1,128)S(1)} %solve.1), channel_id=1, replica_groups={{224,32,160,208,240,16,48,96,144,176,192,0,80,112,128,64,232,40,168,216..., dimensions={0} | all-to-all | bytes 98304 | tf_op jit(solution)/shard_map/all_to_all | solution.py:499
  46.9 0.0 copy-done
  46.9 0.0 copy-done.1
  46.9 2.6 %update.1 = (f32[8,16,1024]{2,1,0:T(8,128)}, f32[64,384]{1,0:T(8,128)S(1)}, f32[64,384]{1,0:T(8,128)S(1)}, f32[32,384]{1,0:T(8,128)}) custom-call(s32[1]{0:T(128)S(6)} %copy.17.live_ref, s32[1]{0:T(128)} %bitcast.half_ref.core_ref, f32[32,384]{1,0:T(8,128)S(1)} %bitcast.18, f32[384,1024]{1,0:T(8,128)S(1)} %get-tuple-element.19.pred_ref, ...), custom_call_target="tpu_custom_call" | custom-call | tf_op jit(solution)/shard_map/update/pallas_call | solution.py:401
  49.5 7.3 %all-to-all-start.3 = ((f32[8,16,1024]{2,1,0:T(8,128)}), f32[8,16,1024]{2,1,0:T(8,128)S(1)}, u32[]{:S(2)}, u32[]{:S(2)}) async-start(f32[8,16,1024]{2,1,0:T(8,128)} %get-tuple-element.26), calls=%async_computation.3 | async-start | bytes 1048576 | tf_op jit(solution)/shard_map/all_to_all | solution.py:499
  56.9 0.0 collective-permute-start.1
  56.9 1.3 %collective-permute-done.1 = f32[64,384]{1,0:T(8,128)S(1)} collective-permute-done((f32[64,384]{1,0:T(8,128)S(1)}, f32[64,384]{1,0:T(8,128)S(1)}, u32[]{:S(2)}, u32[]{:S(2)}) %collective-permute-start.1) | collective-permute-done | bytes 98336 | tf_op jit(solution)/shard_map/ppermute | solution.py:553
  58.2 2.2 %collective-permute-start.4 = (f32[64,384]{1,0:T(8,128)S(1)}, f32[64,384]{1,0:T(8,128)S(1)}, u32[]{:S(2)}, u32[]{:S(2)}) collective-permute-start(f32[64,384]{1,0:T(8,128)S(1)} %add.36), channel_id=1, source_target_pairs={{0,192},{8,200},{16,208},{24,216},{32,224},{40,232},{48,240},{56,2... | collective-permute-start | bytes 294920 | tf_op jit(solution)/shard_map/ppermute | solution.py:555
  60.3 0.4 collective-permute-start.3
  60.8 1.6 %collective-permute-start.2 = (f32[64,384]{1,0:T(8,128)S(1)}, f32[64,384]{1,0:T(8,128)S(1)}, u32[]{:S(2)}, u32[]{:S(2)}) collective-permute-start(f32[64,384]{1,0:T(8,128)S(1)} %add.36), channel_id=1, source_target_pairs={{0,64},{8,72},{16,80},{24,88},{32,96},{40,104},{48,112},{56,120},{... | collective-permute-start | bytes 294920 | tf_op jit(solution)/shard_map/ppermute | solution.py:555
  62.4 2.1 %collective-permute-done.4 = f32[64,384]{1,0:T(8,128)S(1)} collective-permute-done((f32[64,384]{1,0:T(8,128)S(1)}, f32[64,384]{1,0:T(8,128)S(1)}, u32[]{:S(2)}, u32[]{:S(2)}) %collective-permute-start.4) | collective-permute-done | bytes 98336 | tf_op jit(solution)/shard_map/ppermute | solution.py:555
  64.5 3.0 %collective-permute-done.3 = f32[64,384]{1,0:T(8,128)S(1)} collective-permute-done((f32[64,384]{1,0:T(8,128)S(1)}, f32[64,384]{1,0:T(8,128)S(1)}, u32[]{:S(2)}, u32[]{:S(2)}) %collective-permute-start.3) | collective-permute-done | bytes 98336 | tf_op jit(solution)/shard_map/ppermute | solution.py:555
  67.5 0.0 collective-permute-done.2
  67.5 1.5 %collective-permute-start.7 = (f32[64,384]{1,0:T(8,128)S(1)}, f32[64,384]{1,0:T(8,128)S(1)}, u32[]{:S(2)}, u32[]{:S(2)}) collective-permute-start(f32[64,384]{1,0:T(8,128)S(1)} %add_add_fusion.1), channel_id=1, source_target_pairs={{0,48},{8,56},{16,32},{24,40},{32,16},{40,24},{48,0},{56,8},{64,11... | collective-permute-start | bytes 294920 | tf_op jit(solution)/shard_map/ppermute | solution.py:555
  69.0 1.3 %collective-permute-start.6 = (f32[64,384]{1,0:T(8,128)S(1)}, f32[64,384]{1,0:T(8,128)S(1)}, u32[]{:S(2)}, u32[]{:S(2)}) collective-permute-start(f32[64,384]{1,0:T(8,128)S(1)} %add_add_fusion.1), channel_id=1, source_target_pairs={{0,32},{8,40},{16,48},{24,56},{32,0},{40,8},{48,16},{56,24},{64,96... | collective-permute-start | bytes 294920 | tf_op jit(solution)/shard_map/ppermute | solution.py:555
  70.3 1.4 %collective-permute-start.5 = (f32[64,384]{1,0:T(8,128)S(1)}, f32[64,384]{1,0:T(8,128)S(1)}, u32[]{:S(2)}, u32[]{:S(2)}) collective-permute-start(f32[64,384]{1,0:T(8,128)S(1)} %add_add_fusion.1), channel_id=1, source_target_pairs={{0,16},{8,24},{16,0},{24,8},{32,48},{40,56},{48,32},{56,40},{64,80... | collective-permute-start | bytes 294920 | tf_op jit(solution)/shard_map/ppermute | solution.py:555
  71.7 0.0 all-to-all-done.3.parts_ref
  71.7 0.8 factor_share.1
  72.5 7.2 %all-to-all-start.4 = ((f32[8,8,1024]{2,1,0:T(8,128)}), f32[8,8,1024]{2,1,0:T(8,128)S(1)}, u32[]{:S(2)}, u32[]{:S(2)}) async-start(f32[8,8,1024]{2,1,0:T(8,128)} %factor_share.1), calls=%async_computation.4 | async-start | bytes 524288 | tf_op jit(solution)/shard_map/all_to_all | solution.py:499
  79.7 0.0 collective-permute-done.7
  79.7 0.0 collective-permute-done.6
  79.7 0.0 collective-permute-done.5
  79.8 0.1 collective-permute-start.8
  79.9 1.2 %collective-permute-done.8.other_ref = f32[32,384]{1,0:T(8,128)S(1)} collective-permute-done((f32[32,384]{1,0:T(8,128)S(1)}, f32[32,384]{1,0:T(8,128)S(1)}, u32[]{:S(2)}, u32[]{:S(2)}) %collective-permute-start.8) | collective-permute-done | bytes 49184 | tf_op jit(solution)/shard_map/ppermute | solution.py:559
  81.1 0.7 joined_score.1
  81.8 3.8 %all-to-all-done.4.value_ref = f32[8,8,1024]{2,1,0:T(8,128)S(1)} async-done(((f32[8,8,1024]{2,1,0:T(8,128)}), f32[8,8,1024]{2,1,0:T(8,128)S(1)}, u32[]{:S(2)}, u32[]{:S(2)}) %all-to-all-start.4) | async-done | bytes 262176 | tf_op jit(solution)/shard_map/all_to_all | solution.py:499
  85.6 0.8 settled.1
  (6 shorter events, 0.1 us)
Async XLA Ops:
  2.9 14.1 %all-to-all-start = ((f32[8,8,128]{2,1,0:T(8,128)}), f32[8,8,128]{2,1,0:T(8,128)S(1)}, u32[]{:S(2)}, u32[]{:S(2)}) async-start(f32[8,8,128]{2,1,0:T(8,128)} %cell_totals.1), calls=%async_computation | async-start | bytes 65536 | tf_op jit(solution)/shard_map/all_to_all | solution.py:499
  18.6 1.8 %collective-permute-start = (f32[16,48,128]{2,1,0:T(8,128)S(1)}, f32[16,48,128]{2,1,0:T(8,128)S(1)}, u32[]{:S(2)}, u32[]{:S(2)}) collective-permute-start(f32[16,48,128]{2,1,0:T(8,128)S(1)} %get-tuple-element.22), channel_id=1, source_target_pairs={{0,8},{8,0},{16,24},{24,16},{32,40},{40,32},{48,56},{56,48},{64,72... | collective-permute-start | bytes 1179656 | tf_op jit(solution)/shard_map/ppermute | solution.py:268
  20.0 27.0 %copy-start = (bf16[1024,64]{0,1:T(8,128)(2,1)S(1)}, bf16[1024,64]{0,1:T(8,128)(2,1)}, u32[]{:S(2)}) copy-start(bf16[1024,64]{0,1:T(8,128)(2,1)} %param.18) | copy-start | bytes 393220
  20.0 27.0 %copy-start.1 = (bf16[384,64]{0,1:T(8,128)(2,1)S(1)}, bf16[384,64]{0,1:T(8,128)(2,1)}, u32[]{:S(2)}) copy-start(bf16[384,64]{0,1:T(8,128)(2,1)} %param.19) | copy-start | bytes 147460
  49.5 22.1 %all-to-all-start.3 = ((f32[8,16,1024]{2,1,0:T(8,128)}), f32[8,16,1024]{2,1,0:T(8,128)S(1)}, u32[]{:S(2)}, u32[]{:S(2)}) async-start(f32[8,16,1024]{2,1,0:T(8,128)} %get-tuple-element.26), calls=%async_computation.3 | async-start | bytes 1048576 | tf_op jit(solution)/shard_map/all_to_all | solution.py:499
  56.9 1.3 %collective-permute-start.1 = (f32[64,384]{1,0:T(8,128)S(1)}, f32[64,384]{1,0:T(8,128)S(1)}, u32[]{:S(2)}, u32[]{:S(2)}) collective-permute-start(f32[64,384]{1,0:T(8,128)S(1)} %get-tuple-element.28), channel_id=1, source_target_pairs={{0,8},{8,0},{16,24},{24,16},{32,40},{40,32},{48,56},{56,48},{64,72... | collective-permute-start | bytes 294920 | tf_op jit(solution)/shard_map/ppermute | solution.py:553
  58.2 6.3 %collective-permute-start.4 = (f32[64,384]{1,0:T(8,128)S(1)}, f32[64,384]{1,0:T(8,128)S(1)}, u32[]{:S(2)}, u32[]{:S(2)}) collective-permute-start(f32[64,384]{1,0:T(8,128)S(1)} %add.36), channel_id=1, source_target_pairs={{0,192},{8,200},{16,208},{24,216},{32,224},{40,232},{48,240},{56,2... | collective-permute-start | bytes 294920 | tf_op jit(solution)/shard_map/ppermute | solution.py:555
  60.3 7.1 %collective-permute-start.3 = (f32[64,384]{1,0:T(8,128)S(1)}, f32[64,384]{1,0:T(8,128)S(1)}, u32[]{:S(2)}, u32[]{:S(2)}) collective-permute-start(f32[64,384]{1,0:T(8,128)S(1)} %add.36), channel_id=1, source_target_pairs={{0,128},{8,136},{16,144},{24,152},{32,160},{40,168},{48,176},{56,1... | collective-permute-start | bytes 294920 | tf_op jit(solution)/shard_map/ppermute | solution.py:555
  60.8 6.7 %collective-permute-start.2 = (f32[64,384]{1,0:T(8,128)S(1)}, f32[64,384]{1,0:T(8,128)S(1)}, u32[]{:S(2)}, u32[]{:S(2)}) collective-permute-start(f32[64,384]{1,0:T(8,128)S(1)} %add.36), channel_id=1, source_target_pairs={{0,64},{8,72},{16,80},{24,88},{32,96},{40,104},{48,112},{56,120},{... | collective-permute-start | bytes 294920 | tf_op jit(solution)/shard_map/ppermute | solution.py:555
  67.5 12.2 %collective-permute-start.7 = (f32[64,384]{1,0:T(8,128)S(1)}, f32[64,384]{1,0:T(8,128)S(1)}, u32[]{:S(2)}, u32[]{:S(2)}) collective-permute-start(f32[64,384]{1,0:T(8,128)S(1)} %add_add_fusion.1), channel_id=1, source_target_pairs={{0,48},{8,56},{16,32},{24,40},{32,16},{40,24},{48,0},{56,8},{64,11... | collective-permute-start | bytes 294920 | tf_op jit(solution)/shard_map/ppermute | solution.py:555
  69.0 10.7 %collective-permute-start.6 = (f32[64,384]{1,0:T(8,128)S(1)}, f32[64,384]{1,0:T(8,128)S(1)}, u32[]{:S(2)}, u32[]{:S(2)}) collective-permute-start(f32[64,384]{1,0:T(8,128)S(1)} %add_add_fusion.1), channel_id=1, source_target_pairs={{0,32},{8,40},{16,48},{24,56},{32,0},{40,8},{48,16},{56,24},{64,96... | collective-permute-start | bytes 294920 | tf_op jit(solution)/shard_map/ppermute | solution.py:555
  70.3 9.4 %collective-permute-start.5 = (f32[64,384]{1,0:T(8,128)S(1)}, f32[64,384]{1,0:T(8,128)S(1)}, u32[]{:S(2)}, u32[]{:S(2)}) collective-permute-start(f32[64,384]{1,0:T(8,128)S(1)} %add_add_fusion.1), channel_id=1, source_target_pairs={{0,16},{8,24},{16,0},{24,8},{32,48},{40,56},{48,32},{56,40},{64,80... | collective-permute-start | bytes 294920 | tf_op jit(solution)/shard_map/ppermute | solution.py:555
  72.5 13.1 %all-to-all-start.4 = ((f32[8,8,1024]{2,1,0:T(8,128)}), f32[8,8,1024]{2,1,0:T(8,128)S(1)}, u32[]{:S(2)}, u32[]{:S(2)}) async-start(f32[8,8,1024]{2,1,0:T(8,128)} %factor_share.1), calls=%async_computation.4 | async-start | bytes 524288 | tf_op jit(solution)/shard_map/all_to_all | solution.py:499
  79.8 1.3 %collective-permute-start.8 = (f32[32,384]{1,0:T(8,128)S(1)}, f32[32,384]{1,0:T(8,128)S(1)}, u32[]{:S(2)}, u32[]{:S(2)}) collective-permute-start(f32[32,384]{1,0:T(8,128)S(1)} %fusion.1.mine_ref), channel_id=1, source_target_pairs={{0,8},{8,0},{16,24},{24,16},{32,40},{40,32},{48,56},{56,48},{64,72... | collective-permute-start | bytes 147464 | tf_op jit(solution)/shard_map/ppermute | solution.py:559

commit v12 on v11

--- a/solution.py
+++ b/solution.py
@@ -528,8 +528,13 @@
 CORE_FIRST = [SAME_CORE[0] + SAME_CORE[1]]
 RING = [[(FIRST[2] + step) % 8 for step in (0, 1, -1, 2, -2, 3, -3, 4)]]
 OTHER_CORE = partners(lambda x, y, c: (x, y, 1 - c))
-ALONG_X = [partners(lambda x, y, c, k=k: (x ^ k, y, c)) for k in (1, 2, 3)]
-ALONG_Y = [partners(lambda x, y, c, k=k: (x, y ^ k, c)) for k in (1, 2, 3)]
+STAGES = [
+    [
+        partners(lambda x, y, c, k=k: (x ^ k, y, c) if c == swap else (x, y ^ k, c))
+        for k in (1, 2, 3)
+    ]
+    for swap in (0, 1)
+]
 
 
 def local(
@@ -551,7 +556,7 @@
     arrived = exchange(pieces, "gene", RING)
 
     value = kept + lax.ppermute(given, "cell", OTHER_CORE)
-    for moves in (ALONG_X, ALONG_Y):
+    for moves in STAGES:
         near, across, beside = (lax.ppermute(value, "cell", pairs) for pairs in moves)
         value = (value + near) + (across + beside)
     gathered = settled(exchange(factor_share(arrived), "gene", RING))

time: 86.8 us -> 86 us (level)
  the two profiles are of different devices: /device:TPU:8 before, /device:TPU:1 now
where the time goes in v12:
time: 86 us; the launch traced here: 84.6 us
  starting transfers between devices  34.4 us (40%)
  blocking collectives  25.6 us (30%)
  Pallas kernels  14.3 us (17%)
  waiting for transfers between devices  8.74 us (10%)
  between operations  1.43 us (2%)
    all_to_all x2, blocking collectives, exchange(): lax.all_to_all(value, axis, split_axis=0, concat_axis=0, tiled=True, axis...  25.6 us
    all_to_all x3, starting transfers between devices, exchange(): lax.all_to_all(value, axis, split_axis=0, concat_axis=0, tiled=True, axis...  23.6 us
    ppermute x6, starting transfers between devices, local(): lax.ppermute(value, 'cell', pairs)  6.68 us
    ppermute x6, waiting for transfers between devices, local(): lax.ppermute(value, 'cell', pairs)  4.29 us
    pallas_call x1, Pallas kernels, prepare(): pl.pallas_call(prepare_kernel, in_specs=[smem()] + [hbm()] * len(arrays),...  3.41 us
    all_to_all x3, waiting for transfers between devices, exchange(): lax.all_to_all(value, axis, split_axis=0, concat_axis=0, tiled=True, axis...  2.61 us
    pallas_call x1, Pallas kernels, update(): pl.pallas_call(update_kernel, in_specs=[smem(), smem()] + [vmem()] * 7, o...  2.58 us
    ppermute x1, starting transfers between devices, local(): other = lax.ppermute(mine, 'cell', OTHER_CORE)  2.39 us
  transfers between devices with their start and end apart: 12, of which 6 were waited for; matrix products, arithmetic and copies ran while one was open for 0% of the time, Pallas kernels for 7%

profile of v12, /device:TPU:1, one launch (start us, length us, event | category | flops | bytes accessed | tf_op | source)
XLA Modules:
  0.0 84.6 jit_solution(2762248831748958583)
XLA Ops:
  0.6 2.3 %cell_totals.1 = f32[8,8,128]{2,1,0:T(8,128)} custom-call(s32[384,1024]{1,0:T(8,128)} %counts_hbm.1), custom_call_target="tpu_custom_call" | custom-call | tf_op jit(solution)/shard_map/cell_totals/pallas_call | solution.py:87
  2.9 10.6 %all-to-all-start = ((f32[8,8,128]{2,1,0:T(8,128)}), f32[8,8,128]{2,1,0:T(8,128)S(1)}, u32[]{:S(2)}, u32[]{:S(2)}) async-start(f32[8,8,128]{2,1,0:T(8,128)} %cell_totals.1), calls=%async_computation | async-start | bytes 65536 | tf_op jit(solution)/shard_map/all_to_all | solution.py:499
  14.1 3.4 %prepare.1 = (f32[384,1024]{1,0:T(8,128)S(1)}, bf16[96,1024]{1,0:T(8,128)(2,1)S(1)}, f32[384,128]{1,0:T(8,128)S(1)}, f32[64,1024]{1,0:T(8,128)S(1)}, f32[64,384]{1,0:T(8,128)S(1)}) custom-call(s32[1]{0:T(128)S(6)} %copy.17.live_ref, s32[384,1024]{1,0:T(8,128)} %counts_hbm.1, s32[1,1024]{1,0:T(1,128)} %bitcast.25, f32[1,1024]{1,0:T(1,128)} %bitcast.26, ...), custom_call_target="tpu_custom_call" | custom-call | tf_op jit(solution)/shard_map/prepare/pallas_call | solution.py:167
  17.5 0.0 all-to-all-done.tot_ref
  17.5 1.6 %gram_given.1 = (f32[384,1024]{1,0:T(8,128)S(1)}, bf16[512,1024]{1,0:T(8,128)(2,1)S(1)}, bf16[512,1024]{1,0:T(8,128)(2,1)S(1)}, f32[16,48,128]{2,1,0:T(8,128)S(1)}) custom-call(s32[1]{0:T(128)S(6)} %copy.17.live_ref, s32[1]{0:T(128)S(6)} %sub.3.half_ref, f32[8,8,128]{2,1,0:T(8,128)S(1)} %all-to-all-done.tot_ref, f32[384,1024]{1,0:T(8,128)S(1)} %get-tuple-element.16.rest_ref, ...), custom_call_target="tpu_custom_call" | custom-call | tf_op jit(solution)/shard_map/gram_given/pallas_call | solution.py:254
  19.1 1.0 %collective-permute-start = (f32[16,48,128]{2,1,0:T(8,128)S(1)}, f32[16,48,128]{2,1,0:T(8,128)S(1)}, u32[]{:S(2)}, u32[]{:S(2)}) collective-permute-start(f32[16,48,128]{2,1,0:T(8,128)S(1)} %get-tuple-element.22), channel_id=1, source_target_pairs={{0,8},{8,0},{16,24},{24,16},{32,40},{40,32},{48,56},{56,48},{64,72... | collective-permute-start | bytes 1179656 | tf_op jit(solution)/shard_map/ppermute | solution.py:268
  20.2 1.3 %gram_kept.1 = f32[16,48,128]{2,1,0:T(8,128)S(1)} custom-call(s32[1]{0:T(128)S(6)} %copy.17.live_ref, s32[1]{0:T(128)} %bitcast.half_ref.core_ref, f32[384,1024]{1,0:T(8,128)S(1)} %get-tuple-element.19.pred_ref, f32[384,128]{1,0:T(8,128)S(1)} %get-tuple-element.18.score_ref, bf16[512,1024]{1,0:T(8,128)(2,1)S(1)} %get-tuple-element.20.hi_ref, ...), custom_call_target="tpu_custom_call" | custom-call | tf_op jit(solution)/shard_map/gram_kept/pallas_call | solution.py:269
  21.5 0.0 copy-start
  21.5 0.0 copy-start.1
  21.5 0.0 collective-permute-done
  21.6 13.5 %all_to_all.25.parts_ref = f32[16,48,128]{2,1,0:T(8,128)S(1)} all-to-all(f32[16,48,128]{2,1,0:T(8,128)S(1)} %add.35), channel_id=1, replica_groups={{224,32,160,208,240,16,48,96,144,176,192,0,80,112,128,64},{232,40,168,2..., dimensions={0} | all-to-all | bytes 786432 | tf_op jit(solution)/shard_map/all_to_all | solution.py:499
  35.0 1.0 %solve.1 = f32[32,1,384]{2,1,0:T(1,128)S(1)} custom-call(f32[16,48,128]{2,1,0:T(8,128)S(1)} %all_to_all.25.parts_ref), custom_call_target="tpu_custom_call" | custom-call | tf_op jit(solution)/shard_map/solve/pallas_call | solution.py:327
  36.0 12.1 %all_to_all.26 = f32[32,1,384]{2,1,0:T(1,128)S(1)} all-to-all(f32[32,1,384]{2,1,0:T(1,128)S(1)} %solve.1), channel_id=1, replica_groups={{224,32,160,208,240,16,48,96,144,176,192,0,80,112,128,64,232,40,168,216..., dimensions={0} | all-to-all | bytes 98304 | tf_op jit(solution)/shard_map/all_to_all | solution.py:499
  48.1 0.0 copy-done
  48.1 0.0 copy-done.1
  48.2 2.6 %update.1 = (f32[8,16,1024]{2,1,0:T(8,128)}, f32[64,384]{1,0:T(8,128)S(1)}, f32[64,384]{1,0:T(8,128)S(1)}, f32[32,384]{1,0:T(8,128)}) custom-call(s32[1]{0:T(128)S(6)} %copy.17.live_ref, s32[1]{0:T(128)} %bitcast.half_ref.core_ref, f32[32,384]{1,0:T(8,128)S(1)} %bitcast.18, f32[384,1024]{1,0:T(8,128)S(1)} %get-tuple-element.19.pred_ref, ...), custom_call_target="tpu_custom_call" | custom-call | tf_op jit(solution)/shard_map/update/pallas_call | solution.py:401
  50.7 7.0 %all-to-all-start.3 = ((f32[8,16,1024]{2,1,0:T(8,128)}), f32[8,16,1024]{2,1,0:T(8,128)S(1)}, u32[]{:S(2)}, u32[]{:S(2)}) async-start(f32[8,16,1024]{2,1,0:T(8,128)} %get-tuple-element.26), calls=%async_computation.3 | async-start | bytes 1048576 | tf_op jit(solution)/shard_map/all_to_all | solution.py:499
  57.8 0.7 collective-permute-start.1
  58.5 0.9 %collective-permute-done.1 = f32[64,384]{1,0:T(8,128)S(1)} collective-permute-done((f32[64,384]{1,0:T(8,128)S(1)}, f32[64,384]{1,0:T(8,128)S(1)}, u32[]{:S(2)}, u32[]{:S(2)}) %collective-permute-start.1) | collective-permute-done | bytes 98336 | tf_op jit(solution)/shard_map/ppermute | solution.py:558
  59.4 2.4 %collective-permute-start.4 = (f32[64,384]{1,0:T(8,128)S(1)}, f32[64,384]{1,0:T(8,128)S(1)}, u32[]{:S(2)}, u32[]{:S(2)}) collective-permute-start(f32[64,384]{1,0:T(8,128)S(1)} %add.36), channel_id=1, source_target_pairs={{0,192},{8,56},{16,208},{24,40},{32,224},{40,24},{48,240},{56,8},{... | collective-permute-start | bytes 294920 | tf_op jit(solution)/shard_map/ppermute | solution.py:560
  61.8 0.7 collective-permute-start.3
  62.5 0.3 collective-permute-start.2
  62.8 1.7 %collective-permute-done.4 = f32[64,384]{1,0:T(8,128)S(1)} collective-permute-done((f32[64,384]{1,0:T(8,128)S(1)}, f32[64,384]{1,0:T(8,128)S(1)}, u32[]{:S(2)}, u32[]{:S(2)}) %collective-permute-start.4) | collective-permute-done | bytes 98336 | tf_op jit(solution)/shard_map/ppermute | solution.py:560
  64.5 2.6 %collective-permute-done.3 = f32[64,384]{1,0:T(8,128)S(1)} collective-permute-done((f32[64,384]{1,0:T(8,128)S(1)}, f32[64,384]{1,0:T(8,128)S(1)}, u32[]{:S(2)}, u32[]{:S(2)}) %collective-permute-start.3) | collective-permute-done | bytes 98336 | tf_op jit(solution)/shard_map/ppermute | solution.py:560
  67.0 0.0 collective-permute-done.2
  67.1 2.1 %collective-permute-start.7 = (f32[64,384]{1,0:T(8,128)S(1)}, f32[64,384]{1,0:T(8,128)S(1)}, u32[]{:S(2)}, u32[]{:S(2)}) collective-permute-start(f32[64,384]{1,0:T(8,128)S(1)} %add_add_fusion.1), channel_id=1, source_target_pairs={{0,48},{8,200},{16,32},{24,216},{32,16},{40,232},{48,0},{56,248},{... | collective-permute-start | bytes 294920 | tf_op jit(solution)/shard_map/ppermute | solution.py:560
  69.2 0.2 collective-permute-start.6
  69.4 1.0 %collective-permute-start.5 = (f32[64,384]{1,0:T(8,128)S(1)}, f32[64,384]{1,0:T(8,128)S(1)}, u32[]{:S(2)}, u32[]{:S(2)}) collective-permute-start(f32[64,384]{1,0:T(8,128)S(1)} %add_add_fusion.1), channel_id=1, source_target_pairs={{0,16},{8,72},{16,0},{24,88},{32,48},{40,104},{48,32},{56,120},{64... | collective-permute-start | bytes 294920 | tf_op jit(solution)/shard_map/ppermute | solution.py:560
  70.4 0.9 %all-to-all-done.3.parts_ref = f32[8,16,1024]{2,1,0:T(8,128)S(1)} async-done(((f32[8,16,1024]{2,1,0:T(8,128)}), f32[8,16,1024]{2,1,0:T(8,128)S(1)}, u32[]{:S(2)}, u32[]{:S(2)}) %all-to-all-start.3) | async-done | bytes 524320 | tf_op jit(solution)/shard_map/all_to_all | solution.py:499
  71.3 0.8 factor_share.1
  72.1 6.0 %all-to-all-start.4 = ((f32[8,8,1024]{2,1,0:T(8,128)}), f32[8,8,1024]{2,1,0:T(8,128)S(1)}, u32[]{:S(2)}, u32[]{:S(2)}) async-start(f32[8,8,1024]{2,1,0:T(8,128)} %factor_share.1), calls=%async_computation.4 | async-start | bytes 524288 | tf_op jit(solution)/shard_map/all_to_all | solution.py:499
  78.1 0.0 collective-permute-done.7
  78.1 0.0 collective-permute-done.6
  78.1 0.0 collective-permute-done.5
  78.2 2.4 %collective-permute-start.8 = (f32[32,384]{1,0:T(8,128)S(1)}, f32[32,384]{1,0:T(8,128)S(1)}, u32[]{:S(2)}, u32[]{:S(2)}) collective-permute-start(f32[32,384]{1,0:T(8,128)S(1)} %fusion.1.mine_ref), channel_id=1, source_target_pairs={{0,8},{8,0},{16,24},{24,16},{32,40},{40,32},{48,56},{56,48},{64,72... | collective-permute-start | bytes 147464 | tf_op jit(solution)/shard_map/ppermute | solution.py:564
  80.6 0.9 %collective-permute-done.8.other_ref = f32[32,384]{1,0:T(8,128)S(1)} collective-permute-done((f32[32,384]{1,0:T(8,128)S(1)}, f32[32,384]{1,0:T(8,128)S(1)}, u32[]{:S(2)}, u32[]{:S(2)}) %collective-permute-start.8) | collective-permute-done | bytes 49184 | tf_op jit(solution)/shard_map/ppermute | solution.py:564
  81.5 0.7 joined_score.1
  82.1 1.7 %all-to-all-done.4.value_ref = f32[8,8,1024]{2,1,0:T(8,128)S(1)} async-done(((f32[8,8,1024]{2,1,0:T(8,128)}), f32[8,8,1024]{2,1,0:T(8,128)S(1)}, u32[]{:S(2)}, u32[]{:S(2)}) %all-to-all-start.4) | async-done | bytes 262176 | tf_op jit(solution)/shard_map/all_to_all | solution.py:499
  83.8 0.8 settled.1
  (6 shorter events, 0.1 us)
Async XLA Ops:
  2.9 14.7 %all-to-all-start = ((f32[8,8,128]{2,1,0:T(8,128)}), f32[8,8,128]{2,1,0:T(8,128)S(1)}, u32[]{:S(2)}, u32[]{:S(2)}) async-start(f32[8,8,128]{2,1,0:T(8,128)} %cell_totals.1), calls=%async_computation | async-start | bytes 65536 | tf_op jit(solution)/shard_map/all_to_all | solution.py:499
  19.1 2.4 %collective-permute-start = (f32[16,48,128]{2,1,0:T(8,128)S(1)}, f32[16,48,128]{2,1,0:T(8,128)S(1)}, u32[]{:S(2)}, u32[]{:S(2)}) collective-permute-start(f32[16,48,128]{2,1,0:T(8,128)S(1)} %get-tuple-element.22), channel_id=1, source_target_pairs={{0,8},{8,0},{16,24},{24,16},{32,40},{40,32},{48,56},{56,48},{64,72... | collective-permute-start | bytes 1179656 | tf_op jit(solution)/shard_map/ppermute | solution.py:268
  21.5 26.7 %copy-start = (bf16[1024,64]{0,1:T(8,128)(2,1)S(1)}, bf16[1024,64]{0,1:T(8,128)(2,1)}, u32[]{:S(2)}) copy-start(bf16[1024,64]{0,1:T(8,128)(2,1)} %param.18) | copy-start | bytes 393220
  21.5 26.7 %copy-start.1 = (bf16[384,64]{0,1:T(8,128)(2,1)S(1)}, bf16[384,64]{0,1:T(8,128)(2,1)}, u32[]{:S(2)}) copy-start(bf16[384,64]{0,1:T(8,128)(2,1)} %param.19) | copy-start | bytes 147460
  50.7 20.6 %all-to-all-start.3 = ((f32[8,16,1024]{2,1,0:T(8,128)}), f32[8,16,1024]{2,1,0:T(8,128)S(1)}, u32[]{:S(2)}, u32[]{:S(2)}) async-start(f32[8,16,1024]{2,1,0:T(8,128)} %get-tuple-element.26), calls=%async_computation.3 | async-start | bytes 1048576 | tf_op jit(solution)/shard_map/all_to_all | solution.py:499
  57.8 1.6 %collective-permute-start.1 = (f32[64,384]{1,0:T(8,128)S(1)}, f32[64,384]{1,0:T(8,128)S(1)}, u32[]{:S(2)}, u32[]{:S(2)}) collective-permute-start(f32[64,384]{1,0:T(8,128)S(1)} %get-tuple-element.28), channel_id=1, source_target_pairs={{0,8},{8,0},{16,24},{24,16},{32,40},{40,32},{48,56},{56,48},{64,72... | collective-permute-start | bytes 294920 | tf_op jit(solution)/shard_map/ppermute | solution.py:558
  59.4 5.1 %collective-permute-start.4 = (f32[64,384]{1,0:T(8,128)S(1)}, f32[64,384]{1,0:T(8,128)S(1)}, u32[]{:S(2)}, u32[]{:S(2)}) collective-permute-start(f32[64,384]{1,0:T(8,128)S(1)} %add.36), channel_id=1, source_target_pairs={{0,192},{8,56},{16,208},{24,40},{32,224},{40,24},{48,240},{56,8},{... | collective-permute-start | bytes 294920 | tf_op jit(solution)/shard_map/ppermute | solution.py:560
  61.8 5.3 %collective-permute-start.3 = (f32[64,384]{1,0:T(8,128)S(1)}, f32[64,384]{1,0:T(8,128)S(1)}, u32[]{:S(2)}, u32[]{:S(2)}) collective-permute-start(f32[64,384]{1,0:T(8,128)S(1)} %add.36), channel_id=1, source_target_pairs={{0,128},{8,40},{16,144},{24,56},{32,160},{40,8},{48,176},{56,24},{... | collective-permute-start | bytes 294920 | tf_op jit(solution)/shard_map/ppermute | solution.py:560
  62.5 4.6 %collective-permute-start.2 = (f32[64,384]{1,0:T(8,128)S(1)}, f32[64,384]{1,0:T(8,128)S(1)}, u32[]{:S(2)}, u32[]{:S(2)}) collective-permute-start(f32[64,384]{1,0:T(8,128)S(1)} %add.36), channel_id=1, source_target_pairs={{0,64},{8,24},{16,80},{24,8},{32,96},{40,56},{48,112},{56,40},{64,... | collective-permute-start | bytes 294920 | tf_op jit(solution)/shard_map/ppermute | solution.py:560
  67.1 11.0 %collective-permute-start.7 = (f32[64,384]{1,0:T(8,128)S(1)}, f32[64,384]{1,0:T(8,128)S(1)}, u32[]{:S(2)}, u32[]{:S(2)}) collective-permute-start(f32[64,384]{1,0:T(8,128)S(1)} %add_add_fusion.1), channel_id=1, source_target_pairs={{0,48},{8,200},{16,32},{24,216},{32,16},{40,232},{48,0},{56,248},{... | collective-permute-start | bytes 294920 | tf_op jit(solution)/shard_map/ppermute | solution.py:560
  69.2 8.9 %collective-permute-start.6 = (f32[64,384]{1,0:T(8,128)S(1)}, f32[64,384]{1,0:T(8,128)S(1)}, u32[]{:S(2)}, u32[]{:S(2)}) collective-permute-start(f32[64,384]{1,0:T(8,128)S(1)} %add_add_fusion.1), channel_id=1, source_target_pairs={{0,32},{8,136},{16,48},{24,152},{32,0},{40,168},{48,16},{56,184},{... | collective-permute-start | bytes 294920 | tf_op jit(solution)/shard_map/ppermute | solution.py:560
  69.4 8.7 %collective-permute-start.5 = (f32[64,384]{1,0:T(8,128)S(1)}, f32[64,384]{1,0:T(8,128)S(1)}, u32[]{:S(2)}, u32[]{:S(2)}) collective-permute-start(f32[64,384]{1,0:T(8,128)S(1)} %add_add_fusion.1), channel_id=1, source_target_pairs={{0,16},{8,72},{16,0},{24,88},{32,48},{40,104},{48,32},{56,120},{64... | collective-permute-start | bytes 294920 | tf_op jit(solution)/shard_map/ppermute | solution.py:560
  72.1 11.7 %all-to-all-start.4 = ((f32[8,8,1024]{2,1,0:T(8,128)}), f32[8,8,1024]{2,1,0:T(8,128)S(1)}, u32[]{:S(2)}, u32[]{:S(2)}) async-start(f32[8,8,1024]{2,1,0:T(8,128)} %factor_share.1), calls=%async_computation.4 | async-start | bytes 524288 | tf_op jit(solution)/shard_map/all_to_all | solution.py:499
  78.2 3.3 %collective-permute-start.8 = (f32[32,384]{1,0:T(8,128)S(1)}, f32[32,384]{1,0:T(8,128)S(1)}, u32[]{:S(2)}, u32[]{:S(2)}) collective-permute-start(f32[32,384]{1,0:T(8,128)S(1)} %fusion.1.mine_ref), channel_id=1, source_target_pairs={{0,8},{8,0},{16,24},{24,16},{32,40},{40,32},{48,56},{56,48},{64,72... | collective-permute-start | bytes 147464 | tf_op jit(solution)/shard_map/ppermute | solution.py:564

commit v13 on v12

--- a/solution.py
+++ b/solution.py
@@ -517,14 +517,17 @@
     return [min((i - at) % size, (at - i) % size) for i in range(size)]
 
 
-def nearest_first(x, y):
+def nearest_first(x, y, core):
     far_x, far_y = around(x, 4), around(y, 4)
-    chips = [(i, j) for i in range(4) for j in range(4)]
+    chips = [(i, j) if core == 0 else (j, i) for i in range(4) for j in range(4)]
     return sorted(chips, key=lambda chip: far_x[chip[0]] + far_y[chip[1]])
 
 
 FIRST = (3, 2, 5)
-SAME_CORE = [[(4 * x + y) * 2 + core for x, y in nearest_first(*FIRST[:2])] for core in range(2)]
+SAME_CORE = [
+    [(4 * x + y) * 2 + core for x, y in nearest_first(*FIRST[:2], core)]
+    for core in range(2)
+]
 CORE_FIRST = [SAME_CORE[0] + SAME_CORE[1]]
 RING = [[(FIRST[2] + step) % 8 for step in (0, 1, -1, 2, -2, 3, -3, 4)]]
 OTHER_CORE = partners(lambda x, y, c: (x, y, 1 - c))

time: 86 us -> 86.1 us (level)
  no operation moved by 1% of the time
where the time goes in v13:
time: 86.1 us; the launch traced here: 84.6 us
  starting transfers between devices  34.4 us (40%)
  blocking collectives  25.6 us (30%)
  Pallas kernels  14.3 us (17%)
  waiting for transfers between devices  8.76 us (10%)
  between operations  1.43 us (2%)
    all_to_all x2, blocking collectives, exchange(): lax.all_to_all(value, axis, split_axis=0, concat_axis=0, tiled=True, axis...  25.6 us
    all_to_all x3, starting transfers between devices, exchange(): lax.all_to_all(value, axis, split_axis=0, concat_axis=0, tiled=True, axis...  23.6 us
    ppermute x6, starting transfers between devices, local(): lax.ppermute(value, 'cell', pairs)  6.68 us
    ppermute x6, waiting for transfers between devices, local(): lax.ppermute(value, 'cell', pairs)  4.31 us
    pallas_call x1, Pallas kernels, prepare(): pl.pallas_call(prepare_kernel, in_specs=[smem()] + [hbm()] * len(arrays),...  3.41 us
    all_to_all x3, waiting for transfers between devices, exchange(): lax.all_to_all(value, axis, split_axis=0, concat_axis=0, tiled=True, axis...  2.6 us
    pallas_call x1, Pallas kernels, update(): pl.pallas_call(update_kernel, in_specs=[smem(), smem()] + [vmem()] * 7, o...  2.58 us
    ppermute x1, starting transfers between devices, local(): other = lax.ppermute(mine, 'cell', OTHER_CORE)  2.39 us
  transfers between devices with their start and end apart: 12, of which 6 were waited for; matrix products, arithmetic and copies ran while one was open for 0% of the time, Pallas kernels for 7%

profile of v13, /device:TPU:1, one launch (start us, length us, event | category | flops | bytes accessed | tf_op | source)
XLA Modules:
  0.0 84.6 jit_solution(16207393393192145737)
XLA Ops:
  0.6 2.3 %cell_totals.1 = f32[8,8,128]{2,1,0:T(8,128)} custom-call(s32[384,1024]{1,0:T(8,128)} %counts_hbm.1), custom_call_target="tpu_custom_call" | custom-call | tf_op jit(solution)/shard_map/cell_totals/pallas_call | solution.py:87
  2.9 10.6 %all-to-all-start = ((f32[8,8,128]{2,1,0:T(8,128)}), f32[8,8,128]{2,1,0:T(8,128)S(1)}, u32[]{:S(2)}, u32[]{:S(2)}) async-start(f32[8,8,128]{2,1,0:T(8,128)} %cell_totals.1), calls=%async_computation | async-start | bytes 65536 | tf_op jit(solution)/shard_map/all_to_all | solution.py:499
  14.1 3.4 %prepare.1 = (f32[384,1024]{1,0:T(8,128)S(1)}, bf16[96,1024]{1,0:T(8,128)(2,1)S(1)}, f32[384,128]{1,0:T(8,128)S(1)}, f32[64,1024]{1,0:T(8,128)S(1)}, f32[64,384]{1,0:T(8,128)S(1)}) custom-call(s32[1]{0:T(128)S(6)} %copy.17.live_ref, s32[384,1024]{1,0:T(8,128)} %counts_hbm.1, s32[1,1024]{1,0:T(1,128)} %bitcast.25, f32[1,1024]{1,0:T(1,128)} %bitcast.26, ...), custom_call_target="tpu_custom_call" | custom-call | tf_op jit(solution)/shard_map/prepare/pallas_call | solution.py:167
  17.5 0.0 all-to-all-done.tot_ref
  17.5 1.6 %gram_given.1 = (f32[384,1024]{1,0:T(8,128)S(1)}, bf16[512,1024]{1,0:T(8,128)(2,1)S(1)}, bf16[512,1024]{1,0:T(8,128)(2,1)S(1)}, f32[16,48,128]{2,1,0:T(8,128)S(1)}) custom-call(s32[1]{0:T(128)S(6)} %copy.17.live_ref, s32[1]{0:T(128)S(6)} %sub.3.half_ref, f32[8,8,128]{2,1,0:T(8,128)S(1)} %all-to-all-done.tot_ref, f32[384,1024]{1,0:T(8,128)S(1)} %get-tuple-element.16.rest_ref, ...), custom_call_target="tpu_custom_call" | custom-call | tf_op jit(solution)/shard_map/gram_given/pallas_call | solution.py:254
  19.1 1.0 %collective-permute-start = (f32[16,48,128]{2,1,0:T(8,128)S(1)}, f32[16,48,128]{2,1,0:T(8,128)S(1)}, u32[]{:S(2)}, u32[]{:S(2)}) collective-permute-start(f32[16,48,128]{2,1,0:T(8,128)S(1)} %get-tuple-element.22), channel_id=1, source_target_pairs={{0,8},{8,0},{16,24},{24,16},{32,40},{40,32},{48,56},{56,48},{64,72... | collective-permute-start | bytes 1179656 | tf_op jit(solution)/shard_map/ppermute | solution.py:268
  20.2 1.3 %gram_kept.1 = f32[16,48,128]{2,1,0:T(8,128)S(1)} custom-call(s32[1]{0:T(128)S(6)} %copy.17.live_ref, s32[1]{0:T(128)} %bitcast.half_ref.core_ref, f32[384,1024]{1,0:T(8,128)S(1)} %get-tuple-element.19.pred_ref, f32[384,128]{1,0:T(8,128)S(1)} %get-tuple-element.18.score_ref, bf16[512,1024]{1,0:T(8,128)(2,1)S(1)} %get-tuple-element.20.hi_ref, ...), custom_call_target="tpu_custom_call" | custom-call | tf_op jit(solution)/shard_map/gram_kept/pallas_call | solution.py:269
  21.5 0.0 copy-start
  21.5 0.0 copy-start.1
  21.5 0.0 collective-permute-done
  21.6 13.7 %all_to_all.25.parts_ref = f32[16,48,128]{2,1,0:T(8,128)S(1)} all-to-all(f32[16,48,128]{2,1,0:T(8,128)S(1)} %add.35), channel_id=1, replica_groups={{224,32,160,208,240,16,48,96,144,176,192,0,80,112,128,64},{232,216,40,1..., dimensions={0} | all-to-all | bytes 786432 | tf_op jit(solution)/shard_map/all_to_all | solution.py:499
  35.3 1.0 %solve.1 = f32[32,1,384]{2,1,0:T(1,128)S(1)} custom-call(f32[16,48,128]{2,1,0:T(8,128)S(1)} %all_to_all.25.parts_ref), custom_call_target="tpu_custom_call" | custom-call | tf_op jit(solution)/shard_map/solve/pallas_call | solution.py:327
  36.3 11.9 %all_to_all.26 = f32[32,1,384]{2,1,0:T(1,128)S(1)} all-to-all(f32[32,1,384]{2,1,0:T(1,128)S(1)} %solve.1), channel_id=1, replica_groups={{224,32,160,208,240,16,48,96,144,176,192,0,80,112,128,64,232,216,40,168..., dimensions={0} | all-to-all | bytes 98304 | tf_op jit(solution)/shard_map/all_to_all | solution.py:499
  48.1 0.0 copy-done
  48.1 0.0 copy-done.1
  48.2 2.6 %update.1 = (f32[8,16,1024]{2,1,0:T(8,128)}, f32[64,384]{1,0:T(8,128)S(1)}, f32[64,384]{1,0:T(8,128)S(1)}, f32[32,384]{1,0:T(8,128)}) custom-call(s32[1]{0:T(128)S(6)} %copy.17.live_ref, s32[1]{0:T(128)} %bitcast.half_ref.core_ref, f32[32,384]{1,0:T(8,128)S(1)} %bitcast.18, f32[384,1024]{1,0:T(8,128)S(1)} %get-tuple-element.19.pred_ref, ...), custom_call_target="tpu_custom_call" | custom-call | tf_op jit(solution)/shard_map/update/pallas_call | solution.py:401
  50.7 7.0 %all-to-all-start.3 = ((f32[8,16,1024]{2,1,0:T(8,128)}), f32[8,16,1024]{2,1,0:T(8,128)S(1)}, u32[]{:S(2)}, u32[]{:S(2)}) async-start(f32[8,16,1024]{2,1,0:T(8,128)} %get-tuple-element.26), calls=%async_computation.3 | async-start | bytes 1048576 | tf_op jit(solution)/shard_map/all_to_all | solution.py:499
  57.8 0.7 collective-permute-start.1
  58.5 0.9 %collective-permute-done.1 = f32[64,384]{1,0:T(8,128)S(1)} collective-permute-done((f32[64,384]{1,0:T(8,128)S(1)}, f32[64,384]{1,0:T(8,128)S(1)}, u32[]{:S(2)}, u32[]{:S(2)}) %collective-permute-start.1) | collective-permute-done | bytes 98336 | tf_op jit(solution)/shard_map/ppermute | solution.py:561
  59.4 2.4 %collective-permute-start.4 = (f32[64,384]{1,0:T(8,128)S(1)}, f32[64,384]{1,0:T(8,128)S(1)}, u32[]{:S(2)}, u32[]{:S(2)}) collective-permute-start(f32[64,384]{1,0:T(8,128)S(1)} %add.36), channel_id=1, source_target_pairs={{0,192},{8,56},{16,208},{24,40},{32,224},{40,24},{48,240},{56,8},{... | collective-permute-start | bytes 294920 | tf_op jit(solution)/shard_map/ppermute | solution.py:563
  61.8 0.7 collective-permute-start.3
  62.5 0.2 collective-permute-start.2
  62.8 1.7 %collective-permute-done.4 = f32[64,384]{1,0:T(8,128)S(1)} collective-permute-done((f32[64,384]{1,0:T(8,128)S(1)}, f32[64,384]{1,0:T(8,128)S(1)}, u32[]{:S(2)}, u32[]{:S(2)}) %collective-permute-start.4) | collective-permute-done | bytes 98336 | tf_op jit(solution)/shard_map/ppermute | solution.py:563
  64.5 2.6 %collective-permute-done.3 = f32[64,384]{1,0:T(8,128)S(1)} collective-permute-done((f32[64,384]{1,0:T(8,128)S(1)}, f32[64,384]{1,0:T(8,128)S(1)}, u32[]{:S(2)}, u32[]{:S(2)}) %collective-permute-start.3) | collective-permute-done | bytes 98336 | tf_op jit(solution)/shard_map/ppermute | solution.py:563
  67.1 0.0 collective-permute-done.2
  67.1 2.1 %collective-permute-start.7 = (f32[64,384]{1,0:T(8,128)S(1)}, f32[64,384]{1,0:T(8,128)S(1)}, u32[]{:S(2)}, u32[]{:S(2)}) collective-permute-start(f32[64,384]{1,0:T(8,128)S(1)} %add_add_fusion.1), channel_id=1, source_target_pairs={{0,48},{8,200},{16,32},{24,216},{32,16},{40,232},{48,0},{56,248},{... | collective-permute-start | bytes 294920 | tf_op jit(solution)/shard_map/ppermute | solution.py:563
  69.2 0.2 collective-permute-start.6
  69.4 1.1 %collective-permute-start.5 = (f32[64,384]{1,0:T(8,128)S(1)}, f32[64,384]{1,0:T(8,128)S(1)}, u32[]{:S(2)}, u32[]{:S(2)}) collective-permute-start(f32[64,384]{1,0:T(8,128)S(1)} %add_add_fusion.1), channel_id=1, source_target_pairs={{0,16},{8,72},{16,0},{24,88},{32,48},{40,104},{48,32},{56,120},{64... | collective-permute-start | bytes 294920 | tf_op jit(solution)/shard_map/ppermute | solution.py:563
  70.4 0.9 %all-to-all-done.3.parts_ref = f32[8,16,1024]{2,1,0:T(8,128)S(1)} async-done(((f32[8,16,1024]{2,1,0:T(8,128)}), f32[8,16,1024]{2,1,0:T(8,128)S(1)}, u32[]{:S(2)}, u32[]{:S(2)}) %all-to-all-start.3) | async-done | bytes 524320 | tf_op jit(solution)/shard_map/all_to_all | solution.py:499
  71.3 0.8 factor_share.1
  72.1 6.0 %all-to-all-start.4 = ((f32[8,8,1024]{2,1,0:T(8,128)}), f32[8,8,1024]{2,1,0:T(8,128)S(1)}, u32[]{:S(2)}, u32[]{:S(2)}) async-start(f32[8,8,1024]{2,1,0:T(8,128)} %factor_share.1), calls=%async_computation.4 | async-start | bytes 524288 | tf_op jit(solution)/shard_map/all_to_all | solution.py:499
  78.1 0.0 collective-permute-done.7
  78.1 0.0 collective-permute-done.6
  78.1 0.0 collective-permute-done.5
  78.2 2.4 %collective-permute-start.8 = (f32[32,384]{1,0:T(8,128)S(1)}, f32[32,384]{1,0:T(8,128)S(1)}, u32[]{:S(2)}, u32[]{:S(2)}) collective-permute-start(f32[32,384]{1,0:T(8,128)S(1)} %fusion.1.mine_ref), channel_id=1, source_target_pairs={{0,8},{8,0},{16,24},{24,16},{32,40},{40,32},{48,56},{56,48},{64,72... | collective-permute-start | bytes 147464 | tf_op jit(solution)/shard_map/ppermute | solution.py:567
  80.6 0.9 %collective-permute-done.8.other_ref = f32[32,384]{1,0:T(8,128)S(1)} collective-permute-done((f32[32,384]{1,0:T(8,128)S(1)}, f32[32,384]{1,0:T(8,128)S(1)}, u32[]{:S(2)}, u32[]{:S(2)}) %collective-permute-start.8) | collective-permute-done | bytes 49184 | tf_op jit(solution)/shard_map/ppermute | solution.py:567
  81.5 0.7 joined_score.1
  82.1 1.7 %all-to-all-done.4.value_ref = f32[8,8,1024]{2,1,0:T(8,128)S(1)} async-done(((f32[8,8,1024]{2,1,0:T(8,128)}), f32[8,8,1024]{2,1,0:T(8,128)S(1)}, u32[]{:S(2)}, u32[]{:S(2)}) %all-to-all-start.4) | async-done | bytes 262176 | tf_op jit(solution)/shard_map/all_to_all | solution.py:499
  83.8 0.8 settled.1
  (6 shorter events, 0.1 us)
Async XLA Ops:
  2.9 14.7 %all-to-all-start = ((f32[8,8,128]{2,1,0:T(8,128)}), f32[8,8,128]{2,1,0:T(8,128)S(1)}, u32[]{:S(2)}, u32[]{:S(2)}) async-start(f32[8,8,128]{2,1,0:T(8,128)} %cell_totals.1), calls=%async_computation | async-start | bytes 65536 | tf_op jit(solution)/shard_map/all_to_all | solution.py:499
  19.1 2.4 %collective-permute-start = (f32[16,48,128]{2,1,0:T(8,128)S(1)}, f32[16,48,128]{2,1,0:T(8,128)S(1)}, u32[]{:S(2)}, u32[]{:S(2)}) collective-permute-start(f32[16,48,128]{2,1,0:T(8,128)S(1)} %get-tuple-element.22), channel_id=1, source_target_pairs={{0,8},{8,0},{16,24},{24,16},{32,40},{40,32},{48,56},{56,48},{64,72... | collective-permute-start | bytes 1179656 | tf_op jit(solution)/shard_map/ppermute | solution.py:268
  21.5 26.7 %copy-start = (bf16[1024,64]{0,1:T(8,128)(2,1)S(1)}, bf16[1024,64]{0,1:T(8,128)(2,1)}, u32[]{:S(2)}) copy-start(bf16[1024,64]{0,1:T(8,128)(2,1)} %param.18) | copy-start | bytes 393220
  21.5 26.7 %copy-start.1 = (bf16[384,64]{0,1:T(8,128)(2,1)S(1)}, bf16[384,64]{0,1:T(8,128)(2,1)}, u32[]{:S(2)}) copy-start(bf16[384,64]{0,1:T(8,128)(2,1)} %param.19) | copy-start | bytes 147460
  50.7 20.6 %all-to-all-start.3 = ((f32[8,16,1024]{2,1,0:T(8,128)}), f32[8,16,1024]{2,1,0:T(8,128)S(1)}, u32[]{:S(2)}, u32[]{:S(2)}) async-start(f32[8,16,1024]{2,1,0:T(8,128)} %get-tuple-element.26), calls=%async_computation.3 | async-start | bytes 1048576 | tf_op jit(solution)/shard_map/all_to_all | solution.py:499
  57.8 1.6 %collective-permute-start.1 = (f32[64,384]{1,0:T(8,128)S(1)}, f32[64,384]{1,0:T(8,128)S(1)}, u32[]{:S(2)}, u32[]{:S(2)}) collective-permute-start(f32[64,384]{1,0:T(8,128)S(1)} %get-tuple-element.28), channel_id=1, source_target_pairs={{0,8},{8,0},{16,24},{24,16},{32,40},{40,32},{48,56},{56,48},{64,72... | collective-permute-start | bytes 294920 | tf_op jit(solution)/shard_map/ppermute | solution.py:561
  59.4 5.1 %collective-permute-start.4 = (f32[64,384]{1,0:T(8,128)S(1)}, f32[64,384]{1,0:T(8,128)S(1)}, u32[]{:S(2)}, u32[]{:S(2)}) collective-permute-start(f32[64,384]{1,0:T(8,128)S(1)} %add.36), channel_id=1, source_target_pairs={{0,192},{8,56},{16,208},{24,40},{32,224},{40,24},{48,240},{56,8},{... | collective-permute-start | bytes 294920 | tf_op jit(solution)/shard_map/ppermute | solution.py:563
  61.8 5.3 %collective-permute-start.3 = (f32[64,384]{1,0:T(8,128)S(1)}, f32[64,384]{1,0:T(8,128)S(1)}, u32[]{:S(2)}, u32[]{:S(2)}) collective-permute-start(f32[64,384]{1,0:T(8,128)S(1)} %add.36), channel_id=1, source_target_pairs={{0,128},{8,40},{16,144},{24,56},{32,160},{40,8},{48,176},{56,24},{... | collective-permute-start | bytes 294920 | tf_op jit(solution)/shard_map/ppermute | solution.py:563
  62.5 4.6 %collective-permute-start.2 = (f32[64,384]{1,0:T(8,128)S(1)}, f32[64,384]{1,0:T(8,128)S(1)}, u32[]{:S(2)}, u32[]{:S(2)}) collective-permute-start(f32[64,384]{1,0:T(8,128)S(1)} %add.36), channel_id=1, source_target_pairs={{0,64},{8,24},{16,80},{24,8},{32,96},{40,56},{48,112},{56,40},{64,... | collective-permute-start | bytes 294920 | tf_op jit(solution)/shard_map/ppermute | solution.py:563
  67.1 11.0 %collective-permute-start.7 = (f32[64,384]{1,0:T(8,128)S(1)}, f32[64,384]{1,0:T(8,128)S(1)}, u32[]{:S(2)}, u32[]{:S(2)}) collective-permute-start(f32[64,384]{1,0:T(8,128)S(1)} %add_add_fusion.1), channel_id=1, source_target_pairs={{0,48},{8,200},{16,32},{24,216},{32,16},{40,232},{48,0},{56,248},{... | collective-permute-start | bytes 294920 | tf_op jit(solution)/shard_map/ppermute | solution.py:563
  69.2 8.9 %collective-permute-start.6 = (f32[64,384]{1,0:T(8,128)S(1)}, f32[64,384]{1,0:T(8,128)S(1)}, u32[]{:S(2)}, u32[]{:S(2)}) collective-permute-start(f32[64,384]{1,0:T(8,128)S(1)} %add_add_fusion.1), channel_id=1, source_target_pairs={{0,32},{8,136},{16,48},{24,152},{32,0},{40,168},{48,16},{56,184},{... | collective-permute-start | bytes 294920 | tf_op jit(solution)/shard_map/ppermute | solution.py:563
  69.4 8.8 %collective-permute-start.5 = (f32[64,384]{1,0:T(8,128)S(1)}, f32[64,384]{1,0:T(8,128)S(1)}, u32[]{:S(2)}, u32[]{:S(2)}) collective-permute-start(f32[64,384]{1,0:T(8,128)S(1)} %add_add_fusion.1), channel_id=1, source_target_pairs={{0,16},{8,72},{16,0},{24,88},{32,48},{40,104},{48,32},{56,120},{64... | collective-permute-start | bytes 294920 | tf_op jit(solution)/shard_map/ppermute | solution.py:563
  72.1 11.7 %all-to-all-start.4 = ((f32[8,8,1024]{2,1,0:T(8,128)}), f32[8,8,1024]{2,1,0:T(8,128)S(1)}, u32[]{:S(2)}, u32[]{:S(2)}) async-start(f32[8,8,1024]{2,1,0:T(8,128)} %factor_share.1), calls=%async_computation.4 | async-start | bytes 524288 | tf_op jit(solution)/shard_map/all_to_all | solution.py:499
  78.2 3.3 %collective-permute-start.8 = (f32[32,384]{1,0:T(8,128)S(1)}, f32[32,384]{1,0:T(8,128)S(1)}, u32[]{:S(2)}, u32[]{:S(2)}) collective-permute-start(f32[32,384]{1,0:T(8,128)S(1)} %fusion.1.mine_ref), channel_id=1, source_target_pairs={{0,8},{8,0},{16,24},{24,16},{32,40},{40,32},{48,56},{56,48},{64,72... | collective-permute-start | bytes 147464 | tf_op jit(solution)/shard_map/ppermute | solution.py:567

commit v14 on v12

--- a/solution.py
+++ b/solution.py
@@ -199,9 +199,10 @@
     for t in range(4):
         part = gram[:, 128 * t : 128 * (t + 1)]
         if at > 0:
-            acc[t] += part
+            acc[t, : part.shape[0], :] += part
         else:
-            acc[t] = part + half_rows(score_ref, half, slice(None)) if t == 3 else part
+            start = part + half_rows(score_ref, half, slice(None)) if t == 3 else part
+            acc[t, : part.shape[0], :] = start
     if at + CHUNK == pred_ref.shape[1]:
         for chip in range(16):
             for t in range(4):
@@ -250,7 +251,7 @@
 def gram_sums(live, core, tot, rest, design, score):
     genes, cells = rest.shape
     packed = jax.ShapeDtypeStruct((16, 48, 128), F32)
-    acc = pltpu.VMEM((4, genes // 2, 128), F32)
+    acc = pltpu.VMEM((4, 256, 128), F32)
     pred, hi, lo, given = pl.pallas_call(
         given_kernel,
         in_specs=[smem(), smem(), vmem(), vmem(), vmem(), vmem()],

time: 86 us -> 86 us (level)
  no operation moved by 1% of the time
where the time goes in v14:
time: 86 us; the launch traced here: 84.6 us
  starting transfers between devices  34.4 us (40%)
  blocking collectives  25.6 us (30%)
  Pallas kernels  14.3 us (17%)
  waiting for transfers between devices  8.74 us (10%)
  between operations  1.43 us (2%)
    all_to_all x2, blocking collectives, exchange(): lax.all_to_all(value, axis, split_axis=0, concat_axis=0, tiled=True, axis...  25.6 us
    all_to_all x3, starting transfers between devices, exchange(): lax.all_to_all(value, axis, split_axis=0, concat_axis=0, tiled=True, axis...  23.6 us
    ppermute x6, starting transfers between devices, local(): lax.ppermute(value, 'cell', pairs)  6.68 us
    ppermute x6, waiting for transfers between devices, local(): lax.ppermute(value, 'cell', pairs)  4.29 us
    pallas_call x1, Pallas kernels, prepare(): pl.pallas_call(prepare_kernel, in_specs=[smem()] + [hbm()] * len(arrays),...  3.41 us
    all_to_all x3, waiting for transfers between devices, exchange(): lax.all_to_all(value, axis, split_axis=0, concat_axis=0, tiled=True, axis...  2.61 us
    pallas_call x1, Pallas kernels, update(): pl.pallas_call(update_kernel, in_specs=[smem(), smem()] + [vmem()] * 7, o...  2.58 us
    ppermute x1, starting transfers between devices, local(): other = lax.ppermute(mine, 'cell', OTHER_CORE)  2.39 us
  transfers between devices with their start and end apart: 12, of which 6 were waited for; matrix products, arithmetic and copies ran while one was open for 0% of the time, Pallas kernels for 7%

profile of v14, /device:TPU:1, one launch (start us, length us, event | category | flops | bytes accessed | tf_op | source)
XLA Modules:
  0.0 84.6 jit_solution(5392023576705197701)
XLA Ops:
  0.6 2.3 %cell_totals.1 = f32[8,8,128]{2,1,0:T(8,128)} custom-call(s32[384,1024]{1,0:T(8,128)} %counts_hbm.1), custom_call_target="tpu_custom_call" | custom-call | tf_op jit(solution)/shard_map/cell_totals/pallas_call | solution.py:87
  2.9 10.6 %all-to-all-start = ((f32[8,8,128]{2,1,0:T(8,128)}), f32[8,8,128]{2,1,0:T(8,128)S(1)}, u32[]{:S(2)}, u32[]{:S(2)}) async-start(f32[8,8,128]{2,1,0:T(8,128)} %cell_totals.1), calls=%async_computation | async-start | bytes 65536 | tf_op jit(solution)/shard_map/all_to_all | solution.py:500
  14.1 3.4 %prepare.1 = (f32[384,1024]{1,0:T(8,128)S(1)}, bf16[96,1024]{1,0:T(8,128)(2,1)S(1)}, f32[384,128]{1,0:T(8,128)S(1)}, f32[64,1024]{1,0:T(8,128)S(1)}, f32[64,384]{1,0:T(8,128)S(1)}) custom-call(s32[1]{0:T(128)S(6)} %copy.17.live_ref, s32[384,1024]{1,0:T(8,128)} %counts_hbm.1, s32[1,1024]{1,0:T(1,128)} %bitcast.25, f32[1,1024]{1,0:T(1,128)} %bitcast.26, ...), custom_call_target="tpu_custom_call" | custom-call | tf_op jit(solution)/shard_map/prepare/pallas_call | solution.py:167
  17.5 0.0 all-to-all-done.tot_ref
  17.5 1.6 %gram_given.1 = (f32[384,1024]{1,0:T(8,128)S(1)}, bf16[512,1024]{1,0:T(8,128)(2,1)S(1)}, bf16[512,1024]{1,0:T(8,128)(2,1)S(1)}, f32[16,48,128]{2,1,0:T(8,128)S(1)}) custom-call(s32[1]{0:T(128)S(6)} %copy.17.live_ref, s32[1]{0:T(128)S(6)} %sub.3.half_ref, f32[8,8,128]{2,1,0:T(8,128)S(1)} %all-to-all-done.tot_ref, f32[384,1024]{1,0:T(8,128)S(1)} %get-tuple-element.16.rest_ref, ...), custom_call_target="tpu_custom_call" | custom-call | tf_op jit(solution)/shard_map/gram_given/pallas_call | solution.py:255
  19.1 1.0 %collective-permute-start = (f32[16,48,128]{2,1,0:T(8,128)S(1)}, f32[16,48,128]{2,1,0:T(8,128)S(1)}, u32[]{:S(2)}, u32[]{:S(2)}) collective-permute-start(f32[16,48,128]{2,1,0:T(8,128)S(1)} %get-tuple-element.22), channel_id=1, source_target_pairs={{0,8},{8,0},{16,24},{24,16},{32,40},{40,32},{48,56},{56,48},{64,72... | collective-permute-start | bytes 1179656 | tf_op jit(solution)/shard_map/ppermute | solution.py:269
  20.2 1.3 %gram_kept.1 = f32[16,48,128]{2,1,0:T(8,128)S(1)} custom-call(s32[1]{0:T(128)S(6)} %copy.17.live_ref, s32[1]{0:T(128)} %bitcast.half_ref.core_ref, f32[384,1024]{1,0:T(8,128)S(1)} %get-tuple-element.19.pred_ref, f32[384,128]{1,0:T(8,128)S(1)} %get-tuple-element.18.score_ref, bf16[512,1024]{1,0:T(8,128)(2,1)S(1)} %get-tuple-element.20.hi_ref, ...), custom_call_target="tpu_custom_call" | custom-call | tf_op jit(solution)/shard_map/gram_kept/pallas_call | solution.py:270
  21.5 0.0 copy-start
  21.5 0.0 copy-start.1
  21.5 0.0 collective-permute-done
  21.6 13.5 %all_to_all.25.parts_ref = f32[16,48,128]{2,1,0:T(8,128)S(1)} all-to-all(f32[16,48,128]{2,1,0:T(8,128)S(1)} %add.35), channel_id=1, replica_groups={{224,32,160,208,240,16,48,96,144,176,192,0,80,112,128,64},{232,40,168,2..., dimensions={0} | all-to-all | bytes 786432 | tf_op jit(solution)/shard_map/all_to_all | solution.py:500
  35.0 1.0 %solve.1 = f32[32,1,384]{2,1,0:T(1,128)S(1)} custom-call(f32[16,48,128]{2,1,0:T(8,128)S(1)} %all_to_all.25.parts_ref), custom_call_target="tpu_custom_call" | custom-call | tf_op jit(solution)/shard_map/solve/pallas_call | solution.py:328
  36.0 12.1 %all_to_all.26 = f32[32,1,384]{2,1,0:T(1,128)S(1)} all-to-all(f32[32,1,384]{2,1,0:T(1,128)S(1)} %solve.1), channel_id=1, replica_groups={{224,32,160,208,240,16,48,96,144,176,192,0,80,112,128,64,232,40,168,216..., dimensions={0} | all-to-all | bytes 98304 | tf_op jit(solution)/shard_map/all_to_all | solution.py:500
  48.1 0.0 copy-done
  48.1 0.0 copy-done.1
  48.2 2.6 %update.1 = (f32[8,16,1024]{2,1,0:T(8,128)}, f32[64,384]{1,0:T(8,128)S(1)}, f32[64,384]{1,0:T(8,128)S(1)}, f32[32,384]{1,0:T(8,128)}) custom-call(s32[1]{0:T(128)S(6)} %copy.17.live_ref, s32[1]{0:T(128)} %bitcast.half_ref.core_ref, f32[32,384]{1,0:T(8,128)S(1)} %bitcast.18, f32[384,1024]{1,0:T(8,128)S(1)} %get-tuple-element.19.pred_ref, ...), custom_call_target="tpu_custom_call" | custom-call | tf_op jit(solution)/shard_map/update/pallas_call | solution.py:402
  50.7 7.0 %all-to-all-start.3 = ((f32[8,16,1024]{2,1,0:T(8,128)}), f32[8,16,1024]{2,1,0:T(8,128)S(1)}, u32[]{:S(2)}, u32[]{:S(2)}) async-start(f32[8,16,1024]{2,1,0:T(8,128)} %get-tuple-element.26), calls=%async_computation.3 | async-start | bytes 1048576 | tf_op jit(solution)/shard_map/all_to_all | solution.py:500
  57.8 0.7 collective-permute-start.1
  58.5 0.9 %collective-permute-done.1 = f32[64,384]{1,0:T(8,128)S(1)} collective-permute-done((f32[64,384]{1,0:T(8,128)S(1)}, f32[64,384]{1,0:T(8,128)S(1)}, u32[]{:S(2)}, u32[]{:S(2)}) %collective-permute-start.1) | collective-permute-done | bytes 98336 | tf_op jit(solution)/shard_map/ppermute | solution.py:559
  59.4 2.4 %collective-permute-start.4 = (f32[64,384]{1,0:T(8,128)S(1)}, f32[64,384]{1,0:T(8,128)S(1)}, u32[]{:S(2)}, u32[]{:S(2)}) collective-permute-start(f32[64,384]{1,0:T(8,128)S(1)} %add.36), channel_id=1, source_target_pairs={{0,192},{8,56},{16,208},{24,40},{32,224},{40,24},{48,240},{56,8},{... | collective-permute-start | bytes 294920 | tf_op jit(solution)/shard_map/ppermute | solution.py:561
  61.8 0.7 collective-permute-start.3
  62.5 0.3 collective-permute-start.2
  62.8 1.7 %collective-permute-done.4 = f32[64,384]{1,0:T(8,128)S(1)} collective-permute-done((f32[64,384]{1,0:T(8,128)S(1)}, f32[64,384]{1,0:T(8,128)S(1)}, u32[]{:S(2)}, u32[]{:S(2)}) %collective-permute-start.4) | collective-permute-done | bytes 98336 | tf_op jit(solution)/shard_map/ppermute | solution.py:561
  64.5 2.6 %collective-permute-done.3 = f32[64,384]{1,0:T(8,128)S(1)} collective-permute-done((f32[64,384]{1,0:T(8,128)S(1)}, f32[64,384]{1,0:T(8,128)S(1)}, u32[]{:S(2)}, u32[]{:S(2)}) %collective-permute-start.3) | collective-permute-done | bytes 98336 | tf_op jit(solution)/shard_map/ppermute | solution.py:561
  67.0 0.0 collective-permute-done.2
  67.1 2.1 %collective-permute-start.7 = (f32[64,384]{1,0:T(8,128)S(1)}, f32[64,384]{1,0:T(8,128)S(1)}, u32[]{:S(2)}, u32[]{:S(2)}) collective-permute-start(f32[64,384]{1,0:T(8,128)S(1)} %add_add_fusion.1), channel_id=1, source_target_pairs={{0,48},{8,200},{16,32},{24,216},{32,16},{40,232},{48,0},{56,248},{... | collective-permute-start | bytes 294920 | tf_op jit(solution)/shard_map/ppermute | solution.py:561
  69.2 0.2 collective-permute-start.6
  69.4 1.0 %collective-permute-start.5 = (f32[64,384]{1,0:T(8,128)S(1)}, f32[64,384]{1,0:T(8,128)S(1)}, u32[]{:S(2)}, u32[]{:S(2)}) collective-permute-start(f32[64,384]{1,0:T(8,128)S(1)} %add_add_fusion.1), channel_id=1, source_target_pairs={{0,16},{8,72},{16,0},{24,88},{32,48},{40,104},{48,32},{56,120},{64... | collective-permute-start | bytes 294920 | tf_op jit(solution)/shard_map/ppermute | solution.py:561
  70.4 0.9 %all-to-all-done.3.parts_ref = f32[8,16,1024]{2,1,0:T(8,128)S(1)} async-done(((f32[8,16,1024]{2,1,0:T(8,128)}), f32[8,16,1024]{2,1,0:T(8,128)S(1)}, u32[]{:S(2)}, u32[]{:S(2)}) %all-to-all-start.3) | async-done | bytes 524320 | tf_op jit(solution)/shard_map/all_to_all | solution.py:500
  71.3 0.8 factor_share.1
  72.1 6.0 %all-to-all-start.4 = ((f32[8,8,1024]{2,1,0:T(8,128)}), f32[8,8,1024]{2,1,0:T(8,128)S(1)}, u32[]{:S(2)}, u32[]{:S(2)}) async-start(f32[8,8,1024]{2,1,0:T(8,128)} %factor_share.1), calls=%async_computation.4 | async-start | bytes 524288 | tf_op jit(solution)/shard_map/all_to_all | solution.py:500
  78.1 0.0 collective-permute-done.7
  78.1 0.0 collective-permute-done.6
  78.1 0.0 collective-permute-done.5
  78.2 2.4 %collective-permute-start.8 = (f32[32,384]{1,0:T(8,128)S(1)}, f32[32,384]{1,0:T(8,128)S(1)}, u32[]{:S(2)}, u32[]{:S(2)}) collective-permute-start(f32[32,384]{1,0:T(8,128)S(1)} %fusion.1.mine_ref), channel_id=1, source_target_pairs={{0,8},{8,0},{16,24},{24,16},{32,40},{40,32},{48,56},{56,48},{64,72... | collective-permute-start | bytes 147464 | tf_op jit(solution)/shard_map/ppermute | solution.py:565
  80.6 0.9 %collective-permute-done.8.other_ref = f32[32,384]{1,0:T(8,128)S(1)} collective-permute-done((f32[32,384]{1,0:T(8,128)S(1)}, f32[32,384]{1,0:T(8,128)S(1)}, u32[]{:S(2)}, u32[]{:S(2)}) %collective-permute-start.8) | collective-permute-done | bytes 49184 | tf_op jit(solution)/shard_map/ppermute | solution.py:565
  81.5 0.7 joined_score.1
  82.1 1.7 %all-to-all-done.4.value_ref = f32[8,8,1024]{2,1,0:T(8,128)S(1)} async-done(((f32[8,8,1024]{2,1,0:T(8,128)}), f32[8,8,1024]{2,1,0:T(8,128)S(1)}, u32[]{:S(2)}, u32[]{:S(2)}) %all-to-all-start.4) | async-done | bytes 262176 | tf_op jit(solution)/shard_map/all_to_all | solution.py:500
  83.8 0.8 settled.1
  (6 shorter events, 0.1 us)
Async XLA Ops:
  2.9 14.7 %all-to-all-start = ((f32[8,8,128]{2,1,0:T(8,128)}), f32[8,8,128]{2,1,0:T(8,128)S(1)}, u32[]{:S(2)}, u32[]{:S(2)}) async-start(f32[8,8,128]{2,1,0:T(8,128)} %cell_totals.1), calls=%async_computation | async-start | bytes 65536 | tf_op jit(solution)/shard_map/all_to_all | solution.py:500
  19.1 2.4 %collective-permute-start = (f32[16,48,128]{2,1,0:T(8,128)S(1)}, f32[16,48,128]{2,1,0:T(8,128)S(1)}, u32[]{:S(2)}, u32[]{:S(2)}) collective-permute-start(f32[16,48,128]{2,1,0:T(8,128)S(1)} %get-tuple-element.22), channel_id=1, source_target_pairs={{0,8},{8,0},{16,24},{24,16},{32,40},{40,32},{48,56},{56,48},{64,72... | collective-permute-start | bytes 1179656 | tf_op jit(solution)/shard_map/ppermute | solution.py:269
  21.5 26.7 %copy-start = (bf16[1024,64]{0,1:T(8,128)(2,1)S(1)}, bf16[1024,64]{0,1:T(8,128)(2,1)}, u32[]{:S(2)}) copy-start(bf16[1024,64]{0,1:T(8,128)(2,1)} %param.18) | copy-start | bytes 393220
  21.5 26.7 %copy-start.1 = (bf16[384,64]{0,1:T(8,128)(2,1)S(1)}, bf16[384,64]{0,1:T(8,128)(2,1)}, u32[]{:S(2)}) copy-start(bf16[384,64]{0,1:T(8,128)(2,1)} %param.19) | copy-start | bytes 147460
  50.7 20.6 %all-to-all-start.3 = ((f32[8,16,1024]{2,1,0:T(8,128)}), f32[8,16,1024]{2,1,0:T(8,128)S(1)}, u32[]{:S(2)}, u32[]{:S(2)}) async-start(f32[8,16,1024]{2,1,0:T(8,128)} %get-tuple-element.26), calls=%async_computation.3 | async-start | bytes 1048576 | tf_op jit(solution)/shard_map/all_to_all | solution.py:500
  57.8 1.6 %collective-permute-start.1 = (f32[64,384]{1,0:T(8,128)S(1)}, f32[64,384]{1,0:T(8,128)S(1)}, u32[]{:S(2)}, u32[]{:S(2)}) collective-permute-start(f32[64,384]{1,0:T(8,128)S(1)} %get-tuple-element.28), channel_id=1, source_target_pairs={{0,8},{8,0},{16,24},{24,16},{32,40},{40,32},{48,56},{56,48},{64,72... | collective-permute-start | bytes 294920 | tf_op jit(solution)/shard_map/ppermute | solution.py:559
  59.4 5.1 %collective-permute-start.4 = (f32[64,384]{1,0:T(8,128)S(1)}, f32[64,384]{1,0:T(8,128)S(1)}, u32[]{:S(2)}, u32[]{:S(2)}) collective-permute-start(f32[64,384]{1,0:T(8,128)S(1)} %add.36), channel_id=1, source_target_pairs={{0,192},{8,56},{16,208},{24,40},{32,224},{40,24},{48,240},{56,8},{... | collective-permute-start | bytes 294920 | tf_op jit(solution)/shard_map/ppermute | solution.py:561
  61.8 5.3 %collective-permute-start.3 = (f32[64,384]{1,0:T(8,128)S(1)}, f32[64,384]{1,0:T(8,128)S(1)}, u32[]{:S(2)}, u32[]{:S(2)}) collective-permute-start(f32[64,384]{1,0:T(8,128)S(1)} %add.36), channel_id=1, source_target_pairs={{0,128},{8,40},{16,144},{24,56},{32,160},{40,8},{48,176},{56,24},{... | collective-permute-start | bytes 294920 | tf_op jit(solution)/shard_map/ppermute | solution.py:561
  62.5 4.6 %collective-permute-start.2 = (f32[64,384]{1,0:T(8,128)S(1)}, f32[64,384]{1,0:T(8,128)S(1)}, u32[]{:S(2)}, u32[]{:S(2)}) collective-permute-start(f32[64,384]{1,0:T(8,128)S(1)} %add.36), channel_id=1, source_target_pairs={{0,64},{8,24},{16,80},{24,8},{32,96},{40,56},{48,112},{56,40},{64,... | collective-permute-start | bytes 294920 | tf_op jit(solution)/shard_map/ppermute | solution.py:561
  67.1 11.0 %collective-permute-start.7 = (f32[64,384]{1,0:T(8,128)S(1)}, f32[64,384]{1,0:T(8,128)S(1)}, u32[]{:S(2)}, u32[]{:S(2)}) collective-permute-start(f32[64,384]{1,0:T(8,128)S(1)} %add_add_fusion.1), channel_id=1, source_target_pairs={{0,48},{8,200},{16,32},{24,216},{32,16},{40,232},{48,0},{56,248},{... | collective-permute-start | bytes 294920 | tf_op jit(solution)/shard_map/ppermute | solution.py:561
  69.2 8.9 %collective-permute-start.6 = (f32[64,384]{1,0:T(8,128)S(1)}, f32[64,384]{1,0:T(8,128)S(1)}, u32[]{:S(2)}, u32[]{:S(2)}) collective-permute-start(f32[64,384]{1,0:T(8,128)S(1)} %add_add_fusion.1), channel_id=1, source_target_pairs={{0,32},{8,136},{16,48},{24,152},{32,0},{40,168},{48,16},{56,184},{... | collective-permute-start | bytes 294920 | tf_op jit(solution)/shard_map/ppermute | solution.py:561
  69.4 8.7 %collective-permute-start.5 = (f32[64,384]{1,0:T(8,128)S(1)}, f32[64,384]{1,0:T(8,128)S(1)}, u32[]{:S(2)}, u32[]{:S(2)}) collective-permute-start(f32[64,384]{1,0:T(8,128)S(1)} %add_add_fusion.1), channel_id=1, source_target_pairs={{0,16},{8,72},{16,0},{24,88},{32,48},{40,104},{48,32},{56,120},{64... | collective-permute-start | bytes 294920 | tf_op jit(solution)/shard_map/ppermute | solution.py:561
  72.1 11.7 %all-to-all-start.4 = ((f32[8,8,1024]{2,1,0:T(8,128)}), f32[8,8,1024]{2,1,0:T(8,128)S(1)}, u32[]{:S(2)}, u32[]{:S(2)}) async-start(f32[8,8,1024]{2,1,0:T(8,128)} %factor_share.1), calls=%async_computation.4 | async-start | bytes 524288 | tf_op jit(solution)/shard_map/all_to_all | solution.py:500
  78.2 3.3 %collective-permute-start.8 = (f32[32,384]{1,0:T(8,128)S(1)}, f32[32,384]{1,0:T(8,128)S(1)}, u32[]{:S(2)}, u32[]{:S(2)}) collective-permute-start(f32[32,384]{1,0:T(8,128)S(1)} %fusion.1.mine_ref), channel_id=1, source_target_pairs={{0,8},{8,0},{16,24},{24,16},{32,40},{40,32},{48,56},{56,48},{64,72... | collective-permute-start | bytes 147464 | tf_op jit(solution)/shard_map/ppermute | solution.py:565
